TPU v7x, 128 devices: a whole 4x4x4 slice. The times are simulated.
128 devices in a mesh: dp: 4 (over y), context: 4 (over z), tensor: 8 (over x, core).
Axes of the slice: x: 4, y: 4, z: 4, core: 2. Of those that a mesh axis runs over, the one named last changes fastest.
Arguments:
- panels: bfloat16 [4, 4, 65, 32, 512], P('dp', 'context', None, None, 'tensor'), may hold values from -6 to 6
- lengths: int32 [4, 4], P('dp'), may hold values from 1 to 65, as said below
- segments: int32 [4, 4096], P('dp', ('context', 'tensor')), may hold values from 0 to 7, never falling along the last dimension, each value on 1 to 1024 neighbouring positions
- front_weight: bfloat16 [512, 1536], P('tensor'), may hold values from -0.25 to 0.25
- conv_kernel: float32 [5, 1536], replicated, may hold values from -2 to 2
- gain: float32 [1536], replicated, may hold values from 0.25 to 1.75
- up_weight: bfloat16 [1536, 6144], P(None, 'tensor'), may hold values from -0.15625 to 0.15625
- down_weight: bfloat16 [6144, 1536], P('tensor'), may hold values from -0.078125 to 0.078125
- cotangent: bfloat16 [4, 4096, 1536], P('dp', ('context', 'tensor')), may hold values from -0.1875 to 0.1875
Outputs:
- grad_front: float32 [512, 1536], P('tensor')
- grad_kernel: float32 [5, 1536], replicated
- grad_gain: float32 [1536], replicated
- grad_up: float32 [1536, 6144], P(None, 'tensor')
- grad_down: float32 [6144, 1536], P('tensor')
Inputs may be any that keep to these rules, and one draw needn't show every extreme that they name: `lengths`: each stream's counts sum to 128; in every stream one loader shard, which one varies, holds exactly 65 panels and every other shard one or more; slots past a shard's count are not used. `segments`: document numbers never fall along a stream; each document spans 1 to 1024 frames.
All inputs are finite; a program needn't handle non-finite values.
Results may differ from a plain program's by a relative error of at most 0.007.
Values may be sent and summed in bfloat16 or wider, within the bound.
No kernel may reach another device: no remote copies, remote signals or barrier semaphores. Data moves between devices by JAX's collectives and lax.ppermute only.
A program may use at most 128 MiB of HBM per device.

v0:
```python
import jax
import jax.numpy as jnp
from jax import lax
from jax.sharding import PartitionSpec as P


def extended(value, sides, width):
    for axis, dim in sides:
        count, length = (lax.axis_size(axis), value.shape[dim])
        up = [(i, (i + 1) % count) for i in range(count - 1)]
        down = [(j, i) for i, j in up]
        last = lax.slice_in_dim(value, length - width, length, axis=dim)
        first = lax.slice_in_dim(value, 0, width, axis=dim)
        before = lax.ppermute(last, axis, up)
        after = lax.ppermute(first, axis, down)
        value = jnp.concatenate([before, value, after], axis=dim)
    return value


def contract_rows(left, right):
    return lax.dot_general(
        left, right, (((0,), (0,)), ((), ())), preferred_element_type=jnp.float32
    )


def contract_cols(left, right):
    return lax.dot_general(
        left, right, (((1,), (1,)), ((), ())), preferred_element_type=jnp.float32
    )


def per_device(
    panels, lengths, segments, front_weight, conv_kernel, gain, up_weight, down_weight, cotangent
):
    tensor_size = lax.axis_size("tensor")
    context_size = lax.axis_size("context")
    owner_index = lax.axis_index("context")
    rows_dev = cotangent.shape[1]
    rows_own = rows_dev * tensor_size
    panel_rows = panels.shape[3]
    per_owner = rows_own // panel_rows
    slots = panels.shape[2]
    feat_local = panels.shape[4]
    held_counts = lengths[0]
    starts = jnp.cumsum(held_counts) - held_counts
    wanted = owner_index * per_owner + jnp.arange(per_owner, dtype=jnp.int32)
    source = jnp.sum((starts[None, :] <= wanted[:, None]).astype(jnp.int32), axis=1) - 1
    collected = lax.all_gather(panels[0], "context", axis=0, tiled=True)
    flattened = collected.reshape(context_size * slots, panel_rows, feat_local)
    received = flattened[source * slots + wanted - starts[source]]
    feature_rows = received.reshape(rows_own, feat_local)
    part = feature_rows
    frames = lax.psum_scatter(
        jnp.dot(part, front_weight, preferred_element_type=jnp.float32),
        "tensor",
        scatter_dimension=0,
        tiled=True,
    ).astype(jnp.bfloat16)
    seg_local = segments[0] + 1
    segment_ext = extended(seg_local, ((("context", "tensor"), 0),), 2)
    same = [
        (segment_ext[j : j + rows_dev] == seg_local).astype(jnp.float32)[:, None] for j in range(5)
    ]
    frame_ext = extended(frames, ((("context", "tensor"), 0),), 2)
    frames_wide = frames.astype(jnp.float32)
    mixed = frames_wide
    for j in range(5):
        mixed = mixed + conv_kernel[j] * same[j] * frame_ext[j : j + rows_dev].astype(jnp.float32)
    center = mixed - jnp.mean(mixed, axis=1, keepdims=True)
    rstd = lax.rsqrt(jnp.mean(center * center, axis=1, keepdims=True) + 1e-05)
    normed = center * rstd
    ln_out = (normed * gain).astype(jnp.bfloat16)
    grad_out = cotangent[0]
    ln_full, grad_full = (
        lax.all_gather(ln_out, "tensor", axis=0, tiled=True),
        lax.all_gather(grad_out, "tensor", axis=0, tiled=True),
    )
    pre = jnp.dot(ln_full, up_weight, preferred_element_type=jnp.float32)
    sig = jax.nn.sigmoid(pre)
    hidden = (pre * sig).astype(jnp.bfloat16)
    down_local = 0.5 * contract_rows(hidden, grad_full)
    dhid = contract_cols(grad_full, down_weight)
    dpre = (0.5 * dhid * sig * (1.0 + pre * (1.0 - sig))).astype(jnp.bfloat16)
    up_local = contract_rows(ln_full, dpre)
    grad_up, grad_down = lax.psum((up_local, down_local), ("dp", "context"))
    part = dpre
    dln = lax.psum_scatter(
        contract_cols(part, up_weight), "tensor", scatter_dimension=0, tiled=True
    )
    gain_local = jnp.sum(dln * normed, axis=0)
    dnorm = dln * gain
    dmixed = grad_out.astype(jnp.float32) + rstd * (
        dnorm
        - jnp.mean(dnorm, axis=1, keepdims=True)
        - normed * jnp.mean(dnorm * normed, axis=1, keepdims=True)
    )
    dmixed = dmixed.astype(jnp.bfloat16)
    grad_ext = extended(dmixed, ((("context", "tensor"), 0),), 2)
    dwide = dmixed.astype(jnp.float32)
    kernel_rows = [
        jnp.sum(dwide * same[j] * frame_ext[j : j + rows_dev].astype(jnp.float32), axis=0)
        for j in range(5)
    ]
    kernel_local = jnp.stack(kernel_rows)
    dframes = dwide
    for j in range(5):
        dframes = dframes + conv_kernel[j] * same[4 - j] * grad_ext[
            4 - j : 4 - j + rows_dev
        ].astype(jnp.float32)
    dframes = dframes.astype(jnp.bfloat16)
    grad_kernel, grad_gain = lax.psum((kernel_local, gain_local), ("dp", "context", "tensor"))
    part = feature_rows
    front_local = contract_rows(part, lax.all_gather(dframes, "tensor", axis=0, tiled=True))
    grad_front = lax.psum(front_local, ("dp", "context"))
    return (grad_front, grad_kernel, grad_gain, grad_up, grad_down)


def solution(mesh):
    return jax.shard_map(
        per_device,
        mesh=mesh,
        in_specs=(
            P("dp", "context", None, None, "tensor"),
            P("dp", None),
            P("dp", ("context", "tensor")),
            P("tensor", None),
            P(),
            P(),
            P(None, "tensor"),
            P("tensor", None),
            P("dp", ("context", "tensor"), None),
        ),
        out_specs=(P("tensor", None), P(), P(), P(None, "tensor"), P("tensor", None)),
        check_vma=False,
    )
```

profile of v0, /device:TPU:0, one launch (start us, length us, event | category | flops | bytes accessed | tf_op | source)
XLA Modules:
  0.0 442.2 jit_solution(10423819770553807727)
XLA Ops:
  7.2 0.0 copy-start
  7.2 0.0 all-gather.11.cloned.1.call-start
  7.2 0.7 all-gather.11.cloned.1.call-update
  7.9 0.0 reduce-scatter.3.cloned.1.call-start
  8.0 0.8 reduce-window.4
  8.8 0.7 bitcast_subtract_fusion
  9.5 0.6 fusion.36
  10.1 0.7 fusion.28
  10.7 0.1 convert_reduce_fusion
  10.8 2.6 fusion.26
  13.4 29.8 %all-gather.11.cloned.1.call-done = bf16[4,1,65,32,64]{2,4,3,1,0:T(8,128)(2,1)} async-done(((bf16[1,1,65,32,64]{2,4,3,1,0:T(8,128)(2,1)}), bf16[4,1,65,32,64]{2,4,3,1,0:T(8,128)(2,1)}) %all-gather.11.cloned.1.call-update) | async-done | bytes 1064976 | tf_op jit(solution)/shard_map/all_gather | solution.py:48
  43.2 5.6 %copy.21 = bf16[4,1,65,32,64]{4,3,2,0,1:T(8,128)(2,1)} copy(bf16[4,1,65,32,64]{2,4,3,1,0:T(8,128)(2,1)} %all-gather.11.cloned.1.call-done) | data formatting | bytes 2129920 | tf_op jit(solution)/shard_map/reshape | solution.py:49
  48.9 2.2 gather_fusion
  51.1 3.6 fusion.37
  54.7 0.0 reduce-scatter.3.cloned.1.call-update
  54.7 0.0 all-gather.7.cloned.1.call-start
  54.8 0.6 copy-done.8
  55.3 0.1 slice_bitcast_fusion.1
  55.4 1.7 collective-permute-start
  57.2 1.3 collective-permute-start.2
  58.5 0.1 slice_reduce_fusion.4
  58.6 2.9 collective-permute-done.2
  61.4 0.1 pad_add_fusion
  61.5 35.7 %reduce-scatter.3.cloned.1.call-done = f32[128,1536]{1,0:T(8,128)} async-done(((f32[1024,1536]{1,0:T(8,128)}), f32[128,1536]{1,0:T(8,128)}) %reduce-scatter.3.cloned.1.call-update) | async-done | bytes 786448 | tf_op jit(solution)/shard_map/reduce_scatter | solution.py:53
  97.1 1.2 convert_element_type.75
  98.4 1.3 collective-permute-start.1
  99.7 1.3 collective-permute-start.3
  101.0 0.1 compare_convert_fusion.2
  101.0 1.7 collective-permute-done.3
  102.7 0.8 fusion.32
  103.5 0.2 multiply_reduce_fusion.2
  103.8 0.9 multiply_convert_fusion.3
  104.7 0.0 all-gather.7.cloned.1.call-update
  104.7 0.0 all-gather.13.cloned.1.call-start
  104.8 0.5 all-gather.13.cloned.1.call-update
  105.3 0.0 reduce-scatter.5.cloned.1.call-start
  105.4 33.8 %all-gather.7.cloned.1.call-done = bf16[1024,1536]{1,0:T(8,128)(2,1)} async-done(((bf16[128,1536]{1,0:T(8,128)(2,1)}), bf16[1024,1536]{1,0:T(8,128)(2,1)}) %all-gather.7.cloned.1.call-update) | async-done | bytes 3145744 | tf_op jit(solution)/shard_map/all_gather | solution.py:75
  139.2 6.2 %fusion.38 = f32[1024,768]{1,0:T(8,128)} fusion(bf16[1024,1536]{1,0:T(8,128)(2,1)} %all-gather.7.cloned.1.call-done, bf16[1536,768]{1,0:T(8,128)(2,1)S(1)} %copy-done), kind=kOutput, calls=%fused_computation.104 | convolution fusion | flops 2415919104 | bytes 8650752 | tf_op jit(solution)/shard_map/dot_general | solution.py:78
  145.4 23.2 %all-gather.13.cloned.1.call-done = bf16[1,1024,1536]{2,1,0:T(8,128)(2,1)} async-done(((bf16[1,128,1536]{2,1,0:T(8,128)(2,1)}), bf16[1,1024,1536]{2,1,0:T(8,128)(2,1)}) %all-gather.13.cloned.1.call-update) | async-done | bytes 3145744 | tf_op jit(solution)/shard_map/all_gather | solution.py:76
  168.5 6.7 %multiply_convert_fusion.1 = bf16[1024,768]{1,0:T(8,128)(2,1)S(1)} fusion(f32[1024,768]{1,0:T(8,128)} %fusion.38, bf16[768,1536]{1,0:T(8,128)(2,1)} %param.16, bf16[1,1024,1536]{2,1,0:T(8,128)(2,1)} %all-gather.13.cloned.1.call-done), kind=kOutput, calls=%fused_computation.6 | convolution fusion | flops 2423783424 | bytes 10223616 | tf_op jit(solution)/shard_map/dot_general | solution.py:27
  175.2 1.2 copy-done.10
  176.4 4.6 %fusion.39 = f32[1024,1536]{1,0:T(8,128)} fusion(bf16[1024,768]{1,0:T(8,128)(2,1)S(1)} %multiply_convert_fusion.1, bf16[1536,768]{1,0:T(8,128)(2,1)S(1)} %copy-done), kind=kOutput, calls=%fused_computation.105 | convolution fusion | flops 2415919104 | bytes 10223616 | tf_op jit(solution)/shard_map/dot_general | solution.py:27
  181.0 0.0 reduce-scatter.5.cloned.1.call-update
  181.0 0.0 all-gather.9.cloned.1.call-start
  181.1 42.6 %reduce-scatter.5.cloned.1.call-done = f32[128,1536]{1,0:T(8,128)} async-done(((f32[1024,1536]{1,0:T(8,128)}), f32[128,1536]{1,0:T(8,128)}) %reduce-scatter.5.cloned.1.call-update) | async-done | bytes 786448 | tf_op jit(solution)/shard_map/reduce_scatter | solution.py:87
  223.6 1.4 multiply_reduce_fusion
  225.1 2.3 fusion.13
  227.4 1.3 collective-permute-start.4
  228.7 3.0 collective-permute-start.5
  231.7 0.8 collective-permute-done.5
  232.5 1.6 fusion.18
  234.1 0.0 all-gather.9.cloned.1.call-update
  234.2 0.2 all-reduce.4.cloned.1.call-start
  234.4 7.4 %fusion.41 = f32[1536,768]{1,0:T(8,128)} fusion(bf16[1024,1536]{1,0:T(8,128)(2,1)} %all-gather.7.cloned.1.call-done, bf16[1024,768]{1,0:T(8,128)(2,1)} %copy-done.10), kind=kOutput, calls=%fused_computation.107 | convolution fusion | flops 2415919104 | bytes 9437184 | tf_op jit(solution)/shard_map/dot_general | solution.py:21
  241.8 4.3 convolution_multiply_fusion
  246.1 20.0 %all-gather.9.cloned.1.call-done = bf16[1024,1536]{1,0:T(8,128)(2,1)} async-done(((bf16[128,1536]{1,0:T(8,128)(2,1)}), bf16[1024,1536]{1,0:T(8,128)(2,1)}) %all-gather.9.cloned.1.call-update) | async-done | bytes 3145744 | tf_op jit(solution)/shard_map/all_gather | solution.py:113
  266.1 3.3 fusion.40
  269.5 0.0 all-reduce.4.cloned.1.call-update
  269.6 0.1 stack.23
  269.6 68.6 %all-reduce = (f32[5,1536]{1,0:T(8,128)}, f32[1536]{0:T(1024)}) all-reduce(f32[5,1536]{1,0:T(8,128)S(1)} %stack.23, f32[1536]{0:T(1024)S(1)} %get-tuple-element.5), channel_id=1, replica_groups=mesh['dp'=4,'context'=4,'tensor'=8] {'dp','context','tensor'}, use_global_device_ids=true, to_apply=%region_14.15 | all-reduce | flops 9216 | bytes 73728 | tf_op jit(solution)/shard_map/psum | solution.py:111
  338.2 88.1 %all-reduce.4.cloned.1.call-done = (f32[64,1536]{1,0:T(8,128)}, f32[1536,768]{1,0:T(8,128)}, f32[768,1536]{1,0:T(8,128)}) async-done(((f32[64,1536]{1,0:T(8,128)}, f32[1536,768]{1,0:T(8,128)}, f32[768,1536]{1,0:T(8,128)}), (f32[64,1536]{1,0:T(8,128)}, f32[1536,768]{1,0:T(8,128)}, f32[768,1536]{1,0:T(8,128)})) %all-reduce.4.cloned.1.call-update) | async-done | bytes 9830416 | tf_op jit(solution)/shard_map/psum | solution.py:114
  426.3 1.9 copy.26
  428.2 5.0 %copy.27 = f32[1536,768]{1,0:T(8,128)} copy(f32[1536,768]{1,0:T(8,128)} %get-tuple-element.53) | data formatting | bytes 9437184
  433.2 2.2 copy.28
  (42 shorter events, 0.2 us)
Async XLA Ops:
  7.2 132.0 %copy-start = (bf16[1536,768]{1,0:T(8,128)(2,1)S(1)}, bf16[1536,768]{1,0:T(8,128)(2,1)}, u32[]{:S(2)}) copy-start(bf16[1536,768]{1,0:T(8,128)(2,1)} %param.15) | copy-start | bytes 7077892
  7.2 43.9 %copy-start.5 = (bf16[64,1536]{1,0:T(8,128)(2,1)S(1)}, bf16[64,1536]{1,0:T(8,128)(2,1)}, u32[]{:S(2)}) copy-start(bf16[64,1536]{1,0:T(8,128)(2,1)} %param.12) | copy-start | bytes 589828
  7.2 36.1 %all-gather.11.cloned.1.call-start = ((), (), s32[]{:S(2)}) async-start(), calls=%async_computation.6 | async-start | bytes 2621440 | tf_op jit(solution)/shard_map/all_gather | solution.py:48
  7.9 89.2 %reduce-scatter.3.cloned.1.call-start = ((), (), s32[]{:S(2)}) async-start(), calls=%async_computation.2 | async-start | bytes 7077888 | tf_op jit(solution)/shard_map/reduce_scatter | solution.py:53
  54.7 0.7 copy-start.8
  54.7 3.8 copy-start.7
  54.7 49.1 %copy-start.6 = (f32[1536]{0:T(1024)S(1)}, f32[1536]{0:T(1024)}, u32[]{:S(2)}) copy-start(f32[1536]{0:T(1024)} %param.14) | copy-start | bytes 18436
  54.7 84.5 %all-gather.7.cloned.1.call-start = ((), (), s32[]{:S(2)}) async-start(), calls=%async_computation.3 | async-start | bytes 3538944 | tf_op jit(solution)/shard_map/all_gather | solution.py:75
  55.4 3.1 collective-permute-start
  57.2 4.3 collective-permute-start.2
  98.3 4.4 copy-start.2
  98.4 2.7 collective-permute-start.1
  99.7 3.1 collective-permute-start.3
  104.7 63.8 %all-gather.13.cloned.1.call-start = ((), (), s32[]{:S(2)}) async-start(), calls=%async_computation.7 | async-start | bytes 3538944 | tf_op jit(solution)/shard_map/all_gather | solution.py:76
  105.3 118.3 %reduce-scatter.5.cloned.1.call-start = ((), (), s32[]{:S(2)}) async-start(), calls=%async_computation.4 | async-start | bytes 7077888 | tf_op jit(solution)/shard_map/reduce_scatter | solution.py:87
  175.2 1.2 copy-start.10
  181.0 44.1 %copy-start.3 = (bf16[128,1536]{1,0:T(8,128)(2,1)S(1)}, bf16[128,1536]{1,0:T(8,128)(2,1)}, u32[]{:S(2)}) copy-start(bf16[128,1536]{1,0:T(8,128)(2,1)} %copy-done.2) | copy-start | bytes 1179652
  181.0 44.1 %copy-start.4 = (bf16[1,128,1536]{2,1,0:T(8,128)(2,1)S(1)}, bf16[1,128,1536]{2,1,0:T(8,128)(2,1)}, u32[]{:S(2)}) copy-start(bf16[1,128,1536]{2,1,0:T(8,128)(2,1)} %param.17) | copy-start | bytes 1179652
  181.0 85.1 %all-gather.9.cloned.1.call-start = ((), (), s32[]{:S(2)}) async-start(), calls=%async_computation.5 | async-start | bytes 3538944 | tf_op jit(solution)/shard_map/all_gather | solution.py:113
  227.4 4.3 collective-permute-start.4
  228.7 3.8 collective-permute-start.5
  234.2 192.1 %all-reduce.4.cloned.1.call-start = ((), (), s32[]{:S(2)}) async-start(), calls=%async_computation.8 | async-start | bytes 19660800 | tf_op jit(solution)/shard_map/psum | solution.py:114
  234.4 7.4 %copy-start.9 = (bf16[1,1024,1536]{2,1,0:T(8,128)(2,1)S(1)}, bf16[1,1024,1536]{2,1,0:T(8,128)(2,1)}, u32[]{:S(2)}) copy-start(bf16[1,1024,1536]{2,1,0:T(8,128)(2,1)} %all-gather.13.cloned.1.call-done) | copy-start | bytes 9437188
  234.4 7.4 %copy-start.11 = (f32[1024,768]{1,0:T(8,128)S(1)}, f32[1024,768]{1,0:T(8,128)}, u32[]{:S(2)}) copy-start(f32[1024,768]{1,0:T(8,128)} %fusion.38) | copy-start | bytes 9437188
  426.3 6.9 %slice-start = ((s8[4718592]{0:T(1024)(128)(4,1)}), s8[4194304]{0:T(1024)(128)(4,1)S(1)}, s32[]{:S(2)}) async-start(s8[4718592]{0:T(1024)(128)(4,1)} %bitcast.64), calls=%async_computation.9 | async-start | bytes 8388608
  428.2 5.0 %slice-start.1 = ((s8[4718592]{0:T(1024)(128)(4,1)}), s8[524288]{0:T(1024)(128)(4,1)S(1)}, s32[]{:S(2)}) async-start(s8[4718592]{0:T(1024)(128)(4,1)} %bitcast.64), calls=%async_computation.10 | async-start | bytes 1048576
  428.2 7.2 %copy-start.1 = (bf16[1536,768]{1,0:T(8,128)(2,1)S(1)}, bf16[1536,768]{1,0:T(8,128)(2,1)}, u32[]{:S(2)}) copy-start(bf16[1536,768]{1,0:T(8,128)(2,1)} %param.15) | copy-start | bytes 7077892
Sparse Core Ops, SparseCore 0:
  9.7 33.5 all-gather.10
  54.8 42.2 reduce-scatter.2
  104.8 34.2 all-gather.6
  140.7 27.7 all-gather.12
  181.1 42.4 reduce-scatter.4
  234.3 31.8 all-gather.8
  271.0 155.2 all-reduce.3
where the time goes:
time: 443 us; the launch traced here: 442 us
  waiting for transfers between devices  280 us (63%)
  blocking collectives  68.6 us (15%)
  matrix products  36 us (8%)
  local copies, waits for them, and re-layouts  19.6 us (4%)
  between operations  14.4 us (3%)
  other arithmetic  13.5 us (3%)
  starting transfers between devices  10.4 us (2%)
    psum x1, waiting for transfers between devices, per_device(): grad_front = lax.psum(front_local, ('dp', 'context'))  88.1 us
    psum x1, blocking collectives, per_device(): lax.psum((kernel_local, gain_local), ('dp', 'context', 'tensor'))  68.6 us
    reduce_scatter x1, waiting for transfers between devices, per_device(): lax.psum_scatter(contract_cols(part, up_weight), 'tensor', scatter_dimens...  42.6 us
    reduce_scatter x1, waiting for transfers between devices, per_device(): lax.psum_scatter(jnp.dot(part, front_weight, preferred_element_type=jnp.f...  35.7 us
    all_gather x1, waiting for transfers between devices, per_device(): lax.all_gather(ln_out, 'tensor', axis=0, tiled=True)  33.8 us
    all_gather x1, waiting for transfers between devices, per_device(): collected = lax.all_gather(panels[0], 'context', axis=0, tiled=True)  29.8 us
    all_gather x1, waiting for transfers between devices, per_device(): lax.all_gather(grad_out, 'tensor', axis=0, tiled=True)  23.2 us
    all_gather x1, waiting for transfers between devices, per_device(): lax.all_gather(dframes, 'tensor', axis=0, tiled=True)  20 us
  transfers between devices with their start and end apart: 13, of which 10 were waited for; matrix products, arithmetic and copies ran while one was open for 5% of the time, Pallas kernels for 0%

commit v1 on v0

v1 whole, which is shorter than its diff:
```python
import functools

import jax
import jax.numpy as jnp
from jax import lax
from jax.experimental import pallas as pl
from jax.experimental.pallas import tpu as pltpu
from jax.sharding import PartitionSpec as P

BF = jnp.bfloat16
F32 = jnp.float32
ORDER = (0, 2, 6, 4)
XOR3 = (1, 3, 2)
UNIT = 16
HALO = 16


def vmem(limit):
    return pltpu.CompilerParams(vmem_limit_bytes=limit << 20)


def cost(flops, nbytes, trans=0):
    return pl.CostEstimate(flops=flops, bytes_accessed=nbytes, transcendentals=trans)


def full(shape):
    return pl.BlockSpec(shape, lambda *_: (0,) * len(shape))


def xor_send(value, axis, mask, size):
    return lax.ppermute(value, axis, [(i, i ^ mask) for i in range(size)])


def select_kernel(scal, panel_ref, seg_ref, *outs):
    owner, start, count = scal[0], scal[1], scal[2]
    rows = 40
    slots = panel_ref.shape[2]
    q = lax.broadcasted_iota(jnp.int32, (rows, slots), 0)
    slot = lax.broadcasted_iota(jnp.int32, (rows, slots), 1)
    picks = []
    for e in range(4):
        base = 32 * (owner ^ e)
        wanted = jnp.where(q < 32, base + q, jnp.where(q == 32, base - 1, base + 32))
        inside = (q < 34) & (wanted >= 0) & (wanted < 128)
        local = wanted - start
        hit = inside & (local == slot) & (slot < count)
        picks.append(hit.astype(F32).astype(BF))
    pick = jnp.concatenate(picks, axis=0)
    scratch = outs[4]
    for i in range(UNIT):
        pair = jnp.concatenate([panel_ref[i], panel_ref[i + UNIT]], axis=0)
        got = lax.dot_general(
            pick, pair, (((1,), (1,)), ((), ())), preferred_element_type=F32
        )
        scratch[pl.ds(i, 4 * rows, stride=UNIT), :] = got
    seg_row = seg_ref[...].astype(F32) + 1.0
    for e in range(4):
        target = owner ^ e
        base = e * rows * UNIT
        if e == 0:
            scratch[pl.ds(base + 34 * UNIT, 1), :] = seg_row
        else:
            up = (target == owner + 1).astype(F32)
            down = (target == owner - 1).astype(F32)
            scratch[pl.ds(base + 35 * UNIT, 1), :] = seg_row * up
            scratch[pl.ds(base + 36 * UNIT, 1), :] = seg_row * down
    for e in range(4):
        outs[e][...] = scratch[pl.ds(e * rows * UNIT, rows * UNIT), :].astype(BF)


def select_panels(scal, panels_t, seg):
    return pl.pallas_call(
        select_kernel,
        out_shape=[jax.ShapeDtypeStruct((640, 128), BF)] * 4,
        in_specs=[
            pl.BlockSpec(memory_space=pltpu.SMEM),
            full(panels_t.shape),
            full(seg.shape),
        ],
        out_specs=[full((640, 128))] * 4,
        grid=(1,),
        scratch_shapes=[pltpu.VMEM((2560, 128), F32)],
        compiler_params=vmem(24),
        cost_estimate=cost(2 * 160 * 65 * 2048, 2 << 20),
    )(scal, panels_t, seg)


def norm_kernel(
    order, a_ref, b_ref, wa_ref, wb_ref, kern_ref, gain_ref,
    ln_ref, normed_ref, rstd_ref, frames_ref, segs_ref, stack_ref,
    units, weight, segs, wide, near_segs,
):
    step = pl.program_id(0)

    @pl.when(step == 0)
    def _():
        lane = lax.broadcasted_iota(jnp.int32, (256, 256), 0)
        out_lane = lax.broadcasted_iota(jnp.int32, (256, 256), 1)
        source = (out_lane // 64 % 2) * 128 + (out_lane // 128) * 64 + out_lane % 64
        swap = (lane == source).astype(F32).astype(BF)
        for d in range(4):
            weight[pl.ds(128 * d, 64), :] = wa_ref[d]
            weight[pl.ds(128 * d + 64, 64), :] = wb_ref[d]
            both = jnp.concatenate([a_ref[d, pl.ds(0, 544), :], b_ref[d, pl.ds(0, 544), :]], axis=1)
            mixed = jnp.dot(both, swap, preferred_element_type=F32).astype(BF)
            for p in range(34):
                at = p + 1 if p < 32 else (0 if p == 32 else 33)
                for half in range(2):
                    units[2 * at + half, :, pl.ds(128 * d, 128)] = mixed[
                        16 * p : 16 * p + 16, 128 * half : 128 * half + 128
                    ]
        eye = (
            lax.broadcasted_iota(jnp.int32, (128, 128), 0)
            == lax.broadcasted_iota(jnp.int32, (128, 128), 1)
        ).astype(F32)
        ones = jnp.ones((128, 128), BF)

        def column(ref, d, q):
            row = ref[d, pl.ds(q * UNIT, 16), :].astype(F32)[0:1]
            return jnp.dot((eye * row).astype(BF), ones, preferred_element_type=F32)

        for c in range(2):
            ref = (a_ref, b_ref)[c]
            for d in range(4):
                at = order[4 * c + d]
                segs[pl.ds(pl.multiple_of(HALO + 128 * at, 16), 128), :] = column(ref, d, 34)

                @pl.when(at == 7)
                def _():
                    segs[pl.ds(0, HALO), :] = column(ref, d, 35)[128 - HALO :]

                @pl.when(at == 0)
                def _():
                    segs[pl.ds(HALO + 1024, HALO), :] = column(ref, d, 36)[:HALO]

    block = order[step]
    unit0 = 8 * block + 1
    rows = units[pl.ds(unit0, 10)].reshape(160, 512)
    frames = jnp.dot(rows, weight[...], preferred_element_type=F32)
    wide[...] = frames.astype(BF).astype(F32)

    @pl.when(step == 0)
    def _():
        stack_ref[...] = rows
        frames_ref[...] = wide[...]
        segs_ref[...] = segs[pl.ds(pl.multiple_of(128 * block, 128), 160), :]

    taps = [kern_ref[pl.ds(j, 1), :] for j in range(5)]
    gain = gain_ref[...]
    near_segs[...] = segs[pl.ds(pl.multiple_of(128 * block, 128), 160), :]

    for r in range(0, 128, 16):
        here = near_segs[pl.ds(HALO + r, 16), :]
        mixed = (1.0 + taps[2]) * wide[pl.ds(HALO + r, 16), :]
        for j in (0, 1, 3, 4):
            same = (near_segs[pl.ds(HALO - 2 + r + j, 16), :] == here).astype(F32)
            same = jnp.concatenate([same] * 12, axis=1)
            mixed = mixed + taps[j] * (same * wide[pl.ds(HALO - 2 + r + j, 16), :])
        mean = jnp.mean(mixed, axis=1, keepdims=True)
        center = mixed - mean
        rstd = lax.rsqrt(jnp.mean(center * center, axis=1, keepdims=True) + 1e-05)
        normed = center * rstd
        ln_ref[pl.ds(r, 16), :] = (normed * gain).astype(BF)

        @pl.when(step == 0)
        def _():
            normed_ref[pl.ds(r, 16), :] = normed
            rstd_ref[pl.ds(r, 16), :] = jnp.broadcast_to(rstd, (16, 128))


def normalise(order, a, b, wa, wb, kern, gain):
    d_model = kern.shape[1]
    return pl.pallas_call(
        norm_kernel,
        grid_spec=pltpu.PrefetchScalarGridSpec(
            num_scalar_prefetch=1,
            grid=(8,),
            in_specs=[
                full(a.shape), full(b.shape), full(wa.shape), full(wb.shape),
                full(kern.shape), full(gain.shape),
            ],
            out_specs=[
                pl.BlockSpec((128, d_model), lambda i, o: (i, 0)),
                full((128, d_model)), full((128, 128)), full((160, d_model)),
                full((160, 128)), full((160, 512)),
            ],
            scratch_shapes=[
                pltpu.VMEM((68, 16, 512), BF),
                pltpu.VMEM((512, d_model), BF),
                pltpu.VMEM((1056, 128), F32),
                pltpu.VMEM((160, d_model), F32),
                pltpu.VMEM((160, 128), F32),
            ],
        ),
        out_shape=[
            jax.ShapeDtypeStruct((1024, d_model), BF),
            jax.ShapeDtypeStruct((128, d_model), F32),
            jax.ShapeDtypeStruct((128, 128), F32),
            jax.ShapeDtypeStruct((160, d_model), F32),
            jax.ShapeDtypeStruct((160, 128), F32),
            jax.ShapeDtypeStruct((160, 512), BF),
        ],
        compiler_params=vmem(40),
        cost_estimate=cost(2 * 1280 * 512 * 1536, 10 << 20),
    )(order, a, b, wa, wb, kern, gain)


def ffn_kernel(ln_ref, ca_ref, cb_ref, up_ref, down_ref, hid_ref, dpre_ref, dln_ref, cot, sem):
    step = pl.program_id(0)

    @pl.when(step == 0)
    def _():
        pltpu.make_async_copy(ca_ref, cot.at[0], sem.at[0]).start()
        pltpu.make_async_copy(cb_ref, cot.at[1], sem.at[1]).start()

    pre = jnp.dot(ln_ref[...], up_ref[...], preferred_element_type=F32)

    @pl.when(step == 0)
    def _():
        pltpu.make_async_copy(ca_ref, cot.at[0], sem.at[0]).wait()

    @pl.when(step == 1)
    def _():
        pltpu.make_async_copy(cb_ref, cot.at[1], sem.at[1]).wait()

    dhid = lax.dot_general(
        cot[step], down_ref[...], (((1,), (1,)), ((), ())), preferred_element_type=F32
    )
    sig = 1.0 / (1.0 + jnp.exp(-pre))
    hid_ref[...] = (pre * sig).astype(BF)
    dpre = (0.5 * dhid * sig * (1.0 + pre * (1.0 - sig))).astype(BF)
    dpre_ref[...] = dpre
    dln_ref[0] = lax.dot_general(
        dpre, up_ref[...], (((1,), (1,)), ((), ())), preferred_element_type=F32
    ).astype(BF)


def feed_forward(ln, ca, cb, up, down):
    rows, d_model = ln.shape
    ff = up.shape[1]
    half = rows // 2
    return pl.pallas_call(
        ffn_kernel,
        grid=(2,),
        in_specs=[
            pl.BlockSpec((half, d_model), lambda i: (i, 0)),
            pl.BlockSpec(memory_space=pl.ANY),
            pl.BlockSpec(memory_space=pl.ANY),
            full(up.shape), full(down.shape),
        ],
        out_specs=[
            pl.BlockSpec((half, ff), lambda i: (i, 0)),
            pl.BlockSpec((half, ff), lambda i: (i, 0)),
            pl.BlockSpec((1, half, d_model), lambda i: (i, 0, 0)),
        ],
        out_shape=[
            jax.ShapeDtypeStruct((rows, ff), BF),
            jax.ShapeDtypeStruct((rows, ff), BF),
            jax.ShapeDtypeStruct((2, half, d_model), BF),
        ],
        scratch_shapes=[pltpu.VMEM((2, half, d_model), BF), pltpu.SemaphoreType.DMA((2,))],
        compiler_params=vmem(48),
        cost_estimate=cost(6 * rows * d_model * ff, 24 << 20, rows * ff),
    )(ln, ca, cb, up, down)


def piece_code(pos, r, k):
    ry, rz = pos[0] ^ (r // 4), pos[1] ^ (r % 4)
    code = (
        (((ry & 1) ^ (ry >> 1)) << 3) | (((rz & 1) ^ (rz >> 1)) << 2) | ((ry >> 1) << 1) | (rz >> 1)
    )
    return ((code << k) | (code >> (4 - k))) & 15


def weight_kernel(k, pos, hid_ref, ca_ref, cb_ref, ln_ref, dpre_ref, keep_ref, send_ref, both):
    half = ca_ref.shape[0]
    rows = (((0,), (0,)), ((), ()))
    down = lax.dot_general(hid_ref[pl.ds(0, half), :], ca_ref[...], rows, preferred_element_type=F32)
    down += lax.dot_general(hid_ref[pl.ds(half, half), :], cb_ref[...], rows, preferred_element_type=F32)
    down = (0.5 * down).astype(BF)
    up = lax.dot_general(ln_ref[...], dpre_ref[...], rows, preferred_element_type=F32).astype(BF)
    for r in range(16):
        code = piece_code(pos, r, k)
        both[code, pl.ds(0, 48), :] = down[48 * r : 48 * r + 48]
        both[code, pl.ds(48, 48), :] = up[48 * r : 48 * r + 48]
    keep_ref[...] = both[pl.ds(0, 8)]
    send_ref[...] = both[pl.ds(8, 8)]


def weight_part(k, pos, hidden, ca, cb, ln, dpre):
    rows = hidden.shape[0]
    half = rows // 2
    return pl.pallas_call(
        functools.partial(weight_kernel, k),
        grid=(1,),
        in_specs=[
            pl.BlockSpec(memory_space=pltpu.SMEM),
            full((rows, 768)),
            pl.BlockSpec((half, 384), lambda i: (0, k)),
            pl.BlockSpec((half, 384), lambda i: (0, k)),
            pl.BlockSpec((rows, 768), lambda i: (0, k // 2)),
            pl.BlockSpec((rows, 384), lambda i: (0, k % 2)),
        ],
        out_specs=[full((8, 96, 384))] * 2,
        out_shape=[jax.ShapeDtypeStruct((8, 96, 384), BF)] * 2,
        scratch_shapes=[pltpu.VMEM((16, 96, 384), BF)],
        compiler_params=vmem(32),
        cost_estimate=cost(4 * rows * 768 * 384, 7 << 20),
    )(pos, hidden, ca, cb, ln, dpre)


def place_kernel(pos, *refs):
    ins, (down_ref, up_ref) = refs[:8], refs[8:]
    for k in range(4):

        @pl.when(pl.program_id(0) == k)
        def _():
            cur, rec = ins[2 * k], ins[2 * k + 1]
            for r in range(16):
                code = piece_code(pos, r, k)

                @pl.when(code < 8)
                def _():
                    down_ref[pl.ds(48 * r, 48), :] = cur[code, pl.ds(0, 48), :].astype(F32)
                    up_ref[pl.ds(48 * r, 48), :] = cur[code, pl.ds(48, 48), :].astype(F32)

                @pl.when(code >= 8)
                def _():
                    down_ref[pl.ds(48 * r, 48), :] = rec[code - 8, pl.ds(0, 48), :].astype(F32)
                    up_ref[pl.ds(48 * r, 48), :] = rec[code - 8, pl.ds(48, 48), :].astype(F32)


def place(pos, pieces):
    return pl.pallas_call(
        place_kernel,
        grid=(4,),
        in_specs=[pl.BlockSpec(memory_space=pltpu.SMEM)] + [full((8, 96, 384))] * 8,
        out_specs=[
            pl.BlockSpec((768, 384), lambda k: (0, k)),
            pl.BlockSpec((768, 384), lambda k: (k // 2, k % 2)),
        ],
        out_shape=[
            jax.ShapeDtypeStruct((768, 1536), F32),
            jax.ShapeDtypeStruct((1536, 768), F32),
        ],
        compiler_params=vmem(32),
        cost_estimate=cost(1 << 20, 14 << 20),
    )(pos, *pieces)


def tail_kernel(
    k0, r0, k1, r1, normed_ref, rstd_ref, frames_ref, segs_ref, stack_ref, cot_ref, kern_ref, gain_ref,
    keep_ref, send_ref, scaled, moved, sums,
):
    sums[...] = jnp.zeros_like(sums)
    taps = [kern_ref[pl.ds(j, 1), :] for j in range(5)]
    gain = gain_ref[...]
    wide_stack = stack_ref[...].astype(F32)
    for j in range(5):
        here = segs_ref[pl.ds(HALO, 128), :]
        same = (segs_ref[pl.ds(HALO - 2 + j, 128), :] == here).astype(F32)
        same = jnp.concatenate([same] * 4, axis=1)
        moved[pl.ds(128 * j, 128), :] = (same * wide_stack[HALO - 2 + j : HALO + 126 + j]).astype(BF)

    def fold(x):
        return x[0:8] + x[8:16]

    for r in range(0, 128, 16):
        at = pl.ds(r, 16)
        dln = jnp.concatenate(
            [k0[at, :].astype(F32) + r0[at, :].astype(F32), k1[at, :].astype(F32) + r1[at, :].astype(F32)], axis=1
        )
        normed = normed_ref[at, :]
        rstd = rstd_ref[at, :][:, 0:1]
        sums[5] += fold(dln * normed)
        dnorm = dln * gain
        m1 = jnp.mean(dnorm, axis=1, keepdims=True)
        m2 = jnp.mean(dnorm * normed, axis=1, keepdims=True)
        dmixed = cot_ref[at, :].astype(F32) + rstd * (dnorm - m1 - normed * m2)
        dmixed = dmixed.astype(BF).astype(F32)
        here = segs_ref[pl.ds(HALO + r, 16), :]
        for j in range(5):
            near = frames_ref[pl.ds(HALO - 2 + r + j, 16), :]
            tap = taps[j]
            if j == 2:
                tap = tap + 1.0
                sums[j] += fold(dmixed * near)
            else:
                same = (segs_ref[pl.ds(HALO - 2 + r + j, 16), :] == here).astype(F32)
                same = jnp.concatenate([same] * 12, axis=1)
                sums[j] += fold(dmixed * (same * near))
            scaled[pl.ds(128 * j + r, 16), :] = (tap * dmixed).astype(BF)

    front = lax.dot_general(
        moved[...], scaled[...], (((0,), (0,)), ((), ())), preferred_element_type=F32
    ).astype(BF)
    for d in range(4):
        keep_ref[pl.ds(64 * d, 64), :] = front[128 * d : 128 * d + 64]
        send_ref[pl.ds(64 * d, 64), :] = front[128 * d + 64 : 128 * d + 128]
    small = jnp.concatenate(
        [jnp.sum(sums[j], axis=0, keepdims=True) for j in range(6)] + [jnp.zeros((2, 1536), F32)], axis=0
    )
    high = small.astype(BF)
    low = (small - high.astype(F32)).astype(BF)
    pair = jnp.concatenate([high.astype(F32), low.astype(F32)], axis=0).astype(BF)
    keep_ref[pl.ds(256, 16), :] = pair
    send_ref[pl.ds(256, 16), :] = pair


def tail(pieces, normed, rstd, frames, segs, stack, cot, kern, gain):
    args = (*pieces, normed, rstd, frames, segs, stack, cot, kern, gain)
    return pl.pallas_call(
        tail_kernel,
        grid=(1,),
        in_specs=[full(a.shape) for a in args],
        out_specs=[full((272, 1536))] * 2,
        out_shape=[jax.ShapeDtypeStruct((272, 1536), BF)] * 2,
        scratch_shapes=[
            pltpu.VMEM((640, 1536), BF), pltpu.VMEM((640, 512), BF), pltpu.VMEM((6, 8, 1536), F32),
        ],
        compiler_params=vmem(32),
        cost_estimate=cost(2 * 640 * 512 * 1536, 6 << 20),
    )(*args)


def split_small(value):
    high = lax.reduce_precision(value, 8, 7)
    return jnp.concatenate([high.astype(BF), (value - high).astype(BF)], axis=0)


def add_rows(pieces, count):
    wide = [p.astype(F32) for p in pieces]
    main = [w[:count] for w in wide]
    small = [w[count : count + 8] + w[count + 8 :] for w in wide]
    if len(wide) == 4:
        pair = lambda v: (v[0] + v[1]) + (v[2] + v[3])
    else:
        pair = lambda v: v[0] + v[1]
    return pair(main), pair(small)


def pack_rows(main, small):
    return jnp.concatenate([main.astype(BF), split_small(small)], axis=0)


def gather_core(value):
    own = jnp.stack([value] + [xor_send(value, "tensor", m, 8) for m in ORDER[1:]])
    return own, xor_send(own, "tensor", 1, 8)


YZ = (("dp", 1), ("context", 1), ("dp", 3), ("context", 3))


def exchange_add(keeps, sends):
    cur, out = list(keeps), list(sends)
    for s in range(4):
        rec = [xor_send(out[k], *YZ[(k + s) % 4], 4) for k in range(4)]
        for k in range(4):
            total = cur[k].astype(F32) + rec[k].astype(F32)
            n = total.shape[0] // 2
            if s < 3:
                cur[k], out[k] = total[:n].astype(BF), total[n:].astype(BF)
            else:
                cur[k] = total.astype(BF)
    pieces = []
    for s in (3, 2, 1, 0):
        rec = [xor_send(cur[k], *YZ[(k + s) % 4], 4) for k in range(4)]
        if s == 0:
            for k in range(4):
                pieces += [cur[k], rec[k]]
        else:
            cur = [jnp.concatenate([cur[k], rec[k]], axis=0) for k in range(4)]
    return pieces


def per_device(
    panels, lengths, segments, front_weight, conv_kernel, gain, up_weight, down_weight, cotangent
):
    y, z, t = lax.axis_index("dp"), lax.axis_index("context"), lax.axis_index("tensor")
    counts = lengths[0]
    before = jnp.arange(4, dtype=jnp.int32) < z
    start = jnp.sum(jnp.where(before, counts, 0))
    count = jnp.sum(jnp.where(jnp.arange(4, dtype=jnp.int32) == z, counts, 0))
    scal = jnp.stack([z, start, count]).astype(jnp.int32)
    order = jnp.stack([t ^ m for m in ORDER] + [t ^ m ^ 1 for m in ORDER]).astype(jnp.int32)
    pos = jnp.stack([y, z]).astype(jnp.int32)
    gain_row = gain[None, :]
    cot = cotangent[0]

    wa, wb = gather_core(front_weight)
    picked = select_panels(scal, jnp.transpose(panels[0, 0], (1, 2, 0)), segments)
    got = [xor_send(picked[e], "context", e, 4) for e in (2, 1, 3)]
    block = picked[0] + got[0] + got[1] + got[2]
    pa, pb = gather_core(block)
    ca, cb = gather_core(cot)
    ca, cb = ca.reshape(512, -1), cb.reshape(512, -1)

    ln, normed, rstd, frames, segs, stack = normalise(order, pa, pb, wa, wb, conv_kernel, gain_row)
    hidden, dpre, dln = feed_forward(ln, ca, cb, up_weight, down_weight)

    dln_rec = xor_send(dln[1], "tensor", 1, 8)
    parts = [weight_part(k, pos, hidden, ca, cb, ln, dpre) for k in range(4)]
    summed = (dln[0].astype(F32) + dln_rec.astype(F32)).astype(BF).reshape(2, 2, 128, 1536)
    send0, send1 = summed[:, 1, :, :768], summed[1, :, :, 768:]
    rec0, rec1 = xor_send(send0, "tensor", 2, 8), xor_send(send1, "tensor", 6, 8)
    sum0 = summed[:, 0, :, :768].astype(F32) + rec0.astype(F32)
    sum1 = summed[0, :, :, 768:].astype(F32) + rec1.astype(F32)
    sum0, sum1 = sum0.astype(BF), sum1.astype(BF)
    end0, end1 = xor_send(sum0[1], "tensor", 6, 8), xor_send(sum1[1], "tensor", 2, 8)

    placed = exchange_add([p[0] for p in parts], [p[1] for p in parts])

    keep, send = tail(
        (sum0[0], end0, sum1[0], end1), normed, rstd, frames, segs, stack, cot, conv_kernel, gain_row
    )
    main, small = add_rows((keep, xor_send(send, "tensor", 1, 8)), 256)
    main = main.astype(BF).reshape(2, 2, 64, 1536)
    pair = split_small(small)

    def payload(blocks, side):
        cols = slice(768 * side, 768 * side + 768)
        return jnp.concatenate([b[..., cols].reshape(-1, 768) for b in blocks] + [pair[:, cols]], axis=0)

    keep0, keep1 = payload([main[:, 0]], 0), payload([main[0]], 1)
    rec0 = xor_send(payload([main[:, 1]], 0), "tensor", 2, 8)
    rec1 = xor_send(payload([main[1]], 1), "tensor", 6, 8)
    ends = []
    for keep_side, rec_side, mask in ((keep0, rec0, 6), (keep1, rec1, 2)):
        value, low = add_rows((keep_side, rec_side), 128)
        low = split_small(low)
        value = value.astype(BF)
        own = jnp.concatenate([value[:64], low], axis=0)
        away = jnp.concatenate([value[64:], low], axis=0)
        ends.append(add_rows((own, xor_send(away, "tensor", mask, 8)), 64))
    value = pack_rows(
        jnp.concatenate([e[0] for e in ends], axis=1), jnp.concatenate([e[1] for e in ends], axis=1)
    )
    for axis in ("context", "dp"):
        near, far, across = [xor_send(value, axis, m, 4) for m in XOR3]
        main, small = add_rows((value, across, near, far), 64)
        if axis == "context":
            value = pack_rows(main, small)
    grad_down, grad_up = place(pos, placed)
    return (main, small[:5], small[5], grad_up, grad_down)


def solution(mesh):
    return jax.shard_map(
        per_device,
        mesh=mesh,
        in_specs=(
            P("dp", "context", None, None, "tensor"),
            P("dp", None),
            P("dp", ("context", "tensor")),
            P("tensor", None),
            P(),
            P(),
            P(None, "tensor"),
            P("tensor", None),
            P("dp", ("context", "tensor"), None),
        ),
        out_specs=(P("tensor", None), P(), P(), P(None, "tensor"), P("tensor", None)),
        check_vma=False,
    )
```

time: 443 us -> 236 us (0.53)
  waiting for transfers between devices: 280 us -> 65.9 us
  starting transfers between devices: 10.4 us -> 87.4 us
  blocking collectives: 68.6 us -> 0 us
  Pallas kernels: 0 us -> 58.1 us
  matrix products: 36 us -> 0 us
  local copies, waits for them, and re-layouts: 19.6 us -> 7.3 us
  between operations: 14.4 us -> 2.1 us
    all_gather x4 -> x0, waiting for transfers between devices: 107 us -> none  [the longest x1 33.8 us: per_device(): lax.all_gather(ln_out, 'tensor', axis=0, tiled=True)]
    psum x1 -> x0, waiting for transfers between devices: 88.1 us -> none  [per_device(): grad_front = lax.psum(front_local, ('dp', 'context'))]
    reduce_scatter x2 -> x0, waiting for transfers between devices: 78.2 us -> none  [the longest x1 42.6 us: per_device(): lax.psum_scatter(contract_cols(part, up_weight), 'tensor', scatter_dimens...]
    ppermute x6 -> x63, starting transfers between devices: 9.93 us -> 87.4 us  [xor_send(): return lax.ppermute(value, axis, [(i, i ^ mask) for i in range(size)])]
    psum x1 -> x0, blocking collectives: 68.6 us -> none  [per_device(): lax.psum((kernel_local, gain_local), ('dp', 'context', 'tensor'))]
    ppermute x6 -> x63, waiting for transfers between devices: 5.34 us -> 65.9 us  [xor_send(): return lax.ppermute(value, axis, [(i, i ^ mask) for i in range(size)])]
    pallas_call x0 -> x9, Pallas kernels: none -> 58.1 us  [the longest x1 24.9 us: normalise(): pl.pallas_call(norm_kernel, grid_spec=pltpu.PrefetchScalarGridSpec(num_sc...]
    dot_general x7 -> x0, matrix products: 36 us -> none  [the longest x3 15 us: contract_rows(): lax.dot_general(left, right, (((0,), (0,)), ((), ())), preferred_element_...]
  transfers between devices with their start and end apart: 13 -> 63, of which waited for: 10 -> 26; matrix products, arithmetic and copies ran while one was open for 5% -> 5% of each run, Pallas kernels for 0% -> 17%
where the time goes in v1:
time: 236 us; the launch traced here: 231 us
  starting transfers between devices  87.4 us (37%)
  waiting for transfers between devices  65.9 us (28%)
  Pallas kernels  58.1 us (25%)
  other arithmetic  10.6 us (4%)
  local copies, waits for them, and re-layouts  7.3 us (3%)
    ppermute x63, starting transfers between devices, xor_send(): return lax.ppermute(value, axis, [(i, i ^ mask) for i in range(size)])  87.4 us
    ppermute x63, waiting for transfers between devices, xor_send(): return lax.ppermute(value, axis, [(i, i ^ mask) for i in range(size)])  65.9 us
    pallas_call x1, Pallas kernels, normalise(): pl.pallas_call(norm_kernel, grid_spec=pltpu.PrefetchScalarGridSpec(num_sc...  24.9 us
    pallas_call x1, Pallas kernels, feed_forward(): pl.pallas_call(ffn_kernel, grid=(2,), in_specs=[pl.BlockSpec((half, d_mod...  14.1 us
    pallas_call x4, Pallas kernels, weight_part(): pl.pallas_call(functools.partial(weight_kernel, k), grid=(1,), in_specs=[...  9.82 us
    unnamed x24, local copies, waits for them, and re-layouts  5.95 us
    pallas_call x1, Pallas kernels, place(): pl.pallas_call(place_kernel, grid=(4,), in_specs=[pl.BlockSpec(memory_spa...  5.14 us
  transfers between devices with their start and end apart: 63, of which 26 were waited for; matrix products, arithmetic and copies ran while one was open for 5% of the time, Pallas kernels for 17%

profile of v1, /device:TPU:0, one launch (start us, length us, event | category | flops | bytes accessed | tf_op | source)
XLA Modules:
  0.0 231.4 jit_solution(3355373464847308405)
XLA Ops:
  0.6 3.2 %collective-permute-start.13 = (bf16[128,1536]{1,0:T(8,128)(2,1)}, bf16[128,1536]{1,0:T(8,128)(2,1)S(1)}, u32[]{:S(2)}, u32[]{:S(2)}) collective-permute-start(bf16[128,1536]{1,0:T(8,128)(2,1)} %bitcast.85), channel_id=1, source_target_pairs={{0,4},{1,5},{2,6},{3,7},{4,0},{5,1},{6,2},{7,3},{8,12},{9,13},{10,... | collective-permute-start | bytes 1179656 | tf_op jit(solution)/shard_map/ppermute | solution.py:31
  6.3 1.4 pad_add_fusion.scal
  10.6 4.1 %collective-permute-start.2 = (bf16[640,128]{1,0:T(8,128)(2,1)S(1)}, bf16[640,128]{1,0:T(8,128)(2,1)S(1)}, u32[]{:S(2)}, u32[]{:S(2)}) collective-permute-start(bf16[640,128]{1,0:T(8,128)(2,1)S(1)} %get-tuple-element.33), channel_id=1, source_target_pairs={{0,24},{8,16},{16,8},{24,0},{1,25},{9,17},{17,9},{25,1},{2,26},{10... | collective-permute-start | bytes 491528 | tf_op jit(solution)/shard_map/ppermute | solution.py:31
  14.7 3.7 %collective-permute-start = (bf16[640,128]{1,0:T(8,128)(2,1)S(1)}, bf16[640,128]{1,0:T(8,128)(2,1)S(1)}, u32[]{:S(2)}, u32[]{:S(2)}) collective-permute-start(bf16[640,128]{1,0:T(8,128)(2,1)S(1)} %get-tuple-element.31), channel_id=1, source_target_pairs={{0,16},{8,24},{16,0},{24,8},{1,17},{9,25},{17,1},{25,9},{2,18},{10... | collective-permute-start | bytes 491528 | tf_op jit(solution)/shard_map/ppermute | solution.py:31
  18.4 3.1 %collective-permute-done.12 = bf16[128,1536]{1,0:T(8,128)(2,1)S(1)} collective-permute-done((bf16[128,1536]{1,0:T(8,128)(2,1)}, bf16[128,1536]{1,0:T(8,128)(2,1)S(1)}, u32[]{:S(2)}, u32[]{:S(2)}) %collective-permute-start.12) | collective-permute-done | bytes 393248 | tf_op jit(solution)/shard_map/ppermute | solution.py:31
  23.3 2.1 collective-permute-start.9
  25.4 2.0 collective-permute-start.8
  27.5 2.7 %collective-permute-start.5 = (bf16[640,128]{1,0:T(8,128)(2,1)S(1)}, bf16[640,128]{1,0:T(8,128)(2,1)S(1)}, u32[]{:S(2)}, u32[]{:S(2)}) collective-permute-start(bf16[640,128]{1,0:T(8,128)(2,1)S(1)} %add_add_fusion), channel_id=1, source_target_pairs={{0,4},{1,5},{2,6},{3,7},{4,0},{5,1},{6,2},{7,3},{8,12},{9,13},{10,... | collective-permute-start | bytes 491528 | tf_op jit(solution)/shard_map/ppermute | solution.py:31
  30.3 2.3 %collective-permute-done.9 = bf16[64,1536]{1,0:T(8,128)(2,1)S(1)} collective-permute-done((bf16[64,1536]{1,0:T(8,128)(2,1)S(1)}, bf16[64,1536]{1,0:T(8,128)(2,1)S(1)}, u32[]{:S(2)}, u32[]{:S(2)}) %collective-permute-start.9) | collective-permute-done | bytes 196640 | tf_op jit(solution)/shard_map/ppermute | solution.py:31
  32.6 2.6 %collective-permute-start.4 = (bf16[640,128]{1,0:T(8,128)(2,1)S(1)}, bf16[640,128]{1,0:T(8,128)(2,1)S(1)}, u32[]{:S(2)}, u32[]{:S(2)}) collective-permute-start(bf16[640,128]{1,0:T(8,128)(2,1)S(1)} %add_add_fusion), channel_id=1, source_target_pairs={{0,6},{1,7},{2,4},{3,5},{4,2},{5,3},{6,0},{7,1},{8,14},{9,15},{10,... | collective-permute-start | bytes 491528 | tf_op jit(solution)/shard_map/ppermute | solution.py:31
  35.2 1.6 collective-permute-done.8
  36.8 1.4 collective-permute-start.3
  40.0 3.4 %collective-permute-done.4 = bf16[640,128]{1,0:T(8,128)(2,1)S(1)} collective-permute-done((bf16[640,128]{1,0:T(8,128)(2,1)S(1)}, bf16[640,128]{1,0:T(8,128)(2,1)S(1)}, u32[]{:S(2)}, u32[]{:S(2)}) %collective-permute-start.4) | collective-permute-done | bytes 163872 | tf_op jit(solution)/shard_map/ppermute | solution.py:31
  44.7 2.2 collective-permute-done.6.b_ref
  46.9 24.9 %shard_map.129 = (bf16[1024,1536]{1,0:T(8,128)(2,1)S(1)}, f32[128,1536]{1,0:T(8,128)S(1)}, f32[128,128]{1,0:T(8,128)S(1)}, f32[160,1536]{1,0:T(8,128)S(1)}, f32[...) custom-call(s32[8]{0:T(128)S(1)} %stack.96.order, bf16[4,640,128]{2,1,0:T(8,128)(2,1)} %pad_maximum_fusion.2.a_ref, ...), custom_call_target="tpu_custom_call" | custom-call | flops 2013265920 | bytes 10485760 | tf_op jit(solution)/shard_map/pallas_call | solution.py:173
  71.8 1.7 copy-done
  74.6 14.1 %shard_map.130 = (bf16[1024,768]{1,0:T(8,128)(2,1)S(1)}, bf16[1024,768]{1,0:T(8,128)(2,1)S(1)}, bf16[2,512,1536]{2,1,0:T(8,128)(2,1)}) custom-call(bf16[1024,1536]{1,0:T(8,128)(2,1)} %copy-done, bf16[512,1536]{1,0:T(8,128)(2,1)S(1)} %bitcast.74, bf16[512,1536]{1,0:T(8,128)(2,1)} %bitcast.79, bf16[1536,768]{1,0:T(8,128)(2,1)} %up_ref.1, ...), custom_call_target="tpu_custom_call" | custom-call | flops 7247757312 | bytes 25165824 | tf_op jit(solution)/shard_map/pallas_call | solution.py:242
  88.8 1.4 copy-done.3
  90.1 2.5 %shard_map.132 = (bf16[8,96,384]{2,1,0:T(8,128)(2,1)S(1)}, bf16[8,96,384]{2,1,0:T(8,128)(2,1)S(1)}) custom-call(s32[2]{0:T(128)S(1)} %pad_add_fusion.1.pos, bf16[1024,768]{1,0:T(8,128)(2,1)S(1)} %get-tuple-element.43.hid_ref, bf16[512,1536]{1,0:T(8,128)(2,1)S(1)} %bitcast.75, bf16[512,1536]{1,0:T(8,128)(2,1)S(1)} %bitcast.80, ...), custom_call_target="tpu_custom_call" | custom-call | flops 1207959552 | bytes 7340032 | tf_op jit(solution)/shard_map/pallas_call | solution.py:293
  92.6 2.5 %shard_map.133 = (bf16[8,96,384]{2,1,0:T(8,128)(2,1)S(1)}, bf16[8,96,384]{2,1,0:T(8,128)(2,1)S(1)}) custom-call(s32[2]{0:T(128)S(1)} %pad_add_fusion.1.pos, bf16[1024,768]{1,0:T(8,128)(2,1)S(1)} %get-tuple-element.43.hid_ref, bf16[512,1536]{1,0:T(8,128)(2,1)S(1)} %bitcast.76, bf16[512,1536]{1,0:T(8,128)(2,1)S(1)} %bitcast.81, ...), custom_call_target="tpu_custom_call" | custom-call | flops 1207959552 | bytes 7340032 | tf_op jit(solution)/shard_map/pallas_call | solution.py:293
  95.1 1.7 collective-permute-start.31
  96.7 1.9 collective-permute-start.39
  98.8 2.5 %shard_map.134 = (bf16[8,96,384]{2,1,0:T(8,128)(2,1)S(1)}, bf16[8,96,384]{2,1,0:T(8,128)(2,1)S(1)}) custom-call(s32[2]{0:T(128)S(1)} %pad_add_fusion.1.pos, bf16[1024,768]{1,0:T(8,128)(2,1)S(1)} %get-tuple-element.43.hid_ref, bf16[512,1536]{1,0:T(8,128)(2,1)S(1)} %bitcast.77, bf16[512,1536]{1,0:T(8,128)(2,1)S(1)} %bitcast.82, ...), custom_call_target="tpu_custom_call" | custom-call | flops 1207959552 | bytes 7340032 | tf_op jit(solution)/shard_map/pallas_call | solution.py:293
  101.2 2.5 %collective-permute-start.47 = (bf16[8,96,384]{2,1,0:T(8,128)(2,1)S(1)}, bf16[8,96,384]{2,1,0:T(8,128)(2,1)S(1)}, u32[]{:S(2)}, u32[]{:S(2)}) collective-permute-start(bf16[8,96,384]{2,1,0:T(8,128)(2,1)S(1)} %get-tuple-element.50), channel_id=1, source_target_pairs={{0,96},{32,64},{64,32},{96,0},{1,97},{33,65},{65,33},{97,1},{2,98}... | collective-permute-start | bytes 1769480 | tf_op jit(solution)/shard_map/ppermute | solution.py:31
  103.7 2.5 %shard_map.135 = (bf16[8,96,384]{2,1,0:T(8,128)(2,1)S(1)}, bf16[8,96,384]{2,1,0:T(8,128)(2,1)S(1)}) custom-call(s32[2]{0:T(128)S(1)} %pad_add_fusion.1.pos, bf16[1024,768]{1,0:T(8,128)(2,1)S(1)} %get-tuple-element.43.hid_ref, bf16[512,1536]{1,0:T(8,128)(2,1)S(1)} %bitcast.78, bf16[512,1536]{1,0:T(8,128)(2,1)S(1)} %bitcast.83, ...), custom_call_target="tpu_custom_call" | custom-call | flops 1207959552 | bytes 7340032 | tf_op jit(solution)/shard_map/pallas_call | solution.py:293
  106.3 2.6 %collective-permute-start.55 = (bf16[8,96,384]{2,1,0:T(8,128)(2,1)S(1)}, bf16[8,96,384]{2,1,0:T(8,128)(2,1)S(1)}, u32[]{:S(2)}, u32[]{:S(2)}) collective-permute-start(bf16[8,96,384]{2,1,0:T(8,128)(2,1)S(1)} %get-tuple-element.52), channel_id=1, source_target_pairs={{0,24},{8,16},{16,8},{24,0},{1,25},{9,17},{17,9},{25,1},{2,26},{10... | collective-permute-start | bytes 1769480 | tf_op jit(solution)/shard_map/ppermute | solution.py:31
  108.9 1.7 collective-permute-done.31
  110.7 2.0 collective-permute-start.32
  112.9 3.1 %collective-permute-start.40 = (bf16[4,96,384]{2,1,0:T(8,128)(2,1)S(1)}, bf16[4,96,384]{2,1,0:T(8,128)(2,1)S(1)}, u32[]{:S(2)}, u32[]{:S(2)}) collective-permute-start(bf16[4,96,384]{2,1,0:T(8,128)(2,1)S(1)} %slice.529), channel_id=1, source_target_pairs={{0,96},{32,64},{64,32},{96,0},{1,97},{33,65},{65,33},{97,1},{2,98}... | collective-permute-start | bytes 884744 | tf_op jit(solution)/shard_map/ppermute | solution.py:31
  116.0 3.0 %collective-permute-done.47 = bf16[8,96,384]{2,1,0:T(8,128)(2,1)S(1)} collective-permute-done((bf16[8,96,384]{2,1,0:T(8,128)(2,1)S(1)}, bf16[8,96,384]{2,1,0:T(8,128)(2,1)S(1)}, u32[]{:S(2)}, u32[]{:S(2)}) %collective-permute-start.47) | collective-permute-done | bytes 589856 | tf_op jit(solution)/shard_map/ppermute | solution.py:31
  119.2 2.2 collective-permute-start.48
  121.4 2.3 collective-permute-done.55
  125.6 2.6 %collective-permute-start.41 = (bf16[2,96,384]{2,1,0:T(8,128)(2,1)S(1)}, bf16[2,96,384]{2,1,0:T(8,128)(2,1)S(1)}, u32[]{:S(2)}, u32[]{:S(2)}) collective-permute-start(bf16[2,96,384]{2,1,0:T(8,128)(2,1)S(1)} %slice.531), channel_id=1, source_target_pairs={{0,24},{8,16},{16,8},{24,0},{1,25},{9,17},{17,9},{25,1},{2,26},{10... | collective-permute-start | bytes 442376 | tf_op jit(solution)/shard_map/ppermute | solution.py:31
  128.2 2.2 collective-permute-done.48
  130.9 1.6 collective-permute-done.56
  133.4 2.3 collective-permute-start.34
  138.7 1.5 collective-permute-start.58
  140.1 2.8 %collective-permute-start.35 = (bf16[1,96,384]{2,1,0:T(8,128)(2,1)S(1)}, bf16[1,96,384]{2,1,0:T(8,128)(2,1)S(1)}, u32[]{:S(2)}, u32[]{:S(2)}) collective-permute-start(bf16[1,96,384]{2,1,0:T(8,128)(2,1)S(1)} %add_convert_fusion.15), channel_id=1, source_target_pairs={{0,24},{8,16},{16,8},{24,0},{1,25},{9,17},{17,9},{25,1},{2,26},{10... | collective-permute-start | bytes 221192 | tf_op jit(solution)/shard_map/ppermute | solution.py:31
  143.5 2.7 %collective-permute-start.18 = (bf16[2,128,768]{2,1,0:T(8,128)(2,1)S(1)}, bf16[2,128,768]{2,1,0:T(8,128)(2,1)S(1)}, u32[]{:S(2)}, u32[]{:S(2)}) collective-permute-start(bf16[2,128,768]{2,1,0:T(8,128)(2,1)S(1)} %slice_bitcast_fusion.3), channel_id=1, source_target_pairs={{0,6},{1,7},{2,4},{3,5},{4,2},{5,3},{6,0},{7,1},{8,14},{9,15},{10,... | collective-permute-start | bytes 1179656 | tf_op jit(solution)/shard_map/ppermute | solution.py:31
  146.4 1.5 collective-permute-start.59
  147.9 4.7 %collective-permute-done.18 = bf16[2,128,768]{2,1,0:T(8,128)(2,1)S(1)} collective-permute-done((bf16[2,128,768]{2,1,0:T(8,128)(2,1)S(1)}, bf16[2,128,768]{2,1,0:T(8,128)(2,1)S(1)}, u32[]{:S(2)}, u32[]{:S(2)}) %collective-permute-start.18) | collective-permute-done | bytes 393248 | tf_op jit(solution)/shard_map/ppermute | solution.py:31
  154.3 2.7 %collective-permute-start.17 = (bf16[128,768]{1,0:T(8,128)(2,1)S(1)}, bf16[128,768]{1,0:T(8,128)(2,1)S(1)}, u32[]{:S(2)}, u32[]{:S(2)}) collective-permute-start(bf16[128,768]{1,0:T(8,128)(2,1)S(1)} %get-tuple-element.73), channel_id=1, source_target_pairs={{0,6},{1,7},{2,4},{3,5},{4,2},{5,3},{6,0},{7,1},{8,14},{9,15},{10,... | collective-permute-start | bytes 589832 | tf_op jit(solution)/shard_map/ppermute | solution.py:31
  158.2 3.1 %collective-permute-done.17.r0 = bf16[128,768]{1,0:T(8,128)(2,1)S(1)} collective-permute-done((bf16[128,768]{1,0:T(8,128)(2,1)S(1)}, bf16[128,768]{1,0:T(8,128)(2,1)S(1)}, u32[]{:S(2)}, u32[]{:S(2)}) %collective-permute-start.17) | collective-permute-done | bytes 196640 | tf_op jit(solution)/shard_map/ppermute | solution.py:31
  161.3 3.1 %collective-permute-start.52 = (bf16[2,96,384]{2,1,0:T(8,128)(2,1)S(1)}, bf16[2,96,384]{2,1,0:T(8,128)(2,1)S(1)}, u32[]{:S(2)}, u32[]{:S(2)}) collective-permute-start(bf16[2,96,384]{2,1,0:T(8,128)(2,1)S(1)} %pad_maximum_fusion.26), channel_id=1, source_target_pairs={{0,32},{32,0},{64,96},{96,64},{1,33},{33,1},{65,97},{97,65},{2,34}... | collective-permute-start | bytes 442376 | tf_op jit(solution)/shard_map/ppermute | solution.py:31
  164.4 2.9 %shard_map.131 = (bf16[272,1536]{1,0:T(8,128)(2,1)S(1)}, bf16[272,1536]{1,0:T(8,128)(2,1)S(1)}) custom-call(bf16[128,768]{1,0:T(8,128)(2,1)S(1)} %get-tuple-element.74.k0, bf16[128,768]{1,0:T(8,128)(2,1)S(1)} %collective-permute-done.17.r0, bf16[128,768]{1,0:T(8,128)(2,1)S(1)} %get-tuple-element.72.k1, bf16[128,768]{1,0:T(8,128)(2,1)S(1)} %collective-permute-done.19.r1, ...), custom_call_target="tpu_custom_call" | custom-call | flops 1006632960 | bytes 6291456 | tf_op jit(solution)/shard_map/pallas_call | solution.py:412
  167.6 2.1 collective-permute-start.37
  169.7 1.6 collective-permute-start.45
  171.3 1.4 collective-permute-start.53
  172.7 1.5 collective-permute-done.60
  174.9 5.2 %collective-permute-done.37 = bf16[4,96,384]{2,1,0:T(8,128)(2,1)S(1)} collective-permute-done((bf16[4,96,384]{2,1,0:T(8,128)(2,1)S(1)}, bf16[4,96,384]{2,1,0:T(8,128)(2,1)S(1)}, u32[]{:S(2)}, u32[]{:S(2)}) %collective-permute-start.37) | collective-permute-done | bytes 294944 | tf_op jit(solution)/shard_map/ppermute | solution.py:31
  181.8 1.4 collective-permute-start.23
  183.5 6.3 %collective-permute-done.23 = bf16[144,768]{1,0:T(8,128)(2,1)S(1)} collective-permute-done((bf16[144,768]{1,0:T(8,128)(2,1)S(1)}, bf16[144,768]{1,0:T(8,128)(2,1)S(1)}, u32[]{:S(2)}, u32[]{:S(2)}) %collective-permute-start.23) | collective-permute-done | bytes 221216 | tf_op jit(solution)/shard_map/ppermute | solution.py:31
  190.8 1.7 collective-permute-start.22
  192.5 2.8 %collective-permute-done.24 = bf16[80,768]{1,0:T(8,128)(2,1)S(1)} collective-permute-done((bf16[80,768]{1,0:T(8,128)(2,1)S(1)}, bf16[80,768]{1,0:T(8,128)(2,1)S(1)}, u32[]{:S(2)}, u32[]{:S(2)}) %collective-permute-start.24) | collective-permute-done | bytes 122912 | tf_op jit(solution)/shard_map/ppermute | solution.py:31
  195.4 1.6 collective-permute-done.22
  197.1 1.4 collective-permute-start.27
  198.5 3.4 %collective-permute-start.25 = (bf16[80,1536]{1,0:T(8,128)(2,1)S(1)}, bf16[80,1536]{1,0:T(8,128)(2,1)S(1)}, u32[]{:S(2)}, u32[]{:S(2)}) collective-permute-start(bf16[80,1536]{1,0:T(8,128)(2,1)S(1)} %get-tuple-element.78), channel_id=1, source_target_pairs={{0,16},{8,24},{16,0},{24,8},{1,17},{9,25},{17,1},{25,9},{2,18},{10... | collective-permute-start | bytes 737288 | tf_op jit(solution)/shard_map/ppermute | solution.py:31
  202.2 6.0 %collective-permute-done.27 = bf16[80,1536]{1,0:T(8,128)(2,1)S(1)} collective-permute-done((bf16[80,1536]{1,0:T(8,128)(2,1)S(1)}, bf16[80,1536]{1,0:T(8,128)(2,1)S(1)}, u32[]{:S(2)}, u32[]{:S(2)}) %collective-permute-start.27) | collective-permute-done | bytes 245792 | tf_op jit(solution)/shard_map/ppermute | solution.py:31
  208.2 1.9 collective-permute-start.54
  210.5 3.6 %collective-permute-done.25 = bf16[80,1536]{1,0:T(8,128)(2,1)S(1)} collective-permute-done((bf16[80,1536]{1,0:T(8,128)(2,1)S(1)}, bf16[80,1536]{1,0:T(8,128)(2,1)S(1)}, u32[]{:S(2)}, u32[]{:S(2)}) %collective-permute-start.25) | collective-permute-done | bytes 245792 | tf_op jit(solution)/shard_map/ppermute | solution.py:31
  214.3 1.8 collective-permute-start.30
  217.2 4.2 %collective-permute-done.46.refs_3_ = bf16[8,96,384]{2,1,0:T(8,128)(2,1)S(1)} collective-permute-done((bf16[8,96,384]{2,1,0:T(8,128)(2,1)S(1)}, bf16[8,96,384]{2,1,0:T(8,128)(2,1)S(1)}, u32[]{:S(2)}, u32[]{:S(2)}) %collective-permute-start.46) | collective-permute-done | bytes 589856 | tf_op jit(solution)/shard_map/ppermute | solution.py:31
  221.4 2.1 collective-permute-start.28
  223.5 5.1 %shard_map.136 = (f32[768,1536]{1,0:T(8,128)}, f32[1536,768]{1,0:T(8,128)}) custom-call(s32[2]{0:T(128)S(1)} %pad_add_fusion.1.pos, bf16[8,96,384]{2,1,0:T(8,128)(2,1)S(1)} %pad_maximum_fusion.3.refs_0_, bf16[8,96,384]{2,1,0:T(8,128)(2,1)S(1)} %collective-permute-done.38.refs_1_, bf16[8,96,384]{2,1,0:T(8,128)(2,1)S(1)} %pad_maximum_fusion.4.refs_2_, ...), custom_call_target="tpu_custom_call" | custom-call | flops 1048576 | bytes 14680064 | tf_op jit(solution)/shard_map/pallas_call | solution.py:334
  (198 shorter events, 29.9 us)
Async XLA Ops:
  0.6 14.1 %collective-permute-start.13 = (bf16[128,1536]{1,0:T(8,128)(2,1)}, bf16[128,1536]{1,0:T(8,128)(2,1)S(1)}, u32[]{:S(2)}, u32[]{:S(2)}) collective-permute-start(bf16[128,1536]{1,0:T(8,128)(2,1)} %bitcast.85), channel_id=1, source_target_pairs={{0,4},{1,5},{2,6},{3,7},{4,0},{5,1},{6,2},{7,3},{8,12},{9,13},{10,... | collective-permute-start | bytes 1179656 | tf_op jit(solution)/shard_map/ppermute | solution.py:31
  3.8 17.8 %collective-permute-start.12 = (bf16[128,1536]{1,0:T(8,128)(2,1)}, bf16[128,1536]{1,0:T(8,128)(2,1)S(1)}, u32[]{:S(2)}, u32[]{:S(2)}) collective-permute-start(bf16[128,1536]{1,0:T(8,128)(2,1)} %bitcast.86), channel_id=1, source_target_pairs={{0,6},{1,7},{2,4},{3,5},{4,2},{5,3},{6,0},{7,1},{8,14},{9,15},{10,... | collective-permute-start | bytes 1179656 | tf_op jit(solution)/shard_map/ppermute | solution.py:31
  5.0 17.0 %collective-permute-start.11 = (bf16[128,1536]{1,0:T(8,128)(2,1)}, bf16[128,1536]{1,0:T(8,128)(2,1)S(1)}, u32[]{:S(2)}, u32[]{:S(2)}) collective-permute-start(bf16[128,1536]{1,0:T(8,128)(2,1)} %bitcast.87), channel_id=1, source_target_pairs={{0,2},{1,3},{2,0},{3,1},{4,6},{5,7},{6,4},{7,5},{8,10},{9,11},{10,... | collective-permute-start | bytes 1179656 | tf_op jit(solution)/shard_map/ppermute | solution.py:31
  10.6 14.8 %collective-permute-start.2 = (bf16[640,128]{1,0:T(8,128)(2,1)S(1)}, bf16[640,128]{1,0:T(8,128)(2,1)S(1)}, u32[]{:S(2)}, u32[]{:S(2)}) collective-permute-start(bf16[640,128]{1,0:T(8,128)(2,1)S(1)} %get-tuple-element.33), channel_id=1, source_target_pairs={{0,24},{8,16},{16,8},{24,0},{1,25},{9,17},{17,9},{25,1},{2,26},{10... | collective-permute-start | bytes 491528 | tf_op jit(solution)/shard_map/ppermute | solution.py:31
  14.7 12.8 %collective-permute-start.1 = (bf16[640,128]{1,0:T(8,128)(2,1)S(1)}, bf16[640,128]{1,0:T(8,128)(2,1)S(1)}, u32[]{:S(2)}, u32[]{:S(2)}) collective-permute-start(bf16[640,128]{1,0:T(8,128)(2,1)S(1)} %get-tuple-element.32), channel_id=1, source_target_pairs={{0,8},{8,0},{16,24},{24,16},{1,9},{9,1},{17,25},{25,17},{2,10},{10... | collective-permute-start | bytes 491528 | tf_op jit(solution)/shard_map/ppermute | solution.py:31
  14.7 12.8 %collective-permute-start = (bf16[640,128]{1,0:T(8,128)(2,1)S(1)}, bf16[640,128]{1,0:T(8,128)(2,1)S(1)}, u32[]{:S(2)}, u32[]{:S(2)}) collective-permute-start(bf16[640,128]{1,0:T(8,128)(2,1)S(1)} %get-tuple-element.31), channel_id=1, source_target_pairs={{0,16},{8,24},{16,0},{24,8},{1,17},{9,25},{17,1},{25,9},{2,18},{10... | collective-permute-start | bytes 491528 | tf_op jit(solution)/shard_map/ppermute | solution.py:31
  23.2 50.3 %collective-permute-start.14 = (bf16[4,128,1536]{2,1,0:T(8,128)(2,1)S(1)}, bf16[4,128,1536]{2,1,0:T(8,128)(2,1)S(1)}, u32[]{:S(2)}, u32[]{:S(2)}) collective-permute-start(bf16[4,128,1536]{2,1,0:T(8,128)(2,1)S(1)} %pad_maximum_fusion), channel_id=1, source_target_pairs={{0,1},{1,0},{2,3},{3,2},{4,5},{5,4},{6,7},{7,6},{8,9},{9,8},{10,11... | collective-permute-start | bytes 4718600 | tf_op jit(solution)/shard_map/ppermute | solution.py:31
  23.3 9.3 %collective-permute-start.9 = (bf16[64,1536]{1,0:T(8,128)(2,1)S(1)}, bf16[64,1536]{1,0:T(8,128)(2,1)S(1)}, u32[]{:S(2)}, u32[]{:S(2)}) collective-permute-start(bf16[64,1536]{1,0:T(8,128)(2,1)S(1)} %copy-done.9), channel_id=1, source_target_pairs={{0,4},{1,5},{2,6},{3,7},{4,0},{5,1},{6,2},{7,3},{8,12},{9,13},{10,... | collective-permute-start | bytes 589832 | tf_op jit(solution)/shard_map/ppermute | solution.py:31
  25.4 11.4 %collective-permute-start.8 = (bf16[64,1536]{1,0:T(8,128)(2,1)S(1)}, bf16[64,1536]{1,0:T(8,128)(2,1)S(1)}, u32[]{:S(2)}, u32[]{:S(2)}) collective-permute-start(bf16[64,1536]{1,0:T(8,128)(2,1)S(1)} %copy-done.9), channel_id=1, source_target_pairs={{0,6},{1,7},{2,4},{3,5},{4,2},{5,3},{6,0},{7,1},{8,14},{9,15},{10,... | collective-permute-start | bytes 589832 | tf_op jit(solution)/shard_map/ppermute | solution.py:31
  27.5 10.8 %collective-permute-start.7 = (bf16[64,1536]{1,0:T(8,128)(2,1)S(1)}, bf16[64,1536]{1,0:T(8,128)(2,1)S(1)}, u32[]{:S(2)}, u32[]{:S(2)}) collective-permute-start(bf16[64,1536]{1,0:T(8,128)(2,1)S(1)} %copy-done.9), channel_id=1, source_target_pairs={{0,2},{1,3},{2,0},{3,1},{4,6},{5,7},{6,4},{7,5},{8,10},{9,11},{10,... | collective-permute-start | bytes 589832 | tf_op jit(solution)/shard_map/ppermute | solution.py:31
  27.5 19.4 %copy-start.7 = (f32[5,1536]{1,0:T(8,128)S(1)}, f32[5,1536]{1,0:T(8,128)}, u32[]{:S(2)}) copy-start(f32[5,1536]{1,0:T(8,128)} %kern_ref.3) | copy-start | bytes 92164
  27.5 12.4 %collective-permute-start.5 = (bf16[640,128]{1,0:T(8,128)(2,1)S(1)}, bf16[640,128]{1,0:T(8,128)(2,1)S(1)}, u32[]{:S(2)}, u32[]{:S(2)}) collective-permute-start(bf16[640,128]{1,0:T(8,128)(2,1)S(1)} %add_add_fusion), channel_id=1, source_target_pairs={{0,4},{1,5},{2,6},{3,7},{4,0},{5,1},{6,2},{7,3},{8,12},{9,13},{10,... | collective-permute-start | bytes 491528 | tf_op jit(solution)/shard_map/ppermute | solution.py:31
  32.6 10.7 %collective-permute-start.4 = (bf16[640,128]{1,0:T(8,128)(2,1)S(1)}, bf16[640,128]{1,0:T(8,128)(2,1)S(1)}, u32[]{:S(2)}, u32[]{:S(2)}) collective-permute-start(bf16[640,128]{1,0:T(8,128)(2,1)S(1)} %add_add_fusion), channel_id=1, source_target_pairs={{0,6},{1,7},{2,4},{3,5},{4,2},{5,3},{6,0},{7,1},{8,14},{9,15},{10,... | collective-permute-start | bytes 491528 | tf_op jit(solution)/shard_map/ppermute | solution.py:31
  36.8 6.5 %collective-permute-start.3 = (bf16[640,128]{1,0:T(8,128)(2,1)S(1)}, bf16[640,128]{1,0:T(8,128)(2,1)S(1)}, u32[]{:S(2)}, u32[]{:S(2)}) collective-permute-start(bf16[640,128]{1,0:T(8,128)(2,1)S(1)} %add_add_fusion), channel_id=1, source_target_pairs={{0,2},{1,3},{2,0},{3,1},{4,6},{5,7},{6,4},{7,5},{8,10},{9,11},{10,... | collective-permute-start | bytes 491528 | tf_op jit(solution)/shard_map/ppermute | solution.py:31
  39.3 7.6 %collective-permute-start.10 = (bf16[4,64,1536]{2,1,0:T(8,128)(2,1)}, bf16[4,64,1536]{2,1,0:T(8,128)(2,1)}, u32[]{:S(2)}, u32[]{:S(2)}) collective-permute-start(bf16[4,64,1536]{2,1,0:T(8,128)(2,1)} %pad_maximum_fusion.1.wa_ref), channel_id=1, source_target_pairs={{0,1},{1,0},{2,3},{3,2},{4,5},{5,4},{6,7},{7,6},{8,9},{9,8},{10,11... | collective-permute-start | bytes 2359304 | tf_op jit(solution)/shard_map/ppermute | solution.py:31
  44.3 2.6 %collective-permute-start.6 = (bf16[4,640,128]{2,1,0:T(8,128)(2,1)}, bf16[4,640,128]{2,1,0:T(8,128)(2,1)}, u32[]{:S(2)}, u32[]{:S(2)}) collective-permute-start(bf16[4,640,128]{2,1,0:T(8,128)(2,1)} %pad_maximum_fusion.2.a_ref), channel_id=1, source_target_pairs={{0,1},{1,0},{2,3},{3,2},{4,5},{5,4},{6,7},{7,6},{8,9},{9,8},{10,11... | collective-permute-start | bytes 1966088 | tf_op jit(solution)/shard_map/ppermute | solution.py:31
  95.1 15.5 %collective-permute-start.31 = (bf16[8,96,384]{2,1,0:T(8,128)(2,1)S(1)}, bf16[8,96,384]{2,1,0:T(8,128)(2,1)S(1)}, u32[]{:S(2)}, u32[]{:S(2)}) collective-permute-start(bf16[8,96,384]{2,1,0:T(8,128)(2,1)S(1)} %get-tuple-element.46), channel_id=1, source_target_pairs={{0,32},{32,0},{64,96},{96,64},{1,33},{33,1},{65,97},{97,65},{2,34}... | collective-permute-start | bytes 1769480 | tf_op jit(solution)/shard_map/ppermute | solution.py:31
  96.7 16.0 %collective-permute-start.39 = (bf16[8,96,384]{2,1,0:T(8,128)(2,1)S(1)}, bf16[8,96,384]{2,1,0:T(8,128)(2,1)S(1)}, u32[]{:S(2)}, u32[]{:S(2)}) collective-permute-start(bf16[8,96,384]{2,1,0:T(8,128)(2,1)S(1)} %get-tuple-element.48), channel_id=1, source_target_pairs={{0,8},{8,0},{16,24},{24,16},{1,9},{9,1},{17,25},{25,17},{2,10},{10... | collective-permute-start | bytes 1769480 | tf_op jit(solution)/shard_map/ppermute | solution.py:31
  101.2 17.8 %collective-permute-start.47 = (bf16[8,96,384]{2,1,0:T(8,128)(2,1)S(1)}, bf16[8,96,384]{2,1,0:T(8,128)(2,1)S(1)}, u32[]{:S(2)}, u32[]{:S(2)}) collective-permute-start(bf16[8,96,384]{2,1,0:T(8,128)(2,1)S(1)} %get-tuple-element.50), channel_id=1, source_target_pairs={{0,96},{32,64},{64,32},{96,0},{1,97},{33,65},{65,33},{97,1},{2,98}... | collective-permute-start | bytes 1769480 | tf_op jit(solution)/shard_map/ppermute | solution.py:31
  106.2 36.9 %collective-permute-start.15 = (bf16[512,1536]{1,0:T(8,128)(2,1)S(1)}, bf16[512,1536]{1,0:T(8,128)(2,1)S(1)}, u32[]{:S(2)}, u32[]{:S(2)}) collective-permute-start(bf16[512,1536]{1,0:T(8,128)(2,1)S(1)} %slice_bitcast_fusion), channel_id=1, source_target_pairs={{0,1},{1,0},{2,3},{3,2},{4,5},{5,4},{6,7},{7,6},{8,9},{9,8},{10,11... | collective-permute-start | bytes 4718600 | tf_op jit(solution)/shard_map/ppermute | solution.py:31
  106.3 17.4 %collective-permute-start.55 = (bf16[8,96,384]{2,1,0:T(8,128)(2,1)S(1)}, bf16[8,96,384]{2,1,0:T(8,128)(2,1)S(1)}, u32[]{:S(2)}, u32[]{:S(2)}) collective-permute-start(bf16[8,96,384]{2,1,0:T(8,128)(2,1)S(1)} %get-tuple-element.52), channel_id=1, source_target_pairs={{0,24},{8,16},{16,8},{24,0},{1,25},{9,17},{17,9},{25,1},{2,26},{10... | collective-permute-start | bytes 1769480 | tf_op jit(solution)/shard_map/ppermute | solution.py:31
  110.7 13.9 %collective-permute-start.32 = (bf16[4,96,384]{2,1,0:T(8,128)(2,1)S(1)}, bf16[4,96,384]{2,1,0:T(8,128)(2,1)S(1)}, u32[]{:S(2)}, u32[]{:S(2)}) collective-permute-start(bf16[4,96,384]{2,1,0:T(8,128)(2,1)S(1)} %slice.523), channel_id=1, source_target_pairs={{0,8},{8,0},{16,24},{24,16},{1,9},{9,1},{17,25},{25,17},{2,10},{10... | collective-permute-start | bytes 884744 | tf_op jit(solution)/shard_map/ppermute | solution.py:31
  112.9 12.5 %collective-permute-start.40 = (bf16[4,96,384]{2,1,0:T(8,128)(2,1)S(1)}, bf16[4,96,384]{2,1,0:T(8,128)(2,1)S(1)}, u32[]{:S(2)}, u32[]{:S(2)}) collective-permute-start(bf16[4,96,384]{2,1,0:T(8,128)(2,1)S(1)} %slice.529), channel_id=1, source_target_pairs={{0,96},{32,64},{64,32},{96,0},{1,97},{33,65},{65,33},{97,1},{2,98}... | collective-permute-start | bytes 884744 | tf_op jit(solution)/shard_map/ppermute | solution.py:31
  119.2 11.2 %collective-permute-start.48 = (bf16[4,96,384]{2,1,0:T(8,128)(2,1)S(1)}, bf16[4,96,384]{2,1,0:T(8,128)(2,1)S(1)}, u32[]{:S(2)}, u32[]{:S(2)}) collective-permute-start(bf16[4,96,384]{2,1,0:T(8,128)(2,1)S(1)} %slice.535), channel_id=1, source_target_pairs={{0,24},{8,16},{16,8},{24,0},{1,25},{9,17},{17,9},{25,1},{2,26},{10... | collective-permute-start | bytes 884744 | tf_op jit(solution)/shard_map/ppermute | solution.py:31
  123.9 8.6 %collective-permute-start.56 = (bf16[4,96,384]{2,1,0:T(8,128)(2,1)S(1)}, bf16[4,96,384]{2,1,0:T(8,128)(2,1)S(1)}, u32[]{:S(2)}, u32[]{:S(2)}) collective-permute-start(bf16[4,96,384]{2,1,0:T(8,128)(2,1)S(1)} %slice.541), channel_id=1, source_target_pairs={{0,32},{32,0},{64,96},{96,64},{1,33},{33,1},{65,97},{97,65},{2,34}... | collective-permute-start | bytes 884744 | tf_op jit(solution)/shard_map/ppermute | solution.py:31
  124.7 8.6 %collective-permute-start.33 = (bf16[2,96,384]{2,1,0:T(8,128)(2,1)S(1)}, bf16[2,96,384]{2,1,0:T(8,128)(2,1)S(1)}, u32[]{:S(2)}, u32[]{:S(2)}) collective-permute-start(bf16[2,96,384]{2,1,0:T(8,128)(2,1)S(1)} %slice.525), channel_id=1, source_target_pairs={{0,96},{32,64},{64,32},{96,0},{1,97},{33,65},{65,33},{97,1},{2,98}... | collective-permute-start | bytes 442376 | tf_op jit(solution)/shard_map/ppermute | solution.py:31
  125.6 10.2 %collective-permute-start.41 = (bf16[2,96,384]{2,1,0:T(8,128)(2,1)S(1)}, bf16[2,96,384]{2,1,0:T(8,128)(2,1)S(1)}, u32[]{:S(2)}, u32[]{:S(2)}) collective-permute-start(bf16[2,96,384]{2,1,0:T(8,128)(2,1)S(1)} %slice.531), channel_id=1, source_target_pairs={{0,24},{8,16},{16,8},{24,0},{1,25},{9,17},{17,9},{25,1},{2,26},{10... | collective-permute-start | bytes 442376 | tf_op jit(solution)/shard_map/ppermute | solution.py:31
  130.5 5.6 %collective-permute-start.49 = (bf16[2,96,384]{2,1,0:T(8,128)(2,1)S(1)}, bf16[2,96,384]{2,1,0:T(8,128)(2,1)S(1)}, u32[]{:S(2)}, u32[]{:S(2)}) collective-permute-start(bf16[2,96,384]{2,1,0:T(8,128)(2,1)S(1)} %slice.537), channel_id=1, source_target_pairs={{0,32},{32,0},{64,96},{96,64},{1,33},{33,1},{65,97},{97,65},{2,34}... | collective-permute-start | bytes 442376 | tf_op jit(solution)/shard_map/ppermute | solution.py:31
  132.6 6.0 %collective-permute-start.57 = (bf16[2,96,384]{2,1,0:T(8,128)(2,1)S(1)}, bf16[2,96,384]{2,1,0:T(8,128)(2,1)S(1)}, u32[]{:S(2)}, u32[]{:S(2)}) collective-permute-start(bf16[2,96,384]{2,1,0:T(8,128)(2,1)S(1)} %slice.543), channel_id=1, source_target_pairs={{0,8},{8,0},{16,24},{24,16},{1,9},{9,1},{17,25},{25,17},{2,10},{10... | collective-permute-start | bytes 442376 | tf_op jit(solution)/shard_map/ppermute | solution.py:31
  133.4 6.7 %collective-permute-start.34 = (bf16[1,96,384]{2,1,0:T(8,128)(2,1)S(1)}, bf16[1,96,384]{2,1,0:T(8,128)(2,1)S(1)}, u32[]{:S(2)}, u32[]{:S(2)}) collective-permute-start(bf16[1,96,384]{2,1,0:T(8,128)(2,1)S(1)} %slice.527), channel_id=1, source_target_pairs={{0,24},{8,16},{16,8},{24,0},{1,25},{9,17},{17,9},{25,1},{2,26},{10... | collective-permute-start | bytes 221192 | tf_op jit(solution)/shard_map/ppermute | solution.py:31
  135.8 7.1 %collective-permute-start.42 = (bf16[1,96,384]{2,1,0:T(8,128)(2,1)S(1)}, bf16[1,96,384]{2,1,0:T(8,128)(2,1)S(1)}, u32[]{:S(2)}, u32[]{:S(2)}) collective-permute-start(bf16[1,96,384]{2,1,0:T(8,128)(2,1)S(1)} %slice.533), channel_id=1, source_target_pairs={{0,32},{32,0},{64,96},{96,64},{1,33},{33,1},{65,97},{97,65},{2,34}... | collective-permute-start | bytes 221192 | tf_op jit(solution)/shard_map/ppermute | solution.py:31
  136.2 10.0 %collective-permute-start.50 = (bf16[1,96,384]{2,1,0:T(8,128)(2,1)S(1)}, bf16[1,96,384]{2,1,0:T(8,128)(2,1)S(1)}, u32[]{:S(2)}, u32[]{:S(2)}) collective-permute-start(bf16[1,96,384]{2,1,0:T(8,128)(2,1)S(1)} %slice.539), channel_id=1, source_target_pairs={{0,8},{8,0},{16,24},{24,16},{1,9},{9,1},{17,25},{25,17},{2,10},{10... | collective-permute-start | bytes 221192 | tf_op jit(solution)/shard_map/ppermute | solution.py:31
  138.7 7.6 %collective-permute-start.58 = (bf16[1,96,384]{2,1,0:T(8,128)(2,1)S(1)}, bf16[1,96,384]{2,1,0:T(8,128)(2,1)S(1)}, u32[]{:S(2)}, u32[]{:S(2)}) collective-permute-start(bf16[1,96,384]{2,1,0:T(8,128)(2,1)S(1)} %slice.545), channel_id=1, source_target_pairs={{0,96},{32,64},{64,32},{96,0},{1,97},{33,65},{65,33},{97,1},{2,98}... | collective-permute-start | bytes 221192 | tf_op jit(solution)/shard_map/ppermute | solution.py:31
  140.1 6.2 %collective-permute-start.35 = (bf16[1,96,384]{2,1,0:T(8,128)(2,1)S(1)}, bf16[1,96,384]{2,1,0:T(8,128)(2,1)S(1)}, u32[]{:S(2)}, u32[]{:S(2)}) collective-permute-start(bf16[1,96,384]{2,1,0:T(8,128)(2,1)S(1)} %add_convert_fusion.15), channel_id=1, source_target_pairs={{0,24},{8,16},{16,8},{24,0},{1,25},{9,17},{17,9},{25,1},{2,26},{10... | collective-permute-start | bytes 221192 | tf_op jit(solution)/shard_map/ppermute | solution.py:31
  142.9 14.1 %collective-permute-start.43 = (bf16[1,96,384]{2,1,0:T(8,128)(2,1)S(1)}, bf16[1,96,384]{2,1,0:T(8,128)(2,1)S(1)}, u32[]{:S(2)}, u32[]{:S(2)}) collective-permute-start(bf16[1,96,384]{2,1,0:T(8,128)(2,1)S(1)} %add_convert_fusion.14), channel_id=1, source_target_pairs={{0,32},{32,0},{64,96},{96,64},{1,33},{33,1},{65,97},{97,65},{2,34}... | collective-permute-start | bytes 221192 | tf_op jit(solution)/shard_map/ppermute | solution.py:31
  143.5 9.1 %collective-permute-start.18 = (bf16[2,128,768]{2,1,0:T(8,128)(2,1)S(1)}, bf16[2,128,768]{2,1,0:T(8,128)(2,1)S(1)}, u32[]{:S(2)}, u32[]{:S(2)}) collective-permute-start(bf16[2,128,768]{2,1,0:T(8,128)(2,1)S(1)} %slice_bitcast_fusion.3), channel_id=1, source_target_pairs={{0,6},{1,7},{2,4},{3,5},{4,2},{5,3},{6,0},{7,1},{8,14},{9,15},{10,... | collective-permute-start | bytes 1179656 | tf_op jit(solution)/shard_map/ppermute | solution.py:31
  146.2 7.9 %collective-permute-start.16 = (bf16[2,128,768]{2,1,0:T(8,128)(2,1)S(1)}, bf16[2,128,768]{2,1,0:T(8,128)(2,1)S(1)}, u32[]{:S(2)}, u32[]{:S(2)}) collective-permute-start(bf16[2,128,768]{2,1,0:T(8,128)(2,1)S(1)} %slice_bitcast_fusion.5), channel_id=1, source_target_pairs={{0,2},{1,3},{2,0},{3,1},{4,6},{5,7},{6,4},{7,5},{8,10},{9,11},{10,... | collective-permute-start | bytes 1179656 | tf_op jit(solution)/shard_map/ppermute | solution.py:31
  146.2 11.0 %collective-permute-start.51 = (bf16[1,96,384]{2,1,0:T(8,128)(2,1)S(1)}, bf16[1,96,384]{2,1,0:T(8,128)(2,1)S(1)}, u32[]{:S(2)}, u32[]{:S(2)}) collective-permute-start(bf16[1,96,384]{2,1,0:T(8,128)(2,1)S(1)} %add_convert_fusion.13), channel_id=1, source_target_pairs={{0,8},{8,0},{16,24},{24,16},{1,9},{9,1},{17,25},{25,17},{2,10},{10... | collective-permute-start | bytes 221192 | tf_op jit(solution)/shard_map/ppermute | solution.py:31
  146.4 21.0 %collective-permute-start.59 = (bf16[1,96,384]{2,1,0:T(8,128)(2,1)S(1)}, bf16[1,96,384]{2,1,0:T(8,128)(2,1)S(1)}, u32[]{:S(2)}, u32[]{:S(2)}) collective-permute-start(bf16[1,96,384]{2,1,0:T(8,128)(2,1)S(1)} %add_convert_fusion.12), channel_id=1, source_target_pairs={{0,96},{32,64},{64,32},{96,0},{1,97},{33,65},{65,33},{97,1},{2,98}... | collective-permute-start | bytes 221192 | tf_op jit(solution)/shard_map/ppermute | solution.py:31
  152.6 14.9 %collective-permute-start.36 = (bf16[2,96,384]{2,1,0:T(8,128)(2,1)S(1)}, bf16[2,96,384]{2,1,0:T(8,128)(2,1)S(1)}, u32[]{:S(2)}, u32[]{:S(2)}) collective-permute-start(bf16[2,96,384]{2,1,0:T(8,128)(2,1)S(1)} %pad_maximum_fusion.24), channel_id=1, source_target_pairs={{0,96},{32,64},{64,32},{96,0},{1,97},{33,65},{65,33},{97,1},{2,98}... | collective-permute-start | bytes 442376 | tf_op jit(solution)/shard_map/ppermute | solution.py:31
  154.3 7.0 %collective-permute-start.17 = (bf16[128,768]{1,0:T(8,128)(2,1)S(1)}, bf16[128,768]{1,0:T(8,128)(2,1)S(1)}, u32[]{:S(2)}, u32[]{:S(2)}) collective-permute-start(bf16[128,768]{1,0:T(8,128)(2,1)S(1)} %get-tuple-element.73), channel_id=1, source_target_pairs={{0,6},{1,7},{2,4},{3,5},{4,2},{5,3},{6,0},{7,1},{8,14},{9,15},{10,... | collective-permute-start | bytes 589832 | tf_op jit(solution)/shard_map/ppermute | solution.py:31
  157.1 7.3 %collective-permute-start.19 = (bf16[128,768]{1,0:T(8,128)(2,1)S(1)}, bf16[128,768]{1,0:T(8,128)(2,1)S(1)}, u32[]{:S(2)}, u32[]{:S(2)}) collective-permute-start(bf16[128,768]{1,0:T(8,128)(2,1)S(1)} %get-tuple-element.71), channel_id=1, source_target_pairs={{0,2},{1,3},{2,0},{3,1},{4,6},{5,7},{6,4},{7,5},{8,10},{9,11},{10,... | collective-permute-start | bytes 589832 | tf_op jit(solution)/shard_map/ppermute | solution.py:31
  157.2 12.4 %collective-permute-start.44 = (bf16[2,96,384]{2,1,0:T(8,128)(2,1)S(1)}, bf16[2,96,384]{2,1,0:T(8,128)(2,1)S(1)}, u32[]{:S(2)}, u32[]{:S(2)}) collective-permute-start(bf16[2,96,384]{2,1,0:T(8,128)(2,1)S(1)} %pad_maximum_fusion.25), channel_id=1, source_target_pairs={{0,24},{8,16},{16,8},{24,0},{1,25},{9,17},{17,9},{25,1},{2,26},{10... | collective-permute-start | bytes 442376 | tf_op jit(solution)/shard_map/ppermute | solution.py:31
  161.3 10.0 %collective-permute-start.52 = (bf16[2,96,384]{2,1,0:T(8,128)(2,1)S(1)}, bf16[2,96,384]{2,1,0:T(8,128)(2,1)S(1)}, u32[]{:S(2)}, u32[]{:S(2)}) collective-permute-start(bf16[2,96,384]{2,1,0:T(8,128)(2,1)S(1)} %pad_maximum_fusion.26), channel_id=1, source_target_pairs={{0,32},{32,0},{64,96},{96,64},{1,33},{33,1},{65,97},{97,65},{2,34}... | collective-permute-start | bytes 442376 | tf_op jit(solution)/shard_map/ppermute | solution.py:31
  167.3 13.8 %collective-permute-start.20 = (bf16[272,1536]{1,0:T(8,128)(2,1)S(1)}, bf16[272,1536]{1,0:T(8,128)(2,1)S(1)}, u32[]{:S(2)}, u32[]{:S(2)}) collective-permute-start(bf16[272,1536]{1,0:T(8,128)(2,1)S(1)} %get-tuple-element.42), channel_id=1, source_target_pairs={{0,1},{1,0},{2,3},{3,2},{4,5},{5,4},{6,7},{7,6},{8,9},{9,8},{10,11... | collective-permute-start | bytes 2506760 | tf_op jit(solution)/shard_map/ppermute | solution.py:31
  167.4 6.7 %collective-permute-start.60 = (bf16[2,96,384]{2,1,0:T(8,128)(2,1)S(1)}, bf16[2,96,384]{2,1,0:T(8,128)(2,1)S(1)}, u32[]{:S(2)}, u32[]{:S(2)}) collective-permute-start(bf16[2,96,384]{2,1,0:T(8,128)(2,1)S(1)} %pad_maximum_fusion.27), channel_id=1, source_target_pairs={{0,8},{8,0},{16,24},{24,16},{1,9},{9,1},{17,25},{25,17},{2,10},{10... | collective-permute-start | bytes 442376 | tf_op jit(solution)/shard_map/ppermute | solution.py:31
  167.6 12.5 %collective-permute-start.37 = (bf16[4,96,384]{2,1,0:T(8,128)(2,1)S(1)}, bf16[4,96,384]{2,1,0:T(8,128)(2,1)S(1)}, u32[]{:S(2)}, u32[]{:S(2)}) collective-permute-start(bf16[4,96,384]{2,1,0:T(8,128)(2,1)S(1)} %pad_maximum_fusion.7), channel_id=1, source_target_pairs={{0,8},{8,0},{16,24},{24,16},{1,9},{9,1},{17,25},{25,17},{2,10},{10... | collective-permute-start | bytes 884744 | tf_op jit(solution)/shard_map/ppermute | solution.py:31
  169.7 11.1 %collective-permute-start.45 = (bf16[4,96,384]{2,1,0:T(8,128)(2,1)S(1)}, bf16[4,96,384]{2,1,0:T(8,128)(2,1)S(1)}, u32[]{:S(2)}, u32[]{:S(2)}) collective-permute-start(bf16[4,96,384]{2,1,0:T(8,128)(2,1)S(1)} %pad_maximum_fusion.8), channel_id=1, source_target_pairs={{0,96},{32,64},{64,32},{96,0},{1,97},{33,65},{65,33},{97,1},{2,98}... | collective-permute-start | bytes 884744 | tf_op jit(solution)/shard_map/ppermute | solution.py:31
  171.3 27.2 %collective-permute-start.53 = (bf16[4,96,384]{2,1,0:T(8,128)(2,1)S(1)}, bf16[4,96,384]{2,1,0:T(8,128)(2,1)S(1)}, u32[]{:S(2)}, u32[]{:S(2)}) collective-permute-start(bf16[4,96,384]{2,1,0:T(8,128)(2,1)S(1)} %pad_maximum_fusion.9), channel_id=1, source_target_pairs={{0,24},{8,16},{16,8},{24,0},{1,25},{9,17},{17,9},{25,1},{2,26},{10... | collective-permute-start | bytes 884744 | tf_op jit(solution)/shard_map/ppermute | solution.py:31
  174.2 27.8 %collective-permute-start.61 = (bf16[4,96,384]{2,1,0:T(8,128)(2,1)S(1)}, bf16[4,96,384]{2,1,0:T(8,128)(2,1)S(1)}, u32[]{:S(2)}, u32[]{:S(2)}) collective-permute-start(bf16[4,96,384]{2,1,0:T(8,128)(2,1)S(1)} %pad_maximum_fusion.10), channel_id=1, source_target_pairs={{0,32},{32,0},{64,96},{96,64},{1,33},{33,1},{65,97},{97,65},{2,34}... | collective-permute-start | bytes 884744 | tf_op jit(solution)/shard_map/ppermute | solution.py:31
  180.1 36.0 %collective-permute-start.38 = (bf16[8,96,384]{2,1,0:T(8,128)(2,1)S(1)}, bf16[8,96,384]{2,1,0:T(8,128)(2,1)S(1)}, u32[]{:S(2)}, u32[]{:S(2)}) collective-permute-start(bf16[8,96,384]{2,1,0:T(8,128)(2,1)S(1)} %pad_maximum_fusion.3.refs_0_), channel_id=1, source_target_pairs={{0,32},{32,0},{64,96},{96,64},{1,33},{33,1},{65,97},{97,65},{2,34}... | collective-permute-start | bytes 1769480 | tf_op jit(solution)/shard_map/ppermute | solution.py:31
  181.8 8.0 %collective-permute-start.23 = (bf16[144,768]{1,0:T(8,128)(2,1)S(1)}, bf16[144,768]{1,0:T(8,128)(2,1)S(1)}, u32[]{:S(2)}, u32[]{:S(2)}) collective-permute-start(bf16[144,768]{1,0:T(8,128)(2,1)S(1)} %get-tuple-element.86), channel_id=1, source_target_pairs={{0,6},{1,7},{2,4},{3,5},{4,2},{5,3},{6,0},{7,1},{8,14},{9,15},{10,... | collective-permute-start | bytes 663560 | tf_op jit(solution)/shard_map/ppermute | solution.py:31
  183.4 6.8 %collective-permute-start.21 = (bf16[144,768]{1,0:T(8,128)(2,1)S(1)}, bf16[144,768]{1,0:T(8,128)(2,1)S(1)}, u32[]{:S(2)}, u32[]{:S(2)}) collective-permute-start(bf16[144,768]{1,0:T(8,128)(2,1)S(1)} %get-tuple-element.90), channel_id=1, source_target_pairs={{0,2},{1,3},{2,0},{3,1},{4,6},{5,7},{6,4},{7,5},{8,10},{9,11},{10,... | collective-permute-start | bytes 663560 | tf_op jit(solution)/shard_map/ppermute | solution.py:31
  190.4 5.0 %collective-permute-start.24 = (bf16[80,768]{1,0:T(8,128)(2,1)S(1)}, bf16[80,768]{1,0:T(8,128)(2,1)S(1)}, u32[]{:S(2)}, u32[]{:S(2)}) collective-permute-start(bf16[80,768]{1,0:T(8,128)(2,1)S(1)} %get-tuple-element.92), channel_id=1, source_target_pairs={{0,2},{1,3},{2,0},{3,1},{4,6},{5,7},{6,4},{7,5},{8,10},{9,11},{10,... | collective-permute-start | bytes 368648 | tf_op jit(solution)/shard_map/ppermute | solution.py:31
  190.8 6.2 %collective-permute-start.22 = (bf16[80,768]{1,0:T(8,128)(2,1)S(1)}, bf16[80,768]{1,0:T(8,128)(2,1)S(1)}, u32[]{:S(2)}, u32[]{:S(2)}) collective-permute-start(bf16[80,768]{1,0:T(8,128)(2,1)S(1)} %get-tuple-element.88), channel_id=1, source_target_pairs={{0,6},{1,7},{2,4},{3,5},{4,2},{5,3},{6,0},{7,1},{8,14},{9,15},{10,... | collective-permute-start | bytes 368648 | tf_op jit(solution)/shard_map/ppermute | solution.py:31
  197.1 11.0 %collective-permute-start.27 = (bf16[80,1536]{1,0:T(8,128)(2,1)S(1)}, bf16[80,1536]{1,0:T(8,128)(2,1)S(1)}, u32[]{:S(2)}, u32[]{:S(2)}) collective-permute-start(bf16[80,1536]{1,0:T(8,128)(2,1)S(1)} %get-tuple-element.78), channel_id=1, source_target_pairs={{0,24},{8,16},{16,8},{24,0},{1,25},{9,17},{17,9},{25,1},{2,26},{10... | collective-permute-start | bytes 737288 | tf_op jit(solution)/shard_map/ppermute | solution.py:31
  198.5 11.6 %collective-permute-start.26 = (bf16[80,1536]{1,0:T(8,128)(2,1)S(1)}, bf16[80,1536]{1,0:T(8,128)(2,1)S(1)}, u32[]{:S(2)}, u32[]{:S(2)}) collective-permute-start(bf16[80,1536]{1,0:T(8,128)(2,1)S(1)} %get-tuple-element.78), channel_id=1, source_target_pairs={{0,8},{8,0},{16,24},{24,16},{1,9},{9,1},{17,25},{25,17},{2,10},{10... | collective-permute-start | bytes 737288 | tf_op jit(solution)/shard_map/ppermute | solution.py:31
  198.5 15.5 %collective-permute-start.25 = (bf16[80,1536]{1,0:T(8,128)(2,1)S(1)}, bf16[80,1536]{1,0:T(8,128)(2,1)S(1)}, u32[]{:S(2)}, u32[]{:S(2)}) collective-permute-start(bf16[80,1536]{1,0:T(8,128)(2,1)S(1)} %get-tuple-element.78), channel_id=1, source_target_pairs={{0,16},{8,24},{16,0},{24,8},{1,17},{9,25},{17,1},{25,9},{2,18},{10... | collective-permute-start | bytes 737288 | tf_op jit(solution)/shard_map/ppermute | solution.py:31
  202.0 19.4 %collective-permute-start.46 = (bf16[8,96,384]{2,1,0:T(8,128)(2,1)S(1)}, bf16[8,96,384]{2,1,0:T(8,128)(2,1)S(1)}, u32[]{:S(2)}, u32[]{:S(2)}) collective-permute-start(bf16[8,96,384]{2,1,0:T(8,128)(2,1)S(1)} %pad_maximum_fusion.4.refs_2_), channel_id=1, source_target_pairs={{0,8},{8,0},{16,24},{24,16},{1,9},{9,1},{17,25},{25,17},{2,10},{10... | collective-permute-start | bytes 1769480 | tf_op jit(solution)/shard_map/ppermute | solution.py:31
  208.2 15.3 %collective-permute-start.54 = (bf16[8,96,384]{2,1,0:T(8,128)(2,1)S(1)}, bf16[8,96,384]{2,1,0:T(8,128)(2,1)S(1)}, u32[]{:S(2)}, u32[]{:S(2)}) collective-permute-start(bf16[8,96,384]{2,1,0:T(8,128)(2,1)S(1)} %pad_maximum_fusion.5.refs_4_), channel_id=1, source_target_pairs={{0,96},{32,64},{64,32},{96,0},{1,97},{33,65},{65,33},{97,1},{2,98}... | collective-permute-start | bytes 1769480 | tf_op jit(solution)/shard_map/ppermute | solution.py:31
  210.1 13.4 %collective-permute-start.62 = (bf16[8,96,384]{2,1,0:T(8,128)(2,1)S(1)}, bf16[8,96,384]{2,1,0:T(8,128)(2,1)S(1)}, u32[]{:S(2)}, u32[]{:S(2)}) collective-permute-start(bf16[8,96,384]{2,1,0:T(8,128)(2,1)S(1)} %pad_maximum_fusion.6.refs_6_), channel_id=1, source_target_pairs={{0,24},{8,16},{16,8},{24,0},{1,25},{9,17},{17,9},{25,1},{2,26},{10... | collective-permute-start | bytes 1769480 | tf_op jit(solution)/shard_map/ppermute | solution.py:31
  214.3 14.3 %collective-permute-start.30 = (bf16[80,1536]{1,0:T(8,128)(2,1)S(1)}, bf16[80,1536]{1,0:T(8,128)(2,1)S(1)}, u32[]{:S(2)}, u32[]{:S(2)}) collective-permute-start(bf16[80,1536]{1,0:T(8,128)(2,1)S(1)} %get-tuple-element.76), channel_id=1, source_target_pairs={{0,96},{32,64},{64,32},{96,0},{1,97},{33,65},{65,33},{97,1},{2,98}... | collective-permute-start | bytes 737288 | tf_op jit(solution)/shard_map/ppermute | solution.py:31
  216.1 12.5 %collective-permute-start.29 = (bf16[80,1536]{1,0:T(8,128)(2,1)S(1)}, bf16[80,1536]{1,0:T(8,128)(2,1)S(1)}, u32[]{:S(2)}, u32[]{:S(2)}) collective-permute-start(bf16[80,1536]{1,0:T(8,128)(2,1)S(1)} %get-tuple-element.76), channel_id=1, source_target_pairs={{0,32},{32,0},{64,96},{96,64},{1,33},{33,1},{65,97},{97,65},{2,34}... | collective-permute-start | bytes 737288 | tf_op jit(solution)/shard_map/ppermute | solution.py:31
  221.4 8.0 %collective-permute-start.28 = (bf16[80,1536]{1,0:T(8,128)(2,1)S(1)}, bf16[80,1536]{1,0:T(8,128)(2,1)S(1)}, u32[]{:S(2)}, u32[]{:S(2)}) collective-permute-start(bf16[80,1536]{1,0:T(8,128)(2,1)S(1)} %get-tuple-element.76), channel_id=1, source_target_pairs={{0,64},{32,96},{64,0},{96,32},{1,65},{33,97},{65,1},{97,33},{2,66}... | collective-permute-start | bytes 737288 | tf_op jit(solution)/shard_map/ppermute | solution.py:31
  (11 other events, 55.1 us)

commit v2 on v1

v2 whole, which is shorter than its diff:
```python
import functools

import jax
import jax.numpy as jnp
from jax import lax
from jax.experimental import pallas as pl
from jax.experimental.pallas import tpu as pltpu
from jax.sharding import PartitionSpec as P

BF = jnp.bfloat16
F32 = jnp.float32
ORDER = (0, 2, 6, 4)
XOR3 = (1, 3, 2)
UNIT = 16
HALO = 16
FIRST = 5 * 10**8


def vmem(limit):
    return pltpu.CompilerParams(vmem_limit_bytes=limit << 20)


def cost(flops, nbytes, trans=0):
    return pl.CostEstimate(flops=flops, bytes_accessed=nbytes, transcendentals=trans)


def full(shape):
    return pl.BlockSpec(shape, lambda *_: (0,) * len(shape))


def fixed(shape):
    return pl.BlockSpec(shape, lambda *_: (0,) * len(shape), pipeline_mode=pl.Buffered(1))


def xor_send(value, axis, mask, size):
    return lax.ppermute(value, axis, [(i, i ^ mask) for i in range(size)])


def select_kernel(lengths, panel_ref, seg_ref, *outs):
    owner = lax.axis_index("context")
    start = jnp.int32(0)
    for shard in range(3):
        start += jnp.where(shard < owner, lengths[0, shard], 0)
    count = lengths[0, owner]
    rows = 40
    slots = panel_ref.shape[2]
    q = lax.broadcasted_iota(jnp.int32, (rows, slots), 0)
    slot = lax.broadcasted_iota(jnp.int32, (rows, slots), 1)
    picks = []
    for e in range(4):
        base = 32 * (owner ^ e)
        wanted = jnp.where(q < 32, base + q, jnp.where(q == 32, base - 1, base + 32))
        inside = (q < 34) & (wanted >= 0) & (wanted < 128)
        local = wanted - start
        hit = inside & (local == slot) & (slot < count)
        picks.append(hit.astype(F32).astype(BF))
    pick = jnp.concatenate(picks, axis=0)
    scratch = outs[4]
    for i in range(UNIT):
        pair = jnp.concatenate([panel_ref[i], panel_ref[i + UNIT]], axis=0)
        got = lax.dot_general(
            pick, pair, (((1,), (1,)), ((), ())), preferred_element_type=F32
        )
        scratch[pl.ds(i, 4 * rows, stride=UNIT), :] = got
    seg_row = seg_ref[...].astype(F32) + 1.0
    for e in range(4):
        target = owner ^ e
        base = e * rows * UNIT
        if e == 0:
            scratch[pl.ds(base + 34 * UNIT, 1), :] = seg_row
        else:
            up = (target == owner + 1).astype(F32)
            down = (target == owner - 1).astype(F32)
            scratch[pl.ds(base + 35 * UNIT, 1), :] = seg_row * up
            scratch[pl.ds(base + 36 * UNIT, 1), :] = seg_row * down
    for e in range(4):
        outs[e][...] = scratch[pl.ds(e * rows * UNIT, rows * UNIT), :].astype(BF)


def select_panels(lengths, panels_t, seg):
    return pl.pallas_call(
        select_kernel,
        out_shape=[jax.ShapeDtypeStruct((640, 128), BF)] * 4,
        in_specs=[
            pl.BlockSpec(memory_space=pltpu.SMEM),
            full(panels_t.shape),
            full(seg.shape),
        ],
        out_specs=[full((640, 128))] * 4,
        grid=(1,),
        scratch_shapes=[pltpu.VMEM((2560, 128), F32)],
        compiler_params=vmem(24),
        cost_estimate=cost(2 * 160 * 65 * 2048, 2 << 20),
    )(lengths, panels_t, seg)


def norm_kernel(
    a_ref, b_ref, wa_ref, wb_ref, kern_ref, gain_ref,
    ln_ref, normed_ref, rstd_ref, frames_ref, segs_ref, stack_ref,
    units, weight, segs, near_segs, wide, near,
):
    step = pl.program_id(0)
    me = lax.axis_index("tensor")

    @pl.when(step == 0)
    def _():
        lane = lax.broadcasted_iota(jnp.int32, (256, 256), 0)
        out_lane = lax.broadcasted_iota(jnp.int32, (256, 256), 1)
        source = (out_lane // 64 % 2) * 128 + (out_lane // 128) * 64 + out_lane % 64
        swap = (lane == source).astype(F32).astype(BF)
        for d in range(4):
            weight[pl.ds(128 * d, 64), :] = wa_ref[d]
            weight[pl.ds(128 * d + 64, 64), :] = wb_ref[d]
            both = jnp.concatenate([a_ref[d, pl.ds(0, 544), :], b_ref[d, pl.ds(0, 544), :]], axis=1)
            mixed = jnp.dot(both, swap, preferred_element_type=F32).astype(BF)
            for p in range(34):
                at = p + 1 if p < 32 else (0 if p == 32 else 33)
                for half in range(2):
                    units[2 * at + half, :, pl.ds(128 * d, 128)] = mixed[
                        16 * p : 16 * p + 16, 128 * half : 128 * half + 128
                    ]
        eye = (
            lax.broadcasted_iota(jnp.int32, (128, 128), 0)
            == lax.broadcasted_iota(jnp.int32, (128, 128), 1)
        ).astype(F32)
        ones = jnp.ones((128, 128), BF)

        def column(ref, d, q):
            row = ref[d, pl.ds(q * UNIT, 16), :].astype(F32)[0:1]
            return jnp.dot((eye * row).astype(BF), ones, preferred_element_type=F32)

        for c in range(2):
            ref = (a_ref, b_ref)[c]
            for d in range(4):
                at = me ^ (ORDER[d] ^ c)
                segs[pl.ds(pl.multiple_of(HALO + 128 * at, 16), 128), :] = column(ref, d, 34)

                @pl.when(at == 7)
                def _():
                    segs[pl.ds(0, HALO), :] = column(ref, d, 35)[128 - HALO :]

                @pl.when(at == 0)
                def _():
                    segs[pl.ds(HALO + 1024, HALO), :] = column(ref, d, 36)[:HALO]

        wide[pl.ds(160, 96), :] = jnp.zeros((96, wide.shape[1]), BF)

    at_step = 7 - step
    spot = lax.rem(at_step, 4)
    block = me ^ (2 * (spot ^ (spot // 2))) ^ (at_step // 4)
    rows = units[pl.ds(8 * block + 1, 10)].reshape(160, 512)
    wide[pl.ds(0, 160), :] = jnp.dot(rows, weight[...], preferred_element_type=F32).astype(BF)
    near_segs[...] = segs[pl.ds(pl.multiple_of(128 * block, 128), 160), :]

    stack_ref[...] = rows
    segs_ref[...] = near_segs[...]

    col = lax.broadcasted_iota(jnp.int32, (128, 256), 1) - lax.broadcasted_iota(jnp.int32, (128, 256), 0)
    here = near_segs[pl.ds(HALO, 128), :]
    shift = []
    for j in (0, 1, 3, 4):
        same = (near_segs[pl.ds(HALO - 2 + j, 128), :] == here).astype(F32)
        same = jnp.concatenate([same, same], axis=1)
        shift.append(jnp.where(col == HALO - 2 + j, same, 0.0).astype(BF))
    near[...] = jnp.dot(jnp.concatenate(shift, axis=0), wide[...], preferred_element_type=F32)

    taps = [kern_ref[pl.ds(j, 1), :] for j in range(5)]
    gain = gain_ref[...]
    for r in range(0, 128, 16):
        mixed = (1.0 + taps[2]) * wide[pl.ds(HALO + r, 16), :].astype(F32)
        for n, j in enumerate((0, 1, 3, 4)):
            mixed = mixed + taps[j] * near[pl.ds(128 * n + r, 16), :]
        mean = jnp.mean(mixed, axis=1, keepdims=True)
        center = mixed - mean
        rstd = lax.rsqrt(jnp.mean(center * center, axis=1, keepdims=True) + 1e-05)
        normed = center * rstd
        ln_ref[pl.ds(r, 16), :] = (normed * gain).astype(BF)
        normed_ref[pl.ds(r, 16), :] = normed
        rstd_ref[pl.ds(r, 16), :] = jnp.broadcast_to(rstd, (16, 128))

    @pl.when(step == 7)
    def _():
        frames_ref[...] = wide[pl.ds(0, 160), :].astype(F32)


def normalise(a, b, wa, wb, kern, gain):
    d_model = kern.shape[1]
    weight = pl.BlockSpec((4, 64, d_model), lambda i: (0, 0, 0))
    return pl.pallas_call(
        norm_kernel,
        grid=(8,),
        in_specs=[full(a.shape), full(b.shape), weight, weight, full(kern.shape), full(gain.shape)],
        out_specs=[
            pl.BlockSpec((128, d_model), lambda i: (7 - i, 0)),
            full((128, d_model)), full((128, 128)), full((160, d_model)),
            full((160, 128)), full((160, 512)),
        ],
        scratch_shapes=[
            pltpu.VMEM((68, 16, 512), BF),
            pltpu.VMEM((512, d_model), BF),
            pltpu.VMEM((1056, 128), F32),
            pltpu.VMEM((160, 128), F32),
            pltpu.VMEM((256, d_model), BF),
            pltpu.VMEM((512, d_model), F32),
        ],
        out_shape=[
            jax.ShapeDtypeStruct((1024, d_model), BF),
            jax.ShapeDtypeStruct((128, d_model), F32),
            jax.ShapeDtypeStruct((128, 128), F32),
            jax.ShapeDtypeStruct((160, d_model), F32),
            jax.ShapeDtypeStruct((160, 128), F32),
            jax.ShapeDtypeStruct((160, 512), BF),
        ],
        compiler_params=vmem(24),
        cost_estimate=cost(12 * 10**9, 10 << 20),
    )(a, b, wa, wb, kern, gain)


def hidden_kernel(ln_ref, up_ref, hid_ref, slope_ref):
    ln = ln_ref[...]
    for c in range(0, up_ref.shape[1], 256):
        part = pl.ds(c, 256)
        pre = jnp.dot(ln, up_ref[:, part], preferred_element_type=F32)
        sig = 1.0 / (1.0 + jnp.exp(-pre))
        hid_ref[:, part] = (pre * sig).astype(BF)
        slope_ref[:, part] = 0.5 * sig * (1.0 + pre * (1.0 - sig))


def hidden_rows(ln, up):
    rows, d_model = ln.shape
    ff = up.shape[1]
    half = rows // 2
    return pl.pallas_call(
        hidden_kernel,
        grid=(2,),
        in_specs=[pl.BlockSpec((half, d_model), lambda i: (i, 0)), fixed(up.shape)],
        out_specs=[pl.BlockSpec((half, ff), lambda i: (i, 0))] * 2,
        out_shape=[jax.ShapeDtypeStruct((rows, ff), BF), jax.ShapeDtypeStruct((rows, ff), F32)],
        compiler_params=vmem(24),
        cost_estimate=cost(2 * rows * d_model * ff, 10 << 20, rows * ff),
    )(ln, up)


def backward_kernel(cot_ref, slope_ref, up_ref, down_ref, dpre_ref, dln_ref):
    cols = (((1,), (1,)), ((), ()))
    grad = cot_ref[...].reshape(dln_ref.shape)
    for c in range(0, up_ref.shape[1], 256):
        part = pl.ds(c, 256)
        dhid = lax.dot_general(grad, down_ref[part, :], cols, preferred_element_type=F32)
        dpre_ref[:, part] = (dhid * slope_ref[:, part]).astype(BF)
    dln_ref[...] = lax.dot_general(
        dpre_ref[...], up_ref[...], cols, preferred_element_type=F32
    ).astype(BF)


def backward_rows(side, cot, slope, up, down):
    d_model, ff = up.shape
    half = slope.shape[0] // 2
    return pl.pallas_call(
        backward_kernel,
        grid=(1,),
        in_specs=[
            full(cot.shape), pl.BlockSpec((half, ff), lambda i: (side, 0)), fixed(up.shape), fixed(down.shape),
        ],
        out_specs=[full((half, ff)), full((half, d_model))],
        out_shape=[jax.ShapeDtypeStruct((half, ff), BF), jax.ShapeDtypeStruct((half, d_model), BF)],
        compiler_params=vmem(32),
        cost_estimate=cost(4 * half * d_model * ff, 10 << 20),
    )(cot, slope, up, down)


PARTS = ((0, 1, 2, 3), (1, 0, 2, 3), (2, 3, 0, 1), (3, 2, 0, 1))
SPREAD = ((0, 1, 2, 3), (1, 2, 3, 0), (2, 3, 0, 1), (3, 0, 1, 2))
YZ = (("dp", 1), ("context", 1), ("dp", 3), ("context", 3))


def piece_code(y, z, r, axes):
    ry, rz = y ^ (r // 4), z ^ (r % 4)
    bits = ((ry & 1) ^ (ry >> 1), (rz & 1) ^ (rz >> 1), ry >> 1, rz >> 1)
    a, b, c, d = (bits[i] for i in axes)
    return (a << 3) | (b << 2) | (c << 1) | d


def weight_kernel(k, hid_ref, ca_ref, cb_ref, ln_ref, da_ref, db_ref, keep_ref, send_ref, both):
    y, z = lax.axis_index("dp"), lax.axis_index("context")
    half = hid_ref.shape[0] // 2
    width = ca_ref.shape[2]
    rows = (((0,), (0,)), ((), ()))
    cot = [ref[...].reshape(half, width) for ref in (ca_ref, cb_ref)]
    down = lax.dot_general(hid_ref[pl.ds(0, half), :], cot[0], rows, preferred_element_type=F32)
    down += lax.dot_general(hid_ref[pl.ds(half, half), :], cot[1], rows, preferred_element_type=F32)
    down = (0.5 * down).astype(BF)
    up = lax.dot_general(ln_ref[pl.ds(0, half), :], da_ref[...], rows, preferred_element_type=F32)
    up += lax.dot_general(ln_ref[pl.ds(half, half), :], db_ref[...], rows, preferred_element_type=F32)
    up = up.astype(BF)
    for r in range(16):
        code = piece_code(y, z, r, PARTS[k])
        both[code, pl.ds(0, 48), :] = down[48 * r : 48 * r + 48]
        both[code, pl.ds(48, 48), :] = up[48 * r : 48 * r + 48]
    keep_ref[...] = both[pl.ds(0, 8)]
    send_ref[...] = both[pl.ds(8, 8)]


def weight_part(k, hidden, ca, cb, ln, dpre_a, dpre_b):
    rows = hidden.shape[0]
    return pl.pallas_call(
        functools.partial(weight_kernel, k),
        grid=(1,),
        in_specs=[
            full((rows, 768)),
            pl.BlockSpec((4, 128, 384), lambda i: (0, 0, k)),
            pl.BlockSpec((4, 128, 384), lambda i: (0, 0, k)),
            pl.BlockSpec((rows, 768), lambda i: (0, k // 2)),
            pl.BlockSpec((rows // 2, 384), lambda i: (0, k % 2)),
            pl.BlockSpec((rows // 2, 384), lambda i: (0, k % 2)),
        ],
        out_specs=[full((8, 96, 384))] * 2,
        out_shape=[jax.ShapeDtypeStruct((8, 96, 384), BF)] * 2,
        scratch_shapes=[pltpu.VMEM((16, 96, 384), BF)],
        compiler_params=vmem(32),
        cost_estimate=cost(4 * rows * 768 * 384, 7 << 20),
    )(hidden, ca, cb, ln, dpre_a, dpre_b)


def place_kernel(*refs):
    ins, (down_ref, up_ref, front_ref, kern_ref, gain_ref) = refs[:8], refs[8:]
    y, z = lax.axis_index("dp"), lax.axis_index("context")
    for k in range(4):

        @pl.when(pl.program_id(0) == k)
        def _():
            pair = ins[2 * k : 2 * k + 2]

            def piece(r, carry):
                code = piece_code(y, z, r, SPREAD[k])
                to = pl.ds(pl.multiple_of(48 * r, 16), 48)
                for side in range(2):

                    @pl.when((code // 8) == side)
                    def _():
                        at = pl.multiple_of((code - 8 * side) * 96, 16)
                        down_ref[to, :] = pair[side][pl.ds(at, 48), :].astype(F32)
                        up_ref[to, :] = pair[side][pl.ds(pl.multiple_of(at + 48, 16), 48), :].astype(F32)

                return carry

            lax.fori_loop(0, 16, piece, 0)
            last = [ref[pl.ds(768, 80), :].astype(F32) for ref in pair]
            front_ref[...] = last[0][:64] + last[1][:64]
            small = (last[0][64:72] + last[0][72:]) + (last[1][64:72] + last[1][72:])
            kern_ref[...] = small[:5]
            gain_ref[...] = small[5:6]


def place(pieces):
    shapes = [(768, 1536), (1536, 768), (64, 1536), (5, 1536), (1, 1536)]
    return pl.pallas_call(
        place_kernel,
        grid=(4,),
        in_specs=[pl.BlockSpec(memory_space=pltpu.VMEM)] * 8,
        out_specs=[
            pl.BlockSpec((768, 384), lambda k: (0, k)),
            pl.BlockSpec((768, 384), lambda k: (k // 2, k % 2)),
            pl.BlockSpec((64, 384), lambda k: (0, k)),
            pl.BlockSpec((5, 384), lambda k: (0, k)),
            pl.BlockSpec((1, 384), lambda k: (0, k)),
        ],
        out_shape=[jax.ShapeDtypeStruct(shape, F32) for shape in shapes],
        compiler_params=vmem(24),
        cost_estimate=cost(1 << 20, 14 << 20),
    )(*pieces)


def high_low(value):
    high = value.astype(BF).astype(F32)
    return jnp.concatenate([high, value - high], axis=0).astype(BF)


def add_small(one, two):
    one, two = one.astype(F32), two.astype(F32)
    return high_low((one[:8] + one[8:]) + (two[:8] + two[8:]))


def tail_kernel(
    k0, r0, k1, r1, normed_ref, rstd_ref, frames_ref, segs_ref, stack_ref, cot_ref, kern_ref, gain_ref,
    keep_ref, send_ref, scaled, moved, sums,
):
    sums[...] = jnp.zeros_like(sums)
    taps = [kern_ref[pl.ds(j, 1), :] for j in range(5)]
    gain = gain_ref[...]
    wide_stack = stack_ref[...].astype(F32)
    for j in range(5):
        here = segs_ref[pl.ds(HALO, 128), :]
        same = (segs_ref[pl.ds(HALO - 2 + j, 128), :] == here).astype(F32)
        same = jnp.concatenate([same] * 4, axis=1)
        moved[pl.ds(128 * j, 128), :] = (same * wide_stack[HALO - 2 + j : HALO + 126 + j]).astype(BF)

    def fold(x):
        return x[0:8] + x[8:16]

    for r in range(0, 128, 16):
        at = pl.ds(r, 16)
        dln = jnp.concatenate(
            [k0[at, :].astype(F32) + r0[at, :].astype(F32), k1[at, :].astype(F32) + r1[at, :].astype(F32)], axis=1
        )
        normed = normed_ref[at, :]
        rstd = rstd_ref[at, :][:, 0:1]
        sums[5] += fold(dln * normed)
        dnorm = dln * gain
        m1 = jnp.mean(dnorm, axis=1, keepdims=True)
        m2 = jnp.mean(dnorm * normed, axis=1, keepdims=True)
        dmixed = cot_ref[at, :].astype(F32) + rstd * (dnorm - m1 - normed * m2)
        dmixed = dmixed.astype(BF).astype(F32)
        here = segs_ref[pl.ds(HALO + r, 16), :]
        for j in range(5):
            near = frames_ref[pl.ds(HALO - 2 + r + j, 16), :]
            tap = taps[j]
            if j == 2:
                tap = tap + 1.0
                sums[j] += fold(dmixed * near)
            else:
                same = (segs_ref[pl.ds(HALO - 2 + r + j, 16), :] == here).astype(F32)
                same = jnp.concatenate([same] * 12, axis=1)
                sums[j] += fold(dmixed * (same * near))
            scaled[pl.ds(128 * j + r, 16), :] = (tap * dmixed).astype(BF)

    front = lax.dot_general(
        moved[...], scaled[...], (((0,), (0,)), ((), ())), preferred_element_type=F32
    )
    for d in range(4):
        keep_ref[pl.ds(64 * d, 64), :] = front[128 * d : 128 * d + 64]
        send_ref[pl.ds(64 * d, 64), :] = front[128 * d + 64 : 128 * d + 128].astype(BF)
    small = jnp.concatenate(
        [jnp.sum(sums[j], axis=0, keepdims=True) for j in range(6)] + [jnp.zeros((2, 1536), F32)], axis=0
    )
    small = high_low(small)
    keep_ref[pl.ds(256, 16), :] = small.astype(F32)
    send_ref[pl.ds(256, 16), :] = small


def tail(pieces, normed, rstd, frames, segs, stack, cot, kern, gain):
    args = (*pieces, normed, rstd, frames, segs, stack, cot, kern, gain)
    return pl.pallas_call(
        tail_kernel,
        grid=(1,),
        in_specs=[full(a.shape) for a in args],
        out_specs=[full((272, 1536))] * 2,
        out_shape=[jax.ShapeDtypeStruct((272, 1536), F32), jax.ShapeDtypeStruct((272, 1536), BF)],
        scratch_shapes=[
            pltpu.VMEM((640, 1536), BF), pltpu.VMEM((640, 512), BF), pltpu.VMEM((6, 8, 1536), F32),
        ],
        compiler_params=vmem(32),
        cost_estimate=cost(60 * 10**9, 6 << 20),
    )(*args)


def gather_core(value):
    own = jnp.stack([value] + [xor_send(value, "tensor", m, 8) for m in ORDER[1:]])
    return own, xor_send(own, "tensor", 1, 8)


def after(value, *others):
    return lax.optimization_barrier((value, *others))[0]


def over(axis, value):
    return xor_send(value, *YZ[axis], 4)


def glue(kernel, outs, *args, flops=5 * 10**8):
    whole = pl.BlockSpec(memory_space=pltpu.VMEM)
    return pl.pallas_call(
        kernel,
        in_specs=[whole] * len(args),
        out_specs=[whole] * len(outs),
        out_shape=[jax.ShapeDtypeStruct(*out) for out in outs],
        compiler_params=vmem(16),
        cost_estimate=cost(flops, 1 << 16),
    )(*args)


def dln_core_kernel(own, rec, keep0, keep1, send0, send1):
    for i in range(4):
        at = pl.ds(128 * i, 128)
        total = own[at, :].astype(F32) + rec[at, :].astype(F32)
        to = pl.ds(128 * (i // 2), 128)
        (send0 if i % 2 else keep0)[to, :] = total[:, :768].astype((send0 if i % 2 else keep0).dtype)
        to = pl.ds(128 * (i % 2), 128)
        (send1 if i // 2 else keep1)[to, :] = total[:, 768:].astype((send1 if i // 2 else keep1).dtype)


def halve_kernel(own, rec, keep, send):
    n = keep.shape[0]
    keep[...] = own[pl.ds(0, n)] + rec[pl.ds(0, n)].astype(F32)
    send[...] = (own[pl.ds(n, n)] + rec[pl.ds(n, n)].astype(F32)).astype(BF)


def halve_first_kernel(own, rec, keep, send):
    n = keep.shape[0]
    keep[...] = own[pl.ds(0, n)].astype(F32) + rec[pl.ds(0, n)].astype(F32)
    send[...] = (own[pl.ds(n, n)].astype(F32) + rec[pl.ds(n, n)].astype(F32)).astype(BF)


def join_kernel(own0, rec0, own1, rec1, keep, send):
    for i, (own, rec) in enumerate(((own0, rec0), (own1, rec1))):
        total = own[...] + rec[...].astype(F32)
        keep[:, pl.ds(96 * i, 96), :] = total[:2]
        send[:, pl.ds(96 * i, 96), :] = total[2:].astype(BF)


def front_core_kernel(own, rec, keep0, keep1, send0, send1):
    for i in range(4):
        at = pl.ds(64 * i, 64)
        total = own[at, :] + rec[at, :].astype(F32)
        to = pl.ds(64 * (i // 2), 64)
        (send0 if i % 2 else keep0)[to, :] = total[:, :768].astype((send0 if i % 2 else keep0).dtype)
        to = pl.ds(64 * (i % 2), 64)
        (send1 if i // 2 else keep1)[to, :] = total[:, 768:].astype((send1 if i // 2 else keep1).dtype)
    small = add_small(own[pl.ds(256, 16), :], rec[pl.ds(256, 16), :])
    for i, (keep, send) in enumerate(((keep0, send0), (keep1, send1))):
        half = small[:, 768 * i : 768 * i + 768]
        keep[pl.ds(128, 16), :] = half.astype(F32)
        send[pl.ds(128, 16), :] = half


def front_x_kernel(own, rec, keep, send):
    keep[pl.ds(0, 64), :] = own[pl.ds(0, 64), :] + rec[pl.ds(0, 64), :].astype(F32)
    send[pl.ds(0, 64), :] = (own[pl.ds(64, 64), :] + rec[pl.ds(64, 64), :].astype(F32)).astype(BF)
    small = add_small(own[pl.ds(128, 16), :], rec[pl.ds(128, 16), :])
    keep[pl.ds(64, 16), :] = small.astype(F32)
    send[pl.ds(64, 16), :] = small


def spread_first_kernel(own, rec, front, front_rec, out0, out1):
    piece = (own[0] + rec[0].astype(F32)).astype(BF)
    front_rows = (front[pl.ds(0, 64), :] + front_rec[pl.ds(0, 64), :].astype(F32)).astype(BF)
    small = add_small(front[pl.ds(64, 16), :], front_rec[pl.ds(64, 16), :])
    for i, out in enumerate((out0, out1)):
        out[pl.ds(0, 96), :] = piece[96 * i : 96 * i + 96]
        out[pl.ds(96, 64), :] = front_rows[:, 384 * i : 384 * i + 384]
        out[pl.ds(160, 16), :] = small[:, 384 * i : 384 * i + 384]


def spread_kernel(own, rec, out):
    n = own.shape[0] - 80
    out[pl.ds(0, n), :] = own[pl.ds(0, n), :]
    out[pl.ds(n, n), :] = rec[pl.ds(0, n), :]
    out[pl.ds(2 * n, 64), :] = (own[pl.ds(n, 64), :].astype(F32) + rec[pl.ds(n, 64), :].astype(F32)).astype(BF)
    out[pl.ds(2 * n + 64, 16), :] = add_small(own[pl.ds(n + 64, 16), :], rec[pl.ds(n + 64, 16), :])


def halve_first(keep, rec):
    return glue(halve_first_kernel, [((4, 96, 384), F32), ((4, 96, 384), BF)], keep, rec)


def reduce_parts(pairs):
    recs = [over(PARTS[k][1], pairs[k][1]) for k in range(4)]
    ends = []
    for k in (0, 2):
        keep, send = glue(
            join_kernel, [((2, 192, 384), F32), ((2, 192, 384), BF)],
            pairs[k][0], recs[k], pairs[k + 1][0], recs[k + 1],
        )
        keep, send = glue(
            halve_kernel, [((1, 192, 384), F32), ((1, 192, 384), BF)], keep, over(PARTS[k][2], send)
        )
        ends.append((keep, over(PARTS[k][3], send)))
    return ends


def spread_parts(ends, fronts):
    bufs = []
    for k in (0, 1):
        bufs += glue(spread_first_kernel, [((176, 384), BF)] * 2, *ends[k], *fronts[k])
    for s in (3, 2, 1):
        recs = [over(SPREAD[k][s], bufs[k]) for k in range(4)]
        rows = 2 * bufs[0].shape[0] - 80
        bufs = [glue(spread_kernel, [((rows, 384), BF)], bufs[k], recs[k])[0] for k in range(4)]
    pieces = []
    for k in range(4):
        pieces += [bufs[k], over(SPREAD[k][0], bufs[k])]
    return pieces


def per_device(
    panels, lengths, segments, front_weight, conv_kernel, gain, up_weight, down_weight, cotangent
):
    gain_row = gain[None, :]
    cot = cotangent[0]

    picked = select_panels(lengths, jnp.transpose(panels[0, 0], (1, 2, 0)), segments)
    *picked, front_weight = lax.optimization_barrier((*picked, front_weight))
    got = [xor_send(picked[e], "context", e, 4) for e in (2, 1, 3)]
    wa, wb = gather_core(front_weight)
    block = picked[0] + got[0] + got[1] + got[2]
    block, cot = lax.optimization_barrier((block, cot))
    pa, pb = gather_core(block)
    others = [xor_send(cot, "tensor", m ^ 1, 8) for m in ORDER]

    ln, normed, rstd, frames, segs, stack = normalise(pa, pb, wa, wb, conv_kernel, gain_row)
    hidden, slope = hidden_rows(ln, up_weight)
    slope, *others = lax.optimization_barrier((slope, *others))
    cb = jnp.stack(others)
    ca = xor_send(cb, "tensor", 1, 8)
    dpre_a, dln_keep = backward_rows(0, ca, slope, up_weight, down_weight)
    dpre_b, dln_send = backward_rows(1, cb, slope, up_weight, down_weight)

    dln_rec = xor_send(dln_send, "tensor", 1, 8)
    k0, k1, s0, s1 = glue(
        dln_core_kernel, [((256, 768), F32)] * 2 + [((256, 768), BF)] * 2, dln_keep, dln_rec
    )
    r0, r1 = xor_send(s0, "tensor", 2, 8), xor_send(s1, "tensor", 6, 8)
    parts = [weight_part(k, hidden, ca, cb, ln, dpre_a, dpre_b) for k in range(4)]
    half = [((128, 768), F32), ((128, 768), BF)]
    k0, s0 = glue(halve_kernel, half, k0, r0)
    k1, s1 = glue(halve_kernel, half, k1, r1)
    pieces = (k0, xor_send(s0, "tensor", 6, 8), k1, xor_send(s1, "tensor", 2, 8))
    keep, send = tail(pieces, normed, rstd, frames, segs, stack, cot, conv_kernel, gain_row)
    pairs = [halve_first(parts[k][0], over(PARTS[k][0], parts[k][1])) for k in range(4)]
    k0, k1, s0, s1 = glue(
        front_core_kernel, [((144, 768), F32)] * 2 + [((144, 768), BF)] * 2,
        keep, xor_send(send, "tensor", 1, 8), flops=FIRST,
    )
    ends = reduce_parts(pairs)
    half = [((80, 768), F32), ((80, 768), BF)]
    k0, s0 = glue(front_x_kernel, half, k0, xor_send(s0, "tensor", 2, 8), flops=FIRST)
    k1, s1 = glue(front_x_kernel, half, k1, xor_send(s1, "tensor", 6, 8), flops=FIRST)
    fronts = (k0, xor_send(s0, "tensor", 6, 8)), (k1, xor_send(s1, "tensor", 2, 8))
    pieces = spread_parts(ends, fronts)
    grad_down, grad_up, grad_front, grad_kernel, grad_gain = place(pieces)
    return (grad_front, grad_kernel, grad_gain[0], grad_up, grad_down)


def solution(mesh):
    return jax.shard_map(
        per_device,
        mesh=mesh,
        in_specs=(
            P("dp", "context", None, None, "tensor"),
            P("dp", None),
            P("dp", ("context", "tensor")),
            P("tensor", None),
            P(),
            P(),
            P(None, "tensor"),
            P("tensor", None),
            P("dp", ("context", "tensor"), None),
        ),
        out_specs=(P("tensor", None), P(), P(), P(None, "tensor"), P("tensor", None)),
        check_vma=False,
    )
```

time: 236 us -> 171 us (0.72); the launches traced: 231 us -> 171 us
  Pallas kernels: 58.1 us -> 40.1 us
  waiting for transfers between devices: 65.9 us -> 50.5 us
  starting transfers between devices: 87.4 us -> 73.7 us
  other arithmetic: 10.6 us -> 1.96 us
  local copies, waits for them, and re-layouts: 7.3 us -> 3.64 us
    pallas_call x2 -> x32, Pallas kernels: 39 us -> 23.1 us  [the longest x1 10.8 us: normalise(): pl.pallas_call(norm_kernel, grid=(8,), in_specs=[full(a.shape), full(b.sh...]
    ppermute x63 -> x54, waiting for transfers between devices: 65.9 us -> 50.5 us  [xor_send(): return lax.ppermute(value, axis, [(i, i ^ mask) for i in range(size)])]
    ppermute x63 -> x54, starting transfers between devices: 87.4 us -> 73.7 us  [xor_send(): return lax.ppermute(value, axis, [(i, i ^ mask) for i in range(size)])]
    unnamed x24 -> x16, local copies, waits for them, and re-layouts: 5.95 us -> 3.63 us
  transfers between devices with their start and end apart: 63 -> 54, of which waited for: 26 -> 25; matrix products, arithmetic and copies ran while one was open for 5% -> 1% of each run, Pallas kernels for 17% -> 20%
where the time goes in v2:
time: 171 us
  starting transfers between devices  73.7 us (43%)
  waiting for transfers between devices  50.5 us (30%)
  Pallas kernels  40.1 us (23%)
  local copies, waits for them, and re-layouts  3.64 us (2%)
  other arithmetic  1.96 us (1%)
    ppermute x54, starting transfers between devices, xor_send(): return lax.ppermute(value, axis, [(i, i ^ mask) for i in range(size)])  73.7 us
    ppermute x54, waiting for transfers between devices, xor_send(): return lax.ppermute(value, axis, [(i, i ^ mask) for i in range(size)])  50.5 us
    pallas_call x1, Pallas kernels, normalise(): pl.pallas_call(norm_kernel, grid=(8,), in_specs=[full(a.shape), full(b.sh...  10.8 us
    pallas_call x4, Pallas kernels, weight_part(): pl.pallas_call(functools.partial(weight_kernel, k), grid=(1,), in_specs=[...  7.98 us
    pallas_call x2, Pallas kernels, backward_rows(): pl.pallas_call(backward_kernel, grid=(1,), in_specs=[full(cot.shape), pl....  6.32 us
    pallas_call x1, Pallas kernels, place(): pl.pallas_call(place_kernel, grid=(4,), in_specs=[pl.BlockSpec(memory_spa...  4.98 us
    unnamed x16, local copies, waits for them, and re-layouts  3.63 us
    pallas_call x1, Pallas kernels, hidden_rows(): pl.pallas_call(hidden_kernel, grid=(2,), in_specs=[pl.BlockSpec((half, d_...  3.51 us
  transfers between devices with their start and end apart: 54, of which 25 were waited for; matrix products, arithmetic and copies ran while one was open for 1% of the time, Pallas kernels for 20%

profile of v2, /device:TPU:0, one launch (start us, length us, event | category | flops | bytes accessed | tf_op | source)
XLA Modules:
  0.0 171.0 jit_solution(4698505644737051406)
XLA Ops:
  0.6 1.0 copy-done.2
  3.0 1.2 shard_map.128
  4.2 4.0 %collective-permute-start = (bf16[640,128]{1,0:T(8,128)(2,1)S(1)}, bf16[640,128]{1,0:T(8,128)(2,1)S(1)}, u32[]{:S(2)}, u32[]{:S(2)}) collective-permute-start(bf16[640,128]{1,0:T(8,128)(2,1)S(1)} %get-tuple-element.89), channel_id=1, source_target_pairs={{0,16},{8,24},{16,0},{24,8},{1,17},{9,25},{17,1},{25,9},{2,18},{10... | collective-permute-start | bytes 491528 | tf_op jit(solution)/shard_map/ppermute | solution.py:36
  8.3 1.0 collective-permute-start.1
  9.3 3.0 %collective-permute-start.9 = (bf16[64,1536]{1,0:T(8,128)(2,1)}, bf16[64,1536]{1,0:T(8,128)(2,1)S(1)}, u32[]{:S(2)}, u32[]{:S(2)}) collective-permute-start(bf16[64,1536]{1,0:T(8,128)(2,1)} %param.12), channel_id=1, source_target_pairs={{0,4},{1,5},{2,6},{3,7},{4,0},{5,1},{6,2},{7,3},{8,12},{9,13},{10,... | collective-permute-start | bytes 589832 | tf_op jit(solution)/shard_map/ppermute | solution.py:36
  12.3 1.1 collective-permute-start.8
  13.5 1.3 collective-permute-start.7
  14.8 2.0 %collective-permute-done.1 = bf16[640,128]{1,0:T(8,128)(2,1)S(1)} collective-permute-done((bf16[640,128]{1,0:T(8,128)(2,1)S(1)}, bf16[640,128]{1,0:T(8,128)(2,1)S(1)}, u32[]{:S(2)}, u32[]{:S(2)}) %collective-permute-start.1) | collective-permute-done | bytes 163872 | tf_op jit(solution)/shard_map/ppermute | solution.py:36
  16.8 3.1 %collective-permute-start.5 = (bf16[640,128]{1,0:T(8,128)(2,1)S(1)}, bf16[640,128]{1,0:T(8,128)(2,1)S(1)}, u32[]{:S(2)}, u32[]{:S(2)}) collective-permute-start(bf16[640,128]{1,0:T(8,128)(2,1)S(1)} %add_add_fusion), channel_id=1, source_target_pairs={{0,4},{1,5},{2,6},{3,7},{4,0},{5,1},{6,2},{7,3},{8,12},{9,13},{10,... | collective-permute-start | bytes 491528 | tf_op jit(solution)/shard_map/ppermute | solution.py:36
  19.9 1.1 collective-permute-start.4
  21.1 1.7 collective-permute-done.8
  22.8 1.0 pad_maximum_fusion.1.wa_ref
  23.9 2.2 %collective-permute-done.5 = bf16[640,128]{1,0:T(8,128)(2,1)S(1)} collective-permute-done((bf16[640,128]{1,0:T(8,128)(2,1)S(1)}, bf16[640,128]{1,0:T(8,128)(2,1)S(1)}, u32[]{:S(2)}, u32[]{:S(2)}) %collective-permute-start.5) | collective-permute-done | bytes 163872 | tf_op jit(solution)/shard_map/ppermute | solution.py:36
  26.1 2.2 %collective-permute-done.4 = bf16[640,128]{1,0:T(8,128)(2,1)S(1)} collective-permute-done((bf16[640,128]{1,0:T(8,128)(2,1)S(1)}, bf16[640,128]{1,0:T(8,128)(2,1)S(1)}, u32[]{:S(2)}, u32[]{:S(2)}) %collective-permute-start.4) | collective-permute-done | bytes 163872 | tf_op jit(solution)/shard_map/ppermute | solution.py:36
  28.7 2.2 %collective-permute-start.14 = (bf16[128,1536]{1,0:T(8,128)(2,1)S(1)}, bf16[128,1536]{1,0:T(8,128)(2,1)S(1)}, u32[]{:S(2)}, u32[]{:S(2)}) collective-permute-start(bf16[128,1536]{1,0:T(8,128)(2,1)S(1)} %bitcast.17), channel_id=1, source_target_pairs={{0,5},{1,4},{2,7},{3,6},{4,1},{5,0},{6,3},{7,2},{8,13},{9,12},{10,... | collective-permute-start | bytes 1179656 | tf_op jit(solution)/shard_map/ppermute | solution.py:36
  30.9 1.7 collective-permute-start.13
  33.1 10.8 %shard_map.129 = (bf16[1024,1536]{1,0:T(8,128)(2,1)S(1)}, f32[128,1536]{1,0:T(8,128)S(1)}, f32[128,128]{1,0:T(8,128)S(1)}, f32[160,1536]{1,0:T(8,128)S(1)}, f32[...) custom-call(bf16[4,640,128]{2,1,0:T(8,128)(2,1)S(1)} %pad_maximum_fusion.2.a_ref, ...), custom_call_target="tpu_custom_call" | custom-call | flops 12000000000 | bytes 10485760 | tf_op jit(solution)/shard_map/pallas_call | solution.py:189
  43.9 3.5 %shard_map.130 = (bf16[1024,768]{1,0:T(8,128)(2,1)S(1)}, f32[1024,768]{1,0:T(8,128)S(1)}) custom-call(bf16[1024,1536]{1,0:T(8,128)(2,1)S(1)} %get-tuple-element.94.ln_ref, bf16[1536,768]{1,0:T(8,128)(2,1)S(1)} %copy-done), custom_call_target="tpu_custom_call" | custom-call | flops 2415919104 | bytes 10485760 | tf_op jit(solution)/shard_map/pallas_call | solution.py:233
  47.4 2.7 %collective-permute-done.13 = bf16[128,1536]{1,0:T(8,128)(2,1)S(1)} collective-permute-done((bf16[128,1536]{1,0:T(8,128)(2,1)S(1)}, bf16[128,1536]{1,0:T(8,128)(2,1)S(1)}, u32[]{:S(2)}, u32[]{:S(2)}) %collective-permute-start.13) | collective-permute-done | bytes 393248 | tf_op jit(solution)/shard_map/ppermute | solution.py:36
  50.5 1.3 copy-done.1
  51.8 3.2 %shard_map.132 = (bf16[512,768]{1,0:T(8,128)(2,1)S(1)}, bf16[512,1536]{1,0:T(8,128)(2,1)S(1)}) custom-call(bf16[4,128,1536]{2,1,0:T(8,128)(2,1)S(1)} %pad_maximum_fusion.cot_ref.cb_ref, f32[1024,768]{1,0:T(8,128)S(1)} %get-tuple-element.102.slope_ref, bf16[1536,768]{1,0:T(8,128)(2,1)S(1)} %copy-done, bf16[768,1536]{1,0:T(8,128)(2,1)S(1)} %copy-done.1), custom_call_target="tpu_custom_call" | custom-call | flops 2415919104 | bytes 10485760 | tf_op jit(solution)/shard_map/pallas_call | solution.py:259
  55.3 3.2 %shard_map.131 = (bf16[512,768]{1,0:T(8,128)(2,1)S(1)}, bf16[512,1536]{1,0:T(8,128)(2,1)S(1)}) custom-call(bf16[4,128,1536]{2,1,0:T(8,128)(2,1)S(1)} %collective-permute-done.15.cot_ref.ca_ref, f32[1024,768]{1,0:T(8,128)S(1)} %get-tuple-element.102.slope_ref, bf16[1536,768]{1,0:T(8,128)(2,1)S(1)} %copy-done, bf16[768,1536]{1,0:T(8,128)(2,1)S(1)} %copy-done.1), custom_call_target="tpu_custom_call" | custom-call | flops 2415919104 | bytes 10485760 | tf_op jit(solution)/shard_map/pallas_call | solution.py:259
  58.9 1.5 collective-permute-start.23
  60.5 1.3 collective-permute-start.25
  61.8 2.0 %shard_map.154 = (bf16[8,96,384]{2,1,0:T(8,128)(2,1)S(1)}, bf16[8,96,384]{2,1,0:T(8,128)(2,1)S(1)}) custom-call(bf16[1024,768]{1,0:T(8,128)(2,1)S(1)} %get-tuple-element.95.hid_ref, bf16[4,128,1536]{2,1,0:T(8,128)(2,1)S(1)} %collective-permute-done.15.cot_ref.ca_ref, bf16[4,128,1536]{2,1,0:T(8,128)(2,1)S(1)} %pad_maximum_fusion.cot_ref.cb_ref, ...), custom_call_target="tpu_custom_call" | custom-call | flops 1207959552 | bytes 7340032 | tf_op jit(solution)/shard_map/pallas_call | solution.py:306
  63.8 3.0 %collective-permute-start.40 = (bf16[8,96,384]{2,1,0:T(8,128)(2,1)S(1)}, bf16[8,96,384]{2,1,0:T(8,128)(2,1)S(1)}, u32[]{:S(2)}, u32[]{:S(2)}) collective-permute-start(bf16[8,96,384]{2,1,0:T(8,128)(2,1)S(1)} %get-tuple-element.145), channel_id=1, source_target_pairs={{0,24},{8,16},{16,8},{24,0},{1,25},{9,17},{17,9},{25,1},{2,26},{10... | collective-permute-start | bytes 1769480 | tf_op jit(solution)/shard_map/ppermute | solution.py:36
  66.8 2.0 %shard_map.152 = (bf16[8,96,384]{2,1,0:T(8,128)(2,1)S(1)}, bf16[8,96,384]{2,1,0:T(8,128)(2,1)S(1)}) custom-call(bf16[1024,768]{1,0:T(8,128)(2,1)S(1)} %get-tuple-element.95.hid_ref, bf16[4,128,1536]{2,1,0:T(8,128)(2,1)S(1)} %collective-permute-done.15.cot_ref.ca_ref, bf16[4,128,1536]{2,1,0:T(8,128)(2,1)S(1)} %pad_maximum_fusion.cot_ref.cb_ref, ...), custom_call_target="tpu_custom_call" | custom-call | flops 1207959552 | bytes 7340032 | tf_op jit(solution)/shard_map/pallas_call | solution.py:306
  68.8 3.1 %collective-permute-start.38 = (bf16[8,96,384]{2,1,0:T(8,128)(2,1)S(1)}, bf16[8,96,384]{2,1,0:T(8,128)(2,1)S(1)}, u32[]{:S(2)}, u32[]{:S(2)}) collective-permute-start(bf16[8,96,384]{2,1,0:T(8,128)(2,1)S(1)} %get-tuple-element.141), channel_id=1, source_target_pairs={{0,96},{32,64},{64,32},{96,0},{1,97},{33,65},{65,33},{97,1},{2,98}... | collective-permute-start | bytes 1769480 | tf_op jit(solution)/shard_map/ppermute | solution.py:36
  72.0 2.1 %collective-permute-start.24 = (bf16[128,768]{1,0:T(8,128)(2,1)S(1)}, bf16[128,768]{1,0:T(8,128)(2,1)S(1)}, u32[]{:S(2)}, u32[]{:S(2)}) collective-permute-start(bf16[128,768]{1,0:T(8,128)(2,1)S(1)} %get-tuple-element.122), channel_id=1, source_target_pairs={{0,6},{1,7},{2,4},{3,5},{4,2},{5,3},{6,0},{7,1},{8,14},{9,15},{10,... | collective-permute-start | bytes 589832 | tf_op jit(solution)/shard_map/ppermute | solution.py:36
  74.2 2.0 %shard_map.135 = (bf16[8,96,384]{2,1,0:T(8,128)(2,1)S(1)}, bf16[8,96,384]{2,1,0:T(8,128)(2,1)S(1)}) custom-call(bf16[1024,768]{1,0:T(8,128)(2,1)S(1)} %get-tuple-element.95.hid_ref, bf16[4,128,1536]{2,1,0:T(8,128)(2,1)S(1)} %collective-permute-done.15.cot_ref.ca_ref, bf16[4,128,1536]{2,1,0:T(8,128)(2,1)S(1)} %pad_maximum_fusion.cot_ref.cb_ref, ...), custom_call_target="tpu_custom_call" | custom-call | flops 1207959552 | bytes 7340032 | tf_op jit(solution)/shard_map/pallas_call | solution.py:306
  76.4 2.0 %shard_map.133 = (bf16[8,96,384]{2,1,0:T(8,128)(2,1)S(1)}, bf16[8,96,384]{2,1,0:T(8,128)(2,1)S(1)}) custom-call(bf16[1024,768]{1,0:T(8,128)(2,1)S(1)} %get-tuple-element.95.hid_ref, bf16[4,128,1536]{2,1,0:T(8,128)(2,1)S(1)} %collective-permute-done.15.cot_ref.ca_ref, bf16[4,128,1536]{2,1,0:T(8,128)(2,1)S(1)} %pad_maximum_fusion.cot_ref.cb_ref, ...), custom_call_target="tpu_custom_call" | custom-call | flops 1207959552 | bytes 7340032 | tf_op jit(solution)/shard_map/pallas_call | solution.py:306
  78.4 1.1 collective-permute-done.24.r0
  80.3 2.9 %shard_map.142 = (f32[272,1536]{1,0:T(8,128)S(1)}, bf16[272,1536]{1,0:T(8,128)(2,1)S(1)}) custom-call(f32[128,768]{1,0:T(8,128)S(1)} %get-tuple-element.121.k0, bf16[128,768]{1,0:T(8,128)(2,1)S(1)} %collective-permute-done.24.r0, f32[128,768]{1,0:T(8,128)S(1)} %get-tuple-element.125.k1, bf16[128,768]{1,0:T(8,128)(2,1)S(1)} %collective-permute-done.26.r1, ...), custom_call_target="tpu_custom_call" | custom-call | flops 60000002048 | bytes 6291456 | tf_op jit(solution)/shard_map/pallas_call | solution.py:443
  83.2 7.2 %collective-permute-done.18.rec = bf16[8,96,384]{2,1,0:T(8,128)(2,1)S(1)} collective-permute-done((bf16[8,96,384]{2,1,0:T(8,128)(2,1)S(1)}, bf16[8,96,384]{2,1,0:T(8,128)(2,1)S(1)}, u32[]{:S(2)}, u32[]{:S(2)}) %collective-permute-start.18) | collective-permute-done | bytes 589856 | tf_op jit(solution)/shard_map/ppermute | solution.py:36
  90.5 1.1 collective-permute-start.19
  91.6 3.7 %collective-permute-done.16.rec = bf16[8,96,384]{2,1,0:T(8,128)(2,1)S(1)} collective-permute-done((bf16[8,96,384]{2,1,0:T(8,128)(2,1)S(1)}, bf16[8,96,384]{2,1,0:T(8,128)(2,1)S(1)}, u32[]{:S(2)}, u32[]{:S(2)}) %collective-permute-start.16) | collective-permute-done | bytes 589856 | tf_op jit(solution)/shard_map/ppermute | solution.py:36
  95.4 1.6 collective-permute-start.17
  97.2 2.0 %collective-permute-start.41 = (bf16[4,96,384]{2,1,0:T(8,128)(2,1)S(1)}, bf16[4,96,384]{2,1,0:T(8,128)(2,1)S(1)}, u32[]{:S(2)}, u32[]{:S(2)}) collective-permute-start(bf16[4,96,384]{2,1,0:T(8,128)(2,1)S(1)} %get-tuple-element.147), channel_id=1, source_target_pairs={{0,96},{32,64},{64,32},{96,0},{1,97},{33,65},{65,33},{97,1},{2,98}... | collective-permute-start | bytes 884744 | tf_op jit(solution)/shard_map/ppermute | solution.py:36
  99.3 3.3 %collective-permute-start.39 = (bf16[4,96,384]{2,1,0:T(8,128)(2,1)S(1)}, bf16[4,96,384]{2,1,0:T(8,128)(2,1)S(1)}, u32[]{:S(2)}, u32[]{:S(2)}) collective-permute-start(bf16[4,96,384]{2,1,0:T(8,128)(2,1)S(1)} %get-tuple-element.143), channel_id=1, source_target_pairs={{0,24},{8,16},{16,8},{24,0},{1,25},{9,17},{17,9},{25,1},{2,26},{10... | collective-permute-start | bytes 884744 | tf_op jit(solution)/shard_map/ppermute | solution.py:36
  102.7 2.2 %collective-permute-start.20 = (bf16[2,192,384]{2,1,0:T(8,128)(2,1)S(1)}, bf16[2,192,384]{2,1,0:T(8,128)(2,1)S(1)}, u32[]{:S(2)}, u32[]{:S(2)}) collective-permute-start(bf16[2,192,384]{2,1,0:T(8,128)(2,1)S(1)} %get-tuple-element.114), channel_id=1, source_target_pairs={{0,96},{32,64},{64,32},{96,0},{1,97},{33,65},{65,33},{97,1},{2,98}... | collective-permute-start | bytes 884744 | tf_op jit(solution)/shard_map/ppermute | solution.py:36
  104.9 3.1 %collective-permute-done.41.rec1 = bf16[4,96,384]{2,1,0:T(8,128)(2,1)S(1)} collective-permute-done((bf16[4,96,384]{2,1,0:T(8,128)(2,1)S(1)}, bf16[4,96,384]{2,1,0:T(8,128)(2,1)S(1)}, u32[]{:S(2)}, u32[]{:S(2)}) %collective-permute-start.41) | collective-permute-done | bytes 294944 | tf_op jit(solution)/shard_map/ppermute | solution.py:36
  108.4 1.6 collective-permute-start.28
  110.0 1.8 %collective-permute-start.44 = (bf16[144,768]{1,0:T(8,128)(2,1)S(1)}, bf16[144,768]{1,0:T(8,128)(2,1)S(1)}, u32[]{:S(2)}, u32[]{:S(2)}) collective-permute-start(bf16[144,768]{1,0:T(8,128)(2,1)S(1)} %get-tuple-element.153), channel_id=1, source_target_pairs={{0,6},{1,7},{2,4},{3,5},{4,2},{5,3},{6,0},{7,1},{8,14},{9,15},{10,... | collective-permute-start | bytes 663560 | tf_op jit(solution)/shard_map/ppermute | solution.py:36
  111.9 2.7 %collective-permute-start.21 = (bf16[1,192,384]{2,1,0:T(8,128)(2,1)S(1)}, bf16[1,192,384]{2,1,0:T(8,128)(2,1)S(1)}, u32[]{:S(2)}, u32[]{:S(2)}) collective-permute-start(bf16[1,192,384]{2,1,0:T(8,128)(2,1)S(1)} %get-tuple-element.116), channel_id=1, source_target_pairs={{0,24},{8,16},{16,8},{24,0},{1,25},{9,17},{17,9},{25,1},{2,26},{10... | collective-permute-start | bytes 442376 | tf_op jit(solution)/shard_map/ppermute | solution.py:36
  114.6 2.1 %collective-permute-start.29 = (bf16[80,768]{1,0:T(8,128)(2,1)S(1)}, bf16[80,768]{1,0:T(8,128)(2,1)S(1)}, u32[]{:S(2)}, u32[]{:S(2)}) collective-permute-start(bf16[80,768]{1,0:T(8,128)(2,1)S(1)} %get-tuple-element.137), channel_id=1, source_target_pairs={{0,6},{1,7},{2,4},{3,5},{4,2},{5,3},{6,0},{7,1},{8,14},{9,15},{10,... | collective-permute-start | bytes 368648 | tf_op jit(solution)/shard_map/ppermute | solution.py:36
  117.1 1.2 collective-permute-done.44.rec
  118.4 2.4 %collective-permute-done.29.front_rec = bf16[80,768]{1,0:T(8,128)(2,1)S(1)} collective-permute-done((bf16[80,768]{1,0:T(8,128)(2,1)S(1)}, bf16[80,768]{1,0:T(8,128)(2,1)S(1)}, u32[]{:S(2)}, u32[]{:S(2)}) %collective-permute-start.29) | collective-permute-done | bytes 122912 | tf_op jit(solution)/shard_map/ppermute | solution.py:36
  120.9 3.3 %collective-permute-start.34 = (bf16[176,384]{1,0:T(8,128)(2,1)S(1)}, bf16[176,384]{1,0:T(8,128)(2,1)S(1)}, u32[]{:S(2)}, u32[]{:S(2)}) collective-permute-start(bf16[176,384]{1,0:T(8,128)(2,1)S(1)} %get-tuple-element.139.own), channel_id=1, source_target_pairs={{0,32},{32,0},{64,96},{96,64},{1,33},{33,1},{65,97},{97,65},{2,34}... | collective-permute-start | bytes 405512 | tf_op jit(solution)/shard_map/ppermute | solution.py:36
  124.1 2.5 %collective-permute-start.30 = (bf16[176,384]{1,0:T(8,128)(2,1)S(1)}, bf16[176,384]{1,0:T(8,128)(2,1)S(1)}, u32[]{:S(2)}, u32[]{:S(2)}) collective-permute-start(bf16[176,384]{1,0:T(8,128)(2,1)S(1)} %get-tuple-element.138.own), channel_id=1, source_target_pairs={{0,24},{8,16},{16,8},{24,0},{1,25},{9,17},{17,9},{25,1},{2,26},{10... | collective-permute-start | bytes 405512 | tf_op jit(solution)/shard_map/ppermute | solution.py:36
  126.8 1.6 collective-permute-start.50
  128.8 1.5 collective-permute-start.35
  130.4 3.3 %collective-permute-start.31 = (bf16[272,384]{1,0:T(8,128)(2,1)S(1)}, bf16[272,384]{1,0:T(8,128)(2,1)S(1)}, u32[]{:S(2)}, u32[]{:S(2)}) collective-permute-start(bf16[272,384]{1,0:T(8,128)(2,1)S(1)} %shard_map.146.own), channel_id=1, source_target_pairs={{0,96},{32,64},{64,32},{96,0},{1,97},{33,65},{65,33},{97,1},{2,98}... | collective-permute-start | bytes 626696 | tf_op jit(solution)/shard_map/ppermute | solution.py:36
  134.7 1.0 collective-permute-start.47
  136.5 2.3 %collective-permute-start.36 = (bf16[464,384]{1,0:T(8,128)(2,1)S(1)}, bf16[464,384]{1,0:T(8,128)(2,1)S(1)}, u32[]{:S(2)}, u32[]{:S(2)}) collective-permute-start(bf16[464,384]{1,0:T(8,128)(2,1)S(1)} %shard_map.150.own), channel_id=1, source_target_pairs={{0,96},{32,64},{64,32},{96,0},{1,97},{33,65},{65,33},{97,1},{2,98}... | collective-permute-start | bytes 1069064 | tf_op jit(solution)/shard_map/ppermute | solution.py:36
  141.1 1.8 %collective-permute-start.48 = (bf16[464,384]{1,0:T(8,128)(2,1)S(1)}, bf16[464,384]{1,0:T(8,128)(2,1)S(1)}, u32[]{:S(2)}, u32[]{:S(2)}) collective-permute-start(bf16[464,384]{1,0:T(8,128)(2,1)S(1)} %shard_map.161.own), channel_id=1, source_target_pairs={{0,24},{8,16},{16,8},{24,0},{1,25},{9,17},{17,9},{25,1},{2,26},{10... | collective-permute-start | bytes 1069064 | tf_op jit(solution)/shard_map/ppermute | solution.py:36
  142.9 3.5 %collective-permute-done.36.rec = bf16[464,384]{1,0:T(8,128)(2,1)S(1)} collective-permute-done((bf16[464,384]{1,0:T(8,128)(2,1)S(1)}, bf16[464,384]{1,0:T(8,128)(2,1)S(1)}, u32[]{:S(2)}, u32[]{:S(2)}) %collective-permute-start.36) | collective-permute-done | bytes 356384 | tf_op jit(solution)/shard_map/ppermute | solution.py:36
  146.5 1.5 collective-permute-start.37
  148.0 2.4 %collective-permute-done.32.rec = bf16[464,384]{1,0:T(8,128)(2,1)S(1)} collective-permute-done((bf16[464,384]{1,0:T(8,128)(2,1)S(1)}, bf16[464,384]{1,0:T(8,128)(2,1)S(1)}, u32[]{:S(2)}, u32[]{:S(2)}) %collective-permute-start.32) | collective-permute-done | bytes 356384 | tf_op jit(solution)/shard_map/ppermute | solution.py:36
  153.6 1.1 collective-permute-start.49
  154.7 4.2 %collective-permute-done.37.refs_3_ = bf16[848,384]{1,0:T(8,128)(2,1)S(1)} collective-permute-done((bf16[848,384]{1,0:T(8,128)(2,1)S(1)}, bf16[848,384]{1,0:T(8,128)(2,1)S(1)}, u32[]{:S(2)}, u32[]{:S(2)}) %collective-permute-start.37) | collective-permute-done | bytes 651296 | tf_op jit(solution)/shard_map/ppermute | solution.py:36
  158.9 2.2 %collective-permute-done.33.refs_1_ = bf16[848,384]{1,0:T(8,128)(2,1)S(1)} collective-permute-done((bf16[848,384]{1,0:T(8,128)(2,1)S(1)}, bf16[848,384]{1,0:T(8,128)(2,1)S(1)}, u32[]{:S(2)}, u32[]{:S(2)}) %collective-permute-start.33) | collective-permute-done | bytes 651296 | tf_op jit(solution)/shard_map/ppermute | solution.py:36
  161.1 2.6 %collective-permute-done.53.refs_7_ = bf16[848,384]{1,0:T(8,128)(2,1)S(1)} collective-permute-done((bf16[848,384]{1,0:T(8,128)(2,1)S(1)}, bf16[848,384]{1,0:T(8,128)(2,1)S(1)}, u32[]{:S(2)}, u32[]{:S(2)}) %collective-permute-start.53) | collective-permute-done | bytes 651296 | tf_op jit(solution)/shard_map/ppermute | solution.py:36
  163.7 1.7 collective-permute-done.49.refs_5_
  165.4 5.0 %shard_map.166 = (f32[768,1536]{1,0:T(8,128)}, f32[1536,768]{1,0:T(8,128)}, f32[64,1536]{1,0:T(8,128)}, f32[5,1536]{1,0:T(8,128)}, f32[1,1536]{1,0:T(1,128)S(1)}) custom-call(bf16[848,384]{1,0:T(8,128)(2,1)S(1)} %shard_map.148.refs_0_, bf16[848,384]{1,0:T(8,128)(2,1)S(1)} %collective-permute-done.33.refs_1_, bf16[848,384]{1,0:T(8,128)(2,1)S(1)} %shard_map.151.refs_2_, ...), custom_call_target="tpu_custom_call" | custom-call | flops 1048576 | bytes 14680064 | tf_op jit(solution)/shard_map/pallas_call | solution.py:357
  (105 shorter events, 15.1 us)
Async XLA Ops:
  0.6 1.0 copy-start.2
  1.7 0.7 copy-start.3
  2.3 0.7 copy-start.4
  4.2 9.2 %collective-permute-start = (bf16[640,128]{1,0:T(8,128)(2,1)S(1)}, bf16[640,128]{1,0:T(8,128)(2,1)S(1)}, u32[]{:S(2)}, u32[]{:S(2)}) collective-permute-start(bf16[640,128]{1,0:T(8,128)(2,1)S(1)} %get-tuple-element.89), channel_id=1, source_target_pairs={{0,16},{8,24},{16,0},{24,8},{1,17},{9,25},{17,1},{25,9},{2,18},{10... | collective-permute-start | bytes 491528 | tf_op jit(solution)/shard_map/ppermute | solution.py:36
  8.3 8.5 %collective-permute-start.1 = (bf16[640,128]{1,0:T(8,128)(2,1)S(1)}, bf16[640,128]{1,0:T(8,128)(2,1)S(1)}, u32[]{:S(2)}, u32[]{:S(2)}) collective-permute-start(bf16[640,128]{1,0:T(8,128)(2,1)S(1)} %get-tuple-element.90), channel_id=1, source_target_pairs={{0,8},{8,0},{16,24},{24,16},{1,9},{9,1},{17,25},{25,17},{2,10},{10... | collective-permute-start | bytes 491528 | tf_op jit(solution)/shard_map/ppermute | solution.py:36
  9.3 7.5 %collective-permute-start.2 = (bf16[640,128]{1,0:T(8,128)(2,1)S(1)}, bf16[640,128]{1,0:T(8,128)(2,1)S(1)}, u32[]{:S(2)}, u32[]{:S(2)}) collective-permute-start(bf16[640,128]{1,0:T(8,128)(2,1)S(1)} %get-tuple-element.91), channel_id=1, source_target_pairs={{0,24},{8,16},{16,8},{24,0},{1,25},{9,17},{17,9},{25,1},{2,26},{10... | collective-permute-start | bytes 491528 | tf_op jit(solution)/shard_map/ppermute | solution.py:36
  9.3 11.8 %collective-permute-start.9 = (bf16[64,1536]{1,0:T(8,128)(2,1)}, bf16[64,1536]{1,0:T(8,128)(2,1)S(1)}, u32[]{:S(2)}, u32[]{:S(2)}) collective-permute-start(bf16[64,1536]{1,0:T(8,128)(2,1)} %param.12), channel_id=1, source_target_pairs={{0,4},{1,5},{2,6},{3,7},{4,0},{5,1},{6,2},{7,3},{8,12},{9,13},{10,... | collective-permute-start | bytes 589832 | tf_op jit(solution)/shard_map/ppermute | solution.py:36
  12.3 10.5 %collective-permute-start.8 = (bf16[64,1536]{1,0:T(8,128)(2,1)}, bf16[64,1536]{1,0:T(8,128)(2,1)S(1)}, u32[]{:S(2)}, u32[]{:S(2)}) collective-permute-start(bf16[64,1536]{1,0:T(8,128)(2,1)} %param.12), channel_id=1, source_target_pairs={{0,6},{1,7},{2,4},{3,5},{4,2},{5,3},{6,0},{7,1},{8,14},{9,15},{10,... | collective-permute-start | bytes 589832 | tf_op jit(solution)/shard_map/ppermute | solution.py:36
  13.5 9.3 %collective-permute-start.7 = (bf16[64,1536]{1,0:T(8,128)(2,1)}, bf16[64,1536]{1,0:T(8,128)(2,1)S(1)}, u32[]{:S(2)}, u32[]{:S(2)}) collective-permute-start(bf16[64,1536]{1,0:T(8,128)(2,1)} %param.12), channel_id=1, source_target_pairs={{0,2},{1,3},{2,0},{3,1},{4,6},{5,7},{6,4},{7,5},{8,10},{9,11},{10,... | collective-permute-start | bytes 589832 | tf_op jit(solution)/shard_map/ppermute | solution.py:36
  16.8 11.8 %copy-start.7 = (f32[1536]{0:T(1024)S(1)}, f32[1536]{0:T(1024)}, u32[]{:S(2)}) copy-start(f32[1536]{0:T(1024)} %param.14) | copy-start | bytes 18436
  16.8 11.8 %copy-start.5 = (bf16[1,128,1536]{2,1,0:T(8,128)(2,1)S(1)}, bf16[1,128,1536]{2,1,0:T(8,128)(2,1)}, u32[]{:S(2)}) copy-start(bf16[1,128,1536]{2,1,0:T(8,128)(2,1)} %param.17) | copy-start | bytes 1179652
  16.8 16.3 %copy-start.6 = (f32[5,1536]{1,0:T(8,128)S(1)}, f32[5,1536]{1,0:T(8,128)}, u32[]{:S(2)}) copy-start(f32[5,1536]{1,0:T(8,128)} %kern_ref.3) | copy-start | bytes 92164
  16.8 9.3 %collective-permute-start.5 = (bf16[640,128]{1,0:T(8,128)(2,1)S(1)}, bf16[640,128]{1,0:T(8,128)(2,1)S(1)}, u32[]{:S(2)}, u32[]{:S(2)}) collective-permute-start(bf16[640,128]{1,0:T(8,128)(2,1)S(1)} %add_add_fusion), channel_id=1, source_target_pairs={{0,4},{1,5},{2,6},{3,7},{4,0},{5,1},{6,2},{7,3},{8,12},{9,13},{10,... | collective-permute-start | bytes 491528 | tf_op jit(solution)/shard_map/ppermute | solution.py:36
  19.9 8.4 %collective-permute-start.4 = (bf16[640,128]{1,0:T(8,128)(2,1)S(1)}, bf16[640,128]{1,0:T(8,128)(2,1)S(1)}, u32[]{:S(2)}, u32[]{:S(2)}) collective-permute-start(bf16[640,128]{1,0:T(8,128)(2,1)S(1)} %add_add_fusion), channel_id=1, source_target_pairs={{0,6},{1,7},{2,4},{3,5},{4,2},{5,3},{6,0},{7,1},{8,14},{9,15},{10,... | collective-permute-start | bytes 491528 | tf_op jit(solution)/shard_map/ppermute | solution.py:36
  21.1 7.4 %collective-permute-start.3 = (bf16[640,128]{1,0:T(8,128)(2,1)S(1)}, bf16[640,128]{1,0:T(8,128)(2,1)S(1)}, u32[]{:S(2)}, u32[]{:S(2)}) collective-permute-start(bf16[640,128]{1,0:T(8,128)(2,1)S(1)} %add_add_fusion), channel_id=1, source_target_pairs={{0,2},{1,3},{2,0},{3,1},{4,6},{5,7},{6,4},{7,5},{8,10},{9,11},{10,... | collective-permute-start | bytes 491528 | tf_op jit(solution)/shard_map/ppermute | solution.py:36
  23.8 9.3 %collective-permute-start.10 = (bf16[4,64,1536]{2,1,0:T(8,128)(2,1)S(1)}, bf16[4,64,1536]{2,1,0:T(8,128)(2,1)S(1)}, u32[]{:S(2)}, u32[]{:S(2)}) collective-permute-start(bf16[4,64,1536]{2,1,0:T(8,128)(2,1)S(1)} %pad_maximum_fusion.1.wa_ref), channel_id=1, source_target_pairs={{0,1},{1,0},{2,3},{3,2},{4,5},{5,4},{6,7},{7,6},{8,9},{9,8},{10,11... | collective-permute-start | bytes 2359304 | tf_op jit(solution)/shard_map/ppermute | solution.py:36
  28.6 4.1 %collective-permute-start.6 = (bf16[4,640,128]{2,1,0:T(8,128)(2,1)S(1)}, bf16[4,640,128]{2,1,0:T(8,128)(2,1)S(1)}, u32[]{:S(2)}, u32[]{:S(2)}) collective-permute-start(bf16[4,640,128]{2,1,0:T(8,128)(2,1)S(1)} %pad_maximum_fusion.2.a_ref), channel_id=1, source_target_pairs={{0,1},{1,0},{2,3},{3,2},{4,5},{5,4},{6,7},{7,6},{8,9},{9,8},{10,11... | collective-permute-start | bytes 1966088 | tf_op jit(solution)/shard_map/ppermute | solution.py:36
  28.7 15.2 %copy-start = (bf16[1536,768]{1,0:T(8,128)(2,1)S(1)}, bf16[1536,768]{1,0:T(8,128)(2,1)}, u32[]{:S(2)}) copy-start(bf16[1536,768]{1,0:T(8,128)(2,1)} %up_ref.5) | copy-start | bytes 7077892
  28.7 18.7 %collective-permute-start.14 = (bf16[128,1536]{1,0:T(8,128)(2,1)S(1)}, bf16[128,1536]{1,0:T(8,128)(2,1)S(1)}, u32[]{:S(2)}, u32[]{:S(2)}) collective-permute-start(bf16[128,1536]{1,0:T(8,128)(2,1)S(1)} %bitcast.17), channel_id=1, source_target_pairs={{0,5},{1,4},{2,7},{3,6},{4,1},{5,0},{6,3},{7,2},{8,13},{9,12},{10,... | collective-permute-start | bytes 1179656 | tf_op jit(solution)/shard_map/ppermute | solution.py:36
  30.9 19.2 %collective-permute-start.13 = (bf16[128,1536]{1,0:T(8,128)(2,1)S(1)}, bf16[128,1536]{1,0:T(8,128)(2,1)S(1)}, u32[]{:S(2)}, u32[]{:S(2)}) collective-permute-start(bf16[128,1536]{1,0:T(8,128)(2,1)S(1)} %bitcast.18), channel_id=1, source_target_pairs={{0,7},{1,6},{2,5},{3,4},{4,3},{5,2},{6,1},{7,0},{8,15},{9,14},{10,... | collective-permute-start | bytes 1179656 | tf_op jit(solution)/shard_map/ppermute | solution.py:36
  32.6 17.5 %collective-permute-start.12 = (bf16[128,1536]{1,0:T(8,128)(2,1)S(1)}, bf16[128,1536]{1,0:T(8,128)(2,1)S(1)}, u32[]{:S(2)}, u32[]{:S(2)}) collective-permute-start(bf16[128,1536]{1,0:T(8,128)(2,1)S(1)} %bitcast.19), channel_id=1, source_target_pairs={{0,3},{1,2},{2,1},{3,0},{4,7},{5,6},{6,5},{7,4},{8,11},{9,10},{10,... | collective-permute-start | bytes 1179656 | tf_op jit(solution)/shard_map/ppermute | solution.py:36
  32.6 17.5 %collective-permute-start.11 = (bf16[128,1536]{1,0:T(8,128)(2,1)S(1)}, bf16[128,1536]{1,0:T(8,128)(2,1)S(1)}, u32[]{:S(2)}, u32[]{:S(2)}) collective-permute-start(bf16[128,1536]{1,0:T(8,128)(2,1)S(1)} %bitcast.20), channel_id=1, source_target_pairs={{0,1},{1,0},{2,3},{3,2},{4,5},{5,4},{6,7},{7,6},{8,9},{9,8},{10,11... | collective-permute-start | bytes 1179656 | tf_op jit(solution)/shard_map/ppermute | solution.py:36
  50.1 1.7 copy-start.1
  50.3 5.0 %collective-permute-start.15 = (bf16[4,128,1536]{2,1,0:T(8,128)(2,1)S(1)}, bf16[4,128,1536]{2,1,0:T(8,128)(2,1)S(1)}, u32[]{:S(2)}, u32[]{:S(2)}) collective-permute-start(bf16[4,128,1536]{2,1,0:T(8,128)(2,1)S(1)} %pad_maximum_fusion.cot_ref.cb_ref), channel_id=1, source_target_pairs={{0,1},{1,0},{2,3},{3,2},{4,5},{5,4},{6,7},{7,6},{8,9},{9,8},{10,11... | collective-permute-start | bytes 4718600 | tf_op jit(solution)/shard_map/ppermute | solution.py:36
  54.9 3.7 %collective-permute-start.22 = (bf16[512,1536]{1,0:T(8,128)(2,1)S(1)}, bf16[512,1536]{1,0:T(8,128)(2,1)S(1)}, u32[]{:S(2)}, u32[]{:S(2)}) collective-permute-start(bf16[512,1536]{1,0:T(8,128)(2,1)S(1)} %get-tuple-element.118), channel_id=1, source_target_pairs={{0,1},{1,0},{2,3},{3,2},{4,5},{5,4},{6,7},{7,6},{8,9},{9,8},{10,11... | collective-permute-start | bytes 4718600 | tf_op jit(solution)/shard_map/ppermute | solution.py:36
  58.9 12.9 %collective-permute-start.23 = (bf16[256,768]{1,0:T(8,128)(2,1)S(1)}, bf16[256,768]{1,0:T(8,128)(2,1)S(1)}, u32[]{:S(2)}, u32[]{:S(2)}) collective-permute-start(bf16[256,768]{1,0:T(8,128)(2,1)S(1)} %get-tuple-element.120), channel_id=1, source_target_pairs={{0,2},{1,3},{2,0},{3,1},{4,6},{5,7},{6,4},{7,5},{8,10},{9,11},{10,... | collective-permute-start | bytes 1179656 | tf_op jit(solution)/shard_map/ppermute | solution.py:36
  60.5 13.6 %collective-permute-start.25 = (bf16[256,768]{1,0:T(8,128)(2,1)S(1)}, bf16[256,768]{1,0:T(8,128)(2,1)S(1)}, u32[]{:S(2)}, u32[]{:S(2)}) collective-permute-start(bf16[256,768]{1,0:T(8,128)(2,1)S(1)} %get-tuple-element.124), channel_id=1, source_target_pairs={{0,6},{1,7},{2,4},{3,5},{4,2},{5,3},{6,0},{7,1},{8,14},{9,15},{10,... | collective-permute-start | bytes 1179656 | tf_op jit(solution)/shard_map/ppermute | solution.py:36
  63.8 33.3 %collective-permute-start.40 = (bf16[8,96,384]{2,1,0:T(8,128)(2,1)S(1)}, bf16[8,96,384]{2,1,0:T(8,128)(2,1)S(1)}, u32[]{:S(2)}, u32[]{:S(2)}) collective-permute-start(bf16[8,96,384]{2,1,0:T(8,128)(2,1)S(1)} %get-tuple-element.145), channel_id=1, source_target_pairs={{0,24},{8,16},{16,8},{24,0},{1,25},{9,17},{17,9},{25,1},{2,26},{10... | collective-permute-start | bytes 1769480 | tf_op jit(solution)/shard_map/ppermute | solution.py:36
  68.8 30.4 %collective-permute-start.38 = (bf16[8,96,384]{2,1,0:T(8,128)(2,1)S(1)}, bf16[8,96,384]{2,1,0:T(8,128)(2,1)S(1)}, u32[]{:S(2)}, u32[]{:S(2)}) collective-permute-start(bf16[8,96,384]{2,1,0:T(8,128)(2,1)S(1)} %get-tuple-element.141), channel_id=1, source_target_pairs={{0,96},{32,64},{64,32},{96,0},{1,97},{33,65},{65,33},{97,1},{2,98}... | collective-permute-start | bytes 1769480 | tf_op jit(solution)/shard_map/ppermute | solution.py:36
  72.0 7.6 %collective-permute-start.24 = (bf16[128,768]{1,0:T(8,128)(2,1)S(1)}, bf16[128,768]{1,0:T(8,128)(2,1)S(1)}, u32[]{:S(2)}, u32[]{:S(2)}) collective-permute-start(bf16[128,768]{1,0:T(8,128)(2,1)S(1)} %get-tuple-element.122), channel_id=1, source_target_pairs={{0,6},{1,7},{2,4},{3,5},{4,2},{5,3},{6,0},{7,1},{8,14},{9,15},{10,... | collective-permute-start | bytes 589832 | tf_op jit(solution)/shard_map/ppermute | solution.py:36
  74.1 6.2 %collective-permute-start.26 = (bf16[128,768]{1,0:T(8,128)(2,1)S(1)}, bf16[128,768]{1,0:T(8,128)(2,1)S(1)}, u32[]{:S(2)}, u32[]{:S(2)}) collective-permute-start(bf16[128,768]{1,0:T(8,128)(2,1)S(1)} %get-tuple-element.126), channel_id=1, source_target_pairs={{0,2},{1,3},{2,0},{3,1},{4,6},{5,7},{6,4},{7,5},{8,10},{9,11},{10,... | collective-permute-start | bytes 589832 | tf_op jit(solution)/shard_map/ppermute | solution.py:36
  76.2 14.2 %collective-permute-start.18 = (bf16[8,96,384]{2,1,0:T(8,128)(2,1)S(1)}, bf16[8,96,384]{2,1,0:T(8,128)(2,1)S(1)}, u32[]{:S(2)}, u32[]{:S(2)}) collective-permute-start(bf16[8,96,384]{2,1,0:T(8,128)(2,1)S(1)} %get-tuple-element.110), channel_id=1, source_target_pairs={{0,8},{8,0},{16,24},{24,16},{1,9},{9,1},{17,25},{25,17},{2,10},{10... | collective-permute-start | bytes 1769480 | tf_op jit(solution)/shard_map/ppermute | solution.py:36
  79.5 15.8 %collective-permute-start.16 = (bf16[8,96,384]{2,1,0:T(8,128)(2,1)S(1)}, bf16[8,96,384]{2,1,0:T(8,128)(2,1)S(1)}, u32[]{:S(2)}, u32[]{:S(2)}) collective-permute-start(bf16[8,96,384]{2,1,0:T(8,128)(2,1)S(1)} %get-tuple-element.106), channel_id=1, source_target_pairs={{0,32},{32,0},{64,96},{96,64},{1,33},{33,1},{65,97},{97,65},{2,34}... | collective-permute-start | bytes 1769480 | tf_op jit(solution)/shard_map/ppermute | solution.py:36
  83.2 25.1 %collective-permute-start.27 = (bf16[272,1536]{1,0:T(8,128)(2,1)S(1)}, bf16[272,1536]{1,0:T(8,128)(2,1)S(1)}, u32[]{:S(2)}, u32[]{:S(2)}) collective-permute-start(bf16[272,1536]{1,0:T(8,128)(2,1)S(1)} %get-tuple-element.133), channel_id=1, source_target_pairs={{0,1},{1,0},{2,3},{3,2},{4,5},{5,4},{6,7},{7,6},{8,9},{9,8},{10,11... | collective-permute-start | bytes 2506760 | tf_op jit(solution)/shard_map/ppermute | solution.py:36
  90.5 12.1 %collective-permute-start.19 = (bf16[4,96,384]{2,1,0:T(8,128)(2,1)S(1)}, bf16[4,96,384]{2,1,0:T(8,128)(2,1)S(1)}, u32[]{:S(2)}, u32[]{:S(2)}) collective-permute-start(bf16[4,96,384]{2,1,0:T(8,128)(2,1)S(1)} %get-tuple-element.112), channel_id=1, source_target_pairs={{0,32},{32,0},{64,96},{96,64},{1,33},{33,1},{65,97},{97,65},{2,34}... | collective-permute-start | bytes 884744 | tf_op jit(solution)/shard_map/ppermute | solution.py:36
  95.4 7.2 %collective-permute-start.17 = (bf16[4,96,384]{2,1,0:T(8,128)(2,1)S(1)}, bf16[4,96,384]{2,1,0:T(8,128)(2,1)S(1)}, u32[]{:S(2)}, u32[]{:S(2)}) collective-permute-start(bf16[4,96,384]{2,1,0:T(8,128)(2,1)S(1)} %get-tuple-element.108), channel_id=1, source_target_pairs={{0,8},{8,0},{16,24},{24,16},{1,9},{9,1},{17,25},{25,17},{2,10},{10... | collective-permute-start | bytes 884744 | tf_op jit(solution)/shard_map/ppermute | solution.py:36
  97.2 10.7 %collective-permute-start.41 = (bf16[4,96,384]{2,1,0:T(8,128)(2,1)S(1)}, bf16[4,96,384]{2,1,0:T(8,128)(2,1)S(1)}, u32[]{:S(2)}, u32[]{:S(2)}) collective-permute-start(bf16[4,96,384]{2,1,0:T(8,128)(2,1)S(1)} %get-tuple-element.147), channel_id=1, source_target_pairs={{0,96},{32,64},{64,32},{96,0},{1,97},{33,65},{65,33},{97,1},{2,98}... | collective-permute-start | bytes 884744 | tf_op jit(solution)/shard_map/ppermute | solution.py:36
  99.3 8.6 %collective-permute-start.39 = (bf16[4,96,384]{2,1,0:T(8,128)(2,1)S(1)}, bf16[4,96,384]{2,1,0:T(8,128)(2,1)S(1)}, u32[]{:S(2)}, u32[]{:S(2)}) collective-permute-start(bf16[4,96,384]{2,1,0:T(8,128)(2,1)S(1)} %get-tuple-element.143), channel_id=1, source_target_pairs={{0,24},{8,16},{16,8},{24,0},{1,25},{9,17},{17,9},{25,1},{2,26},{10... | collective-permute-start | bytes 884744 | tf_op jit(solution)/shard_map/ppermute | solution.py:36
  102.7 9.1 %collective-permute-start.20 = (bf16[2,192,384]{2,1,0:T(8,128)(2,1)S(1)}, bf16[2,192,384]{2,1,0:T(8,128)(2,1)S(1)}, u32[]{:S(2)}, u32[]{:S(2)}) collective-permute-start(bf16[2,192,384]{2,1,0:T(8,128)(2,1)S(1)} %get-tuple-element.114), channel_id=1, source_target_pairs={{0,96},{32,64},{64,32},{96,0},{1,97},{33,65},{65,33},{97,1},{2,98}... | collective-permute-start | bytes 884744 | tf_op jit(solution)/shard_map/ppermute | solution.py:36
  108.1 8.6 %collective-permute-start.42 = (bf16[2,192,384]{2,1,0:T(8,128)(2,1)S(1)}, bf16[2,192,384]{2,1,0:T(8,128)(2,1)S(1)}, u32[]{:S(2)}, u32[]{:S(2)}) collective-permute-start(bf16[2,192,384]{2,1,0:T(8,128)(2,1)S(1)} %get-tuple-element.149), channel_id=1, source_target_pairs={{0,32},{32,0},{64,96},{96,64},{1,33},{33,1},{65,97},{97,65},{2,34}... | collective-permute-start | bytes 884744 | tf_op jit(solution)/shard_map/ppermute | solution.py:36
  108.4 6.1 %collective-permute-start.28 = (bf16[144,768]{1,0:T(8,128)(2,1)S(1)}, bf16[144,768]{1,0:T(8,128)(2,1)S(1)}, u32[]{:S(2)}, u32[]{:S(2)}) collective-permute-start(bf16[144,768]{1,0:T(8,128)(2,1)S(1)} %get-tuple-element.135), channel_id=1, source_target_pairs={{0,2},{1,3},{2,0},{3,1},{4,6},{5,7},{6,4},{7,5},{8,10},{9,11},{10,... | collective-permute-start | bytes 663560 | tf_op jit(solution)/shard_map/ppermute | solution.py:36
  110.0 8.2 %collective-permute-start.44 = (bf16[144,768]{1,0:T(8,128)(2,1)S(1)}, bf16[144,768]{1,0:T(8,128)(2,1)S(1)}, u32[]{:S(2)}, u32[]{:S(2)}) collective-permute-start(bf16[144,768]{1,0:T(8,128)(2,1)S(1)} %get-tuple-element.153), channel_id=1, source_target_pairs={{0,6},{1,7},{2,4},{3,5},{4,2},{5,3},{6,0},{7,1},{8,14},{9,15},{10,... | collective-permute-start | bytes 663560 | tf_op jit(solution)/shard_map/ppermute | solution.py:36
  111.9 6.5 %collective-permute-start.21 = (bf16[1,192,384]{2,1,0:T(8,128)(2,1)S(1)}, bf16[1,192,384]{2,1,0:T(8,128)(2,1)S(1)}, u32[]{:S(2)}, u32[]{:S(2)}) collective-permute-start(bf16[1,192,384]{2,1,0:T(8,128)(2,1)S(1)} %get-tuple-element.116), channel_id=1, source_target_pairs={{0,24},{8,16},{16,8},{24,0},{1,25},{9,17},{17,9},{25,1},{2,26},{10... | collective-permute-start | bytes 442376 | tf_op jit(solution)/shard_map/ppermute | solution.py:36
  114.6 6.2 %collective-permute-start.29 = (bf16[80,768]{1,0:T(8,128)(2,1)S(1)}, bf16[80,768]{1,0:T(8,128)(2,1)S(1)}, u32[]{:S(2)}, u32[]{:S(2)}) collective-permute-start(bf16[80,768]{1,0:T(8,128)(2,1)S(1)} %get-tuple-element.137), channel_id=1, source_target_pairs={{0,6},{1,7},{2,4},{3,5},{4,2},{5,3},{6,0},{7,1},{8,14},{9,15},{10,... | collective-permute-start | bytes 368648 | tf_op jit(solution)/shard_map/ppermute | solution.py:36
  116.8 9.9 %collective-permute-start.43 = (bf16[1,192,384]{2,1,0:T(8,128)(2,1)S(1)}, bf16[1,192,384]{2,1,0:T(8,128)(2,1)S(1)}, u32[]{:S(2)}, u32[]{:S(2)}) collective-permute-start(bf16[1,192,384]{2,1,0:T(8,128)(2,1)S(1)} %get-tuple-element.151), channel_id=1, source_target_pairs={{0,8},{8,0},{16,24},{24,16},{1,9},{9,1},{17,25},{25,17},{2,10},{10... | collective-permute-start | bytes 442376 | tf_op jit(solution)/shard_map/ppermute | solution.py:36
  118.3 8.4 %collective-permute-start.45 = (bf16[80,768]{1,0:T(8,128)(2,1)S(1)}, bf16[80,768]{1,0:T(8,128)(2,1)S(1)}, u32[]{:S(2)}, u32[]{:S(2)}) collective-permute-start(bf16[80,768]{1,0:T(8,128)(2,1)S(1)} %get-tuple-element.155), channel_id=1, source_target_pairs={{0,2},{1,3},{2,0},{3,1},{4,6},{5,7},{6,4},{7,5},{8,10},{9,11},{10,... | collective-permute-start | bytes 368648 | tf_op jit(solution)/shard_map/ppermute | solution.py:36
  120.9 7.9 %collective-permute-start.34 = (bf16[176,384]{1,0:T(8,128)(2,1)S(1)}, bf16[176,384]{1,0:T(8,128)(2,1)S(1)}, u32[]{:S(2)}, u32[]{:S(2)}) collective-permute-start(bf16[176,384]{1,0:T(8,128)(2,1)S(1)} %get-tuple-element.139.own), channel_id=1, source_target_pairs={{0,32},{32,0},{64,96},{96,64},{1,33},{33,1},{65,97},{97,65},{2,34}... | collective-permute-start | bytes 405512 | tf_op jit(solution)/shard_map/ppermute | solution.py:36
  124.1 6.2 %collective-permute-start.30 = (bf16[176,384]{1,0:T(8,128)(2,1)S(1)}, bf16[176,384]{1,0:T(8,128)(2,1)S(1)}, u32[]{:S(2)}, u32[]{:S(2)}) collective-permute-start(bf16[176,384]{1,0:T(8,128)(2,1)S(1)} %get-tuple-element.138.own), channel_id=1, source_target_pairs={{0,24},{8,16},{16,8},{24,0},{1,25},{9,17},{17,9},{25,1},{2,26},{10... | collective-permute-start | bytes 405512 | tf_op jit(solution)/shard_map/ppermute | solution.py:36
  126.8 7.7 %collective-permute-start.50 = (bf16[176,384]{1,0:T(8,128)(2,1)S(1)}, bf16[176,384]{1,0:T(8,128)(2,1)S(1)}, u32[]{:S(2)}, u32[]{:S(2)}) collective-permute-start(bf16[176,384]{1,0:T(8,128)(2,1)S(1)} %get-tuple-element.157.own), channel_id=1, source_target_pairs={{0,96},{32,64},{64,32},{96,0},{1,97},{33,65},{65,33},{97,1},{2,98}... | collective-permute-start | bytes 405512 | tf_op jit(solution)/shard_map/ppermute | solution.py:36
  128.4 6.3 %collective-permute-start.46 = (bf16[176,384]{1,0:T(8,128)(2,1)S(1)}, bf16[176,384]{1,0:T(8,128)(2,1)S(1)}, u32[]{:S(2)}, u32[]{:S(2)}) collective-permute-start(bf16[176,384]{1,0:T(8,128)(2,1)S(1)} %get-tuple-element.156.own), channel_id=1, source_target_pairs={{0,8},{8,0},{16,24},{24,16},{1,9},{9,1},{17,25},{25,17},{2,10},{10... | collective-permute-start | bytes 405512 | tf_op jit(solution)/shard_map/ppermute | solution.py:36
  128.8 7.6 %collective-permute-start.35 = (bf16[272,384]{1,0:T(8,128)(2,1)S(1)}, bf16[272,384]{1,0:T(8,128)(2,1)S(1)}, u32[]{:S(2)}, u32[]{:S(2)}) collective-permute-start(bf16[272,384]{1,0:T(8,128)(2,1)S(1)} %shard_map.149.own), channel_id=1, source_target_pairs={{0,24},{8,16},{16,8},{24,0},{1,25},{9,17},{17,9},{25,1},{2,26},{10... | collective-permute-start | bytes 626696 | tf_op jit(solution)/shard_map/ppermute | solution.py:36
  130.4 8.6 %collective-permute-start.31 = (bf16[272,384]{1,0:T(8,128)(2,1)S(1)}, bf16[272,384]{1,0:T(8,128)(2,1)S(1)}, u32[]{:S(2)}, u32[]{:S(2)}) collective-permute-start(bf16[272,384]{1,0:T(8,128)(2,1)S(1)} %shard_map.146.own), channel_id=1, source_target_pairs={{0,96},{32,64},{64,32},{96,0},{1,97},{33,65},{65,33},{97,1},{2,98}... | collective-permute-start | bytes 626696 | tf_op jit(solution)/shard_map/ppermute | solution.py:36
  134.6 5.9 %collective-permute-start.51 = (bf16[272,384]{1,0:T(8,128)(2,1)S(1)}, bf16[272,384]{1,0:T(8,128)(2,1)S(1)}, u32[]{:S(2)}, u32[]{:S(2)}) collective-permute-start(bf16[272,384]{1,0:T(8,128)(2,1)S(1)} %shard_map.163.own), channel_id=1, source_target_pairs={{0,8},{8,0},{16,24},{24,16},{1,9},{9,1},{17,25},{25,17},{2,10},{10... | collective-permute-start | bytes 626696 | tf_op jit(solution)/shard_map/ppermute | solution.py:36
  134.7 6.3 %collective-permute-start.47 = (bf16[272,384]{1,0:T(8,128)(2,1)S(1)}, bf16[272,384]{1,0:T(8,128)(2,1)S(1)}, u32[]{:S(2)}, u32[]{:S(2)}) collective-permute-start(bf16[272,384]{1,0:T(8,128)(2,1)S(1)} %shard_map.160.own), channel_id=1, source_target_pairs={{0,32},{32,0},{64,96},{96,64},{1,33},{33,1},{65,97},{97,65},{2,34}... | collective-permute-start | bytes 626696 | tf_op jit(solution)/shard_map/ppermute | solution.py:36
  136.5 9.9 %collective-permute-start.36 = (bf16[464,384]{1,0:T(8,128)(2,1)S(1)}, bf16[464,384]{1,0:T(8,128)(2,1)S(1)}, u32[]{:S(2)}, u32[]{:S(2)}) collective-permute-start(bf16[464,384]{1,0:T(8,128)(2,1)S(1)} %shard_map.150.own), channel_id=1, source_target_pairs={{0,96},{32,64},{64,32},{96,0},{1,97},{33,65},{65,33},{97,1},{2,98}... | collective-permute-start | bytes 1069064 | tf_op jit(solution)/shard_map/ppermute | solution.py:36
  139.1 11.3 %collective-permute-start.32 = (bf16[464,384]{1,0:T(8,128)(2,1)S(1)}, bf16[464,384]{1,0:T(8,128)(2,1)S(1)}, u32[]{:S(2)}, u32[]{:S(2)}) collective-permute-start(bf16[464,384]{1,0:T(8,128)(2,1)S(1)} %shard_map.147.own), channel_id=1, source_target_pairs={{0,8},{8,0},{16,24},{24,16},{1,9},{9,1},{17,25},{25,17},{2,10},{10... | collective-permute-start | bytes 1069064 | tf_op jit(solution)/shard_map/ppermute | solution.py:36
  140.5 11.3 %collective-permute-start.52 = (bf16[464,384]{1,0:T(8,128)(2,1)S(1)}, bf16[464,384]{1,0:T(8,128)(2,1)S(1)}, u32[]{:S(2)}, u32[]{:S(2)}) collective-permute-start(bf16[464,384]{1,0:T(8,128)(2,1)S(1)} %shard_map.164.own), channel_id=1, source_target_pairs={{0,32},{32,0},{64,96},{96,64},{1,33},{33,1},{65,97},{97,65},{2,34}... | collective-permute-start | bytes 1069064 | tf_op jit(solution)/shard_map/ppermute | solution.py:36
  141.1 12.4 %collective-permute-start.48 = (bf16[464,384]{1,0:T(8,128)(2,1)S(1)}, bf16[464,384]{1,0:T(8,128)(2,1)S(1)}, u32[]{:S(2)}, u32[]{:S(2)}) collective-permute-start(bf16[464,384]{1,0:T(8,128)(2,1)S(1)} %shard_map.161.own), channel_id=1, source_target_pairs={{0,24},{8,16},{16,8},{24,0},{1,25},{9,17},{17,9},{25,1},{2,26},{10... | collective-permute-start | bytes 1069064 | tf_op jit(solution)/shard_map/ppermute | solution.py:36
  146.5 12.4 %collective-permute-start.37 = (bf16[848,384]{1,0:T(8,128)(2,1)S(1)}, bf16[848,384]{1,0:T(8,128)(2,1)S(1)}, u32[]{:S(2)}, u32[]{:S(2)}) collective-permute-start(bf16[848,384]{1,0:T(8,128)(2,1)S(1)} %shard_map.151.refs_2_), channel_id=1, source_target_pairs={{0,8},{8,0},{16,24},{24,16},{1,9},{9,1},{17,25},{25,17},{2,10},{10... | collective-permute-start | bytes 1953800 | tf_op jit(solution)/shard_map/ppermute | solution.py:36
  150.5 10.6 %collective-permute-start.33 = (bf16[848,384]{1,0:T(8,128)(2,1)S(1)}, bf16[848,384]{1,0:T(8,128)(2,1)S(1)}, u32[]{:S(2)}, u32[]{:S(2)}) collective-permute-start(bf16[848,384]{1,0:T(8,128)(2,1)S(1)} %shard_map.148.refs_0_), channel_id=1, source_target_pairs={{0,32},{32,0},{64,96},{96,64},{1,33},{33,1},{65,97},{97,65},{2,34}... | collective-permute-start | bytes 1953800 | tf_op jit(solution)/shard_map/ppermute | solution.py:36
  151.9 11.8 %collective-permute-start.53 = (bf16[848,384]{1,0:T(8,128)(2,1)S(1)}, bf16[848,384]{1,0:T(8,128)(2,1)S(1)}, u32[]{:S(2)}, u32[]{:S(2)}) collective-permute-start(bf16[848,384]{1,0:T(8,128)(2,1)S(1)} %shard_map.165.refs_6_), channel_id=1, source_target_pairs={{0,24},{8,16},{16,8},{24,0},{1,25},{9,17},{17,9},{25,1},{2,26},{10... | collective-permute-start | bytes 1953800 | tf_op jit(solution)/shard_map/ppermute | solution.py:36
  153.6 11.8 %collective-permute-start.49 = (bf16[848,384]{1,0:T(8,128)(2,1)S(1)}, bf16[848,384]{1,0:T(8,128)(2,1)S(1)}, u32[]{:S(2)}, u32[]{:S(2)}) collective-permute-start(bf16[848,384]{1,0:T(8,128)(2,1)S(1)} %shard_map.162.refs_4_), channel_id=1, source_target_pairs={{0,96},{32,64},{64,32},{96,0},{1,97},{33,65},{65,33},{97,1},{2,98}... | collective-permute-start | bytes 1953800 | tf_op jit(solution)/shard_map/ppermute | solution.py:36

commit v3 on v2

--- a/solution.py
+++ b/solution.py
@@ -28,15 +28,23 @@
     return pl.BlockSpec(shape, lambda *_: (0,) * len(shape))
 
 
-def fixed(shape):
-    return pl.BlockSpec(shape, lambda *_: (0,) * len(shape), pipeline_mode=pl.Buffered(1))
+WHOLE = pl.BlockSpec(memory_space=pltpu.VMEM)
 
 
 def xor_send(value, axis, mask, size):
     return lax.ppermute(value, axis, [(i, i ^ mask) for i in range(size)])
 
 
-def select_kernel(lengths, panel_ref, seg_ref, *outs):
+def select_kernel(lengths_hbm, panel_hbm, seg_hbm, *outs):
+    lengths, panel_ref, seg_ref, sem = outs[5:]
+    copies = [
+        pltpu.make_async_copy(src, dst, sem.at[i])
+        for i, (src, dst) in enumerate(((panel_hbm, panel_ref), (seg_hbm, seg_ref), (lengths_hbm, lengths)))
+    ]
+    for copy in copies:
+        copy.start()
+    for copy in copies:
+        copy.wait()
     owner = lax.axis_index("context")
     start = jnp.int32(0)
     for shard in range(3):
@@ -81,15 +89,16 @@
     return pl.pallas_call(
         select_kernel,
         out_shape=[jax.ShapeDtypeStruct((640, 128), BF)] * 4,
-        in_specs=[
-            pl.BlockSpec(memory_space=pltpu.SMEM),
-            full(panels_t.shape),
-            full(seg.shape),
+        in_specs=[pl.BlockSpec(memory_space=pl.ANY)] * 3,
+        out_specs=[WHOLE] * 4,
+        scratch_shapes=[
+            pltpu.VMEM((2560, 128), F32),
+            pltpu.SMEM(lengths.shape, jnp.int32),
+            pltpu.VMEM(panels_t.shape, BF),
+            pltpu.VMEM(seg.shape, jnp.int32),
+            pltpu.SemaphoreType.DMA((3,)),
         ],
-        out_specs=[full((640, 128))] * 4,
-        grid=(1,),
-        scratch_shapes=[pltpu.VMEM((2560, 128), F32)],
-        compiler_params=vmem(24),
+        compiler_params=vmem(56),
         cost_estimate=cost(2 * 160 * 65 * 2048, 2 << 20),
     )(lengths, panels_t, seg)
 
@@ -97,7 +106,7 @@
 def norm_kernel(
     a_ref, b_ref, wa_ref, wb_ref, kern_ref, gain_ref,
     ln_ref, normed_ref, rstd_ref, frames_ref, segs_ref, stack_ref,
-    units, weight, segs, near_segs, wide, near,
+    units, weight, segs, *blocks,
 ):
     step = pl.program_id(0)
     me = lax.axis_index("tensor")
@@ -143,9 +152,22 @@
                 def _():
                     segs[pl.ds(HALO + 1024, HALO), :] = column(ref, d, 36)[:HALO]
 
-        wide[pl.ds(160, 96), :] = jnp.zeros((96, wide.shape[1]), BF)
-
-    at_step = 7 - step
+        for wide in (blocks[1], blocks[4]):
+            wide[pl.ds(160, 96), :] = jnp.zeros((96, wide.shape[1]), BF)
+
+    outs = (ln_ref, normed_ref, rstd_ref, segs_ref, stack_ref)
+    for i in range(2):
+        norm_block(me, 7 - 2 * step - i, kern_ref, gain_ref, units, weight, segs, *blocks[3 * i : 3 * i + 3], *outs)
+
+    @pl.when(step == 3)
+    def _():
+        frames_ref[...] = blocks[4][pl.ds(0, 160), :].astype(F32)
+
+
+def norm_block(
+    me, at_step, kern_ref, gain_ref, units, weight, segs, near_segs, wide, near,
+    ln_ref, normed_ref, rstd_ref, segs_ref, stack_ref,
+):
     spot = lax.rem(at_step, 4)
     block = me ^ (2 * (spot ^ (spot // 2))) ^ (at_step // 4)
     rows = units[pl.ds(8 * block + 1, 10)].reshape(160, 512)
@@ -174,35 +196,29 @@
         center = mixed - mean
         rstd = lax.rsqrt(jnp.mean(center * center, axis=1, keepdims=True) + 1e-05)
         normed = center * rstd
-        ln_ref[pl.ds(r, 16), :] = (normed * gain).astype(BF)
+        ln_ref[pl.ds(pl.multiple_of(128 * at_step + r, 16), 16), :] = (normed * gain).astype(BF)
         normed_ref[pl.ds(r, 16), :] = normed
         rstd_ref[pl.ds(r, 16), :] = jnp.broadcast_to(rstd, (16, 128))
 
-    @pl.when(step == 7)
-    def _():
-        frames_ref[...] = wide[pl.ds(0, 160), :].astype(F32)
-
 
 def normalise(a, b, wa, wb, kern, gain):
     d_model = kern.shape[1]
-    weight = pl.BlockSpec((4, 64, d_model), lambda i: (0, 0, 0))
     return pl.pallas_call(
         norm_kernel,
-        grid=(8,),
-        in_specs=[full(a.shape), full(b.shape), weight, weight, full(kern.shape), full(gain.shape)],
-        out_specs=[
-            pl.BlockSpec((128, d_model), lambda i: (7 - i, 0)),
-            full((128, d_model)), full((128, 128)), full((160, d_model)),
-            full((160, 128)), full((160, 512)),
-        ],
+        grid=(4,),
+        in_specs=[WHOLE] * 6,
+        out_specs=[WHOLE] * 6,
         scratch_shapes=[
             pltpu.VMEM((68, 16, 512), BF),
             pltpu.VMEM((512, d_model), BF),
             pltpu.VMEM((1056, 128), F32),
+        ]
+        + [
             pltpu.VMEM((160, 128), F32),
             pltpu.VMEM((256, d_model), BF),
             pltpu.VMEM((512, d_model), F32),
-        ],
+        ]
+        * 2,
         out_shape=[
             jax.ShapeDtypeStruct((1024, d_model), BF),
             jax.ShapeDtypeStruct((128, d_model), F32),
@@ -211,43 +227,49 @@
             jax.ShapeDtypeStruct((160, 128), F32),
             jax.ShapeDtypeStruct((160, 512), BF),
         ],
-        compiler_params=vmem(24),
+        compiler_params=vmem(20),
         cost_estimate=cost(12 * 10**9, 10 << 20),
     )(a, b, wa, wb, kern, gain)
 
 
-def hidden_kernel(ln_ref, up_ref, hid_ref, slope_ref):
-    ln = ln_ref[...]
-    for c in range(0, up_ref.shape[1], 256):
-        part = pl.ds(c, 256)
-        pre = jnp.dot(ln, up_ref[:, part], preferred_element_type=F32)
-        sig = 1.0 / (1.0 + jnp.exp(-pre))
-        hid_ref[:, part] = (pre * sig).astype(BF)
-        slope_ref[:, part] = 0.5 * sig * (1.0 + pre * (1.0 - sig))
-
-
-def hidden_rows(ln, up):
+def hidden_kernel(ln_ref, up_ref, down_ref, hid_ref, slope_ref):
+    del down_ref
+    half = ln_ref.shape[0] // 2
+
+    def block(r, carry):
+        rows = pl.ds(pl.multiple_of(half * r, 128), half)
+        for c in range(0, up_ref.shape[1], 256):
+            part = pl.ds(c, 256)
+            pre = jnp.dot(ln_ref[rows, :], up_ref[:, part], preferred_element_type=F32)
+            sig = 1.0 / (1.0 + jnp.exp(-pre))
+            hid_ref[rows, part] = (pre * sig).astype(BF)
+            slope_ref[rows, part] = 0.5 * sig * (1.0 + pre * (1.0 - sig))
+        return carry
+
+    lax.fori_loop(0, 2, block, 0)
+
+
+def hidden_rows(ln, up, down):
     rows, d_model = ln.shape
     ff = up.shape[1]
-    half = rows // 2
     return pl.pallas_call(
         hidden_kernel,
-        grid=(2,),
-        in_specs=[pl.BlockSpec((half, d_model), lambda i: (i, 0)), fixed(up.shape)],
-        out_specs=[pl.BlockSpec((half, ff), lambda i: (i, 0))] * 2,
+        in_specs=[WHOLE] * 3,
+        out_specs=[WHOLE] * 2,
         out_shape=[jax.ShapeDtypeStruct((rows, ff), BF), jax.ShapeDtypeStruct((rows, ff), F32)],
-        compiler_params=vmem(24),
+        compiler_params=vmem(12),
         cost_estimate=cost(2 * rows * d_model * ff, 10 << 20, rows * ff),
-    )(ln, up)
-
-
-def backward_kernel(cot_ref, slope_ref, up_ref, down_ref, dpre_ref, dln_ref):
+    )(ln, up, down)
+
+
+def backward_kernel(side, cot_ref, slope_ref, up_ref, down_ref, dpre_ref, dln_ref):
     cols = (((1,), (1,)), ((), ()))
+    rows = dln_ref.shape[0]
     grad = cot_ref[...].reshape(dln_ref.shape)
     for c in range(0, up_ref.shape[1], 256):
         part = pl.ds(c, 256)
         dhid = lax.dot_general(grad, down_ref[part, :], cols, preferred_element_type=F32)
-        dpre_ref[:, part] = (dhid * slope_ref[:, part]).astype(BF)
+        dpre_ref[:, part] = (dhid * slope_ref[pl.ds(rows * side, rows), part]).astype(BF)
     dln_ref[...] = lax.dot_general(
         dpre_ref[...], up_ref[...], cols, preferred_element_type=F32
     ).astype(BF)
@@ -257,14 +279,11 @@
     d_model, ff = up.shape
     half = slope.shape[0] // 2
     return pl.pallas_call(
-        backward_kernel,
-        grid=(1,),
-        in_specs=[
-            full(cot.shape), pl.BlockSpec((half, ff), lambda i: (side, 0)), fixed(up.shape), fixed(down.shape),
-        ],
-        out_specs=[full((half, ff)), full((half, d_model))],
+        functools.partial(backward_kernel, side),
+        in_specs=[WHOLE] * 4,
+        out_specs=[WHOLE] * 2,
         out_shape=[jax.ShapeDtypeStruct((half, ff), BF), jax.ShapeDtypeStruct((half, d_model), BF)],
-        compiler_params=vmem(32),
+        compiler_params=vmem(12),
         cost_estimate=cost(4 * half * d_model * ff, 10 << 20),
     )(cot, slope, up, down)
 
@@ -284,14 +303,14 @@
 def weight_kernel(k, hid_ref, ca_ref, cb_ref, ln_ref, da_ref, db_ref, keep_ref, send_ref, both):
     y, z = lax.axis_index("dp"), lax.axis_index("context")
     half = hid_ref.shape[0] // 2
-    width = ca_ref.shape[2]
+    cols, wide_cols, ff_cols = pl.ds(384 * k, 384), pl.ds(768 * (k // 2), 768), pl.ds(384 * (k % 2), 384)
     rows = (((0,), (0,)), ((), ()))
-    cot = [ref[...].reshape(half, width) for ref in (ca_ref, cb_ref)]
+    cot = [ref[:, :, cols].reshape(half, 384) for ref in (ca_ref, cb_ref)]
     down = lax.dot_general(hid_ref[pl.ds(0, half), :], cot[0], rows, preferred_element_type=F32)
     down += lax.dot_general(hid_ref[pl.ds(half, half), :], cot[1], rows, preferred_element_type=F32)
     down = (0.5 * down).astype(BF)
-    up = lax.dot_general(ln_ref[pl.ds(0, half), :], da_ref[...], rows, preferred_element_type=F32)
-    up += lax.dot_general(ln_ref[pl.ds(half, half), :], db_ref[...], rows, preferred_element_type=F32)
+    up = lax.dot_general(ln_ref[pl.ds(0, half), wide_cols], da_ref[:, ff_cols], rows, preferred_element_type=F32)
+    up += lax.dot_general(ln_ref[pl.ds(half, half), wide_cols], db_ref[:, ff_cols], rows, preferred_element_type=F32)
     up = up.astype(BF)
     for r in range(16):
         code = piece_code(y, z, r, PARTS[k])
@@ -305,70 +324,82 @@
     rows = hidden.shape[0]
     return pl.pallas_call(
         functools.partial(weight_kernel, k),
-        grid=(1,),
-        in_specs=[
-            full((rows, 768)),
-            pl.BlockSpec((4, 128, 384), lambda i: (0, 0, k)),
-            pl.BlockSpec((4, 128, 384), lambda i: (0, 0, k)),
-            pl.BlockSpec((rows, 768), lambda i: (0, k // 2)),
-            pl.BlockSpec((rows // 2, 384), lambda i: (0, k % 2)),
-            pl.BlockSpec((rows // 2, 384), lambda i: (0, k % 2)),
-        ],
-        out_specs=[full((8, 96, 384))] * 2,
+        in_specs=[WHOLE] * 6,
+        out_specs=[WHOLE] * 2,
         out_shape=[jax.ShapeDtypeStruct((8, 96, 384), BF)] * 2,
         scratch_shapes=[pltpu.VMEM((16, 96, 384), BF)],
-        compiler_params=vmem(32),
+        compiler_params=vmem(14),
         cost_estimate=cost(4 * rows * 768 * 384, 7 << 20),
     )(hidden, ca, cb, ln, dpre_a, dpre_b)
 
 
-def place_kernel(*refs):
-    ins, (down_ref, up_ref, front_ref, kern_ref, gain_ref) = refs[:8], refs[8:]
+def piece_row(y, z, code, axes):
+    bits = [0] * 4
+    for i, axis in enumerate(axes):
+        bits[axis] = (code >> (3 - i)) & 1
+    ay, az, by, bz = bits
+    return 4 * (y ^ (2 * by | (ay ^ by))) + (z ^ (2 * bz | (az ^ bz)))
+
+
+def place_pieces(side, bufs, down_ref, up_ref, stage, sems):
     y, z = lax.axis_index("dp"), lax.axis_index("context")
+    copies = []
     for k in range(4):
-
-        @pl.when(pl.program_id(0) == k)
-        def _():
-            pair = ins[2 * k : 2 * k + 2]
-
-            def piece(r, carry):
-                code = piece_code(y, z, r, SPREAD[k])
-                to = pl.ds(pl.multiple_of(48 * r, 16), 48)
-                for side in range(2):
-
-                    @pl.when((code // 8) == side)
-                    def _():
-                        at = pl.multiple_of((code - 8 * side) * 96, 16)
-                        down_ref[to, :] = pair[side][pl.ds(at, 48), :].astype(F32)
-                        up_ref[to, :] = pair[side][pl.ds(pl.multiple_of(at + 48, 16), 48), :].astype(F32)
-
-                return carry
-
-            lax.fori_loop(0, 16, piece, 0)
-            last = [ref[pl.ds(768, 80), :].astype(F32) for ref in pair]
-            front_ref[...] = last[0][:64] + last[1][:64]
-            small = (last[0][64:72] + last[0][72:]) + (last[1][64:72] + last[1][72:])
-            kern_ref[...] = small[:5]
-            gain_ref[...] = small[5:6]
-
-
-def place(pieces):
-    shapes = [(768, 1536), (1536, 768), (64, 1536), (5, 1536), (1, 1536)]
-    return pl.pallas_call(
-        place_kernel,
-        grid=(4,),
-        in_specs=[pl.BlockSpec(memory_space=pltpu.VMEM)] * 8,
-        out_specs=[
-            pl.BlockSpec((768, 384), lambda k: (0, k)),
-            pl.BlockSpec((768, 384), lambda k: (k // 2, k % 2)),
-            pl.BlockSpec((64, 384), lambda k: (0, k)),
-            pl.BlockSpec((5, 384), lambda k: (0, k)),
-            pl.BlockSpec((1, 384), lambda k: (0, k)),
-        ],
-        out_shape=[jax.ShapeDtypeStruct(shape, F32) for shape in shapes],
-        compiler_params=vmem(24),
-        cost_estimate=cost(1 << 20, 14 << 20),
-    )(*pieces)
+        for c in range(8):
+            row = 48 * piece_row(y, z, 8 * side + c, SPREAD[k])
+            for i, (out, row0, col0) in enumerate(((down_ref, 0, 384 * k), (up_ref, 768 * (k // 2), 384 * (k % 2)))):
+                stage[k, c, i] = bufs[k][pl.ds(96 * c + 48 * i, 48), :].astype(F32)
+                to = out.at[pl.ds(pl.multiple_of(row0 + row, 16), 48), pl.ds(col0, 384)]
+                copies.append(pltpu.make_async_copy(stage.at[k, c, i], to, sems.at[k, c, i]))
+                copies[-1].start()
+    return copies
+
+
+def place_own_kernel(*refs):
+    for copy in place_pieces(0, refs[:4], *refs[4:]):
+        copy.wait()
+
+
+def place_rest_kernel(*refs):
+    own, rec = refs[:4], refs[4:8]
+    down_ref, up_ref, front_ref, kern_ref, gain_ref, stage, sems = refs[10:]
+    copies = place_pieces(1, rec, down_ref, up_ref, stage, sems)
+    for k in range(4):
+        last = [ref[pl.ds(768, 80), :].astype(F32) for ref in (own[k], rec[k])]
+        cols = pl.ds(384 * k, 384)
+        front_ref[:, cols] = last[0][:64] + last[1][:64]
+        small = (last[0][64:72] + last[0][72:]) + (last[1][64:72] + last[1][72:])
+        kern_ref[:, cols] = small[:5]
+        gain_ref[cols] = small[5]
+    for copy in copies:
+        copy.wait()
+
+
+def place(own, rec):
+    big = [jax.ShapeDtypeStruct((768, 1536), F32), jax.ShapeDtypeStruct((1536, 768), F32)]
+    hbm = pl.BlockSpec(memory_space=pl.ANY)
+    small = [(64, 1536), (5, 1536), (1536,)]
+    scratch = [pltpu.VMEM((4, 8, 2, 48, 384), F32), pltpu.SemaphoreType.DMA((4, 8, 2))]
+    started = pl.pallas_call(
+        place_own_kernel,
+        in_specs=[WHOLE] * 4,
+        out_specs=[hbm] * 2,
+        out_shape=big,
+        scratch_shapes=scratch,
+        compiler_params=vmem(40),
+        cost_estimate=cost(1 << 20, 7 << 20),
+    )(*own)
+    return pl.pallas_call(
+        place_rest_kernel,
+        grid=(1,),
+        in_specs=[WHOLE] * 8 + [hbm] * 2,
+        out_specs=[hbm] * 2 + [full(shape) for shape in small],
+        out_shape=big + [jax.ShapeDtypeStruct(shape, F32) for shape in small],
+        input_output_aliases={8: 0, 9: 1},
+        scratch_shapes=scratch,
+        compiler_params=vmem(40),
+        cost_estimate=cost(1 << 20, 7 << 20),
+    )(*own, *rec, *started)
 
 
 def high_low(value):
@@ -382,7 +413,7 @@
 
 
 def tail_kernel(
-    k0, r0, k1, r1, normed_ref, rstd_ref, frames_ref, segs_ref, stack_ref, cot_ref, kern_ref, gain_ref,
+    dln_ref, rec_ref, normed_ref, rstd_ref, frames_ref, segs_ref, stack_ref, cot_ref, kern_ref, gain_ref,
     keep_ref, send_ref, scaled, moved, sums,
 ):
     sums[...] = jnp.zeros_like(sums)
@@ -400,9 +431,7 @@
 
     for r in range(0, 128, 16):
         at = pl.ds(r, 16)
-        dln = jnp.concatenate(
-            [k0[at, :].astype(F32) + r0[at, :].astype(F32), k1[at, :].astype(F32) + r1[at, :].astype(F32)], axis=1
-        )
+        dln = dln_ref[at, :] + rec_ref[at, :].astype(F32)
         normed = normed_ref[at, :]
         rstd = rstd_ref[at, :][:, 0:1]
         sums[5] += fold(dln * normed)
@@ -442,14 +471,13 @@
     args = (*pieces, normed, rstd, frames, segs, stack, cot, kern, gain)
     return pl.pallas_call(
         tail_kernel,
-        grid=(1,),
-        in_specs=[full(a.shape) for a in args],
-        out_specs=[full((272, 1536))] * 2,
+        in_specs=[WHOLE] * len(args),
+        out_specs=[WHOLE] * 2,
         out_shape=[jax.ShapeDtypeStruct((272, 1536), F32), jax.ShapeDtypeStruct((272, 1536), BF)],
         scratch_shapes=[
             pltpu.VMEM((640, 1536), BF), pltpu.VMEM((640, 512), BF), pltpu.VMEM((6, 8, 1536), F32),
         ],
-        compiler_params=vmem(32),
+        compiler_params=vmem(16),
         cost_estimate=cost(60 * 10**9, 6 << 20),
     )(*args)
 
@@ -468,25 +496,24 @@
 
 
 def glue(kernel, outs, *args, flops=5 * 10**8):
-    whole = pl.BlockSpec(memory_space=pltpu.VMEM)
     return pl.pallas_call(
         kernel,
-        in_specs=[whole] * len(args),
-        out_specs=[whole] * len(outs),
+        in_specs=[WHOLE] * len(args),
+        out_specs=[WHOLE] * len(outs),
         out_shape=[jax.ShapeDtypeStruct(*out) for out in outs],
         compiler_params=vmem(16),
         cost_estimate=cost(flops, 1 << 16),
     )(*args)
 
 
-def dln_core_kernel(own, rec, keep0, keep1, send0, send1):
+def dln_core_kernel(own, rec, keep, send):
     for i in range(4):
-        at = pl.ds(128 * i, 128)
+        at, to = pl.ds(128 * i, 128), pl.ds(128 * (i // 2), 128)
         total = own[at, :].astype(F32) + rec[at, :].astype(F32)
-        to = pl.ds(128 * (i // 2), 128)
-        (send0 if i % 2 else keep0)[to, :] = total[:, :768].astype((send0 if i % 2 else keep0).dtype)
-        to = pl.ds(128 * (i % 2), 128)
-        (send1 if i // 2 else keep1)[to, :] = total[:, 768:].astype((send1 if i // 2 else keep1).dtype)
+        if i % 2:
+            send[to, :] = total.astype(BF)
+        else:
+            keep[to, :] = total
 
 
 def halve_kernel(own, rec, keep, send):
@@ -512,10 +539,10 @@
     for i in range(4):
         at = pl.ds(64 * i, 64)
         total = own[at, :] + rec[at, :].astype(F32)
-        to = pl.ds(64 * (i // 2), 64)
-        (send0 if i % 2 else keep0)[to, :] = total[:, :768].astype((send0 if i % 2 else keep0).dtype)
-        to = pl.ds(64 * (i % 2), 64)
-        (send1 if i // 2 else keep1)[to, :] = total[:, 768:].astype((send1 if i // 2 else keep1).dtype)
+        out = send0 if i % 2 else keep0
+        out[pl.ds(64 * (i // 2), 64), :] = total[:, :768].astype(out.dtype)
+        out = send1 if i // 2 else keep1
+        out[pl.ds(64 * (i % 2), 64), :] = total[:, 768:].astype(out.dtype)
     small = add_small(own[pl.ds(256, 16), :], rec[pl.ds(256, 16), :])
     for i, (keep, send) in enumerate(((keep0, send0), (keep1, send1))):
         half = small[:, 768 * i : 768 * i + 768]
@@ -537,8 +564,9 @@
     small = add_small(front[pl.ds(64, 16), :], front_rec[pl.ds(64, 16), :])
     for i, out in enumerate((out0, out1)):
         out[pl.ds(0, 96), :] = piece[96 * i : 96 * i + 96]
-        out[pl.ds(96, 64), :] = front_rows[:, 384 * i : 384 * i + 384]
-        out[pl.ds(160, 16), :] = small[:, 384 * i : 384 * i + 384]
+        cols = slice(384 * i, 384 * i + 384)
+        out[pl.ds(96, 64), :] = front_rows[:, cols]
+        out[pl.ds(160, 16), :] = small[:, cols]
 
 
 def spread_kernel(own, rec, out):
@@ -553,19 +581,18 @@
     return glue(halve_first_kernel, [((4, 96, 384), F32), ((4, 96, 384), BF)], keep, rec)
 
 
-def reduce_parts(pairs):
-    recs = [over(PARTS[k][1], pairs[k][1]) for k in range(4)]
-    ends = []
-    for k in (0, 2):
-        keep, send = glue(
-            join_kernel, [((2, 192, 384), F32), ((2, 192, 384), BF)],
-            pairs[k][0], recs[k], pairs[k + 1][0], recs[k + 1],
-        )
-        keep, send = glue(
-            halve_kernel, [((1, 192, 384), F32), ((1, 192, 384), BF)], keep, over(PARTS[k][2], send)
-        )
-        ends.append((keep, over(PARTS[k][3], send)))
-    return ends
+def join_parts(k, pairs, recs):
+    return glue(
+        join_kernel, [((2, 192, 384), F32), ((2, 192, 384), BF)],
+        pairs[k][0], recs[0], pairs[k + 1][0], recs[1],
+    )
+
+
+def reduce_ends(k, keep, send):
+    keep, send = glue(
+        halve_kernel, [((1, 192, 384), F32), ((1, 192, 384), BF)], keep, over(PARTS[k][2], send)
+    )
+    return keep, over(PARTS[k][3], send)
 
 
 def spread_parts(ends, fronts):
@@ -576,10 +603,7 @@
         recs = [over(SPREAD[k][s], bufs[k]) for k in range(4)]
         rows = 2 * bufs[0].shape[0] - 80
         bufs = [glue(spread_kernel, [((rows, 384), BF)], bufs[k], recs[k])[0] for k in range(4)]
-    pieces = []
-    for k in range(4):
-        pieces += [bufs[k], over(SPREAD[k][0], bufs[k])]
-    return pieces
+    return bufs, [over(SPREAD[k][0], bufs[k]) for k in range(4)]
 
 
 def per_device(
@@ -598,7 +622,7 @@
     others = [xor_send(cot, "tensor", m ^ 1, 8) for m in ORDER]
 
     ln, normed, rstd, frames, segs, stack = normalise(pa, pb, wa, wb, conv_kernel, gain_row)
-    hidden, slope = hidden_rows(ln, up_weight)
+    hidden, slope = hidden_rows(ln, up_weight, down_weight)
     slope, *others = lax.optimization_barrier((slope, *others))
     cb = jnp.stack(others)
     ca = xor_send(cb, "tensor", 1, 8)
@@ -606,29 +630,35 @@
     dpre_b, dln_send = backward_rows(1, cb, slope, up_weight, down_weight)
 
     dln_rec = xor_send(dln_send, "tensor", 1, 8)
-    k0, k1, s0, s1 = glue(
-        dln_core_kernel, [((256, 768), F32)] * 2 + [((256, 768), BF)] * 2, dln_keep, dln_rec
+    keep, send = glue(
+        dln_core_kernel, [((256, 1536), F32), ((256, 1536), BF)], dln_keep, dln_rec
     )
-    r0, r1 = xor_send(s0, "tensor", 2, 8), xor_send(s1, "tensor", 6, 8)
+    rec = xor_send(send, "tensor", 2, 8)
     parts = [weight_part(k, hidden, ca, cb, ln, dpre_a, dpre_b) for k in range(4)]
-    half = [((128, 768), F32), ((128, 768), BF)]
-    k0, s0 = glue(halve_kernel, half, k0, r0)
-    k1, s1 = glue(halve_kernel, half, k1, r1)
-    pieces = (k0, xor_send(s0, "tensor", 6, 8), k1, xor_send(s1, "tensor", 2, 8))
+    firsts = [over(PARTS[k][0], parts[k][1]) for k in range(4)]
+    pairs = [halve_first(parts[0][0], firsts[0])]
+    rec = after(rec, pairs[0][1], *[p[0] for p in parts[1:]])
+    keep, send = glue(halve_kernel, [((128, 1536), F32), ((128, 1536), BF)], keep, rec)
+    pairs.append(halve_first(parts[1][0], firsts[1]))
+    send = after(send, pairs[1][1])
+    rec = xor_send(send, "tensor", 6, 8)
+    pairs += [halve_first(parts[k][0], firsts[k]) for k in (2, 3)]
+    seconds = [over(PARTS[k][1], pairs[k][1]) for k in range(4)]
+    joined = join_parts(0, pairs, seconds[:2])
+    pieces = (keep, after(rec, joined[1], *seconds[2:]))
     keep, send = tail(pieces, normed, rstd, frames, segs, stack, cot, conv_kernel, gain_row)
-    pairs = [halve_first(parts[k][0], over(PARTS[k][0], parts[k][1])) for k in range(4)]
+    ends = reduce_ends(0, *joined), reduce_ends(2, *join_parts(2, pairs, seconds[2:]))
     k0, k1, s0, s1 = glue(
         front_core_kernel, [((144, 768), F32)] * 2 + [((144, 768), BF)] * 2,
         keep, xor_send(send, "tensor", 1, 8), flops=FIRST,
     )
-    ends = reduce_parts(pairs)
     half = [((80, 768), F32), ((80, 768), BF)]
     k0, s0 = glue(front_x_kernel, half, k0, xor_send(s0, "tensor", 2, 8), flops=FIRST)
     k1, s1 = glue(front_x_kernel, half, k1, xor_send(s1, "tensor", 6, 8), flops=FIRST)
     fronts = (k0, xor_send(s0, "tensor", 6, 8)), (k1, xor_send(s1, "tensor", 2, 8))
-    pieces = spread_parts(ends, fronts)
-    grad_down, grad_up, grad_front, grad_kernel, grad_gain = place(pieces)
-    return (grad_front, grad_kernel, grad_gain[0], grad_up, grad_down)
+    own, rec = spread_parts(ends, fronts)
+    grad_down, grad_up, grad_front, grad_kernel, grad_gain = place(own, rec)
+    return (grad_front, grad_kernel, grad_gain, grad_up, grad_down)
 
 
 def solution(mesh):

time: 171 us -> 164 us (0.959)
  local copies, waits for them, and re-layouts: 3.64 us -> 0.04 us
  waiting for transfers between devices: 50.5 us -> 47.7 us
  starting transfers between devices: 73.7 us -> 71.7 us
    unnamed x16 -> x10, local copies, waits for them, and re-layouts: 3.63 us -> 0.03 us
    ppermute x54 -> x52, waiting for transfers between devices: 50.5 us -> 47.7 us  [xor_send(): return lax.ppermute(value, axis, [(i, i ^ mask) for i in range(size)])]
    ppermute x54 -> x52, starting transfers between devices: 73.7 us -> 71.7 us  [xor_send(): return lax.ppermute(value, axis, [(i, i ^ mask) for i in range(size)])]
  transfers between devices with their start and end apart: 54 -> 52, of which waited for: 25 -> 27; matrix products, arithmetic and copies ran while one was open for 1% -> 1% of each run, Pallas kernels for 20% -> 20%
where the time goes in v3:
time: 164 us
  starting transfers between devices  71.7 us (44%)
  waiting for transfers between devices  47.7 us (29%)
  Pallas kernels  41.2 us (25%)
  other arithmetic  2.27 us (1%)
    ppermute x52, starting transfers between devices, xor_send(): return lax.ppermute(value, axis, [(i, i ^ mask) for i in range(size)])  71.7 us
    ppermute x52, waiting for transfers between devices, xor_send(): return lax.ppermute(value, axis, [(i, i ^ mask) for i in range(size)])  47.7 us
    pallas_call x1, Pallas kernels, normalise(): pl.pallas_call(norm_kernel, grid=(4,), in_specs=[WHOLE] * 6, out_specs=[W...  9.45 us
    pallas_call x4, Pallas kernels, weight_part(): pl.pallas_call(functools.partial(weight_kernel, k), in_specs=[WHOLE] * 6,...  7.67 us
    pallas_call x2, Pallas kernels, backward_rows(): pl.pallas_call(functools.partial(backward_kernel, side), in_specs=[WHOLE]...  6.35 us
    pallas_call x1, Pallas kernels, place(): pl.pallas_call(place_rest_kernel, grid=(1,), in_specs=[WHOLE] * 8 + [hbm]...  3.52 us
    pallas_call x1, Pallas kernels, hidden_rows(): pl.pallas_call(hidden_kernel, in_specs=[WHOLE] * 3, out_specs=[WHOLE] * 2...  3.51 us
  transfers between devices with their start and end apart: 52, of which 27 were waited for; matrix products, arithmetic and copies ran while one was open for 1% of the time, Pallas kernels for 20%

profile of v3, /device:TPU:0, one launch (start us, length us, event | category | flops | bytes accessed | tf_op | source)
XLA Modules:
  0.0 164.0 jit_solution(11360391693042211099)
XLA Ops:
  0.6 2.6 %shard_map.128 = (bf16[640,128]{1,0:T(8,128)(2,1)}, bf16[640,128]{1,0:T(8,128)(2,1)}, bf16[640,128]{1,0:T(8,128)(2,1)}, bf16[640,128]{1,0:T(8,128)(2,1)}) custom-call(s32[1,4]{1,0:T(1,128)} %lengths_hbm.1, bf16[32,64,65]{2,1,0:T(8,128)(2,1)} %bitcast.22, s32[1,128]{1,0:T(1,128)} %seg_hbm.1), custom_call_target="tpu_custom_call" | custom-call | flops 42598400 | bytes 2097152 | tf_op jit(solution)/shard_map/pallas_call | solution.py:89
  3.2 4.0 %collective-permute-start = (bf16[640,128]{1,0:T(8,128)(2,1)}, bf16[640,128]{1,0:T(8,128)(2,1)S(1)}, u32[]{:S(2)}, u32[]{:S(2)}) collective-permute-start(bf16[640,128]{1,0:T(8,128)(2,1)} %get-tuple-element.90), channel_id=1, source_target_pairs={{0,16},{8,24},{16,0},{24,8},{1,17},{9,25},{17,1},{25,9},{2,18},{10... | collective-permute-start | bytes 491528 | tf_op jit(solution)/shard_map/ppermute | solution.py:35
  7.3 1.0 collective-permute-start.1
  8.3 3.0 %collective-permute-start.9 = (bf16[64,1536]{1,0:T(8,128)(2,1)}, bf16[64,1536]{1,0:T(8,128)(2,1)S(1)}, u32[]{:S(2)}, u32[]{:S(2)}) collective-permute-start(bf16[64,1536]{1,0:T(8,128)(2,1)} %param.12), channel_id=1, source_target_pairs={{0,4},{1,5},{2,6},{3,7},{4,0},{5,1},{6,2},{7,3},{8,12},{9,13},{10,... | collective-permute-start | bytes 589832 | tf_op jit(solution)/shard_map/ppermute | solution.py:35
  11.3 1.1 collective-permute-start.8
  12.5 1.5 collective-permute-start.7
  14.0 2.0 %collective-permute-done.1 = bf16[640,128]{1,0:T(8,128)(2,1)S(1)} collective-permute-done((bf16[640,128]{1,0:T(8,128)(2,1)}, bf16[640,128]{1,0:T(8,128)(2,1)S(1)}, u32[]{:S(2)}, u32[]{:S(2)}) %collective-permute-start.1) | collective-permute-done | bytes 163872 | tf_op jit(solution)/shard_map/ppermute | solution.py:35
  16.0 1.0 add_add_fusion
  16.9 3.1 %collective-permute-start.5 = (bf16[640,128]{1,0:T(8,128)(2,1)S(1)}, bf16[640,128]{1,0:T(8,128)(2,1)S(1)}, u32[]{:S(2)}, u32[]{:S(2)}) collective-permute-start(bf16[640,128]{1,0:T(8,128)(2,1)S(1)} %add_add_fusion), channel_id=1, source_target_pairs={{0,4},{1,5},{2,6},{3,7},{4,0},{5,1},{6,2},{7,3},{8,12},{9,13},{10,... | collective-permute-start | bytes 491528 | tf_op jit(solution)/shard_map/ppermute | solution.py:35
  20.0 1.1 collective-permute-start.4
  21.2 1.0 pad_maximum_fusion.1.wa_ref
  22.3 2.4 %collective-permute-done.5 = bf16[640,128]{1,0:T(8,128)(2,1)S(1)} collective-permute-done((bf16[640,128]{1,0:T(8,128)(2,1)S(1)}, bf16[640,128]{1,0:T(8,128)(2,1)S(1)}, u32[]{:S(2)}, u32[]{:S(2)}) %collective-permute-start.5) | collective-permute-done | bytes 163872 | tf_op jit(solution)/shard_map/ppermute | solution.py:35
  24.7 2.9 %collective-permute-done.4 = bf16[640,128]{1,0:T(8,128)(2,1)S(1)} collective-permute-done((bf16[640,128]{1,0:T(8,128)(2,1)S(1)}, bf16[640,128]{1,0:T(8,128)(2,1)S(1)}, u32[]{:S(2)}, u32[]{:S(2)}) %collective-permute-start.4) | collective-permute-done | bytes 163872 | tf_op jit(solution)/shard_map/ppermute | solution.py:35
  27.8 2.1 %collective-permute-start.14 = (bf16[128,1536]{1,0:T(8,128)(2,1)S(1)}, bf16[128,1536]{1,0:T(8,128)(2,1)S(1)}, u32[]{:S(2)}, u32[]{:S(2)}) collective-permute-start(bf16[128,1536]{1,0:T(8,128)(2,1)S(1)} %bitcast.16), channel_id=1, source_target_pairs={{0,5},{1,4},{2,7},{3,6},{4,1},{5,0},{6,3},{7,2},{8,13},{9,12},{10,... | collective-permute-start | bytes 1179656 | tf_op jit(solution)/shard_map/ppermute | solution.py:35
  29.9 1.7 %collective-permute-start.13 = (bf16[128,1536]{1,0:T(8,128)(2,1)S(1)}, bf16[128,1536]{1,0:T(8,128)(2,1)S(1)}, u32[]{:S(2)}, u32[]{:S(2)}) collective-permute-start(bf16[128,1536]{1,0:T(8,128)(2,1)S(1)} %bitcast.17), channel_id=1, source_target_pairs={{0,7},{1,6},{2,5},{3,4},{4,3},{5,2},{6,1},{7,0},{8,15},{9,14},{10,... | collective-permute-start | bytes 1179656 | tf_op jit(solution)/shard_map/ppermute | solution.py:35
  32.1 9.4 %shard_map.129 = (bf16[1024,1536]{1,0:T(8,128)(2,1)S(1)}, f32[128,1536]{1,0:T(8,128)S(1)}, f32[128,128]{1,0:T(8,128)S(1)}, f32[160,1536]{1,0:T(8,128)S(1)}, f32[...) custom-call(bf16[4,640,128]{2,1,0:T(8,128)(2,1)S(1)} %pad_maximum_fusion.2.a_ref, ...), custom_call_target="tpu_custom_call" | custom-call | flops 12000000000 | bytes 10485760 | tf_op jit(solution)/shard_map/pallas_call | solution.py:206
  41.6 3.5 %shard_map.130 = (bf16[1024,768]{1,0:T(8,128)(2,1)S(1)}, f32[1024,768]{1,0:T(8,128)S(1)}) custom-call(bf16[1024,1536]{1,0:T(8,128)(2,1)S(1)} %get-tuple-element.95.ln_ref, bf16[1536,768]{1,0:T(8,128)(2,1)S(1)} %copy-done, bf16[768,1536]{1,0:T(8,128)(2,1)S(1)} %copy-done.1), custom_call_target="tpu_custom_call" | custom-call | flops 2415919104 | bytes 10485760 | tf_op jit(solution)/shard_map/pallas_call | solution.py:255
  45.1 4.1 %collective-permute-done.13 = bf16[128,1536]{1,0:T(8,128)(2,1)S(1)} collective-permute-done((bf16[128,1536]{1,0:T(8,128)(2,1)S(1)}, bf16[128,1536]{1,0:T(8,128)(2,1)S(1)}, u32[]{:S(2)}, u32[]{:S(2)}) %collective-permute-start.13) | collective-permute-done | bytes 393248 | tf_op jit(solution)/shard_map/ppermute | solution.py:35
  49.6 3.2 %shard_map.132 = (bf16[512,768]{1,0:T(8,128)(2,1)S(1)}, bf16[512,1536]{1,0:T(8,128)(2,1)S(1)}) custom-call(bf16[4,128,1536]{2,1,0:T(8,128)(2,1)S(1)} %pad_maximum_fusion.cot_ref.cb_ref, f32[1024,768]{1,0:T(8,128)S(1)} %get-tuple-element.103.slope_ref, bf16[1536,768]{1,0:T(8,128)(2,1)S(1)} %copy-done, bf16[768,1536]{1,0:T(8,128)(2,1)S(1)} %copy-done.1), custom_call_target="tpu_custom_call" | custom-call | flops 2415919104 | bytes 10485760 | tf_op jit(solution)/shard_map/pallas_call | solution.py:281
  53.5 3.2 %shard_map.131 = (bf16[512,768]{1,0:T(8,128)(2,1)S(1)}, bf16[512,1536]{1,0:T(8,128)(2,1)S(1)}) custom-call(bf16[4,128,1536]{2,1,0:T(8,128)(2,1)S(1)} %collective-permute-done.15.cot_ref.ca_ref, f32[1024,768]{1,0:T(8,128)S(1)} %get-tuple-element.103.slope_ref, bf16[1536,768]{1,0:T(8,128)(2,1)S(1)} %copy-done, bf16[768,1536]{1,0:T(8,128)(2,1)S(1)} %copy-done.1), custom_call_target="tpu_custom_call" | custom-call | flops 2415919104 | bytes 10485760 | tf_op jit(solution)/shard_map/pallas_call | solution.py:281
  56.7 1.9 %shard_map.133 = (bf16[8,96,384]{2,1,0:T(8,128)(2,1)S(1)}, bf16[8,96,384]{2,1,0:T(8,128)(2,1)S(1)}) custom-call(bf16[1024,768]{1,0:T(8,128)(2,1)S(1)} %get-tuple-element.96.hid_ref, bf16[4,128,1536]{2,1,0:T(8,128)(2,1)S(1)} %collective-permute-done.15.cot_ref.ca_ref, bf16[4,128,1536]{2,1,0:T(8,128)(2,1)S(1)} %pad_maximum_fusion.cot_ref.cb_ref, ...), custom_call_target="tpu_custom_call" | custom-call | flops 1207959552 | bytes 7340032 | tf_op jit(solution)/shard_map/pallas_call | solution.py:325
  58.6 1.7 %collective-permute-start.16 = (bf16[8,96,384]{2,1,0:T(8,128)(2,1)S(1)}, bf16[8,96,384]{2,1,0:T(8,128)(2,1)S(1)}, u32[]{:S(2)}, u32[]{:S(2)}) collective-permute-start(bf16[8,96,384]{2,1,0:T(8,128)(2,1)S(1)} %get-tuple-element.107), channel_id=1, source_target_pairs={{0,32},{32,0},{64,96},{96,64},{1,33},{33,1},{65,97},{97,65},{2,34}... | collective-permute-start | bytes 1769480 | tf_op jit(solution)/shard_map/ppermute | solution.py:35
  60.6 1.4 collective-permute-start.23
  62.0 1.9 %shard_map.135 = (bf16[8,96,384]{2,1,0:T(8,128)(2,1)S(1)}, bf16[8,96,384]{2,1,0:T(8,128)(2,1)S(1)}) custom-call(bf16[1024,768]{1,0:T(8,128)(2,1)S(1)} %get-tuple-element.96.hid_ref, bf16[4,128,1536]{2,1,0:T(8,128)(2,1)S(1)} %collective-permute-done.15.cot_ref.ca_ref, bf16[4,128,1536]{2,1,0:T(8,128)(2,1)S(1)} %pad_maximum_fusion.cot_ref.cb_ref, ...), custom_call_target="tpu_custom_call" | custom-call | flops 1207959552 | bytes 7340032 | tf_op jit(solution)/shard_map/pallas_call | solution.py:325
  63.9 1.1 collective-permute-start.18
  65.0 1.9 %shard_map.141 = (bf16[8,96,384]{2,1,0:T(8,128)(2,1)S(1)}, bf16[8,96,384]{2,1,0:T(8,128)(2,1)S(1)}) custom-call(bf16[1024,768]{1,0:T(8,128)(2,1)S(1)} %get-tuple-element.96.hid_ref, bf16[4,128,1536]{2,1,0:T(8,128)(2,1)S(1)} %collective-permute-done.15.cot_ref.ca_ref, bf16[4,128,1536]{2,1,0:T(8,128)(2,1)S(1)} %pad_maximum_fusion.cot_ref.cb_ref, ...), custom_call_target="tpu_custom_call" | custom-call | flops 1207959552 | bytes 7340032 | tf_op jit(solution)/shard_map/pallas_call | solution.py:325
  66.9 2.9 %collective-permute-start.27 = (bf16[8,96,384]{2,1,0:T(8,128)(2,1)S(1)}, bf16[8,96,384]{2,1,0:T(8,128)(2,1)S(1)}, u32[]{:S(2)}, u32[]{:S(2)}) collective-permute-start(bf16[8,96,384]{2,1,0:T(8,128)(2,1)S(1)} %get-tuple-element.130), channel_id=1, source_target_pairs={{0,24},{8,16},{16,8},{24,0},{1,25},{9,17},{17,9},{25,1},{2,26},{10... | collective-permute-start | bytes 1769480 | tf_op jit(solution)/shard_map/ppermute | solution.py:35
  69.8 1.9 %shard_map.140 = (bf16[8,96,384]{2,1,0:T(8,128)(2,1)S(1)}, bf16[8,96,384]{2,1,0:T(8,128)(2,1)S(1)}) custom-call(bf16[1024,768]{1,0:T(8,128)(2,1)S(1)} %get-tuple-element.96.hid_ref, bf16[4,128,1536]{2,1,0:T(8,128)(2,1)S(1)} %collective-permute-done.15.cot_ref.ca_ref, bf16[4,128,1536]{2,1,0:T(8,128)(2,1)S(1)} %pad_maximum_fusion.cot_ref.cb_ref, ...), custom_call_target="tpu_custom_call" | custom-call | flops 1207959552 | bytes 7340032 | tf_op jit(solution)/shard_map/pallas_call | solution.py:325
  71.8 2.3 %collective-permute-start.25 = (bf16[8,96,384]{2,1,0:T(8,128)(2,1)S(1)}, bf16[8,96,384]{2,1,0:T(8,128)(2,1)S(1)}, u32[]{:S(2)}, u32[]{:S(2)}) collective-permute-start(bf16[8,96,384]{2,1,0:T(8,128)(2,1)S(1)} %get-tuple-element.128), channel_id=1, source_target_pairs={{0,96},{32,64},{64,32},{96,0},{1,97},{33,65},{65,33},{97,1},{2,98}... | collective-permute-start | bytes 1769480 | tf_op jit(solution)/shard_map/ppermute | solution.py:35
  74.2 4.6 %collective-permute-done.18.rec = bf16[8,96,384]{2,1,0:T(8,128)(2,1)S(1)} collective-permute-done((bf16[8,96,384]{2,1,0:T(8,128)(2,1)S(1)}, bf16[8,96,384]{2,1,0:T(8,128)(2,1)S(1)}, u32[]{:S(2)}, u32[]{:S(2)}) %collective-permute-start.18) | collective-permute-done | bytes 589856 | tf_op jit(solution)/shard_map/ppermute | solution.py:35
  78.9 1.0 collective-permute-done.23.rec
  80.1 2.6 %collective-permute-start.24 = (bf16[128,1536]{1,0:T(8,128)(2,1)S(1)}, bf16[128,1536]{1,0:T(8,128)(2,1)S(1)}, u32[]{:S(2)}, u32[]{:S(2)}) collective-permute-start(bf16[128,1536]{1,0:T(8,128)(2,1)S(1)} %get-tuple-element.127), channel_id=1, source_target_pairs={{0,6},{1,7},{2,4},{3,5},{4,2},{5,3},{6,0},{7,1},{8,14},{9,15},{10,... | collective-permute-start | bytes 1179656 | tf_op jit(solution)/shard_map/ppermute | solution.py:35
  82.7 1.0 collective-permute-start.17
  84.3 3.1 %collective-permute-start.28 = (bf16[4,96,384]{2,1,0:T(8,128)(2,1)S(1)}, bf16[4,96,384]{2,1,0:T(8,128)(2,1)S(1)}, u32[]{:S(2)}, u32[]{:S(2)}) collective-permute-start(bf16[4,96,384]{2,1,0:T(8,128)(2,1)S(1)} %get-tuple-element.131), channel_id=1, source_target_pairs={{0,96},{32,64},{64,32},{96,0},{1,97},{33,65},{65,33},{97,1},{2,98}... | collective-permute-start | bytes 884744 | tf_op jit(solution)/shard_map/ppermute | solution.py:35
  88.4 2.3 %collective-permute-start.26 = (bf16[4,96,384]{2,1,0:T(8,128)(2,1)S(1)}, bf16[4,96,384]{2,1,0:T(8,128)(2,1)S(1)}, u32[]{:S(2)}, u32[]{:S(2)}) collective-permute-start(bf16[4,96,384]{2,1,0:T(8,128)(2,1)S(1)} %get-tuple-element.129), channel_id=1, source_target_pairs={{0,24},{8,16},{16,8},{24,0},{1,25},{9,17},{17,9},{25,1},{2,26},{10... | collective-permute-start | bytes 884744 | tf_op jit(solution)/shard_map/ppermute | solution.py:35
  91.1 2.5 %collective-permute-done.28.rec1 = bf16[4,96,384]{2,1,0:T(8,128)(2,1)S(1)} collective-permute-done((bf16[4,96,384]{2,1,0:T(8,128)(2,1)S(1)}, bf16[4,96,384]{2,1,0:T(8,128)(2,1)S(1)}, u32[]{:S(2)}, u32[]{:S(2)}) %collective-permute-start.28) | collective-permute-done | bytes 294944 | tf_op jit(solution)/shard_map/ppermute | solution.py:35
  93.6 3.0 %collective-permute-done.26.rec0 = bf16[4,96,384]{2,1,0:T(8,128)(2,1)S(1)} collective-permute-done((bf16[4,96,384]{2,1,0:T(8,128)(2,1)S(1)}, bf16[4,96,384]{2,1,0:T(8,128)(2,1)S(1)}, u32[]{:S(2)}, u32[]{:S(2)}) %collective-permute-start.26) | collective-permute-done | bytes 294944 | tf_op jit(solution)/shard_map/ppermute | solution.py:35
  96.6 2.8 %shard_map.145 = (f32[272,1536]{1,0:T(8,128)S(1)}, bf16[272,1536]{1,0:T(8,128)(2,1)S(1)}) custom-call(f32[128,1536]{1,0:T(8,128)S(1)} %get-tuple-element.125.dln_ref, bf16[128,1536]{1,0:T(8,128)(2,1)S(1)} %collective-permute-done.24.rec_ref, f32[128,1536]{1,0:T(8,128)S(1)} %get-tuple-element.133.normed_ref, f32[128,128]{1,0:T(8,128)S(1)} %get-tuple-element.134.rstd_ref, ...), custom_call_target="tpu_custom_call" | custom-call | flops 60000002048 | bytes 6291456 | tf_op jit(solution)/shard_map/pallas_call | solution.py:472
  99.5 1.6 collective-permute-start.20
  102.1 2.0 %collective-permute-start.30 = (bf16[144,768]{1,0:T(8,128)(2,1)S(1)}, bf16[144,768]{1,0:T(8,128)(2,1)S(1)}, u32[]{:S(2)}, u32[]{:S(2)}) collective-permute-start(bf16[144,768]{1,0:T(8,128)(2,1)S(1)} %get-tuple-element.141), channel_id=1, source_target_pairs={{0,2},{1,3},{2,0},{3,1},{4,6},{5,7},{6,4},{7,5},{8,10},{9,11},{10,... | collective-permute-start | bytes 663560 | tf_op jit(solution)/shard_map/ppermute | solution.py:35
  104.1 2.4 %collective-permute-start.40 = (bf16[144,768]{1,0:T(8,128)(2,1)S(1)}, bf16[144,768]{1,0:T(8,128)(2,1)S(1)}, u32[]{:S(2)}, u32[]{:S(2)}) collective-permute-start(bf16[144,768]{1,0:T(8,128)(2,1)S(1)} %get-tuple-element.153), channel_id=1, source_target_pairs={{0,6},{1,7},{2,4},{3,5},{4,2},{5,3},{6,0},{7,1},{8,14},{9,15},{10,... | collective-permute-start | bytes 663560 | tf_op jit(solution)/shard_map/ppermute | solution.py:35
  106.5 3.6 %collective-permute-done.20.rec = bf16[2,192,384]{2,1,0:T(8,128)(2,1)S(1)} collective-permute-done((bf16[2,192,384]{2,1,0:T(8,128)(2,1)S(1)}, bf16[2,192,384]{2,1,0:T(8,128)(2,1)S(1)}, u32[]{:S(2)}, u32[]{:S(2)}) %collective-permute-start.20) | collective-permute-done | bytes 294944 | tf_op jit(solution)/shard_map/ppermute | solution.py:35
  110.2 2.1 %collective-permute-start.21 = (bf16[1,192,384]{2,1,0:T(8,128)(2,1)S(1)}, bf16[1,192,384]{2,1,0:T(8,128)(2,1)S(1)}, u32[]{:S(2)}, u32[]{:S(2)}) collective-permute-start(bf16[1,192,384]{2,1,0:T(8,128)(2,1)S(1)} %get-tuple-element.117), channel_id=1, source_target_pairs={{0,24},{8,16},{16,8},{24,0},{1,25},{9,17},{17,9},{25,1},{2,26},{10... | collective-permute-start | bytes 442376 | tf_op jit(solution)/shard_map/ppermute | solution.py:35
  112.4 1.1 collective-permute-start.31
  114.5 2.4 %collective-permute-done.21.rec = bf16[1,192,384]{2,1,0:T(8,128)(2,1)S(1)} collective-permute-done((bf16[1,192,384]{2,1,0:T(8,128)(2,1)S(1)}, bf16[1,192,384]{2,1,0:T(8,128)(2,1)S(1)}, u32[]{:S(2)}, u32[]{:S(2)}) %collective-permute-start.21) | collective-permute-done | bytes 147488 | tf_op jit(solution)/shard_map/ppermute | solution.py:35
  116.9 1.7 %collective-permute-done.31.front_rec = bf16[80,768]{1,0:T(8,128)(2,1)S(1)} collective-permute-done((bf16[80,768]{1,0:T(8,128)(2,1)S(1)}, bf16[80,768]{1,0:T(8,128)(2,1)S(1)}, u32[]{:S(2)}, u32[]{:S(2)}) %collective-permute-start.31) | collective-permute-done | bytes 122912 | tf_op jit(solution)/shard_map/ppermute | solution.py:35
  118.7 1.2 collective-permute-start.32
  120.1 1.6 collective-permute-start.45
  121.7 2.1 %collective-permute-done.35.rec = bf16[176,384]{1,0:T(8,128)(2,1)S(1)} collective-permute-done((bf16[176,384]{1,0:T(8,128)(2,1)S(1)}, bf16[176,384]{1,0:T(8,128)(2,1)S(1)}, u32[]{:S(2)}, u32[]{:S(2)}) %collective-permute-start.35) | collective-permute-done | bytes 135200 | tf_op jit(solution)/shard_map/ppermute | solution.py:35
  123.8 1.2 collective-permute-start.36
  125.1 1.5 collective-permute-start.33
  126.7 1.7 %collective-permute-start.46 = (bf16[272,384]{1,0:T(8,128)(2,1)S(1)}, bf16[272,384]{1,0:T(8,128)(2,1)S(1)}, u32[]{:S(2)}, u32[]{:S(2)}) collective-permute-start(bf16[272,384]{1,0:T(8,128)(2,1)S(1)} %shard_map.162.own), channel_id=1, source_target_pairs={{0,8},{8,0},{16,24},{24,16},{1,9},{9,1},{17,25},{25,17},{2,10},{10... | collective-permute-start | bytes 626696 | tf_op jit(solution)/shard_map/ppermute | solution.py:35
  129.3 1.6 collective-permute-done.36.rec
  131.6 1.8 %collective-permute-done.33.rec = bf16[272,384]{1,0:T(8,128)(2,1)S(1)} collective-permute-done((bf16[272,384]{1,0:T(8,128)(2,1)S(1)}, bf16[272,384]{1,0:T(8,128)(2,1)S(1)}, u32[]{:S(2)}, u32[]{:S(2)}) %collective-permute-start.33) | collective-permute-done | bytes 208928 | tf_op jit(solution)/shard_map/ppermute | solution.py:35
  134.2 2.7 %collective-permute-start.47 = (bf16[464,384]{1,0:T(8,128)(2,1)S(1)}, bf16[464,384]{1,0:T(8,128)(2,1)S(1)}, u32[]{:S(2)}, u32[]{:S(2)}) collective-permute-start(bf16[464,384]{1,0:T(8,128)(2,1)S(1)} %shard_map.163.own), channel_id=1, source_target_pairs={{0,32},{32,0},{64,96},{96,64},{1,33},{33,1},{65,97},{97,65},{2,34}... | collective-permute-start | bytes 1069064 | tf_op jit(solution)/shard_map/ppermute | solution.py:35
  136.9 2.1 %collective-permute-start.44 = (bf16[464,384]{1,0:T(8,128)(2,1)S(1)}, bf16[464,384]{1,0:T(8,128)(2,1)S(1)}, u32[]{:S(2)}, u32[]{:S(2)}) collective-permute-start(bf16[464,384]{1,0:T(8,128)(2,1)S(1)} %shard_map.160.own), channel_id=1, source_target_pairs={{0,24},{8,16},{16,8},{24,0},{1,25},{9,17},{17,9},{25,1},{2,26},{10... | collective-permute-start | bytes 1069064 | tf_op jit(solution)/shard_map/ppermute | solution.py:35
  140.0 2.7 %collective-permute-done.34.rec = bf16[464,384]{1,0:T(8,128)(2,1)S(1)} collective-permute-done((bf16[464,384]{1,0:T(8,128)(2,1)S(1)}, bf16[464,384]{1,0:T(8,128)(2,1)S(1)}, u32[]{:S(2)}, u32[]{:S(2)}) %collective-permute-start.34) | collective-permute-done | bytes 356384 | tf_op jit(solution)/shard_map/ppermute | solution.py:35
  142.8 3.2 %collective-permute-start.48 = (bf16[848,384]{1,0:T(8,128)(2,1)S(1)}, bf16[848,384]{1,0:T(8,128)(2,1)S(1)}, u32[]{:S(2)}, u32[]{:S(2)}) collective-permute-start(bf16[848,384]{1,0:T(8,128)(2,1)S(1)} %shard_map.151.refs_0_), channel_id=1, source_target_pairs={{0,32},{32,0},{64,96},{96,64},{1,33},{33,1},{65,97},{97,65},{2,34}... | collective-permute-start | bytes 1953800 | tf_op jit(solution)/shard_map/ppermute | solution.py:35
  146.1 0.9 collective-permute-start.51
  147.6 4.1 %collective-permute-start.50 = (bf16[848,384]{1,0:T(8,128)(2,1)S(1)}, bf16[848,384]{1,0:T(8,128)(2,1)S(1)}, u32[]{:S(2)}, u32[]{:S(2)}) collective-permute-start(bf16[848,384]{1,0:T(8,128)(2,1)S(1)} %shard_map.161.refs_2_), channel_id=1, source_target_pairs={{0,96},{32,64},{64,32},{96,0},{1,97},{33,65},{65,33},{97,1},{2,98}... | collective-permute-start | bytes 1953800 | tf_op jit(solution)/shard_map/ppermute | solution.py:35
  151.8 2.8 %shard_map.165 = (f32[768,1536]{1,0:T(8,128)}, f32[1536,768]{1,0:T(8,128)}) custom-call(bf16[848,384]{1,0:T(8,128)(2,1)S(1)} %shard_map.151.refs_0_, bf16[848,384]{1,0:T(8,128)(2,1)S(1)} %shard_map.154.refs_1_, bf16[848,384]{1,0:T(8,128)(2,1)S(1)} %shard_map.161.refs_2_, bf16[848,384]{1,0:T(8,128)(2,1)S(1)} %shard_map.164.refs_3_), custom_call_target="tpu_custom_call" | custom-call | flops 1048576 | bytes 7340032 | tf_op jit(solution)/shard_map/pallas_call | solution.py:383
  154.9 1.3 collective-permute-done.48.refs_4_
  156.2 3.4 %collective-permute-done.51.refs_7_ = bf16[848,384]{1,0:T(8,128)(2,1)S(1)} collective-permute-done((bf16[848,384]{1,0:T(8,128)(2,1)S(1)}, bf16[848,384]{1,0:T(8,128)(2,1)S(1)}, u32[]{:S(2)}, u32[]{:S(2)}) %collective-permute-start.51) | collective-permute-done | bytes 651296 | tf_op jit(solution)/shard_map/ppermute | solution.py:35
  160.3 3.5 %shard_map.166 = (f32[768,1536]{1,0:T(8,128)}, f32[1536,768]{1,0:T(8,128)}, f32[64,1536]{1,0:T(8,128)}, f32[5,1536]{1,0:T(8,128)}, f32[1536]{0:T(1024)}) custom-call(bf16[848,384]{1,0:T(8,128)(2,1)S(1)} %shard_map.151.refs_0_, bf16[848,384]{1,0:T(8,128)(2,1)S(1)} %shard_map.154.refs_1_, ...), custom_call_target="tpu_custom_call", output_to_operand_aliasing={{0}: (8, {}), {1}: (9, {})} | custom-call | flops 1048576 | bytes 7340032 | tf_op jit(solution)/shard_map/pallas_call | solution.py:392
  (94 shorter events, 12.4 us)
Async XLA Ops:
  3.2 9.3 %collective-permute-start = (bf16[640,128]{1,0:T(8,128)(2,1)}, bf16[640,128]{1,0:T(8,128)(2,1)S(1)}, u32[]{:S(2)}, u32[]{:S(2)}) collective-permute-start(bf16[640,128]{1,0:T(8,128)(2,1)} %get-tuple-element.90), channel_id=1, source_target_pairs={{0,16},{8,24},{16,0},{24,8},{1,17},{9,25},{17,1},{25,9},{2,18},{10... | collective-permute-start | bytes 491528 | tf_op jit(solution)/shard_map/ppermute | solution.py:35
  7.3 8.7 %collective-permute-start.1 = (bf16[640,128]{1,0:T(8,128)(2,1)}, bf16[640,128]{1,0:T(8,128)(2,1)S(1)}, u32[]{:S(2)}, u32[]{:S(2)}) collective-permute-start(bf16[640,128]{1,0:T(8,128)(2,1)} %get-tuple-element.91), channel_id=1, source_target_pairs={{0,8},{8,0},{16,24},{24,16},{1,9},{9,1},{17,25},{25,17},{2,10},{10... | collective-permute-start | bytes 491528 | tf_op jit(solution)/shard_map/ppermute | solution.py:35
  8.3 7.7 %collective-permute-start.2 = (bf16[640,128]{1,0:T(8,128)(2,1)}, bf16[640,128]{1,0:T(8,128)(2,1)S(1)}, u32[]{:S(2)}, u32[]{:S(2)}) collective-permute-start(bf16[640,128]{1,0:T(8,128)(2,1)} %get-tuple-element.92), channel_id=1, source_target_pairs={{0,24},{8,16},{16,8},{24,0},{1,25},{9,17},{17,9},{25,1},{2,26},{10... | collective-permute-start | bytes 491528 | tf_op jit(solution)/shard_map/ppermute | solution.py:35
  8.3 12.9 %collective-permute-start.9 = (bf16[64,1536]{1,0:T(8,128)(2,1)}, bf16[64,1536]{1,0:T(8,128)(2,1)S(1)}, u32[]{:S(2)}, u32[]{:S(2)}) collective-permute-start(bf16[64,1536]{1,0:T(8,128)(2,1)} %param.12), channel_id=1, source_target_pairs={{0,4},{1,5},{2,6},{3,7},{4,0},{5,1},{6,2},{7,3},{8,12},{9,13},{10,... | collective-permute-start | bytes 589832 | tf_op jit(solution)/shard_map/ppermute | solution.py:35
  11.3 9.9 %collective-permute-start.8 = (bf16[64,1536]{1,0:T(8,128)(2,1)}, bf16[64,1536]{1,0:T(8,128)(2,1)S(1)}, u32[]{:S(2)}, u32[]{:S(2)}) collective-permute-start(bf16[64,1536]{1,0:T(8,128)(2,1)} %param.12), channel_id=1, source_target_pairs={{0,6},{1,7},{2,4},{3,5},{4,2},{5,3},{6,0},{7,1},{8,14},{9,15},{10,... | collective-permute-start | bytes 589832 | tf_op jit(solution)/shard_map/ppermute | solution.py:35
  12.5 8.7 %collective-permute-start.7 = (bf16[64,1536]{1,0:T(8,128)(2,1)}, bf16[64,1536]{1,0:T(8,128)(2,1)S(1)}, u32[]{:S(2)}, u32[]{:S(2)}) collective-permute-start(bf16[64,1536]{1,0:T(8,128)(2,1)} %param.12), channel_id=1, source_target_pairs={{0,2},{1,3},{2,0},{3,1},{4,6},{5,7},{6,4},{7,5},{8,10},{9,11},{10,... | collective-permute-start | bytes 589832 | tf_op jit(solution)/shard_map/ppermute | solution.py:35
  16.9 10.9 %copy-start.4 = (f32[1536]{0:T(1024)S(1)}, f32[1536]{0:T(1024)}, u32[]{:S(2)}) copy-start(f32[1536]{0:T(1024)} %param.14) | copy-start | bytes 18436
  16.9 10.9 %copy-start.2 = (bf16[1,128,1536]{2,1,0:T(8,128)(2,1)S(1)}, bf16[1,128,1536]{2,1,0:T(8,128)(2,1)}, u32[]{:S(2)}) copy-start(bf16[1,128,1536]{2,1,0:T(8,128)(2,1)} %param.17) | copy-start | bytes 1179652
  16.9 15.2 %copy-start.3 = (f32[5,1536]{1,0:T(8,128)S(1)}, f32[5,1536]{1,0:T(8,128)}, u32[]{:S(2)}) copy-start(f32[5,1536]{1,0:T(8,128)} %kern_ref.3) | copy-start | bytes 92164
  16.9 7.8 %collective-permute-start.5 = (bf16[640,128]{1,0:T(8,128)(2,1)S(1)}, bf16[640,128]{1,0:T(8,128)(2,1)S(1)}, u32[]{:S(2)}, u32[]{:S(2)}) collective-permute-start(bf16[640,128]{1,0:T(8,128)(2,1)S(1)} %add_add_fusion), channel_id=1, source_target_pairs={{0,4},{1,5},{2,6},{3,7},{4,0},{5,1},{6,2},{7,3},{8,12},{9,13},{10,... | collective-permute-start | bytes 491528 | tf_op jit(solution)/shard_map/ppermute | solution.py:35
  20.0 7.5 %collective-permute-start.4 = (bf16[640,128]{1,0:T(8,128)(2,1)S(1)}, bf16[640,128]{1,0:T(8,128)(2,1)S(1)}, u32[]{:S(2)}, u32[]{:S(2)}) collective-permute-start(bf16[640,128]{1,0:T(8,128)(2,1)S(1)} %add_add_fusion), channel_id=1, source_target_pairs={{0,6},{1,7},{2,4},{3,5},{4,2},{5,3},{6,0},{7,1},{8,14},{9,15},{10,... | collective-permute-start | bytes 491528 | tf_op jit(solution)/shard_map/ppermute | solution.py:35
  21.2 6.4 %collective-permute-start.3 = (bf16[640,128]{1,0:T(8,128)(2,1)S(1)}, bf16[640,128]{1,0:T(8,128)(2,1)S(1)}, u32[]{:S(2)}, u32[]{:S(2)}) collective-permute-start(bf16[640,128]{1,0:T(8,128)(2,1)S(1)} %add_add_fusion), channel_id=1, source_target_pairs={{0,2},{1,3},{2,0},{3,1},{4,6},{5,7},{6,4},{7,5},{8,10},{9,11},{10,... | collective-permute-start | bytes 491528 | tf_op jit(solution)/shard_map/ppermute | solution.py:35
  22.2 9.9 %collective-permute-start.10 = (bf16[4,64,1536]{2,1,0:T(8,128)(2,1)S(1)}, bf16[4,64,1536]{2,1,0:T(8,128)(2,1)S(1)}, u32[]{:S(2)}, u32[]{:S(2)}) collective-permute-start(bf16[4,64,1536]{2,1,0:T(8,128)(2,1)S(1)} %pad_maximum_fusion.1.wa_ref), channel_id=1, source_target_pairs={{0,1},{1,0},{2,3},{3,2},{4,5},{5,4},{6,7},{7,6},{8,9},{9,8},{10,11... | collective-permute-start | bytes 2359304 | tf_op jit(solution)/shard_map/ppermute | solution.py:35
  27.7 4.0 %collective-permute-start.6 = (bf16[4,640,128]{2,1,0:T(8,128)(2,1)S(1)}, bf16[4,640,128]{2,1,0:T(8,128)(2,1)S(1)}, u32[]{:S(2)}, u32[]{:S(2)}) collective-permute-start(bf16[4,640,128]{2,1,0:T(8,128)(2,1)S(1)} %pad_maximum_fusion.2.a_ref), channel_id=1, source_target_pairs={{0,1},{1,0},{2,3},{3,2},{4,5},{5,4},{6,7},{7,6},{8,9},{9,8},{10,11... | collective-permute-start | bytes 1966088 | tf_op jit(solution)/shard_map/ppermute | solution.py:35
  27.8 13.8 %copy-start = (bf16[1536,768]{1,0:T(8,128)(2,1)S(1)}, bf16[1536,768]{1,0:T(8,128)(2,1)}, u32[]{:S(2)}) copy-start(bf16[1536,768]{1,0:T(8,128)(2,1)} %up_ref.5) | copy-start | bytes 7077892
  27.8 13.8 %copy-start.1 = (bf16[768,1536]{1,0:T(8,128)(2,1)S(1)}, bf16[768,1536]{1,0:T(8,128)(2,1)}, u32[]{:S(2)}) copy-start(bf16[768,1536]{1,0:T(8,128)(2,1)} %down_ref.5) | copy-start | bytes 7077892
  27.8 17.3 %collective-permute-start.14 = (bf16[128,1536]{1,0:T(8,128)(2,1)S(1)}, bf16[128,1536]{1,0:T(8,128)(2,1)S(1)}, u32[]{:S(2)}, u32[]{:S(2)}) collective-permute-start(bf16[128,1536]{1,0:T(8,128)(2,1)S(1)} %bitcast.16), channel_id=1, source_target_pairs={{0,5},{1,4},{2,7},{3,6},{4,1},{5,0},{6,3},{7,2},{8,13},{9,12},{10,... | collective-permute-start | bytes 1179656 | tf_op jit(solution)/shard_map/ppermute | solution.py:35
  29.9 19.3 %collective-permute-start.13 = (bf16[128,1536]{1,0:T(8,128)(2,1)S(1)}, bf16[128,1536]{1,0:T(8,128)(2,1)S(1)}, u32[]{:S(2)}, u32[]{:S(2)}) collective-permute-start(bf16[128,1536]{1,0:T(8,128)(2,1)S(1)} %bitcast.17), channel_id=1, source_target_pairs={{0,7},{1,6},{2,5},{3,4},{4,3},{5,2},{6,1},{7,0},{8,15},{9,14},{10,... | collective-permute-start | bytes 1179656 | tf_op jit(solution)/shard_map/ppermute | solution.py:35
  31.6 17.6 %collective-permute-start.12 = (bf16[128,1536]{1,0:T(8,128)(2,1)S(1)}, bf16[128,1536]{1,0:T(8,128)(2,1)S(1)}, u32[]{:S(2)}, u32[]{:S(2)}) collective-permute-start(bf16[128,1536]{1,0:T(8,128)(2,1)S(1)} %bitcast.18), channel_id=1, source_target_pairs={{0,3},{1,2},{2,1},{3,0},{4,7},{5,6},{6,5},{7,4},{8,11},{9,10},{10,... | collective-permute-start | bytes 1179656 | tf_op jit(solution)/shard_map/ppermute | solution.py:35
  31.6 17.6 %collective-permute-start.11 = (bf16[128,1536]{1,0:T(8,128)(2,1)S(1)}, bf16[128,1536]{1,0:T(8,128)(2,1)S(1)}, u32[]{:S(2)}, u32[]{:S(2)}) collective-permute-start(bf16[128,1536]{1,0:T(8,128)(2,1)S(1)} %bitcast.19), channel_id=1, source_target_pairs={{0,1},{1,0},{2,3},{3,2},{4,5},{5,4},{6,7},{7,6},{8,9},{9,8},{10,11... | collective-permute-start | bytes 1179656 | tf_op jit(solution)/shard_map/ppermute | solution.py:35
  49.4 4.0 %collective-permute-start.15 = (bf16[4,128,1536]{2,1,0:T(8,128)(2,1)S(1)}, bf16[4,128,1536]{2,1,0:T(8,128)(2,1)S(1)}, u32[]{:S(2)}, u32[]{:S(2)}) collective-permute-start(bf16[4,128,1536]{2,1,0:T(8,128)(2,1)S(1)} %pad_maximum_fusion.cot_ref.cb_ref), channel_id=1, source_target_pairs={{0,1},{1,0},{2,3},{3,2},{4,5},{5,4},{6,7},{7,6},{8,9},{9,8},{10,11... | collective-permute-start | bytes 4718600 | tf_op jit(solution)/shard_map/ppermute | solution.py:35
  52.8 7.4 %collective-permute-start.22 = (bf16[512,1536]{1,0:T(8,128)(2,1)S(1)}, bf16[512,1536]{1,0:T(8,128)(2,1)S(1)}, u32[]{:S(2)}, u32[]{:S(2)}) collective-permute-start(bf16[512,1536]{1,0:T(8,128)(2,1)S(1)} %get-tuple-element.119), channel_id=1, source_target_pairs={{0,1},{1,0},{2,3},{3,2},{4,5},{5,4},{6,7},{7,6},{8,9},{9,8},{10,11... | collective-permute-start | bytes 4718600 | tf_op jit(solution)/shard_map/ppermute | solution.py:35
  58.6 15.4 %collective-permute-start.16 = (bf16[8,96,384]{2,1,0:T(8,128)(2,1)S(1)}, bf16[8,96,384]{2,1,0:T(8,128)(2,1)S(1)}, u32[]{:S(2)}, u32[]{:S(2)}) collective-permute-start(bf16[8,96,384]{2,1,0:T(8,128)(2,1)S(1)} %get-tuple-element.107), channel_id=1, source_target_pairs={{0,32},{32,0},{64,96},{96,64},{1,33},{33,1},{65,97},{97,65},{2,34}... | collective-permute-start | bytes 1769480 | tf_op jit(solution)/shard_map/ppermute | solution.py:35
  60.6 19.4 %collective-permute-start.23 = (bf16[256,1536]{1,0:T(8,128)(2,1)S(1)}, bf16[256,1536]{1,0:T(8,128)(2,1)S(1)}, u32[]{:S(2)}, u32[]{:S(2)}) collective-permute-start(bf16[256,1536]{1,0:T(8,128)(2,1)S(1)} %get-tuple-element.121), channel_id=1, source_target_pairs={{0,2},{1,3},{2,0},{3,1},{4,6},{5,7},{6,4},{7,5},{8,10},{9,11},{10,... | collective-permute-start | bytes 2359304 | tf_op jit(solution)/shard_map/ppermute | solution.py:35
  63.9 14.9 %collective-permute-start.18 = (bf16[8,96,384]{2,1,0:T(8,128)(2,1)S(1)}, bf16[8,96,384]{2,1,0:T(8,128)(2,1)S(1)}, u32[]{:S(2)}, u32[]{:S(2)}) collective-permute-start(bf16[8,96,384]{2,1,0:T(8,128)(2,1)S(1)} %get-tuple-element.111), channel_id=1, source_target_pairs={{0,8},{8,0},{16,24},{24,16},{1,9},{9,1},{17,25},{25,17},{2,10},{10... | collective-permute-start | bytes 1769480 | tf_op jit(solution)/shard_map/ppermute | solution.py:35
  66.9 17.2 %collective-permute-start.27 = (bf16[8,96,384]{2,1,0:T(8,128)(2,1)S(1)}, bf16[8,96,384]{2,1,0:T(8,128)(2,1)S(1)}, u32[]{:S(2)}, u32[]{:S(2)}) collective-permute-start(bf16[8,96,384]{2,1,0:T(8,128)(2,1)S(1)} %get-tuple-element.130), channel_id=1, source_target_pairs={{0,24},{8,16},{16,8},{24,0},{1,25},{9,17},{17,9},{25,1},{2,26},{10... | collective-permute-start | bytes 1769480 | tf_op jit(solution)/shard_map/ppermute | solution.py:35
  71.8 16.4 %collective-permute-start.25 = (bf16[8,96,384]{2,1,0:T(8,128)(2,1)S(1)}, bf16[8,96,384]{2,1,0:T(8,128)(2,1)S(1)}, u32[]{:S(2)}, u32[]{:S(2)}) collective-permute-start(bf16[8,96,384]{2,1,0:T(8,128)(2,1)S(1)} %get-tuple-element.128), channel_id=1, source_target_pairs={{0,96},{32,64},{64,32},{96,0},{1,97},{33,65},{65,33},{97,1},{2,98}... | collective-permute-start | bytes 1769480 | tf_op jit(solution)/shard_map/ppermute | solution.py:35
  80.1 16.5 %collective-permute-start.24 = (bf16[128,1536]{1,0:T(8,128)(2,1)S(1)}, bf16[128,1536]{1,0:T(8,128)(2,1)S(1)}, u32[]{:S(2)}, u32[]{:S(2)}) collective-permute-start(bf16[128,1536]{1,0:T(8,128)(2,1)S(1)} %get-tuple-element.127), channel_id=1, source_target_pairs={{0,6},{1,7},{2,4},{3,5},{4,2},{5,3},{6,0},{7,1},{8,14},{9,15},{10,... | collective-permute-start | bytes 1179656 | tf_op jit(solution)/shard_map/ppermute | solution.py:35
  82.7 8.0 %collective-permute-start.17 = (bf16[4,96,384]{2,1,0:T(8,128)(2,1)S(1)}, bf16[4,96,384]{2,1,0:T(8,128)(2,1)S(1)}, u32[]{:S(2)}, u32[]{:S(2)}) collective-permute-start(bf16[4,96,384]{2,1,0:T(8,128)(2,1)S(1)} %get-tuple-element.109), channel_id=1, source_target_pairs={{0,8},{8,0},{16,24},{24,16},{1,9},{9,1},{17,25},{25,17},{2,10},{10... | collective-permute-start | bytes 884744 | tf_op jit(solution)/shard_map/ppermute | solution.py:35
  83.7 7.3 %collective-permute-start.19 = (bf16[4,96,384]{2,1,0:T(8,128)(2,1)S(1)}, bf16[4,96,384]{2,1,0:T(8,128)(2,1)S(1)}, u32[]{:S(2)}, u32[]{:S(2)}) collective-permute-start(bf16[4,96,384]{2,1,0:T(8,128)(2,1)S(1)} %get-tuple-element.113), channel_id=1, source_target_pairs={{0,32},{32,0},{64,96},{96,64},{1,33},{33,1},{65,97},{97,65},{2,34}... | collective-permute-start | bytes 884744 | tf_op jit(solution)/shard_map/ppermute | solution.py:35
  84.3 9.4 %collective-permute-start.28 = (bf16[4,96,384]{2,1,0:T(8,128)(2,1)S(1)}, bf16[4,96,384]{2,1,0:T(8,128)(2,1)S(1)}, u32[]{:S(2)}, u32[]{:S(2)}) collective-permute-start(bf16[4,96,384]{2,1,0:T(8,128)(2,1)S(1)} %get-tuple-element.131), channel_id=1, source_target_pairs={{0,96},{32,64},{64,32},{96,0},{1,97},{33,65},{65,33},{97,1},{2,98}... | collective-permute-start | bytes 884744 | tf_op jit(solution)/shard_map/ppermute | solution.py:35
  88.4 8.2 %collective-permute-start.26 = (bf16[4,96,384]{2,1,0:T(8,128)(2,1)S(1)}, bf16[4,96,384]{2,1,0:T(8,128)(2,1)S(1)}, u32[]{:S(2)}, u32[]{:S(2)}) collective-permute-start(bf16[4,96,384]{2,1,0:T(8,128)(2,1)S(1)} %get-tuple-element.129), channel_id=1, source_target_pairs={{0,24},{8,16},{16,8},{24,0},{1,25},{9,17},{17,9},{25,1},{2,26},{10... | collective-permute-start | bytes 884744 | tf_op jit(solution)/shard_map/ppermute | solution.py:35
  99.4 2.4 %collective-permute-start.29 = (bf16[272,1536]{1,0:T(8,128)(2,1)S(1)}, bf16[272,1536]{1,0:T(8,128)(2,1)S(1)}, u32[]{:S(2)}, u32[]{:S(2)}) collective-permute-start(bf16[272,1536]{1,0:T(8,128)(2,1)S(1)} %get-tuple-element.139), channel_id=1, source_target_pairs={{0,1},{1,0},{2,3},{3,2},{4,5},{5,4},{6,7},{7,6},{8,9},{9,8},{10,11... | collective-permute-start | bytes 2506760 | tf_op jit(solution)/shard_map/ppermute | solution.py:35
  99.5 10.6 %collective-permute-start.20 = (bf16[2,192,384]{2,1,0:T(8,128)(2,1)S(1)}, bf16[2,192,384]{2,1,0:T(8,128)(2,1)S(1)}, u32[]{:S(2)}, u32[]{:S(2)}) collective-permute-start(bf16[2,192,384]{2,1,0:T(8,128)(2,1)S(1)} %get-tuple-element.115), channel_id=1, source_target_pairs={{0,96},{32,64},{64,32},{96,0},{1,97},{33,65},{65,33},{97,1},{2,98}... | collective-permute-start | bytes 884744 | tf_op jit(solution)/shard_map/ppermute | solution.py:35
  101.3 12.3 %collective-permute-start.38 = (bf16[2,192,384]{2,1,0:T(8,128)(2,1)S(1)}, bf16[2,192,384]{2,1,0:T(8,128)(2,1)S(1)}, u32[]{:S(2)}, u32[]{:S(2)}) collective-permute-start(bf16[2,192,384]{2,1,0:T(8,128)(2,1)S(1)} %get-tuple-element.149), channel_id=1, source_target_pairs={{0,32},{32,0},{64,96},{96,64},{1,33},{33,1},{65,97},{97,65},{2,34}... | collective-permute-start | bytes 884744 | tf_op jit(solution)/shard_map/ppermute | solution.py:35
  102.1 10.3 %collective-permute-start.30 = (bf16[144,768]{1,0:T(8,128)(2,1)S(1)}, bf16[144,768]{1,0:T(8,128)(2,1)S(1)}, u32[]{:S(2)}, u32[]{:S(2)}) collective-permute-start(bf16[144,768]{1,0:T(8,128)(2,1)S(1)} %get-tuple-element.141), channel_id=1, source_target_pairs={{0,2},{1,3},{2,0},{3,1},{4,6},{5,7},{6,4},{7,5},{8,10},{9,11},{10,... | collective-permute-start | bytes 663560 | tf_op jit(solution)/shard_map/ppermute | solution.py:35
  104.1 9.6 %collective-permute-start.40 = (bf16[144,768]{1,0:T(8,128)(2,1)S(1)}, bf16[144,768]{1,0:T(8,128)(2,1)S(1)}, u32[]{:S(2)}, u32[]{:S(2)}) collective-permute-start(bf16[144,768]{1,0:T(8,128)(2,1)S(1)} %get-tuple-element.153), channel_id=1, source_target_pairs={{0,6},{1,7},{2,4},{3,5},{4,2},{5,3},{6,0},{7,1},{8,14},{9,15},{10,... | collective-permute-start | bytes 663560 | tf_op jit(solution)/shard_map/ppermute | solution.py:35
  110.2 6.7 %collective-permute-start.21 = (bf16[1,192,384]{2,1,0:T(8,128)(2,1)S(1)}, bf16[1,192,384]{2,1,0:T(8,128)(2,1)S(1)}, u32[]{:S(2)}, u32[]{:S(2)}) collective-permute-start(bf16[1,192,384]{2,1,0:T(8,128)(2,1)S(1)} %get-tuple-element.117), channel_id=1, source_target_pairs={{0,24},{8,16},{16,8},{24,0},{1,25},{9,17},{17,9},{25,1},{2,26},{10... | collective-permute-start | bytes 442376 | tf_op jit(solution)/shard_map/ppermute | solution.py:35
  112.4 6.2 %collective-permute-start.31 = (bf16[80,768]{1,0:T(8,128)(2,1)S(1)}, bf16[80,768]{1,0:T(8,128)(2,1)S(1)}, u32[]{:S(2)}, u32[]{:S(2)}) collective-permute-start(bf16[80,768]{1,0:T(8,128)(2,1)S(1)} %get-tuple-element.143), channel_id=1, source_target_pairs={{0,6},{1,7},{2,4},{3,5},{4,2},{5,3},{6,0},{7,1},{8,14},{9,15},{10,... | collective-permute-start | bytes 368648 | tf_op jit(solution)/shard_map/ppermute | solution.py:35
  113.6 6.4 %collective-permute-start.39 = (bf16[1,192,384]{2,1,0:T(8,128)(2,1)S(1)}, bf16[1,192,384]{2,1,0:T(8,128)(2,1)S(1)}, u32[]{:S(2)}, u32[]{:S(2)}) collective-permute-start(bf16[1,192,384]{2,1,0:T(8,128)(2,1)S(1)} %get-tuple-element.151), channel_id=1, source_target_pairs={{0,8},{8,0},{16,24},{24,16},{1,9},{9,1},{17,25},{25,17},{2,10},{10... | collective-permute-start | bytes 442376 | tf_op jit(solution)/shard_map/ppermute | solution.py:35
  113.8 6.2 %collective-permute-start.41 = (bf16[80,768]{1,0:T(8,128)(2,1)S(1)}, bf16[80,768]{1,0:T(8,128)(2,1)S(1)}, u32[]{:S(2)}, u32[]{:S(2)}) collective-permute-start(bf16[80,768]{1,0:T(8,128)(2,1)S(1)} %get-tuple-element.155), channel_id=1, source_target_pairs={{0,2},{1,3},{2,0},{3,1},{4,6},{5,7},{6,4},{7,5},{8,10},{9,11},{10,... | collective-permute-start | bytes 368648 | tf_op jit(solution)/shard_map/ppermute | solution.py:35
  118.7 5.1 %collective-permute-start.35 = (bf16[176,384]{1,0:T(8,128)(2,1)S(1)}, bf16[176,384]{1,0:T(8,128)(2,1)S(1)}, u32[]{:S(2)}, u32[]{:S(2)}) collective-permute-start(bf16[176,384]{1,0:T(8,128)(2,1)S(1)} %get-tuple-element.145.own), channel_id=1, source_target_pairs={{0,32},{32,0},{64,96},{96,64},{1,33},{33,1},{65,97},{97,65},{2,34}... | collective-permute-start | bytes 405512 | tf_op jit(solution)/shard_map/ppermute | solution.py:35
  118.7 6.4 %collective-permute-start.32 = (bf16[176,384]{1,0:T(8,128)(2,1)S(1)}, bf16[176,384]{1,0:T(8,128)(2,1)S(1)}, u32[]{:S(2)}, u32[]{:S(2)}) collective-permute-start(bf16[176,384]{1,0:T(8,128)(2,1)S(1)} %get-tuple-element.144.own), channel_id=1, source_target_pairs={{0,24},{8,16},{16,8},{24,0},{1,25},{9,17},{17,9},{25,1},{2,26},{10... | collective-permute-start | bytes 405512 | tf_op jit(solution)/shard_map/ppermute | solution.py:35
  120.1 6.6 %collective-permute-start.45 = (bf16[176,384]{1,0:T(8,128)(2,1)S(1)}, bf16[176,384]{1,0:T(8,128)(2,1)S(1)}, u32[]{:S(2)}, u32[]{:S(2)}) collective-permute-start(bf16[176,384]{1,0:T(8,128)(2,1)S(1)} %get-tuple-element.157.own), channel_id=1, source_target_pairs={{0,96},{32,64},{64,32},{96,0},{1,97},{33,65},{65,33},{97,1},{2,98}... | collective-permute-start | bytes 405512 | tf_op jit(solution)/shard_map/ppermute | solution.py:35
  121.7 6.7 %collective-permute-start.42 = (bf16[176,384]{1,0:T(8,128)(2,1)S(1)}, bf16[176,384]{1,0:T(8,128)(2,1)S(1)}, u32[]{:S(2)}, u32[]{:S(2)}) collective-permute-start(bf16[176,384]{1,0:T(8,128)(2,1)S(1)} %get-tuple-element.156.own), channel_id=1, source_target_pairs={{0,8},{8,0},{16,24},{24,16},{1,9},{9,1},{17,25},{25,17},{2,10},{10... | collective-permute-start | bytes 405512 | tf_op jit(solution)/shard_map/ppermute | solution.py:35
  123.8 7.1 %collective-permute-start.36 = (bf16[272,384]{1,0:T(8,128)(2,1)S(1)}, bf16[272,384]{1,0:T(8,128)(2,1)S(1)}, u32[]{:S(2)}, u32[]{:S(2)}) collective-permute-start(bf16[272,384]{1,0:T(8,128)(2,1)S(1)} %shard_map.152.own), channel_id=1, source_target_pairs={{0,24},{8,16},{16,8},{24,0},{1,25},{9,17},{17,9},{25,1},{2,26},{10... | collective-permute-start | bytes 626696 | tf_op jit(solution)/shard_map/ppermute | solution.py:35
  125.1 8.3 %collective-permute-start.33 = (bf16[272,384]{1,0:T(8,128)(2,1)S(1)}, bf16[272,384]{1,0:T(8,128)(2,1)S(1)}, u32[]{:S(2)}, u32[]{:S(2)}) collective-permute-start(bf16[272,384]{1,0:T(8,128)(2,1)S(1)} %shard_map.149.own), channel_id=1, source_target_pairs={{0,96},{32,64},{64,32},{96,0},{1,97},{33,65},{65,33},{97,1},{2,98}... | collective-permute-start | bytes 626696 | tf_op jit(solution)/shard_map/ppermute | solution.py:35
  126.7 7.4 %collective-permute-start.46 = (bf16[272,384]{1,0:T(8,128)(2,1)S(1)}, bf16[272,384]{1,0:T(8,128)(2,1)S(1)}, u32[]{:S(2)}, u32[]{:S(2)}) collective-permute-start(bf16[272,384]{1,0:T(8,128)(2,1)S(1)} %shard_map.162.own), channel_id=1, source_target_pairs={{0,8},{8,0},{16,24},{24,16},{1,9},{9,1},{17,25},{25,17},{2,10},{10... | collective-permute-start | bytes 626696 | tf_op jit(solution)/shard_map/ppermute | solution.py:35
  128.5 8.4 %collective-permute-start.43 = (bf16[272,384]{1,0:T(8,128)(2,1)S(1)}, bf16[272,384]{1,0:T(8,128)(2,1)S(1)}, u32[]{:S(2)}, u32[]{:S(2)}) collective-permute-start(bf16[272,384]{1,0:T(8,128)(2,1)S(1)} %shard_map.159.own), channel_id=1, source_target_pairs={{0,32},{32,0},{64,96},{96,64},{1,33},{33,1},{65,97},{97,65},{2,34}... | collective-permute-start | bytes 626696 | tf_op jit(solution)/shard_map/ppermute | solution.py:35
  130.9 8.9 %collective-permute-start.37 = (bf16[464,384]{1,0:T(8,128)(2,1)S(1)}, bf16[464,384]{1,0:T(8,128)(2,1)S(1)}, u32[]{:S(2)}, u32[]{:S(2)}) collective-permute-start(bf16[464,384]{1,0:T(8,128)(2,1)S(1)} %shard_map.153.own), channel_id=1, source_target_pairs={{0,96},{32,64},{64,32},{96,0},{1,97},{33,65},{65,33},{97,1},{2,98}... | collective-permute-start | bytes 1069064 | tf_op jit(solution)/shard_map/ppermute | solution.py:35
  133.5 9.2 %collective-permute-start.34 = (bf16[464,384]{1,0:T(8,128)(2,1)S(1)}, bf16[464,384]{1,0:T(8,128)(2,1)S(1)}, u32[]{:S(2)}, u32[]{:S(2)}) collective-permute-start(bf16[464,384]{1,0:T(8,128)(2,1)S(1)} %shard_map.150.own), channel_id=1, source_target_pairs={{0,8},{8,0},{16,24},{24,16},{1,9},{9,1},{17,25},{25,17},{2,10},{10... | collective-permute-start | bytes 1069064 | tf_op jit(solution)/shard_map/ppermute | solution.py:35
  134.2 11.8 %collective-permute-start.47 = (bf16[464,384]{1,0:T(8,128)(2,1)S(1)}, bf16[464,384]{1,0:T(8,128)(2,1)S(1)}, u32[]{:S(2)}, u32[]{:S(2)}) collective-permute-start(bf16[464,384]{1,0:T(8,128)(2,1)S(1)} %shard_map.163.own), channel_id=1, source_target_pairs={{0,32},{32,0},{64,96},{96,64},{1,33},{33,1},{65,97},{97,65},{2,34}... | collective-permute-start | bytes 1069064 | tf_op jit(solution)/shard_map/ppermute | solution.py:35
  136.9 10.6 %collective-permute-start.44 = (bf16[464,384]{1,0:T(8,128)(2,1)S(1)}, bf16[464,384]{1,0:T(8,128)(2,1)S(1)}, u32[]{:S(2)}, u32[]{:S(2)}) collective-permute-start(bf16[464,384]{1,0:T(8,128)(2,1)S(1)} %shard_map.160.own), channel_id=1, source_target_pairs={{0,24},{8,16},{16,8},{24,0},{1,25},{9,17},{17,9},{25,1},{2,26},{10... | collective-permute-start | bytes 1069064 | tf_op jit(solution)/shard_map/ppermute | solution.py:35
  140.0 14.9 %collective-permute-start.49 = (bf16[848,384]{1,0:T(8,128)(2,1)S(1)}, bf16[848,384]{1,0:T(8,128)(2,1)S(1)}, u32[]{:S(2)}, u32[]{:S(2)}) collective-permute-start(bf16[848,384]{1,0:T(8,128)(2,1)S(1)} %shard_map.154.refs_1_), channel_id=1, source_target_pairs={{0,8},{8,0},{16,24},{24,16},{1,9},{9,1},{17,25},{25,17},{2,10},{10... | collective-permute-start | bytes 1953800 | tf_op jit(solution)/shard_map/ppermute | solution.py:35
  142.8 13.4 %collective-permute-start.48 = (bf16[848,384]{1,0:T(8,128)(2,1)S(1)}, bf16[848,384]{1,0:T(8,128)(2,1)S(1)}, u32[]{:S(2)}, u32[]{:S(2)}) collective-permute-start(bf16[848,384]{1,0:T(8,128)(2,1)S(1)} %shard_map.151.refs_0_), channel_id=1, source_target_pairs={{0,32},{32,0},{64,96},{96,64},{1,33},{33,1},{65,97},{97,65},{2,34}... | collective-permute-start | bytes 1953800 | tf_op jit(solution)/shard_map/ppermute | solution.py:35
  146.1 13.5 %collective-permute-start.51 = (bf16[848,384]{1,0:T(8,128)(2,1)S(1)}, bf16[848,384]{1,0:T(8,128)(2,1)S(1)}, u32[]{:S(2)}, u32[]{:S(2)}) collective-permute-start(bf16[848,384]{1,0:T(8,128)(2,1)S(1)} %shard_map.164.refs_3_), channel_id=1, source_target_pairs={{0,24},{8,16},{16,8},{24,0},{1,25},{9,17},{17,9},{25,1},{2,26},{10... | collective-permute-start | bytes 1953800 | tf_op jit(solution)/shard_map/ppermute | solution.py:35
  147.6 12.7 %collective-permute-start.50 = (bf16[848,384]{1,0:T(8,128)(2,1)S(1)}, bf16[848,384]{1,0:T(8,128)(2,1)S(1)}, u32[]{:S(2)}, u32[]{:S(2)}) collective-permute-start(bf16[848,384]{1,0:T(8,128)(2,1)S(1)} %shard_map.161.refs_2_), channel_id=1, source_target_pairs={{0,96},{32,64},{64,32},{96,0},{1,97},{33,65},{65,33},{97,1},{2,98}... | collective-permute-start | bytes 1953800 | tf_op jit(solution)/shard_map/ppermute | solution.py:35

commit v4 on v3

--- a/solution.py
+++ b/solution.py
@@ -232,7 +232,7 @@
     )(a, b, wa, wb, kern, gain)
 
 
-def hidden_kernel(ln_ref, up_ref, down_ref, hid_ref, slope_ref):
+def hidden_kernel(ln_ref, up_ref, down_ref, hid_ref, slope_ref, ln_t_ref):
     del down_ref
     half = ln_ref.shape[0] // 2
 
@@ -242,8 +242,11 @@
             part = pl.ds(c, 256)
             pre = jnp.dot(ln_ref[rows, :], up_ref[:, part], preferred_element_type=F32)
             sig = 1.0 / (1.0 + jnp.exp(-pre))
-            hid_ref[rows, part] = (pre * sig).astype(BF)
+            hid_ref[r, part, :] = (pre * sig).astype(BF).T
             slope_ref[rows, part] = 0.5 * sig * (1.0 + pre * (1.0 - sig))
+        for c in range(0, ln_ref.shape[1], 256):
+            part = pl.ds(c, 256)
+            ln_t_ref[r, part, :] = ln_ref[rows, part].T
         return carry
 
     lax.fori_loop(0, 2, block, 0)
@@ -255,8 +258,12 @@
     return pl.pallas_call(
         hidden_kernel,
         in_specs=[WHOLE] * 3,
-        out_specs=[WHOLE] * 2,
-        out_shape=[jax.ShapeDtypeStruct((rows, ff), BF), jax.ShapeDtypeStruct((rows, ff), F32)],
+        out_specs=[WHOLE] * 3,
+        out_shape=[
+            jax.ShapeDtypeStruct((2, ff, rows // 2), BF),
+            jax.ShapeDtypeStruct((rows, ff), F32),
+            jax.ShapeDtypeStruct((2, d_model, rows // 2), BF),
+        ],
         compiler_params=vmem(12),
         cost_estimate=cost(2 * rows * d_model * ff, 10 << 20, rows * ff),
     )(ln, up, down)
@@ -302,15 +309,14 @@
 
 def weight_kernel(k, hid_ref, ca_ref, cb_ref, ln_ref, da_ref, db_ref, keep_ref, send_ref, both):
     y, z = lax.axis_index("dp"), lax.axis_index("context")
-    half = hid_ref.shape[0] // 2
-    cols, wide_cols, ff_cols = pl.ds(384 * k, 384), pl.ds(768 * (k // 2), 768), pl.ds(384 * (k % 2), 384)
-    rows = (((0,), (0,)), ((), ()))
+    half = hid_ref.shape[2]
+    cols, wide, ff_cols = pl.ds(384 * k, 384), pl.ds(768 * (k // 2), 768), pl.ds(384 * (k % 2), 384)
     cot = [ref[:, :, cols].reshape(half, 384) for ref in (ca_ref, cb_ref)]
-    down = lax.dot_general(hid_ref[pl.ds(0, half), :], cot[0], rows, preferred_element_type=F32)
-    down += lax.dot_general(hid_ref[pl.ds(half, half), :], cot[1], rows, preferred_element_type=F32)
+    down = jnp.dot(hid_ref[0], cot[0], preferred_element_type=F32)
+    down += jnp.dot(hid_ref[1], cot[1], preferred_element_type=F32)
     down = (0.5 * down).astype(BF)
-    up = lax.dot_general(ln_ref[pl.ds(0, half), wide_cols], da_ref[:, ff_cols], rows, preferred_element_type=F32)
-    up += lax.dot_general(ln_ref[pl.ds(half, half), wide_cols], db_ref[:, ff_cols], rows, preferred_element_type=F32)
+    up = jnp.dot(ln_ref[0, wide, :], da_ref[:, ff_cols], preferred_element_type=F32)
+    up += jnp.dot(ln_ref[1, wide, :], db_ref[:, ff_cols], preferred_element_type=F32)
     up = up.astype(BF)
     for r in range(16):
         code = piece_code(y, z, r, PARTS[k])
@@ -321,7 +327,7 @@
 
 
 def weight_part(k, hidden, ca, cb, ln, dpre_a, dpre_b):
-    rows = hidden.shape[0]
+    rows = 2 * hidden.shape[2]
     return pl.pallas_call(
         functools.partial(weight_kernel, k),
         in_specs=[WHOLE] * 6,
@@ -362,8 +368,8 @@
 
 def place_rest_kernel(*refs):
     own, rec = refs[:4], refs[4:8]
-    down_ref, up_ref, front_ref, kern_ref, gain_ref, stage, sems = refs[10:]
-    copies = place_pieces(1, rec, down_ref, up_ref, stage, sems)
+    down_ref, up_ref, *small_out = refs[10:15]
+    stage, sems, front_ref, kern_ref, gain_ref, small_sems = refs[15:]
     for k in range(4):
         last = [ref[pl.ds(768, 80), :].astype(F32) for ref in (own[k], rec[k])]
         cols = pl.ds(384 * k, 384)
@@ -371,7 +377,13 @@
         small = (last[0][64:72] + last[0][72:]) + (last[1][64:72] + last[1][72:])
         kern_ref[:, cols] = small[:5]
         gain_ref[cols] = small[5]
+    copies = [
+        pltpu.make_async_copy(src, dst, small_sems.at[i])
+        for i, (src, dst) in enumerate(zip((front_ref, kern_ref, gain_ref), small_out))
+    ]
     for copy in copies:
+        copy.start()
+    for copy in copies + place_pieces(1, rec, down_ref, up_ref, stage, sems):
         copy.wait()
 
 
@@ -391,12 +403,13 @@
     )(*own)
     return pl.pallas_call(
         place_rest_kernel,
-        grid=(1,),
         in_specs=[WHOLE] * 8 + [hbm] * 2,
-        out_specs=[hbm] * 2 + [full(shape) for shape in small],
+        out_specs=[hbm] * 5,
         out_shape=big + [jax.ShapeDtypeStruct(shape, F32) for shape in small],
         input_output_aliases={8: 0, 9: 1},
-        scratch_shapes=scratch,
+        scratch_shapes=scratch
+        + [pltpu.VMEM(shape, F32) for shape in small]
+        + [pltpu.SemaphoreType.DMA((3,))],
         compiler_params=vmem(40),
         cost_estimate=cost(1 << 20, 7 << 20),
     )(*own, *rec, *started)
@@ -506,6 +519,10 @@
     )(*args)
 
 
+def sum_kernel(one, two, three, four, out):
+    out[...] = (one[...] + two[...]) + (three[...] + four[...])
+
+
 def dln_core_kernel(own, rec, keep, send):
     for i in range(4):
         at, to = pl.ds(128 * i, 128), pl.ds(128 * (i // 2), 128)
@@ -613,16 +630,16 @@
     cot = cotangent[0]
 
     picked = select_panels(lengths, jnp.transpose(panels[0, 0], (1, 2, 0)), segments)
-    *picked, front_weight = lax.optimization_barrier((*picked, front_weight))
+    front_weight = after(front_weight, picked[0])
     got = [xor_send(picked[e], "context", e, 4) for e in (2, 1, 3)]
     wa, wb = gather_core(front_weight)
-    block = picked[0] + got[0] + got[1] + got[2]
-    block, cot = lax.optimization_barrier((block, cot))
+    (block,) = glue(sum_kernel, [((640, 128), BF)], picked[0], *got)
+    cot_later = after(cot, block)
     pa, pb = gather_core(block)
-    others = [xor_send(cot, "tensor", m ^ 1, 8) for m in ORDER]
+    others = [xor_send(cot_later, "tensor", m ^ 1, 8) for m in ORDER]
 
     ln, normed, rstd, frames, segs, stack = normalise(pa, pb, wa, wb, conv_kernel, gain_row)
-    hidden, slope = hidden_rows(ln, up_weight, down_weight)
+    hidden, slope, ln_t = hidden_rows(ln, up_weight, down_weight)
     slope, *others = lax.optimization_barrier((slope, *others))
     cb = jnp.stack(others)
     ca = xor_send(cb, "tensor", 1, 8)
@@ -634,7 +651,7 @@
         dln_core_kernel, [((256, 1536), F32), ((256, 1536), BF)], dln_keep, dln_rec
     )
     rec = xor_send(send, "tensor", 2, 8)
-    parts = [weight_part(k, hidden, ca, cb, ln, dpre_a, dpre_b) for k in range(4)]
+    parts = [weight_part(k, hidden, ca, cb, ln_t, dpre_a, dpre_b) for k in range(4)]
     firsts = [over(PARTS[k][0], parts[k][1]) for k in range(4)]
     pairs = [halve_first(parts[0][0], firsts[0])]
     rec = after(rec, pairs[0][1], *[p[0] for p in parts[1:]])

time: 164 us -> 164 us (level)
  waiting for transfers between devices: 47.7 us -> 49.6 us
  other arithmetic: 2.27 us -> 0.38 us
    ppermute x52, waiting for transfers between devices: 47.7 us -> 49.6 us  [xor_send(): return lax.ppermute(value, axis, [(i, i ^ mask) for i in range(size)])]
  transfers between devices with their start and end apart: 52 -> 52, of which waited for: 27 -> 27; matrix products, arithmetic and copies ran while one was open for 1% -> 0% of each run, Pallas kernels for 20% -> 20%
where the time goes in v4:
time: 164 us
  starting transfers between devices  70.7 us (43%)
  waiting for transfers between devices  49.6 us (30%)
  Pallas kernels  40.6 us (25%)
    ppermute x52, starting transfers between devices, xor_send(): return lax.ppermute(value, axis, [(i, i ^ mask) for i in range(size)])  70.7 us
    ppermute x52, waiting for transfers between devices, xor_send(): return lax.ppermute(value, axis, [(i, i ^ mask) for i in range(size)])  49.6 us
    pallas_call x1, Pallas kernels, normalise(): pl.pallas_call(norm_kernel, grid=(4,), in_specs=[WHOLE] * 6, out_specs=[W...  9.46 us
    pallas_call x4, Pallas kernels, weight_part(): pl.pallas_call(functools.partial(weight_kernel, k), in_specs=[WHOLE] * 6,...  7.56 us
    pallas_call x2, Pallas kernels, backward_rows(): pl.pallas_call(functools.partial(backward_kernel, side), in_specs=[WHOLE]...  6.32 us
    pallas_call x1, Pallas kernels, hidden_rows(): pl.pallas_call(hidden_kernel, in_specs=[WHOLE] * 3, out_specs=[WHOLE] * 3...  3.61 us
  transfers between devices with their start and end apart: 52, of which 27 were waited for; matrix products, arithmetic and copies ran while one was open for 0% of the time, Pallas kernels for 20%

profile of v4, /device:TPU:0, one launch (start us, length us, event | category | flops | bytes accessed | tf_op | source)
XLA Modules:
  0.0 163.5 jit_solution(16910241650334394096)
XLA Ops:
  0.6 2.6 %shard_map.128 = (bf16[640,128]{1,0:T(8,128)(2,1)}, bf16[640,128]{1,0:T(8,128)(2,1)}, bf16[640,128]{1,0:T(8,128)(2,1)}, bf16[640,128]{1,0:T(8,128)(2,1)}) custom-call(s32[1,4]{1,0:T(1,128)} %lengths_hbm.1, bf16[32,64,65]{2,1,0:T(8,128)(2,1)} %bitcast.22, s32[1,128]{1,0:T(1,128)} %seg_hbm.1), custom_call_target="tpu_custom_call" | custom-call | flops 42598400 | bytes 2097152 | tf_op jit(solution)/shard_map/pallas_call | solution.py:89
  3.3 4.0 %collective-permute-start = (bf16[640,128]{1,0:T(8,128)(2,1)}, bf16[640,128]{1,0:T(8,128)(2,1)S(1)}, u32[]{:S(2)}, u32[]{:S(2)}) collective-permute-start(bf16[640,128]{1,0:T(8,128)(2,1)} %get-tuple-element.82), channel_id=1, source_target_pairs={{0,16},{8,24},{16,0},{24,8},{1,17},{9,25},{17,1},{25,9},{2,18},{10... | collective-permute-start | bytes 491528 | tf_op jit(solution)/shard_map/ppermute | solution.py:35
  7.3 1.0 collective-permute-start.1
  8.3 3.0 %collective-permute-start.9 = (bf16[64,1536]{1,0:T(8,128)(2,1)}, bf16[64,1536]{1,0:T(8,128)(2,1)S(1)}, u32[]{:S(2)}, u32[]{:S(2)}) collective-permute-start(bf16[64,1536]{1,0:T(8,128)(2,1)} %param.12), channel_id=1, source_target_pairs={{0,4},{1,5},{2,6},{3,7},{4,0},{5,1},{6,2},{7,3},{8,12},{9,13},{10,... | collective-permute-start | bytes 589832 | tf_op jit(solution)/shard_map/ppermute | solution.py:35
  11.3 1.1 collective-permute-start.8
  12.5 1.5 collective-permute-start.7
  14.0 2.0 %collective-permute-done.1.three = bf16[640,128]{1,0:T(8,128)(2,1)S(1)} collective-permute-done((bf16[640,128]{1,0:T(8,128)(2,1)}, bf16[640,128]{1,0:T(8,128)(2,1)S(1)}, u32[]{:S(2)}, u32[]{:S(2)}) %collective-permute-start.1) | collective-permute-done | bytes 163872 | tf_op jit(solution)/shard_map/ppermute | solution.py:35
  16.0 0.9 copy-done.3
  17.0 3.1 %collective-permute-start.5 = (bf16[640,128]{1,0:T(8,128)(2,1)S(1)}, bf16[640,128]{1,0:T(8,128)(2,1)S(1)}, u32[]{:S(2)}, u32[]{:S(2)}) collective-permute-start(bf16[640,128]{1,0:T(8,128)(2,1)S(1)} %shard_map.129), channel_id=1, source_target_pairs={{0,4},{1,5},{2,6},{3,7},{4,0},{5,1},{6,2},{7,3},{8,12},{9,13},{10,... | collective-permute-start | bytes 491528 | tf_op jit(solution)/shard_map/ppermute | solution.py:35
  20.1 1.1 collective-permute-start.4
  21.5 3.2 %collective-permute-done.5 = bf16[640,128]{1,0:T(8,128)(2,1)S(1)} collective-permute-done((bf16[640,128]{1,0:T(8,128)(2,1)S(1)}, bf16[640,128]{1,0:T(8,128)(2,1)S(1)}, u32[]{:S(2)}, u32[]{:S(2)}) %collective-permute-start.5) | collective-permute-done | bytes 163872 | tf_op jit(solution)/shard_map/ppermute | solution.py:35
  24.7 2.9 %collective-permute-done.4 = bf16[640,128]{1,0:T(8,128)(2,1)S(1)} collective-permute-done((bf16[640,128]{1,0:T(8,128)(2,1)S(1)}, bf16[640,128]{1,0:T(8,128)(2,1)S(1)}, u32[]{:S(2)}, u32[]{:S(2)}) %collective-permute-start.4) | collective-permute-done | bytes 163872 | tf_op jit(solution)/shard_map/ppermute | solution.py:35
  27.9 2.1 %collective-permute-start.14 = (bf16[128,1536]{1,0:T(8,128)(2,1)S(1)}, bf16[128,1536]{1,0:T(8,128)(2,1)S(1)}, u32[]{:S(2)}, u32[]{:S(2)}) collective-permute-start(bf16[128,1536]{1,0:T(8,128)(2,1)S(1)} %bitcast.17), channel_id=1, source_target_pairs={{0,5},{1,4},{2,7},{3,6},{4,1},{5,0},{6,3},{7,2},{8,13},{9,12},{10,... | collective-permute-start | bytes 1179656 | tf_op jit(solution)/shard_map/ppermute | solution.py:35
  30.0 1.7 %collective-permute-start.13 = (bf16[128,1536]{1,0:T(8,128)(2,1)S(1)}, bf16[128,1536]{1,0:T(8,128)(2,1)S(1)}, u32[]{:S(2)}, u32[]{:S(2)}) collective-permute-start(bf16[128,1536]{1,0:T(8,128)(2,1)S(1)} %bitcast.18), channel_id=1, source_target_pairs={{0,7},{1,6},{2,5},{3,4},{4,3},{5,2},{6,1},{7,0},{8,15},{9,14},{10,... | collective-permute-start | bytes 1179656 | tf_op jit(solution)/shard_map/ppermute | solution.py:35
  32.2 9.5 %shard_map.130 = (bf16[1024,1536]{1,0:T(8,128)(2,1)S(1)}, f32[128,1536]{1,0:T(8,128)S(1)}, f32[128,128]{1,0:T(8,128)S(1)}, f32[160,1536]{1,0:T(8,128)S(1)}, f32[...) custom-call(bf16[4,640,128]{2,1,0:T(8,128)(2,1)S(1)} %pad_maximum_fusion.2.a_ref, ...), custom_call_target="tpu_custom_call" | custom-call | flops 12000000000 | bytes 10485760 | tf_op jit(solution)/shard_map/pallas_call | solution.py:206
  41.7 3.6 %shard_map.131 = (bf16[2,768,512]{2,1,0:T(8,128)(2,1)S(1)}, f32[1024,768]{1,0:T(8,128)S(1)}, bf16[2,1536,512]{2,1,0:T(8,128)(2,1)S(1)}) custom-call(bf16[1024,1536]{1,0:T(8,128)(2,1)S(1)} %get-tuple-element.86.ln_ref, bf16[1536,768]{1,0:T(8,128)(2,1)S(1)} %copy-done, bf16[768,1536]{1,0:T(8,128)(2,1)S(1)} %copy-done.1), custom_call_target="tpu_custom_call" | custom-call | flops 2415919104 | bytes 10485760 | tf_op jit(solution)/shard_map/pallas_call | solution.py:258
  45.3 4.0 %collective-permute-done.13 = bf16[128,1536]{1,0:T(8,128)(2,1)S(1)} collective-permute-done((bf16[128,1536]{1,0:T(8,128)(2,1)S(1)}, bf16[128,1536]{1,0:T(8,128)(2,1)S(1)}, u32[]{:S(2)}, u32[]{:S(2)}) %collective-permute-start.13) | collective-permute-done | bytes 393248 | tf_op jit(solution)/shard_map/ppermute | solution.py:35
  49.9 3.2 %shard_map.133 = (bf16[512,768]{1,0:T(8,128)(2,1)S(1)}, bf16[512,1536]{1,0:T(8,128)(2,1)S(1)}) custom-call(bf16[4,128,1536]{2,1,0:T(8,128)(2,1)S(1)} %pad_maximum_fusion.cot_ref.cb_ref, f32[1024,768]{1,0:T(8,128)S(1)} %get-tuple-element.95.slope_ref, bf16[1536,768]{1,0:T(8,128)(2,1)S(1)} %copy-done, bf16[768,1536]{1,0:T(8,128)(2,1)S(1)} %copy-done.1), custom_call_target="tpu_custom_call" | custom-call | flops 2415919104 | bytes 10485760 | tf_op jit(solution)/shard_map/pallas_call | solution.py:288
  53.5 3.2 %shard_map.132 = (bf16[512,768]{1,0:T(8,128)(2,1)S(1)}, bf16[512,1536]{1,0:T(8,128)(2,1)S(1)}) custom-call(bf16[4,128,1536]{2,1,0:T(8,128)(2,1)S(1)} %collective-permute-done.15.cot_ref.ca_ref, f32[1024,768]{1,0:T(8,128)S(1)} %get-tuple-element.95.slope_ref, bf16[1536,768]{1,0:T(8,128)(2,1)S(1)} %copy-done, bf16[768,1536]{1,0:T(8,128)(2,1)S(1)} %copy-done.1), custom_call_target="tpu_custom_call" | custom-call | flops 2415919104 | bytes 10485760 | tf_op jit(solution)/shard_map/pallas_call | solution.py:288
  56.7 1.9 %shard_map.134 = (bf16[8,96,384]{2,1,0:T(8,128)(2,1)S(1)}, bf16[8,96,384]{2,1,0:T(8,128)(2,1)S(1)}) custom-call(bf16[2,768,512]{2,1,0:T(8,128)(2,1)S(1)} %get-tuple-element.87.hid_ref, bf16[4,128,1536]{2,1,0:T(8,128)(2,1)S(1)} %collective-permute-done.15.cot_ref.ca_ref, bf16[4,128,1536]{2,1,0:T(8,128)(2,1)S(1)} %pad_maximum_fusion.cot_ref.cb_ref, ...), custom_call_target="tpu_custom_call" | custom-call | flops 1207959552 | bytes 7340032 | tf_op jit(solution)/shard_map/pallas_call | solution.py:331
  58.6 1.6 %collective-permute-start.16 = (bf16[8,96,384]{2,1,0:T(8,128)(2,1)S(1)}, bf16[8,96,384]{2,1,0:T(8,128)(2,1)S(1)}, u32[]{:S(2)}, u32[]{:S(2)}) collective-permute-start(bf16[8,96,384]{2,1,0:T(8,128)(2,1)S(1)} %get-tuple-element.99), channel_id=1, source_target_pairs={{0,32},{32,0},{64,96},{96,64},{1,33},{33,1},{65,97},{97,65},{2,34}... | collective-permute-start | bytes 1769480 | tf_op jit(solution)/shard_map/ppermute | solution.py:35
  60.6 1.4 collective-permute-start.23
  62.0 1.9 %shard_map.136 = (bf16[8,96,384]{2,1,0:T(8,128)(2,1)S(1)}, bf16[8,96,384]{2,1,0:T(8,128)(2,1)S(1)}) custom-call(bf16[2,768,512]{2,1,0:T(8,128)(2,1)S(1)} %get-tuple-element.87.hid_ref, bf16[4,128,1536]{2,1,0:T(8,128)(2,1)S(1)} %collective-permute-done.15.cot_ref.ca_ref, bf16[4,128,1536]{2,1,0:T(8,128)(2,1)S(1)} %pad_maximum_fusion.cot_ref.cb_ref, ...), custom_call_target="tpu_custom_call" | custom-call | flops 1207959552 | bytes 7340032 | tf_op jit(solution)/shard_map/pallas_call | solution.py:331
  63.9 1.1 collective-permute-start.18
  65.0 1.9 %shard_map.142 = (bf16[8,96,384]{2,1,0:T(8,128)(2,1)S(1)}, bf16[8,96,384]{2,1,0:T(8,128)(2,1)S(1)}) custom-call(bf16[2,768,512]{2,1,0:T(8,128)(2,1)S(1)} %get-tuple-element.87.hid_ref, bf16[4,128,1536]{2,1,0:T(8,128)(2,1)S(1)} %collective-permute-done.15.cot_ref.ca_ref, bf16[4,128,1536]{2,1,0:T(8,128)(2,1)S(1)} %pad_maximum_fusion.cot_ref.cb_ref, ...), custom_call_target="tpu_custom_call" | custom-call | flops 1207959552 | bytes 7340032 | tf_op jit(solution)/shard_map/pallas_call | solution.py:331
  66.9 2.9 %collective-permute-start.27 = (bf16[8,96,384]{2,1,0:T(8,128)(2,1)S(1)}, bf16[8,96,384]{2,1,0:T(8,128)(2,1)S(1)}, u32[]{:S(2)}, u32[]{:S(2)}) collective-permute-start(bf16[8,96,384]{2,1,0:T(8,128)(2,1)S(1)} %get-tuple-element.122), channel_id=1, source_target_pairs={{0,24},{8,16},{16,8},{24,0},{1,25},{9,17},{17,9},{25,1},{2,26},{10... | collective-permute-start | bytes 1769480 | tf_op jit(solution)/shard_map/ppermute | solution.py:35
  69.8 1.9 %shard_map.141 = (bf16[8,96,384]{2,1,0:T(8,128)(2,1)S(1)}, bf16[8,96,384]{2,1,0:T(8,128)(2,1)S(1)}) custom-call(bf16[2,768,512]{2,1,0:T(8,128)(2,1)S(1)} %get-tuple-element.87.hid_ref, bf16[4,128,1536]{2,1,0:T(8,128)(2,1)S(1)} %collective-permute-done.15.cot_ref.ca_ref, bf16[4,128,1536]{2,1,0:T(8,128)(2,1)S(1)} %pad_maximum_fusion.cot_ref.cb_ref, ...), custom_call_target="tpu_custom_call" | custom-call | flops 1207959552 | bytes 7340032 | tf_op jit(solution)/shard_map/pallas_call | solution.py:331
  71.7 2.3 %collective-permute-start.25 = (bf16[8,96,384]{2,1,0:T(8,128)(2,1)S(1)}, bf16[8,96,384]{2,1,0:T(8,128)(2,1)S(1)}, u32[]{:S(2)}, u32[]{:S(2)}) collective-permute-start(bf16[8,96,384]{2,1,0:T(8,128)(2,1)S(1)} %get-tuple-element.120), channel_id=1, source_target_pairs={{0,96},{32,64},{64,32},{96,0},{1,97},{33,65},{65,33},{97,1},{2,98}... | collective-permute-start | bytes 1769480 | tf_op jit(solution)/shard_map/ppermute | solution.py:35
  74.2 4.6 %collective-permute-done.18.rec = bf16[8,96,384]{2,1,0:T(8,128)(2,1)S(1)} collective-permute-done((bf16[8,96,384]{2,1,0:T(8,128)(2,1)S(1)}, bf16[8,96,384]{2,1,0:T(8,128)(2,1)S(1)}, u32[]{:S(2)}, u32[]{:S(2)}) %collective-permute-start.18) | collective-permute-done | bytes 589856 | tf_op jit(solution)/shard_map/ppermute | solution.py:35
  78.9 1.1 collective-permute-done.23.rec
  80.1 2.6 %collective-permute-start.24 = (bf16[128,1536]{1,0:T(8,128)(2,1)S(1)}, bf16[128,1536]{1,0:T(8,128)(2,1)S(1)}, u32[]{:S(2)}, u32[]{:S(2)}) collective-permute-start(bf16[128,1536]{1,0:T(8,128)(2,1)S(1)} %get-tuple-element.119), channel_id=1, source_target_pairs={{0,6},{1,7},{2,4},{3,5},{4,2},{5,3},{6,0},{7,1},{8,14},{9,15},{10,... | collective-permute-start | bytes 1179656 | tf_op jit(solution)/shard_map/ppermute | solution.py:35
  82.6 1.0 collective-permute-start.17
  84.2 3.1 %collective-permute-start.28 = (bf16[4,96,384]{2,1,0:T(8,128)(2,1)S(1)}, bf16[4,96,384]{2,1,0:T(8,128)(2,1)S(1)}, u32[]{:S(2)}, u32[]{:S(2)}) collective-permute-start(bf16[4,96,384]{2,1,0:T(8,128)(2,1)S(1)} %get-tuple-element.123), channel_id=1, source_target_pairs={{0,96},{32,64},{64,32},{96,0},{1,97},{33,65},{65,33},{97,1},{2,98}... | collective-permute-start | bytes 884744 | tf_op jit(solution)/shard_map/ppermute | solution.py:35
  88.2 2.2 %collective-permute-start.26 = (bf16[4,96,384]{2,1,0:T(8,128)(2,1)S(1)}, bf16[4,96,384]{2,1,0:T(8,128)(2,1)S(1)}, u32[]{:S(2)}, u32[]{:S(2)}) collective-permute-start(bf16[4,96,384]{2,1,0:T(8,128)(2,1)S(1)} %get-tuple-element.121), channel_id=1, source_target_pairs={{0,24},{8,16},{16,8},{24,0},{1,25},{9,17},{17,9},{25,1},{2,26},{10... | collective-permute-start | bytes 884744 | tf_op jit(solution)/shard_map/ppermute | solution.py:35
  91.1 2.5 %collective-permute-done.28.rec1 = bf16[4,96,384]{2,1,0:T(8,128)(2,1)S(1)} collective-permute-done((bf16[4,96,384]{2,1,0:T(8,128)(2,1)S(1)}, bf16[4,96,384]{2,1,0:T(8,128)(2,1)S(1)}, u32[]{:S(2)}, u32[]{:S(2)}) %collective-permute-start.28) | collective-permute-done | bytes 294944 | tf_op jit(solution)/shard_map/ppermute | solution.py:35
  93.5 2.7 %collective-permute-done.26.rec0 = bf16[4,96,384]{2,1,0:T(8,128)(2,1)S(1)} collective-permute-done((bf16[4,96,384]{2,1,0:T(8,128)(2,1)S(1)}, bf16[4,96,384]{2,1,0:T(8,128)(2,1)S(1)}, u32[]{:S(2)}, u32[]{:S(2)}) %collective-permute-start.26) | collective-permute-done | bytes 294944 | tf_op jit(solution)/shard_map/ppermute | solution.py:35
  96.2 2.9 %shard_map.146 = (f32[272,1536]{1,0:T(8,128)S(1)}, bf16[272,1536]{1,0:T(8,128)(2,1)S(1)}) custom-call(f32[128,1536]{1,0:T(8,128)S(1)} %get-tuple-element.117.dln_ref, bf16[128,1536]{1,0:T(8,128)(2,1)S(1)} %collective-permute-done.24.rec_ref, f32[128,1536]{1,0:T(8,128)S(1)} %get-tuple-element.125.normed_ref, f32[128,128]{1,0:T(8,128)S(1)} %get-tuple-element.126.rstd_ref, ...), custom_call_target="tpu_custom_call" | custom-call | flops 60000002048 | bytes 6291456 | tf_op jit(solution)/shard_map/pallas_call | solution.py:485
  99.2 1.7 %collective-permute-start.20 = (bf16[2,192,384]{2,1,0:T(8,128)(2,1)S(1)}, bf16[2,192,384]{2,1,0:T(8,128)(2,1)S(1)}, u32[]{:S(2)}, u32[]{:S(2)}) collective-permute-start(bf16[2,192,384]{2,1,0:T(8,128)(2,1)S(1)} %get-tuple-element.107), channel_id=1, source_target_pairs={{0,96},{32,64},{64,32},{96,0},{1,97},{33,65},{65,33},{97,1},{2,98}... | collective-permute-start | bytes 884744 | tf_op jit(solution)/shard_map/ppermute | solution.py:35
  101.8 2.0 %collective-permute-start.30 = (bf16[144,768]{1,0:T(8,128)(2,1)S(1)}, bf16[144,768]{1,0:T(8,128)(2,1)S(1)}, u32[]{:S(2)}, u32[]{:S(2)}) collective-permute-start(bf16[144,768]{1,0:T(8,128)(2,1)S(1)} %get-tuple-element.133), channel_id=1, source_target_pairs={{0,2},{1,3},{2,0},{3,1},{4,6},{5,7},{6,4},{7,5},{8,10},{9,11},{10,... | collective-permute-start | bytes 663560 | tf_op jit(solution)/shard_map/ppermute | solution.py:35
  103.8 2.4 %collective-permute-start.40 = (bf16[144,768]{1,0:T(8,128)(2,1)S(1)}, bf16[144,768]{1,0:T(8,128)(2,1)S(1)}, u32[]{:S(2)}, u32[]{:S(2)}) collective-permute-start(bf16[144,768]{1,0:T(8,128)(2,1)S(1)} %get-tuple-element.145), channel_id=1, source_target_pairs={{0,6},{1,7},{2,4},{3,5},{4,2},{5,3},{6,0},{7,1},{8,14},{9,15},{10,... | collective-permute-start | bytes 663560 | tf_op jit(solution)/shard_map/ppermute | solution.py:35
  106.2 3.6 %collective-permute-done.20.rec = bf16[2,192,384]{2,1,0:T(8,128)(2,1)S(1)} collective-permute-done((bf16[2,192,384]{2,1,0:T(8,128)(2,1)S(1)}, bf16[2,192,384]{2,1,0:T(8,128)(2,1)S(1)}, u32[]{:S(2)}, u32[]{:S(2)}) %collective-permute-start.20) | collective-permute-done | bytes 294944 | tf_op jit(solution)/shard_map/ppermute | solution.py:35
  109.9 2.3 %collective-permute-start.21 = (bf16[1,192,384]{2,1,0:T(8,128)(2,1)S(1)}, bf16[1,192,384]{2,1,0:T(8,128)(2,1)S(1)}, u32[]{:S(2)}, u32[]{:S(2)}) collective-permute-start(bf16[1,192,384]{2,1,0:T(8,128)(2,1)S(1)} %get-tuple-element.109), channel_id=1, source_target_pairs={{0,24},{8,16},{16,8},{24,0},{1,25},{9,17},{17,9},{25,1},{2,26},{10... | collective-permute-start | bytes 442376 | tf_op jit(solution)/shard_map/ppermute | solution.py:35
  112.2 1.1 collective-permute-start.31
  114.2 2.3 %collective-permute-done.21.rec = bf16[1,192,384]{2,1,0:T(8,128)(2,1)S(1)} collective-permute-done((bf16[1,192,384]{2,1,0:T(8,128)(2,1)S(1)}, bf16[1,192,384]{2,1,0:T(8,128)(2,1)S(1)}, u32[]{:S(2)}, u32[]{:S(2)}) %collective-permute-start.21) | collective-permute-done | bytes 147488 | tf_op jit(solution)/shard_map/ppermute | solution.py:35
  116.6 1.8 %collective-permute-done.31.front_rec = bf16[80,768]{1,0:T(8,128)(2,1)S(1)} collective-permute-done((bf16[80,768]{1,0:T(8,128)(2,1)S(1)}, bf16[80,768]{1,0:T(8,128)(2,1)S(1)}, u32[]{:S(2)}, u32[]{:S(2)}) %collective-permute-start.31) | collective-permute-done | bytes 122912 | tf_op jit(solution)/shard_map/ppermute | solution.py:35
  118.5 1.1 collective-permute-start.32
  119.7 1.7 %collective-permute-start.45 = (bf16[176,384]{1,0:T(8,128)(2,1)S(1)}, bf16[176,384]{1,0:T(8,128)(2,1)S(1)}, u32[]{:S(2)}, u32[]{:S(2)}) collective-permute-start(bf16[176,384]{1,0:T(8,128)(2,1)S(1)} %get-tuple-element.149.own), channel_id=1, source_target_pairs={{0,96},{32,64},{64,32},{96,0},{1,97},{33,65},{65,33},{97,1},{2,98}... | collective-permute-start | bytes 405512 | tf_op jit(solution)/shard_map/ppermute | solution.py:35
  121.4 2.1 %collective-permute-done.35.rec = bf16[176,384]{1,0:T(8,128)(2,1)S(1)} collective-permute-done((bf16[176,384]{1,0:T(8,128)(2,1)S(1)}, bf16[176,384]{1,0:T(8,128)(2,1)S(1)}, u32[]{:S(2)}, u32[]{:S(2)}) %collective-permute-start.35) | collective-permute-done | bytes 135200 | tf_op jit(solution)/shard_map/ppermute | solution.py:35
  123.6 1.1 collective-permute-start.36
  125.1 1.3 collective-permute-start.33
  126.5 1.8 %collective-permute-start.46 = (bf16[272,384]{1,0:T(8,128)(2,1)S(1)}, bf16[272,384]{1,0:T(8,128)(2,1)S(1)}, u32[]{:S(2)}, u32[]{:S(2)}) collective-permute-start(bf16[272,384]{1,0:T(8,128)(2,1)S(1)} %shard_map.163.own), channel_id=1, source_target_pairs={{0,8},{8,0},{16,24},{24,16},{1,9},{9,1},{17,25},{25,17},{2,10},{10... | collective-permute-start | bytes 626696 | tf_op jit(solution)/shard_map/ppermute | solution.py:35
  129.1 1.6 collective-permute-done.36.rec
  131.3 2.2 %collective-permute-done.33.rec = bf16[272,384]{1,0:T(8,128)(2,1)S(1)} collective-permute-done((bf16[272,384]{1,0:T(8,128)(2,1)S(1)}, bf16[272,384]{1,0:T(8,128)(2,1)S(1)}, u32[]{:S(2)}, u32[]{:S(2)}) %collective-permute-start.33) | collective-permute-done | bytes 208928 | tf_op jit(solution)/shard_map/ppermute | solution.py:35
  134.0 2.6 %collective-permute-start.47 = (bf16[464,384]{1,0:T(8,128)(2,1)S(1)}, bf16[464,384]{1,0:T(8,128)(2,1)S(1)}, u32[]{:S(2)}, u32[]{:S(2)}) collective-permute-start(bf16[464,384]{1,0:T(8,128)(2,1)S(1)} %shard_map.164.own), channel_id=1, source_target_pairs={{0,32},{32,0},{64,96},{96,64},{1,33},{33,1},{65,97},{97,65},{2,34}... | collective-permute-start | bytes 1069064 | tf_op jit(solution)/shard_map/ppermute | solution.py:35
  136.7 2.2 %collective-permute-start.44 = (bf16[464,384]{1,0:T(8,128)(2,1)S(1)}, bf16[464,384]{1,0:T(8,128)(2,1)S(1)}, u32[]{:S(2)}, u32[]{:S(2)}) collective-permute-start(bf16[464,384]{1,0:T(8,128)(2,1)S(1)} %shard_map.161.own), channel_id=1, source_target_pairs={{0,24},{8,16},{16,8},{24,0},{1,25},{9,17},{17,9},{25,1},{2,26},{10... | collective-permute-start | bytes 1069064 | tf_op jit(solution)/shard_map/ppermute | solution.py:35
  138.8 1.0 collective-permute-done.37.rec
  140.0 2.8 %collective-permute-done.34.rec = bf16[464,384]{1,0:T(8,128)(2,1)S(1)} collective-permute-done((bf16[464,384]{1,0:T(8,128)(2,1)S(1)}, bf16[464,384]{1,0:T(8,128)(2,1)S(1)}, u32[]{:S(2)}, u32[]{:S(2)}) %collective-permute-start.34) | collective-permute-done | bytes 356384 | tf_op jit(solution)/shard_map/ppermute | solution.py:35
  142.9 3.1 %collective-permute-start.48 = (bf16[848,384]{1,0:T(8,128)(2,1)S(1)}, bf16[848,384]{1,0:T(8,128)(2,1)S(1)}, u32[]{:S(2)}, u32[]{:S(2)}) collective-permute-start(bf16[848,384]{1,0:T(8,128)(2,1)S(1)} %shard_map.152.refs_0_), channel_id=1, source_target_pairs={{0,32},{32,0},{64,96},{96,64},{1,33},{33,1},{65,97},{97,65},{2,34}... | collective-permute-start | bytes 1953800 | tf_op jit(solution)/shard_map/ppermute | solution.py:35
  146.7 1.0 collective-permute-done.44.rec
  147.7 4.1 %collective-permute-start.50 = (bf16[848,384]{1,0:T(8,128)(2,1)S(1)}, bf16[848,384]{1,0:T(8,128)(2,1)S(1)}, u32[]{:S(2)}, u32[]{:S(2)}) collective-permute-start(bf16[848,384]{1,0:T(8,128)(2,1)S(1)} %shard_map.162.refs_2_), channel_id=1, source_target_pairs={{0,96},{32,64},{64,32},{96,0},{1,97},{33,65},{65,33},{97,1},{2,98}... | collective-permute-start | bytes 1953800 | tf_op jit(solution)/shard_map/ppermute | solution.py:35
  151.8 2.8 %shard_map.166 = (f32[768,1536]{1,0:T(8,128)}, f32[1536,768]{1,0:T(8,128)}) custom-call(bf16[848,384]{1,0:T(8,128)(2,1)S(1)} %shard_map.152.refs_0_, bf16[848,384]{1,0:T(8,128)(2,1)S(1)} %shard_map.155.refs_1_, bf16[848,384]{1,0:T(8,128)(2,1)S(1)} %shard_map.162.refs_2_, bf16[848,384]{1,0:T(8,128)(2,1)S(1)} %shard_map.165.refs_3_), custom_call_target="tpu_custom_call" | custom-call | flops 1048576 | bytes 7340032 | tf_op jit(solution)/shard_map/pallas_call | solution.py:395
  155.9 3.4 %collective-permute-done.51.refs_7_ = bf16[848,384]{1,0:T(8,128)(2,1)S(1)} collective-permute-done((bf16[848,384]{1,0:T(8,128)(2,1)S(1)}, bf16[848,384]{1,0:T(8,128)(2,1)S(1)}, u32[]{:S(2)}, u32[]{:S(2)}) %collective-permute-start.51) | collective-permute-done | bytes 651296 | tf_op jit(solution)/shard_map/ppermute | solution.py:35
  159.3 1.0 collective-permute-done.50.refs_6_
  160.3 3.0 %shard_map.167 = (f32[768,1536]{1,0:T(8,128)}, f32[1536,768]{1,0:T(8,128)}, f32[64,1536]{1,0:T(8,128)}, f32[5,1536]{1,0:T(8,128)}, f32[1536]{0:T(1024)}) custom-call(bf16[848,384]{1,0:T(8,128)(2,1)S(1)} %shard_map.152.refs_0_, bf16[848,384]{1,0:T(8,128)(2,1)S(1)} %shard_map.155.refs_1_, ...), custom_call_target="tpu_custom_call", output_to_operand_aliasing={{0}: (8, {}), {1}: (9, {})} | custom-call | flops 1048576 | bytes 7340032 | tf_op jit(solution)/shard_map/pallas_call | solution.py:404
  (98 shorter events, 11.8 us)
Async XLA Ops:
  0.6 20.7 %copy-start.5 = (bf16[64,1536]{1,0:T(8,128)(2,1)S(1)}, bf16[64,1536]{1,0:T(8,128)(2,1)}, u32[]{:S(2)}) copy-start(bf16[64,1536]{1,0:T(8,128)(2,1)} %param.12) | copy-start | bytes 589828
  3.3 9.3 %collective-permute-start = (bf16[640,128]{1,0:T(8,128)(2,1)}, bf16[640,128]{1,0:T(8,128)(2,1)S(1)}, u32[]{:S(2)}, u32[]{:S(2)}) collective-permute-start(bf16[640,128]{1,0:T(8,128)(2,1)} %get-tuple-element.82), channel_id=1, source_target_pairs={{0,16},{8,24},{16,0},{24,8},{1,17},{9,25},{17,1},{25,9},{2,18},{10... | collective-permute-start | bytes 491528 | tf_op jit(solution)/shard_map/ppermute | solution.py:35
  7.3 8.7 %collective-permute-start.1 = (bf16[640,128]{1,0:T(8,128)(2,1)}, bf16[640,128]{1,0:T(8,128)(2,1)S(1)}, u32[]{:S(2)}, u32[]{:S(2)}) collective-permute-start(bf16[640,128]{1,0:T(8,128)(2,1)} %get-tuple-element.83), channel_id=1, source_target_pairs={{0,8},{8,0},{16,24},{24,16},{1,9},{9,1},{17,25},{25,17},{2,10},{10... | collective-permute-start | bytes 491528 | tf_op jit(solution)/shard_map/ppermute | solution.py:35
  8.3 7.7 %collective-permute-start.2 = (bf16[640,128]{1,0:T(8,128)(2,1)}, bf16[640,128]{1,0:T(8,128)(2,1)S(1)}, u32[]{:S(2)}, u32[]{:S(2)}) collective-permute-start(bf16[640,128]{1,0:T(8,128)(2,1)} %get-tuple-element.84), channel_id=1, source_target_pairs={{0,24},{8,16},{16,8},{24,0},{1,25},{9,17},{17,9},{25,1},{2,26},{10... | collective-permute-start | bytes 491528 | tf_op jit(solution)/shard_map/ppermute | solution.py:35
  8.3 12.9 %collective-permute-start.9 = (bf16[64,1536]{1,0:T(8,128)(2,1)}, bf16[64,1536]{1,0:T(8,128)(2,1)S(1)}, u32[]{:S(2)}, u32[]{:S(2)}) collective-permute-start(bf16[64,1536]{1,0:T(8,128)(2,1)} %param.12), channel_id=1, source_target_pairs={{0,4},{1,5},{2,6},{3,7},{4,0},{5,1},{6,2},{7,3},{8,12},{9,13},{10,... | collective-permute-start | bytes 589832 | tf_op jit(solution)/shard_map/ppermute | solution.py:35
  11.3 9.9 %collective-permute-start.8 = (bf16[64,1536]{1,0:T(8,128)(2,1)}, bf16[64,1536]{1,0:T(8,128)(2,1)S(1)}, u32[]{:S(2)}, u32[]{:S(2)}) collective-permute-start(bf16[64,1536]{1,0:T(8,128)(2,1)} %param.12), channel_id=1, source_target_pairs={{0,6},{1,7},{2,4},{3,5},{4,2},{5,3},{6,0},{7,1},{8,14},{9,15},{10,... | collective-permute-start | bytes 589832 | tf_op jit(solution)/shard_map/ppermute | solution.py:35
  12.5 8.7 %collective-permute-start.7 = (bf16[64,1536]{1,0:T(8,128)(2,1)}, bf16[64,1536]{1,0:T(8,128)(2,1)S(1)}, u32[]{:S(2)}, u32[]{:S(2)}) collective-permute-start(bf16[64,1536]{1,0:T(8,128)(2,1)} %param.12), channel_id=1, source_target_pairs={{0,2},{1,3},{2,0},{3,1},{4,6},{5,7},{6,4},{7,5},{8,10},{9,11},{10,... | collective-permute-start | bytes 589832 | tf_op jit(solution)/shard_map/ppermute | solution.py:35
  16.0 0.9 copy-start.3
  17.0 10.8 %copy-start.6 = (f32[1536]{0:T(1024)S(1)}, f32[1536]{0:T(1024)}, u32[]{:S(2)}) copy-start(f32[1536]{0:T(1024)} %param.14) | copy-start | bytes 18436
  17.0 10.9 %copy-start.2 = (bf16[1,128,1536]{2,1,0:T(8,128)(2,1)S(1)}, bf16[1,128,1536]{2,1,0:T(8,128)(2,1)}, u32[]{:S(2)}) copy-start(bf16[1,128,1536]{2,1,0:T(8,128)(2,1)} %param.17) | copy-start | bytes 1179652
  17.0 15.2 %copy-start.4 = (f32[5,1536]{1,0:T(8,128)S(1)}, f32[5,1536]{1,0:T(8,128)}, u32[]{:S(2)}) copy-start(f32[5,1536]{1,0:T(8,128)} %kern_ref.3) | copy-start | bytes 92164
  17.0 7.7 %collective-permute-start.5 = (bf16[640,128]{1,0:T(8,128)(2,1)S(1)}, bf16[640,128]{1,0:T(8,128)(2,1)S(1)}, u32[]{:S(2)}, u32[]{:S(2)}) collective-permute-start(bf16[640,128]{1,0:T(8,128)(2,1)S(1)} %shard_map.129), channel_id=1, source_target_pairs={{0,4},{1,5},{2,6},{3,7},{4,0},{5,1},{6,2},{7,3},{8,12},{9,13},{10,... | collective-permute-start | bytes 491528 | tf_op jit(solution)/shard_map/ppermute | solution.py:35
  20.1 7.5 %collective-permute-start.4 = (bf16[640,128]{1,0:T(8,128)(2,1)S(1)}, bf16[640,128]{1,0:T(8,128)(2,1)S(1)}, u32[]{:S(2)}, u32[]{:S(2)}) collective-permute-start(bf16[640,128]{1,0:T(8,128)(2,1)S(1)} %shard_map.129), channel_id=1, source_target_pairs={{0,6},{1,7},{2,4},{3,5},{4,2},{5,3},{6,0},{7,1},{8,14},{9,15},{10,... | collective-permute-start | bytes 491528 | tf_op jit(solution)/shard_map/ppermute | solution.py:35
  21.3 6.4 %collective-permute-start.3 = (bf16[640,128]{1,0:T(8,128)(2,1)S(1)}, bf16[640,128]{1,0:T(8,128)(2,1)S(1)}, u32[]{:S(2)}, u32[]{:S(2)}) collective-permute-start(bf16[640,128]{1,0:T(8,128)(2,1)S(1)} %shard_map.129), channel_id=1, source_target_pairs={{0,2},{1,3},{2,0},{3,1},{4,6},{5,7},{6,4},{7,5},{8,10},{9,11},{10,... | collective-permute-start | bytes 491528 | tf_op jit(solution)/shard_map/ppermute | solution.py:35
  21.4 10.8 %collective-permute-start.10 = (bf16[4,64,1536]{2,1,0:T(8,128)(2,1)S(1)}, bf16[4,64,1536]{2,1,0:T(8,128)(2,1)S(1)}, u32[]{:S(2)}, u32[]{:S(2)}) collective-permute-start(bf16[4,64,1536]{2,1,0:T(8,128)(2,1)S(1)} %pad_maximum_fusion.1.wa_ref), channel_id=1, source_target_pairs={{0,1},{1,0},{2,3},{3,2},{4,5},{5,4},{6,7},{7,6},{8,9},{9,8},{10,11... | collective-permute-start | bytes 2359304 | tf_op jit(solution)/shard_map/ppermute | solution.py:35
  27.7 3.9 %collective-permute-start.6 = (bf16[4,640,128]{2,1,0:T(8,128)(2,1)S(1)}, bf16[4,640,128]{2,1,0:T(8,128)(2,1)S(1)}, u32[]{:S(2)}, u32[]{:S(2)}) collective-permute-start(bf16[4,640,128]{2,1,0:T(8,128)(2,1)S(1)} %pad_maximum_fusion.2.a_ref), channel_id=1, source_target_pairs={{0,1},{1,0},{2,3},{3,2},{4,5},{5,4},{6,7},{7,6},{8,9},{9,8},{10,11... | collective-permute-start | bytes 1966088 | tf_op jit(solution)/shard_map/ppermute | solution.py:35
  27.9 13.8 %copy-start = (bf16[1536,768]{1,0:T(8,128)(2,1)S(1)}, bf16[1536,768]{1,0:T(8,128)(2,1)}, u32[]{:S(2)}) copy-start(bf16[1536,768]{1,0:T(8,128)(2,1)} %up_ref.5) | copy-start | bytes 7077892
  27.9 13.8 %copy-start.1 = (bf16[768,1536]{1,0:T(8,128)(2,1)S(1)}, bf16[768,1536]{1,0:T(8,128)(2,1)}, u32[]{:S(2)}) copy-start(bf16[768,1536]{1,0:T(8,128)(2,1)} %down_ref.5) | copy-start | bytes 7077892
  27.9 17.4 %collective-permute-start.14 = (bf16[128,1536]{1,0:T(8,128)(2,1)S(1)}, bf16[128,1536]{1,0:T(8,128)(2,1)S(1)}, u32[]{:S(2)}, u32[]{:S(2)}) collective-permute-start(bf16[128,1536]{1,0:T(8,128)(2,1)S(1)} %bitcast.17), channel_id=1, source_target_pairs={{0,5},{1,4},{2,7},{3,6},{4,1},{5,0},{6,3},{7,2},{8,13},{9,12},{10,... | collective-permute-start | bytes 1179656 | tf_op jit(solution)/shard_map/ppermute | solution.py:35
  30.0 19.3 %collective-permute-start.13 = (bf16[128,1536]{1,0:T(8,128)(2,1)S(1)}, bf16[128,1536]{1,0:T(8,128)(2,1)S(1)}, u32[]{:S(2)}, u32[]{:S(2)}) collective-permute-start(bf16[128,1536]{1,0:T(8,128)(2,1)S(1)} %bitcast.18), channel_id=1, source_target_pairs={{0,7},{1,6},{2,5},{3,4},{4,3},{5,2},{6,1},{7,0},{8,15},{9,14},{10,... | collective-permute-start | bytes 1179656 | tf_op jit(solution)/shard_map/ppermute | solution.py:35
  31.7 17.6 %collective-permute-start.12 = (bf16[128,1536]{1,0:T(8,128)(2,1)S(1)}, bf16[128,1536]{1,0:T(8,128)(2,1)S(1)}, u32[]{:S(2)}, u32[]{:S(2)}) collective-permute-start(bf16[128,1536]{1,0:T(8,128)(2,1)S(1)} %bitcast.19), channel_id=1, source_target_pairs={{0,3},{1,2},{2,1},{3,0},{4,7},{5,6},{6,5},{7,4},{8,11},{9,10},{10,... | collective-permute-start | bytes 1179656 | tf_op jit(solution)/shard_map/ppermute | solution.py:35
  31.7 17.6 %collective-permute-start.11 = (bf16[128,1536]{1,0:T(8,128)(2,1)S(1)}, bf16[128,1536]{1,0:T(8,128)(2,1)S(1)}, u32[]{:S(2)}, u32[]{:S(2)}) collective-permute-start(bf16[128,1536]{1,0:T(8,128)(2,1)S(1)} %bitcast.20), channel_id=1, source_target_pairs={{0,1},{1,0},{2,3},{3,2},{4,5},{5,4},{6,7},{7,6},{8,9},{9,8},{10,11... | collective-permute-start | bytes 1179656 | tf_op jit(solution)/shard_map/ppermute | solution.py:35
  49.5 4.0 %collective-permute-start.15 = (bf16[4,128,1536]{2,1,0:T(8,128)(2,1)S(1)}, bf16[4,128,1536]{2,1,0:T(8,128)(2,1)S(1)}, u32[]{:S(2)}, u32[]{:S(2)}) collective-permute-start(bf16[4,128,1536]{2,1,0:T(8,128)(2,1)S(1)} %pad_maximum_fusion.cot_ref.cb_ref), channel_id=1, source_target_pairs={{0,1},{1,0},{2,3},{3,2},{4,5},{5,4},{6,7},{7,6},{8,9},{9,8},{10,11... | collective-permute-start | bytes 4718600 | tf_op jit(solution)/shard_map/ppermute | solution.py:35
  53.0 7.2 %collective-permute-start.22 = (bf16[512,1536]{1,0:T(8,128)(2,1)S(1)}, bf16[512,1536]{1,0:T(8,128)(2,1)S(1)}, u32[]{:S(2)}, u32[]{:S(2)}) collective-permute-start(bf16[512,1536]{1,0:T(8,128)(2,1)S(1)} %get-tuple-element.111), channel_id=1, source_target_pairs={{0,1},{1,0},{2,3},{3,2},{4,5},{5,4},{6,7},{7,6},{8,9},{9,8},{10,11... | collective-permute-start | bytes 4718600 | tf_op jit(solution)/shard_map/ppermute | solution.py:35
  58.6 15.4 %collective-permute-start.16 = (bf16[8,96,384]{2,1,0:T(8,128)(2,1)S(1)}, bf16[8,96,384]{2,1,0:T(8,128)(2,1)S(1)}, u32[]{:S(2)}, u32[]{:S(2)}) collective-permute-start(bf16[8,96,384]{2,1,0:T(8,128)(2,1)S(1)} %get-tuple-element.99), channel_id=1, source_target_pairs={{0,32},{32,0},{64,96},{96,64},{1,33},{33,1},{65,97},{97,65},{2,34}... | collective-permute-start | bytes 1769480 | tf_op jit(solution)/shard_map/ppermute | solution.py:35
  60.6 19.4 %collective-permute-start.23 = (bf16[256,1536]{1,0:T(8,128)(2,1)S(1)}, bf16[256,1536]{1,0:T(8,128)(2,1)S(1)}, u32[]{:S(2)}, u32[]{:S(2)}) collective-permute-start(bf16[256,1536]{1,0:T(8,128)(2,1)S(1)} %get-tuple-element.113), channel_id=1, source_target_pairs={{0,2},{1,3},{2,0},{3,1},{4,6},{5,7},{6,4},{7,5},{8,10},{9,11},{10,... | collective-permute-start | bytes 2359304 | tf_op jit(solution)/shard_map/ppermute | solution.py:35
  63.9 14.9 %collective-permute-start.18 = (bf16[8,96,384]{2,1,0:T(8,128)(2,1)S(1)}, bf16[8,96,384]{2,1,0:T(8,128)(2,1)S(1)}, u32[]{:S(2)}, u32[]{:S(2)}) collective-permute-start(bf16[8,96,384]{2,1,0:T(8,128)(2,1)S(1)} %get-tuple-element.103), channel_id=1, source_target_pairs={{0,8},{8,0},{16,24},{24,16},{1,9},{9,1},{17,25},{25,17},{2,10},{10... | collective-permute-start | bytes 1769480 | tf_op jit(solution)/shard_map/ppermute | solution.py:35
  66.9 17.2 %collective-permute-start.27 = (bf16[8,96,384]{2,1,0:T(8,128)(2,1)S(1)}, bf16[8,96,384]{2,1,0:T(8,128)(2,1)S(1)}, u32[]{:S(2)}, u32[]{:S(2)}) collective-permute-start(bf16[8,96,384]{2,1,0:T(8,128)(2,1)S(1)} %get-tuple-element.122), channel_id=1, source_target_pairs={{0,24},{8,16},{16,8},{24,0},{1,25},{9,17},{17,9},{25,1},{2,26},{10... | collective-permute-start | bytes 1769480 | tf_op jit(solution)/shard_map/ppermute | solution.py:35
  71.7 16.4 %collective-permute-start.25 = (bf16[8,96,384]{2,1,0:T(8,128)(2,1)S(1)}, bf16[8,96,384]{2,1,0:T(8,128)(2,1)S(1)}, u32[]{:S(2)}, u32[]{:S(2)}) collective-permute-start(bf16[8,96,384]{2,1,0:T(8,128)(2,1)S(1)} %get-tuple-element.120), channel_id=1, source_target_pairs={{0,96},{32,64},{64,32},{96,0},{1,97},{33,65},{65,33},{97,1},{2,98}... | collective-permute-start | bytes 1769480 | tf_op jit(solution)/shard_map/ppermute | solution.py:35
  80.1 16.1 %collective-permute-start.24 = (bf16[128,1536]{1,0:T(8,128)(2,1)S(1)}, bf16[128,1536]{1,0:T(8,128)(2,1)S(1)}, u32[]{:S(2)}, u32[]{:S(2)}) collective-permute-start(bf16[128,1536]{1,0:T(8,128)(2,1)S(1)} %get-tuple-element.119), channel_id=1, source_target_pairs={{0,6},{1,7},{2,4},{3,5},{4,2},{5,3},{6,0},{7,1},{8,14},{9,15},{10,... | collective-permute-start | bytes 1179656 | tf_op jit(solution)/shard_map/ppermute | solution.py:35
  82.6 7.8 %collective-permute-start.17 = (bf16[4,96,384]{2,1,0:T(8,128)(2,1)S(1)}, bf16[4,96,384]{2,1,0:T(8,128)(2,1)S(1)}, u32[]{:S(2)}, u32[]{:S(2)}) collective-permute-start(bf16[4,96,384]{2,1,0:T(8,128)(2,1)S(1)} %get-tuple-element.101), channel_id=1, source_target_pairs={{0,8},{8,0},{16,24},{24,16},{1,9},{9,1},{17,25},{25,17},{2,10},{10... | collective-permute-start | bytes 884744 | tf_op jit(solution)/shard_map/ppermute | solution.py:35
  83.6 7.3 %collective-permute-start.19 = (bf16[4,96,384]{2,1,0:T(8,128)(2,1)S(1)}, bf16[4,96,384]{2,1,0:T(8,128)(2,1)S(1)}, u32[]{:S(2)}, u32[]{:S(2)}) collective-permute-start(bf16[4,96,384]{2,1,0:T(8,128)(2,1)S(1)} %get-tuple-element.105), channel_id=1, source_target_pairs={{0,32},{32,0},{64,96},{96,64},{1,33},{33,1},{65,97},{97,65},{2,34}... | collective-permute-start | bytes 884744 | tf_op jit(solution)/shard_map/ppermute | solution.py:35
  84.2 9.3 %collective-permute-start.28 = (bf16[4,96,384]{2,1,0:T(8,128)(2,1)S(1)}, bf16[4,96,384]{2,1,0:T(8,128)(2,1)S(1)}, u32[]{:S(2)}, u32[]{:S(2)}) collective-permute-start(bf16[4,96,384]{2,1,0:T(8,128)(2,1)S(1)} %get-tuple-element.123), channel_id=1, source_target_pairs={{0,96},{32,64},{64,32},{96,0},{1,97},{33,65},{65,33},{97,1},{2,98}... | collective-permute-start | bytes 884744 | tf_op jit(solution)/shard_map/ppermute | solution.py:35
  88.2 8.0 %collective-permute-start.26 = (bf16[4,96,384]{2,1,0:T(8,128)(2,1)S(1)}, bf16[4,96,384]{2,1,0:T(8,128)(2,1)S(1)}, u32[]{:S(2)}, u32[]{:S(2)}) collective-permute-start(bf16[4,96,384]{2,1,0:T(8,128)(2,1)S(1)} %get-tuple-element.121), channel_id=1, source_target_pairs={{0,24},{8,16},{16,8},{24,0},{1,25},{9,17},{17,9},{25,1},{2,26},{10... | collective-permute-start | bytes 884744 | tf_op jit(solution)/shard_map/ppermute | solution.py:35
  99.1 2.4 %collective-permute-start.29 = (bf16[272,1536]{1,0:T(8,128)(2,1)S(1)}, bf16[272,1536]{1,0:T(8,128)(2,1)S(1)}, u32[]{:S(2)}, u32[]{:S(2)}) collective-permute-start(bf16[272,1536]{1,0:T(8,128)(2,1)S(1)} %get-tuple-element.131), channel_id=1, source_target_pairs={{0,1},{1,0},{2,3},{3,2},{4,5},{5,4},{6,7},{7,6},{8,9},{9,8},{10,11... | collective-permute-start | bytes 2506760 | tf_op jit(solution)/shard_map/ppermute | solution.py:35
  99.2 10.6 %collective-permute-start.20 = (bf16[2,192,384]{2,1,0:T(8,128)(2,1)S(1)}, bf16[2,192,384]{2,1,0:T(8,128)(2,1)S(1)}, u32[]{:S(2)}, u32[]{:S(2)}) collective-permute-start(bf16[2,192,384]{2,1,0:T(8,128)(2,1)S(1)} %get-tuple-element.107), channel_id=1, source_target_pairs={{0,96},{32,64},{64,32},{96,0},{1,97},{33,65},{65,33},{97,1},{2,98}... | collective-permute-start | bytes 884744 | tf_op jit(solution)/shard_map/ppermute | solution.py:35
  101.0 12.3 %collective-permute-start.38 = (bf16[2,192,384]{2,1,0:T(8,128)(2,1)S(1)}, bf16[2,192,384]{2,1,0:T(8,128)(2,1)S(1)}, u32[]{:S(2)}, u32[]{:S(2)}) collective-permute-start(bf16[2,192,384]{2,1,0:T(8,128)(2,1)S(1)} %get-tuple-element.141), channel_id=1, source_target_pairs={{0,32},{32,0},{64,96},{96,64},{1,33},{33,1},{65,97},{97,65},{2,34}... | collective-permute-start | bytes 884744 | tf_op jit(solution)/shard_map/ppermute | solution.py:35
  101.8 10.4 %collective-permute-start.30 = (bf16[144,768]{1,0:T(8,128)(2,1)S(1)}, bf16[144,768]{1,0:T(8,128)(2,1)S(1)}, u32[]{:S(2)}, u32[]{:S(2)}) collective-permute-start(bf16[144,768]{1,0:T(8,128)(2,1)S(1)} %get-tuple-element.133), channel_id=1, source_target_pairs={{0,2},{1,3},{2,0},{3,1},{4,6},{5,7},{6,4},{7,5},{8,10},{9,11},{10,... | collective-permute-start | bytes 663560 | tf_op jit(solution)/shard_map/ppermute | solution.py:35
  103.8 9.7 %collective-permute-start.40 = (bf16[144,768]{1,0:T(8,128)(2,1)S(1)}, bf16[144,768]{1,0:T(8,128)(2,1)S(1)}, u32[]{:S(2)}, u32[]{:S(2)}) collective-permute-start(bf16[144,768]{1,0:T(8,128)(2,1)S(1)} %get-tuple-element.145), channel_id=1, source_target_pairs={{0,6},{1,7},{2,4},{3,5},{4,2},{5,3},{6,0},{7,1},{8,14},{9,15},{10,... | collective-permute-start | bytes 663560 | tf_op jit(solution)/shard_map/ppermute | solution.py:35
  109.9 6.7 %collective-permute-start.21 = (bf16[1,192,384]{2,1,0:T(8,128)(2,1)S(1)}, bf16[1,192,384]{2,1,0:T(8,128)(2,1)S(1)}, u32[]{:S(2)}, u32[]{:S(2)}) collective-permute-start(bf16[1,192,384]{2,1,0:T(8,128)(2,1)S(1)} %get-tuple-element.109), channel_id=1, source_target_pairs={{0,24},{8,16},{16,8},{24,0},{1,25},{9,17},{17,9},{25,1},{2,26},{10... | collective-permute-start | bytes 442376 | tf_op jit(solution)/shard_map/ppermute | solution.py:35
  112.2 6.2 %collective-permute-start.31 = (bf16[80,768]{1,0:T(8,128)(2,1)S(1)}, bf16[80,768]{1,0:T(8,128)(2,1)S(1)}, u32[]{:S(2)}, u32[]{:S(2)}) collective-permute-start(bf16[80,768]{1,0:T(8,128)(2,1)S(1)} %get-tuple-element.135), channel_id=1, source_target_pairs={{0,6},{1,7},{2,4},{3,5},{4,2},{5,3},{6,0},{7,1},{8,14},{9,15},{10,... | collective-permute-start | bytes 368648 | tf_op jit(solution)/shard_map/ppermute | solution.py:35
  113.4 6.3 %collective-permute-start.39 = (bf16[1,192,384]{2,1,0:T(8,128)(2,1)S(1)}, bf16[1,192,384]{2,1,0:T(8,128)(2,1)S(1)}, u32[]{:S(2)}, u32[]{:S(2)}) collective-permute-start(bf16[1,192,384]{2,1,0:T(8,128)(2,1)S(1)} %get-tuple-element.143), channel_id=1, source_target_pairs={{0,8},{8,0},{16,24},{24,16},{1,9},{9,1},{17,25},{25,17},{2,10},{10... | collective-permute-start | bytes 442376 | tf_op jit(solution)/shard_map/ppermute | solution.py:35
  113.5 6.1 %collective-permute-start.41 = (bf16[80,768]{1,0:T(8,128)(2,1)S(1)}, bf16[80,768]{1,0:T(8,128)(2,1)S(1)}, u32[]{:S(2)}, u32[]{:S(2)}) collective-permute-start(bf16[80,768]{1,0:T(8,128)(2,1)S(1)} %get-tuple-element.147), channel_id=1, source_target_pairs={{0,2},{1,3},{2,0},{3,1},{4,6},{5,7},{6,4},{7,5},{8,10},{9,11},{10,... | collective-permute-start | bytes 368648 | tf_op jit(solution)/shard_map/ppermute | solution.py:35
  118.5 5.1 %collective-permute-start.35 = (bf16[176,384]{1,0:T(8,128)(2,1)S(1)}, bf16[176,384]{1,0:T(8,128)(2,1)S(1)}, u32[]{:S(2)}, u32[]{:S(2)}) collective-permute-start(bf16[176,384]{1,0:T(8,128)(2,1)S(1)} %get-tuple-element.137.own), channel_id=1, source_target_pairs={{0,32},{32,0},{64,96},{96,64},{1,33},{33,1},{65,97},{97,65},{2,34}... | collective-permute-start | bytes 405512 | tf_op jit(solution)/shard_map/ppermute | solution.py:35
  118.5 6.5 %collective-permute-start.32 = (bf16[176,384]{1,0:T(8,128)(2,1)S(1)}, bf16[176,384]{1,0:T(8,128)(2,1)S(1)}, u32[]{:S(2)}, u32[]{:S(2)}) collective-permute-start(bf16[176,384]{1,0:T(8,128)(2,1)S(1)} %get-tuple-element.136.own), channel_id=1, source_target_pairs={{0,24},{8,16},{16,8},{24,0},{1,25},{9,17},{17,9},{25,1},{2,26},{10... | collective-permute-start | bytes 405512 | tf_op jit(solution)/shard_map/ppermute | solution.py:35
  119.7 6.7 %collective-permute-start.45 = (bf16[176,384]{1,0:T(8,128)(2,1)S(1)}, bf16[176,384]{1,0:T(8,128)(2,1)S(1)}, u32[]{:S(2)}, u32[]{:S(2)}) collective-permute-start(bf16[176,384]{1,0:T(8,128)(2,1)S(1)} %get-tuple-element.149.own), channel_id=1, source_target_pairs={{0,96},{32,64},{64,32},{96,0},{1,97},{33,65},{65,33},{97,1},{2,98}... | collective-permute-start | bytes 405512 | tf_op jit(solution)/shard_map/ppermute | solution.py:35
  121.4 6.9 %collective-permute-start.42 = (bf16[176,384]{1,0:T(8,128)(2,1)S(1)}, bf16[176,384]{1,0:T(8,128)(2,1)S(1)}, u32[]{:S(2)}, u32[]{:S(2)}) collective-permute-start(bf16[176,384]{1,0:T(8,128)(2,1)S(1)} %get-tuple-element.148.own), channel_id=1, source_target_pairs={{0,8},{8,0},{16,24},{24,16},{1,9},{9,1},{17,25},{25,17},{2,10},{10... | collective-permute-start | bytes 405512 | tf_op jit(solution)/shard_map/ppermute | solution.py:35
  123.6 7.1 %collective-permute-start.36 = (bf16[272,384]{1,0:T(8,128)(2,1)S(1)}, bf16[272,384]{1,0:T(8,128)(2,1)S(1)}, u32[]{:S(2)}, u32[]{:S(2)}) collective-permute-start(bf16[272,384]{1,0:T(8,128)(2,1)S(1)} %shard_map.153.own), channel_id=1, source_target_pairs={{0,24},{8,16},{16,8},{24,0},{1,25},{9,17},{17,9},{25,1},{2,26},{10... | collective-permute-start | bytes 626696 | tf_op jit(solution)/shard_map/ppermute | solution.py:35
  125.1 8.4 %collective-permute-start.33 = (bf16[272,384]{1,0:T(8,128)(2,1)S(1)}, bf16[272,384]{1,0:T(8,128)(2,1)S(1)}, u32[]{:S(2)}, u32[]{:S(2)}) collective-permute-start(bf16[272,384]{1,0:T(8,128)(2,1)S(1)} %shard_map.150.own), channel_id=1, source_target_pairs={{0,96},{32,64},{64,32},{96,0},{1,97},{33,65},{65,33},{97,1},{2,98}... | collective-permute-start | bytes 626696 | tf_op jit(solution)/shard_map/ppermute | solution.py:35
  126.5 7.5 %collective-permute-start.46 = (bf16[272,384]{1,0:T(8,128)(2,1)S(1)}, bf16[272,384]{1,0:T(8,128)(2,1)S(1)}, u32[]{:S(2)}, u32[]{:S(2)}) collective-permute-start(bf16[272,384]{1,0:T(8,128)(2,1)S(1)} %shard_map.163.own), channel_id=1, source_target_pairs={{0,8},{8,0},{16,24},{24,16},{1,9},{9,1},{17,25},{25,17},{2,10},{10... | collective-permute-start | bytes 626696 | tf_op jit(solution)/shard_map/ppermute | solution.py:35
  128.3 8.3 %collective-permute-start.43 = (bf16[272,384]{1,0:T(8,128)(2,1)S(1)}, bf16[272,384]{1,0:T(8,128)(2,1)S(1)}, u32[]{:S(2)}, u32[]{:S(2)}) collective-permute-start(bf16[272,384]{1,0:T(8,128)(2,1)S(1)} %shard_map.160.own), channel_id=1, source_target_pairs={{0,32},{32,0},{64,96},{96,64},{1,33},{33,1},{65,97},{97,65},{2,34}... | collective-permute-start | bytes 626696 | tf_op jit(solution)/shard_map/ppermute | solution.py:35
  130.7 9.1 %collective-permute-start.37 = (bf16[464,384]{1,0:T(8,128)(2,1)S(1)}, bf16[464,384]{1,0:T(8,128)(2,1)S(1)}, u32[]{:S(2)}, u32[]{:S(2)}) collective-permute-start(bf16[464,384]{1,0:T(8,128)(2,1)S(1)} %shard_map.154.own), channel_id=1, source_target_pairs={{0,96},{32,64},{64,32},{96,0},{1,97},{33,65},{65,33},{97,1},{2,98}... | collective-permute-start | bytes 1069064 | tf_op jit(solution)/shard_map/ppermute | solution.py:35
  133.6 9.2 %collective-permute-start.34 = (bf16[464,384]{1,0:T(8,128)(2,1)S(1)}, bf16[464,384]{1,0:T(8,128)(2,1)S(1)}, u32[]{:S(2)}, u32[]{:S(2)}) collective-permute-start(bf16[464,384]{1,0:T(8,128)(2,1)S(1)} %shard_map.151.own), channel_id=1, source_target_pairs={{0,8},{8,0},{16,24},{24,16},{1,9},{9,1},{17,25},{25,17},{2,10},{10... | collective-permute-start | bytes 1069064 | tf_op jit(solution)/shard_map/ppermute | solution.py:35
  134.0 12.0 %collective-permute-start.47 = (bf16[464,384]{1,0:T(8,128)(2,1)S(1)}, bf16[464,384]{1,0:T(8,128)(2,1)S(1)}, u32[]{:S(2)}, u32[]{:S(2)}) collective-permute-start(bf16[464,384]{1,0:T(8,128)(2,1)S(1)} %shard_map.164.own), channel_id=1, source_target_pairs={{0,32},{32,0},{64,96},{96,64},{1,33},{33,1},{65,97},{97,65},{2,34}... | collective-permute-start | bytes 1069064 | tf_op jit(solution)/shard_map/ppermute | solution.py:35
  136.7 11.0 %collective-permute-start.44 = (bf16[464,384]{1,0:T(8,128)(2,1)S(1)}, bf16[464,384]{1,0:T(8,128)(2,1)S(1)}, u32[]{:S(2)}, u32[]{:S(2)}) collective-permute-start(bf16[464,384]{1,0:T(8,128)(2,1)S(1)} %shard_map.161.own), channel_id=1, source_target_pairs={{0,24},{8,16},{16,8},{24,0},{1,25},{9,17},{17,9},{25,1},{2,26},{10... | collective-permute-start | bytes 1069064 | tf_op jit(solution)/shard_map/ppermute | solution.py:35
  139.9 15.1 %collective-permute-start.49 = (bf16[848,384]{1,0:T(8,128)(2,1)S(1)}, bf16[848,384]{1,0:T(8,128)(2,1)S(1)}, u32[]{:S(2)}, u32[]{:S(2)}) collective-permute-start(bf16[848,384]{1,0:T(8,128)(2,1)S(1)} %shard_map.155.refs_1_), channel_id=1, source_target_pairs={{0,8},{8,0},{16,24},{24,16},{1,9},{9,1},{17,25},{25,17},{2,10},{10... | collective-permute-start | bytes 1953800 | tf_op jit(solution)/shard_map/ppermute | solution.py:35
  142.9 13.0 %collective-permute-start.48 = (bf16[848,384]{1,0:T(8,128)(2,1)S(1)}, bf16[848,384]{1,0:T(8,128)(2,1)S(1)}, u32[]{:S(2)}, u32[]{:S(2)}) collective-permute-start(bf16[848,384]{1,0:T(8,128)(2,1)S(1)} %shard_map.152.refs_0_), channel_id=1, source_target_pairs={{0,32},{32,0},{64,96},{96,64},{1,33},{33,1},{65,97},{97,65},{2,34}... | collective-permute-start | bytes 1953800 | tf_op jit(solution)/shard_map/ppermute | solution.py:35
  146.1 13.2 %collective-permute-start.51 = (bf16[848,384]{1,0:T(8,128)(2,1)S(1)}, bf16[848,384]{1,0:T(8,128)(2,1)S(1)}, u32[]{:S(2)}, u32[]{:S(2)}) collective-permute-start(bf16[848,384]{1,0:T(8,128)(2,1)S(1)} %shard_map.165.refs_3_), channel_id=1, source_target_pairs={{0,24},{8,16},{16,8},{24,0},{1,25},{9,17},{17,9},{25,1},{2,26},{10... | collective-permute-start | bytes 1953800 | tf_op jit(solution)/shard_map/ppermute | solution.py:35
  147.7 12.6 %collective-permute-start.50 = (bf16[848,384]{1,0:T(8,128)(2,1)S(1)}, bf16[848,384]{1,0:T(8,128)(2,1)S(1)}, u32[]{:S(2)}, u32[]{:S(2)}) collective-permute-start(bf16[848,384]{1,0:T(8,128)(2,1)S(1)} %shard_map.162.refs_2_), channel_id=1, source_target_pairs={{0,96},{32,64},{64,32},{96,0},{1,97},{33,65},{65,33},{97,1},{2,98}... | collective-permute-start | bytes 1953800 | tf_op jit(solution)/shard_map/ppermute | solution.py:35

commit v5 on v4

--- a/solution.py
+++ b/solution.py
@@ -307,7 +307,7 @@
     return (a << 3) | (b << 2) | (c << 1) | d
 
 
-def weight_kernel(k, hid_ref, ca_ref, cb_ref, ln_ref, da_ref, db_ref, keep_ref, send_ref, both):
+def weight_kernel(k, hid_ref, ca_ref, cb_ref, ln_ref, da_ref, db_ref, keep_ref, send_ref):
     y, z = lax.axis_index("dp"), lax.axis_index("context")
     half = hid_ref.shape[2]
     cols, wide, ff_cols = pl.ds(384 * k, 384), pl.ds(768 * (k // 2), 768), pl.ds(384 * (k % 2), 384)
@@ -318,12 +318,17 @@
     up = jnp.dot(ln_ref[0, wide, :], da_ref[:, ff_cols], preferred_element_type=F32)
     up += jnp.dot(ln_ref[1, wide, :], db_ref[:, ff_cols], preferred_element_type=F32)
     up = up.astype(BF)
+    flip = (4, 1, 12, 3)[PARTS[k][0]]
     for r in range(16):
+        if r > r ^ flip:
+            continue
         code = piece_code(y, z, r, PARTS[k])
-        both[code, pl.ds(0, 48), :] = down[48 * r : 48 * r + 48]
-        both[code, pl.ds(48, 48), :] = up[48 * r : 48 * r + 48]
-    keep_ref[...] = both[pl.ds(0, 8)]
-    send_ref[...] = both[pl.ds(8, 8)]
+        mine, low = code < 8, code & 7
+        for at, value in ((0, down), (48, up)):
+            one = value[48 * r : 48 * r + 48]
+            two = value[48 * (r ^ flip) : 48 * (r ^ flip) + 48]
+            keep_ref[low, pl.ds(at, 48), :] = lax.select(mine, one, two)
+            send_ref[low, pl.ds(at, 48), :] = lax.select(mine, two, one)
 
 
 def weight_part(k, hidden, ca, cb, ln, dpre_a, dpre_b):
@@ -333,7 +338,6 @@
         in_specs=[WHOLE] * 6,
         out_specs=[WHOLE] * 2,
         out_shape=[jax.ShapeDtypeStruct((8, 96, 384), BF)] * 2,
-        scratch_shapes=[pltpu.VMEM((16, 96, 384), BF)],
         compiler_params=vmem(14),
         cost_estimate=cost(4 * rows * 768 * 384, 7 << 20),
     )(hidden, ca, cb, ln, dpre_a, dpre_b)

time: 164 us -> 164 us (level)
  waiting for transfers between devices: 49.6 us -> 51.7 us
    ppermute x52, waiting for transfers between devices: 49.6 us -> 51.7 us  [xor_send(): return lax.ppermute(value, axis, [(i, i ^ mask) for i in range(size)])]
  transfers between devices with their start and end apart: 52 -> 52, of which waited for: 27 -> 27; matrix products, arithmetic and copies ran while one was open for 0% -> 0% of each run, Pallas kernels for 20% -> 19%
where the time goes in v5:
time: 164 us
  starting transfers between devices  69.3 us (42%)
  waiting for transfers between devices  51.7 us (32%)
  Pallas kernels  40.3 us (25%)
    ppermute x52, starting transfers between devices, xor_send(): return lax.ppermute(value, axis, [(i, i ^ mask) for i in range(size)])  69.3 us
    ppermute x52, waiting for transfers between devices, xor_send(): return lax.ppermute(value, axis, [(i, i ^ mask) for i in range(size)])  51.7 us
    pallas_call x1, Pallas kernels, normalise(): pl.pallas_call(norm_kernel, grid=(4,), in_specs=[WHOLE] * 6, out_specs=[W...  9.46 us
    pallas_call x4, Pallas kernels, weight_part(): pl.pallas_call(functools.partial(weight_kernel, k), in_specs=[WHOLE] * 6,...  7.19 us
    pallas_call x2, Pallas kernels, backward_rows(): pl.pallas_call(functools.partial(backward_kernel, side), in_specs=[WHOLE]...  6.32 us
    pallas_call x1, Pallas kernels, hidden_rows(): pl.pallas_call(hidden_kernel, in_specs=[WHOLE] * 3, out_specs=[WHOLE] * 3...  3.61 us
  transfers between devices with their start and end apart: 52, of which 27 were waited for; matrix products, arithmetic and copies ran while one was open for 0% of the time, Pallas kernels for 19%

profile of v5, /device:TPU:0, one launch (start us, length us, event | category | flops | bytes accessed | tf_op | source)
XLA Modules:
  0.0 163.9 jit_solution(11801910092506280405)
XLA Ops:
  0.6 2.6 %shard_map.128 = (bf16[640,128]{1,0:T(8,128)(2,1)}, bf16[640,128]{1,0:T(8,128)(2,1)}, bf16[640,128]{1,0:T(8,128)(2,1)}, bf16[640,128]{1,0:T(8,128)(2,1)}) custom-call(s32[1,4]{1,0:T(1,128)} %lengths_hbm.1, bf16[32,64,65]{2,1,0:T(8,128)(2,1)} %bitcast.22, s32[1,128]{1,0:T(1,128)} %seg_hbm.1), custom_call_target="tpu_custom_call" | custom-call | flops 42598400 | bytes 2097152 | tf_op jit(solution)/shard_map/pallas_call | solution.py:89
  3.3 4.0 %collective-permute-start = (bf16[640,128]{1,0:T(8,128)(2,1)}, bf16[640,128]{1,0:T(8,128)(2,1)S(1)}, u32[]{:S(2)}, u32[]{:S(2)}) collective-permute-start(bf16[640,128]{1,0:T(8,128)(2,1)} %get-tuple-element.82), channel_id=1, source_target_pairs={{0,16},{8,24},{16,0},{24,8},{1,17},{9,25},{17,1},{25,9},{2,18},{10... | collective-permute-start | bytes 491528 | tf_op jit(solution)/shard_map/ppermute | solution.py:35
  7.3 1.0 collective-permute-start.1
  8.3 3.0 %collective-permute-start.9 = (bf16[64,1536]{1,0:T(8,128)(2,1)}, bf16[64,1536]{1,0:T(8,128)(2,1)S(1)}, u32[]{:S(2)}, u32[]{:S(2)}) collective-permute-start(bf16[64,1536]{1,0:T(8,128)(2,1)} %param.12), channel_id=1, source_target_pairs={{0,4},{1,5},{2,6},{3,7},{4,0},{5,1},{6,2},{7,3},{8,12},{9,13},{10,... | collective-permute-start | bytes 589832 | tf_op jit(solution)/shard_map/ppermute | solution.py:35
  11.3 1.1 collective-permute-start.8
  12.5 1.5 collective-permute-start.7
  14.0 2.0 %collective-permute-done.1.three = bf16[640,128]{1,0:T(8,128)(2,1)S(1)} collective-permute-done((bf16[640,128]{1,0:T(8,128)(2,1)}, bf16[640,128]{1,0:T(8,128)(2,1)S(1)}, u32[]{:S(2)}, u32[]{:S(2)}) %collective-permute-start.1) | collective-permute-done | bytes 163872 | tf_op jit(solution)/shard_map/ppermute | solution.py:35
  16.0 0.9 copy-done.3
  17.0 3.1 %collective-permute-start.5 = (bf16[640,128]{1,0:T(8,128)(2,1)S(1)}, bf16[640,128]{1,0:T(8,128)(2,1)S(1)}, u32[]{:S(2)}, u32[]{:S(2)}) collective-permute-start(bf16[640,128]{1,0:T(8,128)(2,1)S(1)} %shard_map.129), channel_id=1, source_target_pairs={{0,4},{1,5},{2,6},{3,7},{4,0},{5,1},{6,2},{7,3},{8,12},{9,13},{10,... | collective-permute-start | bytes 491528 | tf_op jit(solution)/shard_map/ppermute | solution.py:35
  20.1 1.1 collective-permute-start.4
  21.5 3.2 %collective-permute-done.5 = bf16[640,128]{1,0:T(8,128)(2,1)S(1)} collective-permute-done((bf16[640,128]{1,0:T(8,128)(2,1)S(1)}, bf16[640,128]{1,0:T(8,128)(2,1)S(1)}, u32[]{:S(2)}, u32[]{:S(2)}) %collective-permute-start.5) | collective-permute-done | bytes 163872 | tf_op jit(solution)/shard_map/ppermute | solution.py:35
  24.7 2.9 %collective-permute-done.4 = bf16[640,128]{1,0:T(8,128)(2,1)S(1)} collective-permute-done((bf16[640,128]{1,0:T(8,128)(2,1)S(1)}, bf16[640,128]{1,0:T(8,128)(2,1)S(1)}, u32[]{:S(2)}, u32[]{:S(2)}) %collective-permute-start.4) | collective-permute-done | bytes 163872 | tf_op jit(solution)/shard_map/ppermute | solution.py:35
  27.9 2.1 %collective-permute-start.14 = (bf16[128,1536]{1,0:T(8,128)(2,1)S(1)}, bf16[128,1536]{1,0:T(8,128)(2,1)S(1)}, u32[]{:S(2)}, u32[]{:S(2)}) collective-permute-start(bf16[128,1536]{1,0:T(8,128)(2,1)S(1)} %bitcast.17), channel_id=1, source_target_pairs={{0,5},{1,4},{2,7},{3,6},{4,1},{5,0},{6,3},{7,2},{8,13},{9,12},{10,... | collective-permute-start | bytes 1179656 | tf_op jit(solution)/shard_map/ppermute | solution.py:35
  30.0 1.7 %collective-permute-start.13 = (bf16[128,1536]{1,0:T(8,128)(2,1)S(1)}, bf16[128,1536]{1,0:T(8,128)(2,1)S(1)}, u32[]{:S(2)}, u32[]{:S(2)}) collective-permute-start(bf16[128,1536]{1,0:T(8,128)(2,1)S(1)} %bitcast.18), channel_id=1, source_target_pairs={{0,7},{1,6},{2,5},{3,4},{4,3},{5,2},{6,1},{7,0},{8,15},{9,14},{10,... | collective-permute-start | bytes 1179656 | tf_op jit(solution)/shard_map/ppermute | solution.py:35
  32.2 9.5 %shard_map.130 = (bf16[1024,1536]{1,0:T(8,128)(2,1)S(1)}, f32[128,1536]{1,0:T(8,128)S(1)}, f32[128,128]{1,0:T(8,128)S(1)}, f32[160,1536]{1,0:T(8,128)S(1)}, f32[...) custom-call(bf16[4,640,128]{2,1,0:T(8,128)(2,1)S(1)} %pad_maximum_fusion.2.a_ref, ...), custom_call_target="tpu_custom_call" | custom-call | flops 12000000000 | bytes 10485760 | tf_op jit(solution)/shard_map/pallas_call | solution.py:206
  41.7 3.6 %shard_map.131 = (bf16[2,768,512]{2,1,0:T(8,128)(2,1)S(1)}, f32[1024,768]{1,0:T(8,128)S(1)}, bf16[2,1536,512]{2,1,0:T(8,128)(2,1)S(1)}) custom-call(bf16[1024,1536]{1,0:T(8,128)(2,1)S(1)} %get-tuple-element.86.ln_ref, bf16[1536,768]{1,0:T(8,128)(2,1)S(1)} %copy-done, bf16[768,1536]{1,0:T(8,128)(2,1)S(1)} %copy-done.1), custom_call_target="tpu_custom_call" | custom-call | flops 2415919104 | bytes 10485760 | tf_op jit(solution)/shard_map/pallas_call | solution.py:258
  45.3 4.0 %collective-permute-done.13 = bf16[128,1536]{1,0:T(8,128)(2,1)S(1)} collective-permute-done((bf16[128,1536]{1,0:T(8,128)(2,1)S(1)}, bf16[128,1536]{1,0:T(8,128)(2,1)S(1)}, u32[]{:S(2)}, u32[]{:S(2)}) %collective-permute-start.13) | collective-permute-done | bytes 393248 | tf_op jit(solution)/shard_map/ppermute | solution.py:35
  49.9 3.2 %shard_map.133 = (bf16[512,768]{1,0:T(8,128)(2,1)S(1)}, bf16[512,1536]{1,0:T(8,128)(2,1)S(1)}) custom-call(bf16[4,128,1536]{2,1,0:T(8,128)(2,1)S(1)} %pad_maximum_fusion.cot_ref.cb_ref, f32[1024,768]{1,0:T(8,128)S(1)} %get-tuple-element.95.slope_ref, bf16[1536,768]{1,0:T(8,128)(2,1)S(1)} %copy-done, bf16[768,1536]{1,0:T(8,128)(2,1)S(1)} %copy-done.1), custom_call_target="tpu_custom_call" | custom-call | flops 2415919104 | bytes 10485760 | tf_op jit(solution)/shard_map/pallas_call | solution.py:288
  53.5 3.2 %shard_map.132 = (bf16[512,768]{1,0:T(8,128)(2,1)S(1)}, bf16[512,1536]{1,0:T(8,128)(2,1)S(1)}) custom-call(bf16[4,128,1536]{2,1,0:T(8,128)(2,1)S(1)} %collective-permute-done.15.cot_ref.ca_ref, f32[1024,768]{1,0:T(8,128)S(1)} %get-tuple-element.95.slope_ref, bf16[1536,768]{1,0:T(8,128)(2,1)S(1)} %copy-done, bf16[768,1536]{1,0:T(8,128)(2,1)S(1)} %copy-done.1), custom_call_target="tpu_custom_call" | custom-call | flops 2415919104 | bytes 10485760 | tf_op jit(solution)/shard_map/pallas_call | solution.py:288
  56.7 1.8 %shard_map.134 = (bf16[8,96,384]{2,1,0:T(8,128)(2,1)S(1)}, bf16[8,96,384]{2,1,0:T(8,128)(2,1)S(1)}) custom-call(bf16[2,768,512]{2,1,0:T(8,128)(2,1)S(1)} %get-tuple-element.87.hid_ref, bf16[4,128,1536]{2,1,0:T(8,128)(2,1)S(1)} %collective-permute-done.15.cot_ref.ca_ref, bf16[4,128,1536]{2,1,0:T(8,128)(2,1)S(1)} %pad_maximum_fusion.cot_ref.cb_ref, ...), custom_call_target="tpu_custom_call" | custom-call | flops 1207959552 | bytes 7340032 | tf_op jit(solution)/shard_map/pallas_call | solution.py:336
  58.5 1.6 %collective-permute-start.16 = (bf16[8,96,384]{2,1,0:T(8,128)(2,1)S(1)}, bf16[8,96,384]{2,1,0:T(8,128)(2,1)S(1)}, u32[]{:S(2)}, u32[]{:S(2)}) collective-permute-start(bf16[8,96,384]{2,1,0:T(8,128)(2,1)S(1)} %get-tuple-element.99), channel_id=1, source_target_pairs={{0,32},{32,0},{64,96},{96,64},{1,33},{33,1},{65,97},{97,65},{2,34}... | collective-permute-start | bytes 1769480 | tf_op jit(solution)/shard_map/ppermute | solution.py:35
  60.5 1.4 collective-permute-start.23
  61.9 1.8 %shard_map.136 = (bf16[8,96,384]{2,1,0:T(8,128)(2,1)S(1)}, bf16[8,96,384]{2,1,0:T(8,128)(2,1)S(1)}) custom-call(bf16[2,768,512]{2,1,0:T(8,128)(2,1)S(1)} %get-tuple-element.87.hid_ref, bf16[4,128,1536]{2,1,0:T(8,128)(2,1)S(1)} %collective-permute-done.15.cot_ref.ca_ref, bf16[4,128,1536]{2,1,0:T(8,128)(2,1)S(1)} %pad_maximum_fusion.cot_ref.cb_ref, ...), custom_call_target="tpu_custom_call" | custom-call | flops 1207959552 | bytes 7340032 | tf_op jit(solution)/shard_map/pallas_call | solution.py:336
  63.7 1.1 collective-permute-start.18
  64.8 1.8 %shard_map.142 = (bf16[8,96,384]{2,1,0:T(8,128)(2,1)S(1)}, bf16[8,96,384]{2,1,0:T(8,128)(2,1)S(1)}) custom-call(bf16[2,768,512]{2,1,0:T(8,128)(2,1)S(1)} %get-tuple-element.87.hid_ref, bf16[4,128,1536]{2,1,0:T(8,128)(2,1)S(1)} %collective-permute-done.15.cot_ref.ca_ref, bf16[4,128,1536]{2,1,0:T(8,128)(2,1)S(1)} %pad_maximum_fusion.cot_ref.cb_ref, ...), custom_call_target="tpu_custom_call" | custom-call | flops 1207959552 | bytes 7340032 | tf_op jit(solution)/shard_map/pallas_call | solution.py:336
  66.6 2.9 %collective-permute-start.27 = (bf16[8,96,384]{2,1,0:T(8,128)(2,1)S(1)}, bf16[8,96,384]{2,1,0:T(8,128)(2,1)S(1)}, u32[]{:S(2)}, u32[]{:S(2)}) collective-permute-start(bf16[8,96,384]{2,1,0:T(8,128)(2,1)S(1)} %get-tuple-element.122), channel_id=1, source_target_pairs={{0,24},{8,16},{16,8},{24,0},{1,25},{9,17},{17,9},{25,1},{2,26},{10... | collective-permute-start | bytes 1769480 | tf_op jit(solution)/shard_map/ppermute | solution.py:35
  69.5 1.8 %shard_map.141 = (bf16[8,96,384]{2,1,0:T(8,128)(2,1)S(1)}, bf16[8,96,384]{2,1,0:T(8,128)(2,1)S(1)}) custom-call(bf16[2,768,512]{2,1,0:T(8,128)(2,1)S(1)} %get-tuple-element.87.hid_ref, bf16[4,128,1536]{2,1,0:T(8,128)(2,1)S(1)} %collective-permute-done.15.cot_ref.ca_ref, bf16[4,128,1536]{2,1,0:T(8,128)(2,1)S(1)} %pad_maximum_fusion.cot_ref.cb_ref, ...), custom_call_target="tpu_custom_call" | custom-call | flops 1207959552 | bytes 7340032 | tf_op jit(solution)/shard_map/pallas_call | solution.py:336
  71.3 2.3 %collective-permute-start.25 = (bf16[8,96,384]{2,1,0:T(8,128)(2,1)S(1)}, bf16[8,96,384]{2,1,0:T(8,128)(2,1)S(1)}, u32[]{:S(2)}, u32[]{:S(2)}) collective-permute-start(bf16[8,96,384]{2,1,0:T(8,128)(2,1)S(1)} %get-tuple-element.120), channel_id=1, source_target_pairs={{0,96},{32,64},{64,32},{96,0},{1,97},{33,65},{65,33},{97,1},{2,98}... | collective-permute-start | bytes 1769480 | tf_op jit(solution)/shard_map/ppermute | solution.py:35
  74.0 4.5 %collective-permute-done.18.rec = bf16[8,96,384]{2,1,0:T(8,128)(2,1)S(1)} collective-permute-done((bf16[8,96,384]{2,1,0:T(8,128)(2,1)S(1)}, bf16[8,96,384]{2,1,0:T(8,128)(2,1)S(1)}, u32[]{:S(2)}, u32[]{:S(2)}) %collective-permute-start.18) | collective-permute-done | bytes 589856 | tf_op jit(solution)/shard_map/ppermute | solution.py:35
  78.7 1.2 collective-permute-done.23.rec
  80.0 2.6 %collective-permute-start.24 = (bf16[128,1536]{1,0:T(8,128)(2,1)S(1)}, bf16[128,1536]{1,0:T(8,128)(2,1)S(1)}, u32[]{:S(2)}, u32[]{:S(2)}) collective-permute-start(bf16[128,1536]{1,0:T(8,128)(2,1)S(1)} %get-tuple-element.119), channel_id=1, source_target_pairs={{0,6},{1,7},{2,4},{3,5},{4,2},{5,3},{6,0},{7,1},{8,14},{9,15},{10,... | collective-permute-start | bytes 1179656 | tf_op jit(solution)/shard_map/ppermute | solution.py:35
  82.5 1.0 collective-permute-start.17
  84.1 3.3 %collective-permute-start.28 = (bf16[4,96,384]{2,1,0:T(8,128)(2,1)S(1)}, bf16[4,96,384]{2,1,0:T(8,128)(2,1)S(1)}, u32[]{:S(2)}, u32[]{:S(2)}) collective-permute-start(bf16[4,96,384]{2,1,0:T(8,128)(2,1)S(1)} %get-tuple-element.123), channel_id=1, source_target_pairs={{0,96},{32,64},{64,32},{96,0},{1,97},{33,65},{65,33},{97,1},{2,98}... | collective-permute-start | bytes 884744 | tf_op jit(solution)/shard_map/ppermute | solution.py:35
  87.6 3.0 %collective-permute-start.26 = (bf16[4,96,384]{2,1,0:T(8,128)(2,1)S(1)}, bf16[4,96,384]{2,1,0:T(8,128)(2,1)S(1)}, u32[]{:S(2)}, u32[]{:S(2)}) collective-permute-start(bf16[4,96,384]{2,1,0:T(8,128)(2,1)S(1)} %get-tuple-element.121), channel_id=1, source_target_pairs={{0,24},{8,16},{16,8},{24,0},{1,25},{9,17},{17,9},{25,1},{2,26},{10... | collective-permute-start | bytes 884744 | tf_op jit(solution)/shard_map/ppermute | solution.py:35
  91.0 2.2 %collective-permute-done.28.rec1 = bf16[4,96,384]{2,1,0:T(8,128)(2,1)S(1)} collective-permute-done((bf16[4,96,384]{2,1,0:T(8,128)(2,1)S(1)}, bf16[4,96,384]{2,1,0:T(8,128)(2,1)S(1)}, u32[]{:S(2)}, u32[]{:S(2)}) %collective-permute-start.28) | collective-permute-done | bytes 294944 | tf_op jit(solution)/shard_map/ppermute | solution.py:35
  93.2 2.5 %collective-permute-done.26.rec0 = bf16[4,96,384]{2,1,0:T(8,128)(2,1)S(1)} collective-permute-done((bf16[4,96,384]{2,1,0:T(8,128)(2,1)S(1)}, bf16[4,96,384]{2,1,0:T(8,128)(2,1)S(1)}, u32[]{:S(2)}, u32[]{:S(2)}) %collective-permute-start.26) | collective-permute-done | bytes 294944 | tf_op jit(solution)/shard_map/ppermute | solution.py:35
  95.6 2.9 %shard_map.146 = (f32[272,1536]{1,0:T(8,128)S(1)}, bf16[272,1536]{1,0:T(8,128)(2,1)S(1)}) custom-call(f32[128,1536]{1,0:T(8,128)S(1)} %get-tuple-element.117.dln_ref, bf16[128,1536]{1,0:T(8,128)(2,1)S(1)} %collective-permute-done.24.rec_ref, f32[128,1536]{1,0:T(8,128)S(1)} %get-tuple-element.125.normed_ref, f32[128,128]{1,0:T(8,128)S(1)} %get-tuple-element.126.rstd_ref, ...), custom_call_target="tpu_custom_call" | custom-call | flops 60000002048 | bytes 6291456 | tf_op jit(solution)/shard_map/pallas_call | solution.py:489
  98.6 1.9 %collective-permute-start.20 = (bf16[2,192,384]{2,1,0:T(8,128)(2,1)S(1)}, bf16[2,192,384]{2,1,0:T(8,128)(2,1)S(1)}, u32[]{:S(2)}, u32[]{:S(2)}) collective-permute-start(bf16[2,192,384]{2,1,0:T(8,128)(2,1)S(1)} %get-tuple-element.107), channel_id=1, source_target_pairs={{0,96},{32,64},{64,32},{96,0},{1,97},{33,65},{65,33},{97,1},{2,98}... | collective-permute-start | bytes 884744 | tf_op jit(solution)/shard_map/ppermute | solution.py:35
  101.2 1.8 %collective-permute-start.30 = (bf16[144,768]{1,0:T(8,128)(2,1)S(1)}, bf16[144,768]{1,0:T(8,128)(2,1)S(1)}, u32[]{:S(2)}, u32[]{:S(2)}) collective-permute-start(bf16[144,768]{1,0:T(8,128)(2,1)S(1)} %get-tuple-element.133), channel_id=1, source_target_pairs={{0,2},{1,3},{2,0},{3,1},{4,6},{5,7},{6,4},{7,5},{8,10},{9,11},{10,... | collective-permute-start | bytes 663560 | tf_op jit(solution)/shard_map/ppermute | solution.py:35
  103.0 2.7 %collective-permute-start.40 = (bf16[144,768]{1,0:T(8,128)(2,1)S(1)}, bf16[144,768]{1,0:T(8,128)(2,1)S(1)}, u32[]{:S(2)}, u32[]{:S(2)}) collective-permute-start(bf16[144,768]{1,0:T(8,128)(2,1)S(1)} %get-tuple-element.145), channel_id=1, source_target_pairs={{0,6},{1,7},{2,4},{3,5},{4,2},{5,3},{6,0},{7,1},{8,14},{9,15},{10,... | collective-permute-start | bytes 663560 | tf_op jit(solution)/shard_map/ppermute | solution.py:35
  105.7 3.5 %collective-permute-done.20.rec = bf16[2,192,384]{2,1,0:T(8,128)(2,1)S(1)} collective-permute-done((bf16[2,192,384]{2,1,0:T(8,128)(2,1)S(1)}, bf16[2,192,384]{2,1,0:T(8,128)(2,1)S(1)}, u32[]{:S(2)}, u32[]{:S(2)}) %collective-permute-start.20) | collective-permute-done | bytes 294944 | tf_op jit(solution)/shard_map/ppermute | solution.py:35
  109.3 3.0 %collective-permute-start.21 = (bf16[1,192,384]{2,1,0:T(8,128)(2,1)S(1)}, bf16[1,192,384]{2,1,0:T(8,128)(2,1)S(1)}, u32[]{:S(2)}, u32[]{:S(2)}) collective-permute-start(bf16[1,192,384]{2,1,0:T(8,128)(2,1)S(1)} %get-tuple-element.109), channel_id=1, source_target_pairs={{0,24},{8,16},{16,8},{24,0},{1,25},{9,17},{17,9},{25,1},{2,26},{10... | collective-permute-start | bytes 442376 | tf_op jit(solution)/shard_map/ppermute | solution.py:35
  112.3 1.1 collective-permute-start.31
  113.8 2.2 %collective-permute-done.21.rec = bf16[1,192,384]{2,1,0:T(8,128)(2,1)S(1)} collective-permute-done((bf16[1,192,384]{2,1,0:T(8,128)(2,1)S(1)}, bf16[1,192,384]{2,1,0:T(8,128)(2,1)S(1)}, u32[]{:S(2)}, u32[]{:S(2)}) %collective-permute-start.21) | collective-permute-done | bytes 147488 | tf_op jit(solution)/shard_map/ppermute | solution.py:35
  116.0 2.5 %collective-permute-done.31.front_rec = bf16[80,768]{1,0:T(8,128)(2,1)S(1)} collective-permute-done((bf16[80,768]{1,0:T(8,128)(2,1)S(1)}, bf16[80,768]{1,0:T(8,128)(2,1)S(1)}, u32[]{:S(2)}, u32[]{:S(2)}) %collective-permute-start.31) | collective-permute-done | bytes 122912 | tf_op jit(solution)/shard_map/ppermute | solution.py:35
  119.2 1.9 %collective-permute-start.45 = (bf16[176,384]{1,0:T(8,128)(2,1)S(1)}, bf16[176,384]{1,0:T(8,128)(2,1)S(1)}, u32[]{:S(2)}, u32[]{:S(2)}) collective-permute-start(bf16[176,384]{1,0:T(8,128)(2,1)S(1)} %get-tuple-element.149.own), channel_id=1, source_target_pairs={{0,96},{32,64},{64,32},{96,0},{1,97},{33,65},{65,33},{97,1},{2,98}... | collective-permute-start | bytes 405512 | tf_op jit(solution)/shard_map/ppermute | solution.py:35
  121.1 2.6 %collective-permute-done.35.rec = bf16[176,384]{1,0:T(8,128)(2,1)S(1)} collective-permute-done((bf16[176,384]{1,0:T(8,128)(2,1)S(1)}, bf16[176,384]{1,0:T(8,128)(2,1)S(1)}, u32[]{:S(2)}, u32[]{:S(2)}) %collective-permute-start.35) | collective-permute-done | bytes 135200 | tf_op jit(solution)/shard_map/ppermute | solution.py:35
  124.2 1.1 collective-permute-done.32.rec
  125.3 0.8 collective-permute-start.33
  126.1 2.4 %collective-permute-start.46 = (bf16[272,384]{1,0:T(8,128)(2,1)S(1)}, bf16[272,384]{1,0:T(8,128)(2,1)S(1)}, u32[]{:S(2)}, u32[]{:S(2)}) collective-permute-start(bf16[272,384]{1,0:T(8,128)(2,1)S(1)} %shard_map.163.own), channel_id=1, source_target_pairs={{0,8},{8,0},{16,24},{24,16},{1,9},{9,1},{17,25},{25,17},{2,10},{10... | collective-permute-start | bytes 626696 | tf_op jit(solution)/shard_map/ppermute | solution.py:35
  128.7 2.1 %collective-permute-done.36.rec = bf16[272,384]{1,0:T(8,128)(2,1)S(1)} collective-permute-done((bf16[272,384]{1,0:T(8,128)(2,1)S(1)}, bf16[272,384]{1,0:T(8,128)(2,1)S(1)}, u32[]{:S(2)}, u32[]{:S(2)}) %collective-permute-start.36) | collective-permute-done | bytes 208928 | tf_op jit(solution)/shard_map/ppermute | solution.py:35
  131.4 2.4 %collective-permute-done.33.rec = bf16[272,384]{1,0:T(8,128)(2,1)S(1)} collective-permute-done((bf16[272,384]{1,0:T(8,128)(2,1)S(1)}, bf16[272,384]{1,0:T(8,128)(2,1)S(1)}, u32[]{:S(2)}, u32[]{:S(2)}) %collective-permute-start.33) | collective-permute-done | bytes 208928 | tf_op jit(solution)/shard_map/ppermute | solution.py:35
  134.2 2.6 %collective-permute-start.47 = (bf16[464,384]{1,0:T(8,128)(2,1)S(1)}, bf16[464,384]{1,0:T(8,128)(2,1)S(1)}, u32[]{:S(2)}, u32[]{:S(2)}) collective-permute-start(bf16[464,384]{1,0:T(8,128)(2,1)S(1)} %shard_map.164.own), channel_id=1, source_target_pairs={{0,32},{32,0},{64,96},{96,64},{1,33},{33,1},{65,97},{97,65},{2,34}... | collective-permute-start | bytes 1069064 | tf_op jit(solution)/shard_map/ppermute | solution.py:35
  136.8 2.1 %collective-permute-start.44 = (bf16[464,384]{1,0:T(8,128)(2,1)S(1)}, bf16[464,384]{1,0:T(8,128)(2,1)S(1)}, u32[]{:S(2)}, u32[]{:S(2)}) collective-permute-start(bf16[464,384]{1,0:T(8,128)(2,1)S(1)} %shard_map.161.own), channel_id=1, source_target_pairs={{0,24},{8,16},{16,8},{24,0},{1,25},{9,17},{17,9},{25,1},{2,26},{10... | collective-permute-start | bytes 1069064 | tf_op jit(solution)/shard_map/ppermute | solution.py:35
  138.9 1.2 collective-permute-done.37.rec
  140.2 3.0 %collective-permute-done.34.rec = bf16[464,384]{1,0:T(8,128)(2,1)S(1)} collective-permute-done((bf16[464,384]{1,0:T(8,128)(2,1)S(1)}, bf16[464,384]{1,0:T(8,128)(2,1)S(1)}, u32[]{:S(2)}, u32[]{:S(2)}) %collective-permute-start.34) | collective-permute-done | bytes 356384 | tf_op jit(solution)/shard_map/ppermute | solution.py:35
  143.3 3.9 %collective-permute-start.48 = (bf16[848,384]{1,0:T(8,128)(2,1)S(1)}, bf16[848,384]{1,0:T(8,128)(2,1)S(1)}, u32[]{:S(2)}, u32[]{:S(2)}) collective-permute-start(bf16[848,384]{1,0:T(8,128)(2,1)S(1)} %shard_map.152.refs_0_), channel_id=1, source_target_pairs={{0,32},{32,0},{64,96},{96,64},{1,33},{33,1},{65,97},{97,65},{2,34}... | collective-permute-start | bytes 1953800 | tf_op jit(solution)/shard_map/ppermute | solution.py:35
  147.3 1.5 collective-permute-done.44.rec
  148.9 3.0 %collective-permute-start.50 = (bf16[848,384]{1,0:T(8,128)(2,1)S(1)}, bf16[848,384]{1,0:T(8,128)(2,1)S(1)}, u32[]{:S(2)}, u32[]{:S(2)}) collective-permute-start(bf16[848,384]{1,0:T(8,128)(2,1)S(1)} %shard_map.162.refs_2_), channel_id=1, source_target_pairs={{0,96},{32,64},{64,32},{96,0},{1,97},{33,65},{65,33},{97,1},{2,98}... | collective-permute-start | bytes 1953800 | tf_op jit(solution)/shard_map/ppermute | solution.py:35
  151.9 2.8 %shard_map.166 = (f32[768,1536]{1,0:T(8,128)}, f32[1536,768]{1,0:T(8,128)}) custom-call(bf16[848,384]{1,0:T(8,128)(2,1)S(1)} %shard_map.152.refs_0_, bf16[848,384]{1,0:T(8,128)(2,1)S(1)} %shard_map.155.refs_1_, bf16[848,384]{1,0:T(8,128)(2,1)S(1)} %shard_map.162.refs_2_, bf16[848,384]{1,0:T(8,128)(2,1)S(1)} %shard_map.165.refs_3_), custom_call_target="tpu_custom_call" | custom-call | flops 1048576 | bytes 7340032 | tf_op jit(solution)/shard_map/pallas_call | solution.py:399
  154.7 0.7 collective-permute-done.49.refs_5_
  156.0 3.4 %collective-permute-done.51.refs_7_ = bf16[848,384]{1,0:T(8,128)(2,1)S(1)} collective-permute-done((bf16[848,384]{1,0:T(8,128)(2,1)S(1)}, bf16[848,384]{1,0:T(8,128)(2,1)S(1)}, u32[]{:S(2)}, u32[]{:S(2)}) %collective-permute-start.51) | collective-permute-done | bytes 651296 | tf_op jit(solution)/shard_map/ppermute | solution.py:35
  159.4 1.3 collective-permute-done.50.refs_6_
  160.7 3.0 %shard_map.167 = (f32[768,1536]{1,0:T(8,128)}, f32[1536,768]{1,0:T(8,128)}, f32[64,1536]{1,0:T(8,128)}, f32[5,1536]{1,0:T(8,128)}, f32[1536]{0:T(1024)}) custom-call(bf16[848,384]{1,0:T(8,128)(2,1)S(1)} %shard_map.152.refs_0_, bf16[848,384]{1,0:T(8,128)(2,1)S(1)} %shard_map.155.refs_1_, ...), custom_call_target="tpu_custom_call", output_to_operand_aliasing={{0}: (8, {}), {1}: (9, {})} | custom-call | flops 1048576 | bytes 7340032 | tf_op jit(solution)/shard_map/pallas_call | solution.py:408
  (98 shorter events, 8.9 us)
Async XLA Ops:
  0.6 20.7 %copy-start.5 = (bf16[64,1536]{1,0:T(8,128)(2,1)S(1)}, bf16[64,1536]{1,0:T(8,128)(2,1)}, u32[]{:S(2)}) copy-start(bf16[64,1536]{1,0:T(8,128)(2,1)} %param.12) | copy-start | bytes 589828
  3.3 9.3 %collective-permute-start = (bf16[640,128]{1,0:T(8,128)(2,1)}, bf16[640,128]{1,0:T(8,128)(2,1)S(1)}, u32[]{:S(2)}, u32[]{:S(2)}) collective-permute-start(bf16[640,128]{1,0:T(8,128)(2,1)} %get-tuple-element.82), channel_id=1, source_target_pairs={{0,16},{8,24},{16,0},{24,8},{1,17},{9,25},{17,1},{25,9},{2,18},{10... | collective-permute-start | bytes 491528 | tf_op jit(solution)/shard_map/ppermute | solution.py:35
  7.3 8.7 %collective-permute-start.1 = (bf16[640,128]{1,0:T(8,128)(2,1)}, bf16[640,128]{1,0:T(8,128)(2,1)S(1)}, u32[]{:S(2)}, u32[]{:S(2)}) collective-permute-start(bf16[640,128]{1,0:T(8,128)(2,1)} %get-tuple-element.83), channel_id=1, source_target_pairs={{0,8},{8,0},{16,24},{24,16},{1,9},{9,1},{17,25},{25,17},{2,10},{10... | collective-permute-start | bytes 491528 | tf_op jit(solution)/shard_map/ppermute | solution.py:35
  8.3 7.7 %collective-permute-start.2 = (bf16[640,128]{1,0:T(8,128)(2,1)}, bf16[640,128]{1,0:T(8,128)(2,1)S(1)}, u32[]{:S(2)}, u32[]{:S(2)}) collective-permute-start(bf16[640,128]{1,0:T(8,128)(2,1)} %get-tuple-element.84), channel_id=1, source_target_pairs={{0,24},{8,16},{16,8},{24,0},{1,25},{9,17},{17,9},{25,1},{2,26},{10... | collective-permute-start | bytes 491528 | tf_op jit(solution)/shard_map/ppermute | solution.py:35
  8.3 12.9 %collective-permute-start.9 = (bf16[64,1536]{1,0:T(8,128)(2,1)}, bf16[64,1536]{1,0:T(8,128)(2,1)S(1)}, u32[]{:S(2)}, u32[]{:S(2)}) collective-permute-start(bf16[64,1536]{1,0:T(8,128)(2,1)} %param.12), channel_id=1, source_target_pairs={{0,4},{1,5},{2,6},{3,7},{4,0},{5,1},{6,2},{7,3},{8,12},{9,13},{10,... | collective-permute-start | bytes 589832 | tf_op jit(solution)/shard_map/ppermute | solution.py:35
  11.3 9.9 %collective-permute-start.8 = (bf16[64,1536]{1,0:T(8,128)(2,1)}, bf16[64,1536]{1,0:T(8,128)(2,1)S(1)}, u32[]{:S(2)}, u32[]{:S(2)}) collective-permute-start(bf16[64,1536]{1,0:T(8,128)(2,1)} %param.12), channel_id=1, source_target_pairs={{0,6},{1,7},{2,4},{3,5},{4,2},{5,3},{6,0},{7,1},{8,14},{9,15},{10,... | collective-permute-start | bytes 589832 | tf_op jit(solution)/shard_map/ppermute | solution.py:35
  12.5 8.7 %collective-permute-start.7 = (bf16[64,1536]{1,0:T(8,128)(2,1)}, bf16[64,1536]{1,0:T(8,128)(2,1)S(1)}, u32[]{:S(2)}, u32[]{:S(2)}) collective-permute-start(bf16[64,1536]{1,0:T(8,128)(2,1)} %param.12), channel_id=1, source_target_pairs={{0,2},{1,3},{2,0},{3,1},{4,6},{5,7},{6,4},{7,5},{8,10},{9,11},{10,... | collective-permute-start | bytes 589832 | tf_op jit(solution)/shard_map/ppermute | solution.py:35
  16.0 0.9 copy-start.3
  17.0 10.8 %copy-start.6 = (f32[1536]{0:T(1024)S(1)}, f32[1536]{0:T(1024)}, u32[]{:S(2)}) copy-start(f32[1536]{0:T(1024)} %param.14) | copy-start | bytes 18436
  17.0 10.9 %copy-start.2 = (bf16[1,128,1536]{2,1,0:T(8,128)(2,1)S(1)}, bf16[1,128,1536]{2,1,0:T(8,128)(2,1)}, u32[]{:S(2)}) copy-start(bf16[1,128,1536]{2,1,0:T(8,128)(2,1)} %param.17) | copy-start | bytes 1179652
  17.0 15.2 %copy-start.4 = (f32[5,1536]{1,0:T(8,128)S(1)}, f32[5,1536]{1,0:T(8,128)}, u32[]{:S(2)}) copy-start(f32[5,1536]{1,0:T(8,128)} %kern_ref.3) | copy-start | bytes 92164
  17.0 7.7 %collective-permute-start.5 = (bf16[640,128]{1,0:T(8,128)(2,1)S(1)}, bf16[640,128]{1,0:T(8,128)(2,1)S(1)}, u32[]{:S(2)}, u32[]{:S(2)}) collective-permute-start(bf16[640,128]{1,0:T(8,128)(2,1)S(1)} %shard_map.129), channel_id=1, source_target_pairs={{0,4},{1,5},{2,6},{3,7},{4,0},{5,1},{6,2},{7,3},{8,12},{9,13},{10,... | collective-permute-start | bytes 491528 | tf_op jit(solution)/shard_map/ppermute | solution.py:35
  20.1 7.5 %collective-permute-start.4 = (bf16[640,128]{1,0:T(8,128)(2,1)S(1)}, bf16[640,128]{1,0:T(8,128)(2,1)S(1)}, u32[]{:S(2)}, u32[]{:S(2)}) collective-permute-start(bf16[640,128]{1,0:T(8,128)(2,1)S(1)} %shard_map.129), channel_id=1, source_target_pairs={{0,6},{1,7},{2,4},{3,5},{4,2},{5,3},{6,0},{7,1},{8,14},{9,15},{10,... | collective-permute-start | bytes 491528 | tf_op jit(solution)/shard_map/ppermute | solution.py:35
  21.3 6.4 %collective-permute-start.3 = (bf16[640,128]{1,0:T(8,128)(2,1)S(1)}, bf16[640,128]{1,0:T(8,128)(2,1)S(1)}, u32[]{:S(2)}, u32[]{:S(2)}) collective-permute-start(bf16[640,128]{1,0:T(8,128)(2,1)S(1)} %shard_map.129), channel_id=1, source_target_pairs={{0,2},{1,3},{2,0},{3,1},{4,6},{5,7},{6,4},{7,5},{8,10},{9,11},{10,... | collective-permute-start | bytes 491528 | tf_op jit(solution)/shard_map/ppermute | solution.py:35
  21.4 10.8 %collective-permute-start.10 = (bf16[4,64,1536]{2,1,0:T(8,128)(2,1)S(1)}, bf16[4,64,1536]{2,1,0:T(8,128)(2,1)S(1)}, u32[]{:S(2)}, u32[]{:S(2)}) collective-permute-start(bf16[4,64,1536]{2,1,0:T(8,128)(2,1)S(1)} %pad_maximum_fusion.1.wa_ref), channel_id=1, source_target_pairs={{0,1},{1,0},{2,3},{3,2},{4,5},{5,4},{6,7},{7,6},{8,9},{9,8},{10,11... | collective-permute-start | bytes 2359304 | tf_op jit(solution)/shard_map/ppermute | solution.py:35
  27.7 3.9 %collective-permute-start.6 = (bf16[4,640,128]{2,1,0:T(8,128)(2,1)S(1)}, bf16[4,640,128]{2,1,0:T(8,128)(2,1)S(1)}, u32[]{:S(2)}, u32[]{:S(2)}) collective-permute-start(bf16[4,640,128]{2,1,0:T(8,128)(2,1)S(1)} %pad_maximum_fusion.2.a_ref), channel_id=1, source_target_pairs={{0,1},{1,0},{2,3},{3,2},{4,5},{5,4},{6,7},{7,6},{8,9},{9,8},{10,11... | collective-permute-start | bytes 1966088 | tf_op jit(solution)/shard_map/ppermute | solution.py:35
  27.9 13.8 %copy-start = (bf16[1536,768]{1,0:T(8,128)(2,1)S(1)}, bf16[1536,768]{1,0:T(8,128)(2,1)}, u32[]{:S(2)}) copy-start(bf16[1536,768]{1,0:T(8,128)(2,1)} %up_ref.5) | copy-start | bytes 7077892
  27.9 13.8 %copy-start.1 = (bf16[768,1536]{1,0:T(8,128)(2,1)S(1)}, bf16[768,1536]{1,0:T(8,128)(2,1)}, u32[]{:S(2)}) copy-start(bf16[768,1536]{1,0:T(8,128)(2,1)} %down_ref.5) | copy-start | bytes 7077892
  27.9 17.4 %collective-permute-start.14 = (bf16[128,1536]{1,0:T(8,128)(2,1)S(1)}, bf16[128,1536]{1,0:T(8,128)(2,1)S(1)}, u32[]{:S(2)}, u32[]{:S(2)}) collective-permute-start(bf16[128,1536]{1,0:T(8,128)(2,1)S(1)} %bitcast.17), channel_id=1, source_target_pairs={{0,5},{1,4},{2,7},{3,6},{4,1},{5,0},{6,3},{7,2},{8,13},{9,12},{10,... | collective-permute-start | bytes 1179656 | tf_op jit(solution)/shard_map/ppermute | solution.py:35
  30.0 19.3 %collective-permute-start.13 = (bf16[128,1536]{1,0:T(8,128)(2,1)S(1)}, bf16[128,1536]{1,0:T(8,128)(2,1)S(1)}, u32[]{:S(2)}, u32[]{:S(2)}) collective-permute-start(bf16[128,1536]{1,0:T(8,128)(2,1)S(1)} %bitcast.18), channel_id=1, source_target_pairs={{0,7},{1,6},{2,5},{3,4},{4,3},{5,2},{6,1},{7,0},{8,15},{9,14},{10,... | collective-permute-start | bytes 1179656 | tf_op jit(solution)/shard_map/ppermute | solution.py:35
  31.7 17.6 %collective-permute-start.12 = (bf16[128,1536]{1,0:T(8,128)(2,1)S(1)}, bf16[128,1536]{1,0:T(8,128)(2,1)S(1)}, u32[]{:S(2)}, u32[]{:S(2)}) collective-permute-start(bf16[128,1536]{1,0:T(8,128)(2,1)S(1)} %bitcast.19), channel_id=1, source_target_pairs={{0,3},{1,2},{2,1},{3,0},{4,7},{5,6},{6,5},{7,4},{8,11},{9,10},{10,... | collective-permute-start | bytes 1179656 | tf_op jit(solution)/shard_map/ppermute | solution.py:35
  31.7 17.6 %collective-permute-start.11 = (bf16[128,1536]{1,0:T(8,128)(2,1)S(1)}, bf16[128,1536]{1,0:T(8,128)(2,1)S(1)}, u32[]{:S(2)}, u32[]{:S(2)}) collective-permute-start(bf16[128,1536]{1,0:T(8,128)(2,1)S(1)} %bitcast.20), channel_id=1, source_target_pairs={{0,1},{1,0},{2,3},{3,2},{4,5},{5,4},{6,7},{7,6},{8,9},{9,8},{10,11... | collective-permute-start | bytes 1179656 | tf_op jit(solution)/shard_map/ppermute | solution.py:35
  49.5 4.0 %collective-permute-start.15 = (bf16[4,128,1536]{2,1,0:T(8,128)(2,1)S(1)}, bf16[4,128,1536]{2,1,0:T(8,128)(2,1)S(1)}, u32[]{:S(2)}, u32[]{:S(2)}) collective-permute-start(bf16[4,128,1536]{2,1,0:T(8,128)(2,1)S(1)} %pad_maximum_fusion.cot_ref.cb_ref), channel_id=1, source_target_pairs={{0,1},{1,0},{2,3},{3,2},{4,5},{5,4},{6,7},{7,6},{8,9},{9,8},{10,11... | collective-permute-start | bytes 4718600 | tf_op jit(solution)/shard_map/ppermute | solution.py:35
  53.0 7.1 %collective-permute-start.22 = (bf16[512,1536]{1,0:T(8,128)(2,1)S(1)}, bf16[512,1536]{1,0:T(8,128)(2,1)S(1)}, u32[]{:S(2)}, u32[]{:S(2)}) collective-permute-start(bf16[512,1536]{1,0:T(8,128)(2,1)S(1)} %get-tuple-element.111), channel_id=1, source_target_pairs={{0,1},{1,0},{2,3},{3,2},{4,5},{5,4},{6,7},{7,6},{8,9},{9,8},{10,11... | collective-permute-start | bytes 4718600 | tf_op jit(solution)/shard_map/ppermute | solution.py:35
  58.5 15.4 %collective-permute-start.16 = (bf16[8,96,384]{2,1,0:T(8,128)(2,1)S(1)}, bf16[8,96,384]{2,1,0:T(8,128)(2,1)S(1)}, u32[]{:S(2)}, u32[]{:S(2)}) collective-permute-start(bf16[8,96,384]{2,1,0:T(8,128)(2,1)S(1)} %get-tuple-element.99), channel_id=1, source_target_pairs={{0,32},{32,0},{64,96},{96,64},{1,33},{33,1},{65,97},{97,65},{2,34}... | collective-permute-start | bytes 1769480 | tf_op jit(solution)/shard_map/ppermute | solution.py:35
  60.5 19.4 %collective-permute-start.23 = (bf16[256,1536]{1,0:T(8,128)(2,1)S(1)}, bf16[256,1536]{1,0:T(8,128)(2,1)S(1)}, u32[]{:S(2)}, u32[]{:S(2)}) collective-permute-start(bf16[256,1536]{1,0:T(8,128)(2,1)S(1)} %get-tuple-element.113), channel_id=1, source_target_pairs={{0,2},{1,3},{2,0},{3,1},{4,6},{5,7},{6,4},{7,5},{8,10},{9,11},{10,... | collective-permute-start | bytes 2359304 | tf_op jit(solution)/shard_map/ppermute | solution.py:35
  63.7 14.9 %collective-permute-start.18 = (bf16[8,96,384]{2,1,0:T(8,128)(2,1)S(1)}, bf16[8,96,384]{2,1,0:T(8,128)(2,1)S(1)}, u32[]{:S(2)}, u32[]{:S(2)}) collective-permute-start(bf16[8,96,384]{2,1,0:T(8,128)(2,1)S(1)} %get-tuple-element.103), channel_id=1, source_target_pairs={{0,8},{8,0},{16,24},{24,16},{1,9},{9,1},{17,25},{25,17},{2,10},{10... | collective-permute-start | bytes 1769480 | tf_op jit(solution)/shard_map/ppermute | solution.py:35
  66.6 17.4 %collective-permute-start.27 = (bf16[8,96,384]{2,1,0:T(8,128)(2,1)S(1)}, bf16[8,96,384]{2,1,0:T(8,128)(2,1)S(1)}, u32[]{:S(2)}, u32[]{:S(2)}) collective-permute-start(bf16[8,96,384]{2,1,0:T(8,128)(2,1)S(1)} %get-tuple-element.122), channel_id=1, source_target_pairs={{0,24},{8,16},{16,8},{24,0},{1,25},{9,17},{17,9},{25,1},{2,26},{10... | collective-permute-start | bytes 1769480 | tf_op jit(solution)/shard_map/ppermute | solution.py:35
  71.3 16.1 %collective-permute-start.25 = (bf16[8,96,384]{2,1,0:T(8,128)(2,1)S(1)}, bf16[8,96,384]{2,1,0:T(8,128)(2,1)S(1)}, u32[]{:S(2)}, u32[]{:S(2)}) collective-permute-start(bf16[8,96,384]{2,1,0:T(8,128)(2,1)S(1)} %get-tuple-element.120), channel_id=1, source_target_pairs={{0,96},{32,64},{64,32},{96,0},{1,97},{33,65},{65,33},{97,1},{2,98}... | collective-permute-start | bytes 1769480 | tf_op jit(solution)/shard_map/ppermute | solution.py:35
  80.0 15.7 %collective-permute-start.24 = (bf16[128,1536]{1,0:T(8,128)(2,1)S(1)}, bf16[128,1536]{1,0:T(8,128)(2,1)S(1)}, u32[]{:S(2)}, u32[]{:S(2)}) collective-permute-start(bf16[128,1536]{1,0:T(8,128)(2,1)S(1)} %get-tuple-element.119), channel_id=1, source_target_pairs={{0,6},{1,7},{2,4},{3,5},{4,2},{5,3},{6,0},{7,1},{8,14},{9,15},{10,... | collective-permute-start | bytes 1179656 | tf_op jit(solution)/shard_map/ppermute | solution.py:35
  82.5 8.0 %collective-permute-start.17 = (bf16[4,96,384]{2,1,0:T(8,128)(2,1)S(1)}, bf16[4,96,384]{2,1,0:T(8,128)(2,1)S(1)}, u32[]{:S(2)}, u32[]{:S(2)}) collective-permute-start(bf16[4,96,384]{2,1,0:T(8,128)(2,1)S(1)} %get-tuple-element.101), channel_id=1, source_target_pairs={{0,8},{8,0},{16,24},{24,16},{1,9},{9,1},{17,25},{25,17},{2,10},{10... | collective-permute-start | bytes 884744 | tf_op jit(solution)/shard_map/ppermute | solution.py:35
  83.5 7.3 %collective-permute-start.19 = (bf16[4,96,384]{2,1,0:T(8,128)(2,1)S(1)}, bf16[4,96,384]{2,1,0:T(8,128)(2,1)S(1)}, u32[]{:S(2)}, u32[]{:S(2)}) collective-permute-start(bf16[4,96,384]{2,1,0:T(8,128)(2,1)S(1)} %get-tuple-element.105), channel_id=1, source_target_pairs={{0,32},{32,0},{64,96},{96,64},{1,33},{33,1},{65,97},{97,65},{2,34}... | collective-permute-start | bytes 884744 | tf_op jit(solution)/shard_map/ppermute | solution.py:35
  84.1 9.0 %collective-permute-start.28 = (bf16[4,96,384]{2,1,0:T(8,128)(2,1)S(1)}, bf16[4,96,384]{2,1,0:T(8,128)(2,1)S(1)}, u32[]{:S(2)}, u32[]{:S(2)}) collective-permute-start(bf16[4,96,384]{2,1,0:T(8,128)(2,1)S(1)} %get-tuple-element.123), channel_id=1, source_target_pairs={{0,96},{32,64},{64,32},{96,0},{1,97},{33,65},{65,33},{97,1},{2,98}... | collective-permute-start | bytes 884744 | tf_op jit(solution)/shard_map/ppermute | solution.py:35
  87.6 8.1 %collective-permute-start.26 = (bf16[4,96,384]{2,1,0:T(8,128)(2,1)S(1)}, bf16[4,96,384]{2,1,0:T(8,128)(2,1)S(1)}, u32[]{:S(2)}, u32[]{:S(2)}) collective-permute-start(bf16[4,96,384]{2,1,0:T(8,128)(2,1)S(1)} %get-tuple-element.121), channel_id=1, source_target_pairs={{0,24},{8,16},{16,8},{24,0},{1,25},{9,17},{17,9},{25,1},{2,26},{10... | collective-permute-start | bytes 884744 | tf_op jit(solution)/shard_map/ppermute | solution.py:35
  98.5 2.4 %collective-permute-start.29 = (bf16[272,1536]{1,0:T(8,128)(2,1)S(1)}, bf16[272,1536]{1,0:T(8,128)(2,1)S(1)}, u32[]{:S(2)}, u32[]{:S(2)}) collective-permute-start(bf16[272,1536]{1,0:T(8,128)(2,1)S(1)} %get-tuple-element.131), channel_id=1, source_target_pairs={{0,1},{1,0},{2,3},{3,2},{4,5},{5,4},{6,7},{7,6},{8,9},{9,8},{10,11... | collective-permute-start | bytes 2506760 | tf_op jit(solution)/shard_map/ppermute | solution.py:35
  98.6 10.6 %collective-permute-start.20 = (bf16[2,192,384]{2,1,0:T(8,128)(2,1)S(1)}, bf16[2,192,384]{2,1,0:T(8,128)(2,1)S(1)}, u32[]{:S(2)}, u32[]{:S(2)}) collective-permute-start(bf16[2,192,384]{2,1,0:T(8,128)(2,1)S(1)} %get-tuple-element.107), channel_id=1, source_target_pairs={{0,96},{32,64},{64,32},{96,0},{1,97},{33,65},{65,33},{97,1},{2,98}... | collective-permute-start | bytes 884744 | tf_op jit(solution)/shard_map/ppermute | solution.py:35
  100.6 12.8 %collective-permute-start.38 = (bf16[2,192,384]{2,1,0:T(8,128)(2,1)S(1)}, bf16[2,192,384]{2,1,0:T(8,128)(2,1)S(1)}, u32[]{:S(2)}, u32[]{:S(2)}) collective-permute-start(bf16[2,192,384]{2,1,0:T(8,128)(2,1)S(1)} %get-tuple-element.141), channel_id=1, source_target_pairs={{0,32},{32,0},{64,96},{96,64},{1,33},{33,1},{65,97},{97,65},{2,34}... | collective-permute-start | bytes 884744 | tf_op jit(solution)/shard_map/ppermute | solution.py:35
  101.2 11.1 %collective-permute-start.30 = (bf16[144,768]{1,0:T(8,128)(2,1)S(1)}, bf16[144,768]{1,0:T(8,128)(2,1)S(1)}, u32[]{:S(2)}, u32[]{:S(2)}) collective-permute-start(bf16[144,768]{1,0:T(8,128)(2,1)S(1)} %get-tuple-element.133), channel_id=1, source_target_pairs={{0,2},{1,3},{2,0},{3,1},{4,6},{5,7},{6,4},{7,5},{8,10},{9,11},{10,... | collective-permute-start | bytes 663560 | tf_op jit(solution)/shard_map/ppermute | solution.py:35
  103.0 10.6 %collective-permute-start.40 = (bf16[144,768]{1,0:T(8,128)(2,1)S(1)}, bf16[144,768]{1,0:T(8,128)(2,1)S(1)}, u32[]{:S(2)}, u32[]{:S(2)}) collective-permute-start(bf16[144,768]{1,0:T(8,128)(2,1)S(1)} %get-tuple-element.145), channel_id=1, source_target_pairs={{0,6},{1,7},{2,4},{3,5},{4,2},{5,3},{6,0},{7,1},{8,14},{9,15},{10,... | collective-permute-start | bytes 663560 | tf_op jit(solution)/shard_map/ppermute | solution.py:35
  109.3 6.7 %collective-permute-start.21 = (bf16[1,192,384]{2,1,0:T(8,128)(2,1)S(1)}, bf16[1,192,384]{2,1,0:T(8,128)(2,1)S(1)}, u32[]{:S(2)}, u32[]{:S(2)}) collective-permute-start(bf16[1,192,384]{2,1,0:T(8,128)(2,1)S(1)} %get-tuple-element.109), channel_id=1, source_target_pairs={{0,24},{8,16},{16,8},{24,0},{1,25},{9,17},{17,9},{25,1},{2,26},{10... | collective-permute-start | bytes 442376 | tf_op jit(solution)/shard_map/ppermute | solution.py:35
  112.3 6.2 %collective-permute-start.31 = (bf16[80,768]{1,0:T(8,128)(2,1)S(1)}, bf16[80,768]{1,0:T(8,128)(2,1)S(1)}, u32[]{:S(2)}, u32[]{:S(2)}) collective-permute-start(bf16[80,768]{1,0:T(8,128)(2,1)S(1)} %get-tuple-element.135), channel_id=1, source_target_pairs={{0,6},{1,7},{2,4},{3,5},{4,2},{5,3},{6,0},{7,1},{8,14},{9,15},{10,... | collective-permute-start | bytes 368648 | tf_op jit(solution)/shard_map/ppermute | solution.py:35
  113.5 5.6 %collective-permute-start.39 = (bf16[1,192,384]{2,1,0:T(8,128)(2,1)S(1)}, bf16[1,192,384]{2,1,0:T(8,128)(2,1)S(1)}, u32[]{:S(2)}, u32[]{:S(2)}) collective-permute-start(bf16[1,192,384]{2,1,0:T(8,128)(2,1)S(1)} %get-tuple-element.143), channel_id=1, source_target_pairs={{0,8},{8,0},{16,24},{24,16},{1,9},{9,1},{17,25},{25,17},{2,10},{10... | collective-permute-start | bytes 442376 | tf_op jit(solution)/shard_map/ppermute | solution.py:35
  113.7 5.5 %collective-permute-start.41 = (bf16[80,768]{1,0:T(8,128)(2,1)S(1)}, bf16[80,768]{1,0:T(8,128)(2,1)S(1)}, u32[]{:S(2)}, u32[]{:S(2)}) collective-permute-start(bf16[80,768]{1,0:T(8,128)(2,1)S(1)} %get-tuple-element.147), channel_id=1, source_target_pairs={{0,2},{1,3},{2,0},{3,1},{4,6},{5,7},{6,4},{7,5},{8,10},{9,11},{10,... | collective-permute-start | bytes 368648 | tf_op jit(solution)/shard_map/ppermute | solution.py:35
  118.6 5.1 %collective-permute-start.35 = (bf16[176,384]{1,0:T(8,128)(2,1)S(1)}, bf16[176,384]{1,0:T(8,128)(2,1)S(1)}, u32[]{:S(2)}, u32[]{:S(2)}) collective-permute-start(bf16[176,384]{1,0:T(8,128)(2,1)S(1)} %get-tuple-element.137.own), channel_id=1, source_target_pairs={{0,32},{32,0},{64,96},{96,64},{1,33},{33,1},{65,97},{97,65},{2,34}... | collective-permute-start | bytes 405512 | tf_op jit(solution)/shard_map/ppermute | solution.py:35
  118.7 6.6 %collective-permute-start.32 = (bf16[176,384]{1,0:T(8,128)(2,1)S(1)}, bf16[176,384]{1,0:T(8,128)(2,1)S(1)}, u32[]{:S(2)}, u32[]{:S(2)}) collective-permute-start(bf16[176,384]{1,0:T(8,128)(2,1)S(1)} %get-tuple-element.136.own), channel_id=1, source_target_pairs={{0,24},{8,16},{16,8},{24,0},{1,25},{9,17},{17,9},{25,1},{2,26},{10... | collective-permute-start | bytes 405512 | tf_op jit(solution)/shard_map/ppermute | solution.py:35
  119.2 6.9 %collective-permute-start.45 = (bf16[176,384]{1,0:T(8,128)(2,1)S(1)}, bf16[176,384]{1,0:T(8,128)(2,1)S(1)}, u32[]{:S(2)}, u32[]{:S(2)}) collective-permute-start(bf16[176,384]{1,0:T(8,128)(2,1)S(1)} %get-tuple-element.149.own), channel_id=1, source_target_pairs={{0,96},{32,64},{64,32},{96,0},{1,97},{33,65},{65,33},{97,1},{2,98}... | collective-permute-start | bytes 405512 | tf_op jit(solution)/shard_map/ppermute | solution.py:35
  121.1 7.5 %collective-permute-start.42 = (bf16[176,384]{1,0:T(8,128)(2,1)S(1)}, bf16[176,384]{1,0:T(8,128)(2,1)S(1)}, u32[]{:S(2)}, u32[]{:S(2)}) collective-permute-start(bf16[176,384]{1,0:T(8,128)(2,1)S(1)} %get-tuple-element.148.own), channel_id=1, source_target_pairs={{0,8},{8,0},{16,24},{24,16},{1,9},{9,1},{17,25},{25,17},{2,10},{10... | collective-permute-start | bytes 405512 | tf_op jit(solution)/shard_map/ppermute | solution.py:35
  123.7 7.1 %collective-permute-start.36 = (bf16[272,384]{1,0:T(8,128)(2,1)S(1)}, bf16[272,384]{1,0:T(8,128)(2,1)S(1)}, u32[]{:S(2)}, u32[]{:S(2)}) collective-permute-start(bf16[272,384]{1,0:T(8,128)(2,1)S(1)} %shard_map.153.own), channel_id=1, source_target_pairs={{0,24},{8,16},{16,8},{24,0},{1,25},{9,17},{17,9},{25,1},{2,26},{10... | collective-permute-start | bytes 626696 | tf_op jit(solution)/shard_map/ppermute | solution.py:35
  125.3 8.6 %collective-permute-start.33 = (bf16[272,384]{1,0:T(8,128)(2,1)S(1)}, bf16[272,384]{1,0:T(8,128)(2,1)S(1)}, u32[]{:S(2)}, u32[]{:S(2)}) collective-permute-start(bf16[272,384]{1,0:T(8,128)(2,1)S(1)} %shard_map.150.own), channel_id=1, source_target_pairs={{0,96},{32,64},{64,32},{96,0},{1,97},{33,65},{65,33},{97,1},{2,98}... | collective-permute-start | bytes 626696 | tf_op jit(solution)/shard_map/ppermute | solution.py:35
  126.1 8.0 %collective-permute-start.46 = (bf16[272,384]{1,0:T(8,128)(2,1)S(1)}, bf16[272,384]{1,0:T(8,128)(2,1)S(1)}, u32[]{:S(2)}, u32[]{:S(2)}) collective-permute-start(bf16[272,384]{1,0:T(8,128)(2,1)S(1)} %shard_map.163.own), channel_id=1, source_target_pairs={{0,8},{8,0},{16,24},{24,16},{1,9},{9,1},{17,25},{25,17},{2,10},{10... | collective-permute-start | bytes 626696 | tf_op jit(solution)/shard_map/ppermute | solution.py:35
  128.6 8.1 %collective-permute-start.43 = (bf16[272,384]{1,0:T(8,128)(2,1)S(1)}, bf16[272,384]{1,0:T(8,128)(2,1)S(1)}, u32[]{:S(2)}, u32[]{:S(2)}) collective-permute-start(bf16[272,384]{1,0:T(8,128)(2,1)S(1)} %shard_map.160.own), channel_id=1, source_target_pairs={{0,32},{32,0},{64,96},{96,64},{1,33},{33,1},{65,97},{97,65},{2,34}... | collective-permute-start | bytes 626696 | tf_op jit(solution)/shard_map/ppermute | solution.py:35
  130.9 9.2 %collective-permute-start.37 = (bf16[464,384]{1,0:T(8,128)(2,1)S(1)}, bf16[464,384]{1,0:T(8,128)(2,1)S(1)}, u32[]{:S(2)}, u32[]{:S(2)}) collective-permute-start(bf16[464,384]{1,0:T(8,128)(2,1)S(1)} %shard_map.154.own), channel_id=1, source_target_pairs={{0,96},{32,64},{64,32},{96,0},{1,97},{33,65},{65,33},{97,1},{2,98}... | collective-permute-start | bytes 1069064 | tf_op jit(solution)/shard_map/ppermute | solution.py:35
  133.9 9.3 %collective-permute-start.34 = (bf16[464,384]{1,0:T(8,128)(2,1)S(1)}, bf16[464,384]{1,0:T(8,128)(2,1)S(1)}, u32[]{:S(2)}, u32[]{:S(2)}) collective-permute-start(bf16[464,384]{1,0:T(8,128)(2,1)S(1)} %shard_map.151.own), channel_id=1, source_target_pairs={{0,8},{8,0},{16,24},{24,16},{1,9},{9,1},{17,25},{25,17},{2,10},{10... | collective-permute-start | bytes 1069064 | tf_op jit(solution)/shard_map/ppermute | solution.py:35
  134.2 13.0 %collective-permute-start.47 = (bf16[464,384]{1,0:T(8,128)(2,1)S(1)}, bf16[464,384]{1,0:T(8,128)(2,1)S(1)}, u32[]{:S(2)}, u32[]{:S(2)}) collective-permute-start(bf16[464,384]{1,0:T(8,128)(2,1)S(1)} %shard_map.164.own), channel_id=1, source_target_pairs={{0,32},{32,0},{64,96},{96,64},{1,33},{33,1},{65,97},{97,65},{2,34}... | collective-permute-start | bytes 1069064 | tf_op jit(solution)/shard_map/ppermute | solution.py:35
  136.8 12.0 %collective-permute-start.44 = (bf16[464,384]{1,0:T(8,128)(2,1)S(1)}, bf16[464,384]{1,0:T(8,128)(2,1)S(1)}, u32[]{:S(2)}, u32[]{:S(2)}) collective-permute-start(bf16[464,384]{1,0:T(8,128)(2,1)S(1)} %shard_map.161.own), channel_id=1, source_target_pairs={{0,24},{8,16},{16,8},{24,0},{1,25},{9,17},{17,9},{25,1},{2,26},{10... | collective-permute-start | bytes 1069064 | tf_op jit(solution)/shard_map/ppermute | solution.py:35
  140.1 15.2 %collective-permute-start.49 = (bf16[848,384]{1,0:T(8,128)(2,1)S(1)}, bf16[848,384]{1,0:T(8,128)(2,1)S(1)}, u32[]{:S(2)}, u32[]{:S(2)}) collective-permute-start(bf16[848,384]{1,0:T(8,128)(2,1)S(1)} %shard_map.155.refs_1_), channel_id=1, source_target_pairs={{0,8},{8,0},{16,24},{24,16},{1,9},{9,1},{17,25},{25,17},{2,10},{10... | collective-permute-start | bytes 1953800 | tf_op jit(solution)/shard_map/ppermute | solution.py:35
  143.3 12.8 %collective-permute-start.48 = (bf16[848,384]{1,0:T(8,128)(2,1)S(1)}, bf16[848,384]{1,0:T(8,128)(2,1)S(1)}, u32[]{:S(2)}, u32[]{:S(2)}) collective-permute-start(bf16[848,384]{1,0:T(8,128)(2,1)S(1)} %shard_map.152.refs_0_), channel_id=1, source_target_pairs={{0,32},{32,0},{64,96},{96,64},{1,33},{33,1},{65,97},{97,65},{2,34}... | collective-permute-start | bytes 1953800 | tf_op jit(solution)/shard_map/ppermute | solution.py:35
  147.2 12.2 %collective-permute-start.51 = (bf16[848,384]{1,0:T(8,128)(2,1)S(1)}, bf16[848,384]{1,0:T(8,128)(2,1)S(1)}, u32[]{:S(2)}, u32[]{:S(2)}) collective-permute-start(bf16[848,384]{1,0:T(8,128)(2,1)S(1)} %shard_map.165.refs_3_), channel_id=1, source_target_pairs={{0,24},{8,16},{16,8},{24,0},{1,25},{9,17},{17,9},{25,1},{2,26},{10... | collective-permute-start | bytes 1953800 | tf_op jit(solution)/shard_map/ppermute | solution.py:35
  148.9 11.8 %collective-permute-start.50 = (bf16[848,384]{1,0:T(8,128)(2,1)S(1)}, bf16[848,384]{1,0:T(8,128)(2,1)S(1)}, u32[]{:S(2)}, u32[]{:S(2)}) collective-permute-start(bf16[848,384]{1,0:T(8,128)(2,1)S(1)} %shard_map.162.refs_2_), channel_id=1, source_target_pairs={{0,96},{32,64},{64,32},{96,0},{1,97},{33,65},{65,33},{97,1},{2,98}... | collective-permute-start | bytes 1953800 | tf_op jit(solution)/shard_map/ppermute | solution.py:35
